TPU v7x, 32 devices: a whole 2x2x4 slice. The times are simulated.
32 devices in a mesh: dp: 8 (over y, x, core), tensor: 4 (over z).
Axes of the slice: x: 2, y: 2, z: 4, core: 2. Of those that a mesh axis runs over, the one named last changes fastest.
Arguments:
- hidden_in: bfloat16 [8, 1024, 2048], P('dp', 'tensor'), may hold values from -6 to 6
- cotangent: bfloat16 [8, 1024, 2048], P('dp', 'tensor'), may hold values from -6 to 6
- lengths: int32 [8], replicated, may hold values from 1 to 1024, 5632 in all
- slot_of_seq: int32 [8], replicated, may hold values from 0 to 7, as said below
- seq_of_slot: int32 [8], replicated, may hold values from 0 to 7, as said below
- qkv_weight: bfloat16 [2048, 3, 2048], P('dp', None, 'tensor'), may hold values from -0.125 to 0.125
- out_weight: bfloat16 [2048, 2048], P('dp', 'tensor'), may hold values from -0.75 to 0.75
- fc1_weight: bfloat16 [2048, 8192], P('dp', 'tensor'), may hold values from -0.125 to 0.125
- fc2_weight: bfloat16 [2048, 8192], P('dp', 'tensor'), may hold values from -0.0625 to 0.0625
- ln_gain: bfloat16 [2048], P(('dp', 'tensor')), may hold values from 0.5 to 1.5
- ln_bias: bfloat16 [2048], P(('dp', 'tensor')), may hold values from -3 to 3
- qkv_bias: bfloat16 [6144], P(('dp', 'tensor')), may hold values from -3 to 3
- out_bias: bfloat16 [2048], P(('dp', 'tensor')), may hold values from -3 to 3
- fc1_bias: bfloat16 [8192], P(('dp', 'tensor')), may hold values from -3 to 3
- fc2_bias: bfloat16 [2048], P(('dp', 'tensor')), may hold values from -3 to 3
Outputs:
- block_out: bfloat16 [8, 1024, 2048], P('dp', 'tensor')
- grad_input: bfloat16 [8, 1024, 2048], P('dp', 'tensor')
- grad_qkv_weight: float32 [2048, 3, 2048], P('dp', None, 'tensor')
- grad_out_weight: float32 [2048, 2048], P('dp', 'tensor')
- grad_fc1_weight: float32 [2048, 8192], P('dp', 'tensor')
- grad_fc2_weight: float32 [2048, 8192], P('dp', 'tensor')
- grad_ln_gain: float32 [2048], P(('dp', 'tensor'))
- grad_ln_bias: float32 [2048], P(('dp', 'tensor'))
- grad_qkv_bias: float32 [6144], P(('dp', 'tensor'))
- grad_out_bias: float32 [2048], P(('dp', 'tensor'))
- grad_fc1_bias: float32 [8192], P(('dp', 'tensor'))
- grad_fc2_bias: float32 [2048], P(('dp', 'tensor'))
Inputs may be any that keep to these rules, and one draw needn't show every extreme that they name: 8 lengths that sum to 5632, the longest exactly 1024; sequence s fills positions 0 to lengths[s] - 1. A permutation: sequence s is computed in slot slot_of_seq[s]; slot p lies on index p // 1 of dp. `seq_of_slot`: the inverse permutation of slot_of_seq.
All inputs are finite; a program needn't handle non-finite values.
Results may differ from a plain program's by a relative error of at most 0.0086.
Values may be sent and summed in bfloat16 or wider, within the bound.
No kernel may reach another device: no remote copies, remote signals or barrier semaphores. Data moves between devices by JAX's collectives and lax.ppermute only.
A program may use at most 256 MiB of HBM per device.

v0:
```python
import math

import jax
import jax.numpy as jnp
from jax import lax
from jax.sharding import PartitionSpec as P

HEAD_DIM = 64
ROT = 32


eps = 1e-05
masked_score = -1e30


def rotary_tables(row_count, col_count):
    half_rot = ROT // 2
    column = jnp.arange(col_count) % HEAD_DIM
    exponent = (2 * (column % half_rot)).astype(jnp.float32) / ROT
    frequency = jnp.exp(-math.log(10000.0) * exponent)
    angles = jnp.arange(row_count).astype(jnp.float32)[:, None] * frequency[None, :]
    inside = column < ROT
    cosine = jnp.where(inside, jnp.cos(angles), 1.0)
    sine_part = jnp.sin(angles)
    ahead_sin = jnp.where(column < half_rot, -sine_part, 0.0)
    behind_sin = jnp.where(inside & (column >= half_rot), sine_part, 0.0)
    return (cosine, ahead_sin, behind_sin)


def rotate(field, tables):
    cosine, ahead_sin, behind_sin = tables
    half_rot = ROT // 2
    return (
        field * cosine
        + jnp.roll(field, -half_rot, axis=-1) * ahead_sin
        + jnp.roll(field, half_rot, axis=-1) * behind_sin
    )


def pick_rows(gathered, shard_rows, wanted):
    shard_count = shard_rows.shape[0]
    inside = (wanted >= 0) & (wanted < shard_count)
    picked = jnp.take(shard_rows, jnp.clip(wanted, 0, shard_count - 1), axis=0)
    return jnp.where(inside[:, None, None], picked, gathered)


def normalize(rows_in):
    row_mean = jnp.mean(rows_in, -1, keepdims=True)
    centred = rows_in - row_mean
    variance = jnp.mean(centred * centred, -1, keepdims=True)
    inv_scale = lax.rsqrt(variance + eps)
    return (centred * inv_scale, inv_scale)


def block_scores(queries, key_heads, first_row, block_rows, length):
    head_count = key_heads.shape[1]
    query_block = queries[first_row : first_row + block_rows].reshape(
        block_rows, head_count, HEAD_DIM
    )
    scores = jnp.einsum(
        "qhd,khd->hqk", query_block, key_heads, preferred_element_type=jnp.float32
    ) * (1.0 / math.sqrt(HEAD_DIM))
    row_ids = first_row + jnp.arange(block_rows, dtype=jnp.int32)
    col_ids = jnp.arange(key_heads.shape[0], dtype=jnp.int32)
    allowed = (col_ids[None, :] <= row_ids[:, None]) & (col_ids[None, :] < length)
    return (jnp.where(allowed[None], scores, masked_score), query_block)


def attend_forward(inputs):
    queries, key_rows, values, length = inputs
    seq_len = queries.shape[0]
    head_count = queries.shape[1] // HEAD_DIM
    key_heads = key_rows.reshape(seq_len, head_count, HEAD_DIM)
    value_heads = values.reshape(seq_len, head_count, HEAD_DIM)
    block_rows = min(512, seq_len)
    mixed_parts = []
    total_parts = []
    for first_row in range(0, seq_len, block_rows):
        scores, query_block = block_scores(queries, key_heads, first_row, block_rows, length)
        row_max = jnp.max(scores, -1, keepdims=True)
        exped = jnp.exp(scores - row_max)
        row_total = jnp.sum(exped, -1, keepdims=True)
        attn_probs = (exped / row_total).astype(jnp.bfloat16)
        attention_mixture = jnp.einsum(
            "hqk,khd->qhd", attn_probs, value_heads, preferred_element_type=jnp.float32
        )
        mixed_parts.append(attention_mixture.reshape(block_rows, head_count * HEAD_DIM))
        total_parts.append(row_max[..., 0] + jnp.log(row_total[..., 0]))
    return (jnp.concatenate(mixed_parts, 0).astype(jnp.bfloat16), jnp.concatenate(total_parts, 1))


def attend_backward(inputs):
    queries, key_rows, values, log_total, grad_mixed, length = inputs
    seq_len = queries.shape[0]
    head_count = queries.shape[1] // HEAD_DIM
    key_heads = key_rows.reshape(seq_len, head_count, HEAD_DIM)
    value_heads = values.reshape(seq_len, head_count, HEAD_DIM)
    block_rows = min(512, seq_len)
    score_scale = 1.0 / math.sqrt(HEAD_DIM)
    grad_query_parts = []
    grad_keys = jnp.zeros((seq_len, head_count, HEAD_DIM), jnp.float32)
    grad_values = jnp.zeros((seq_len, head_count, HEAD_DIM), jnp.float32)
    for first_row in range(0, seq_len, block_rows):
        scores, query_block = block_scores(queries, key_heads, first_row, block_rows, length)
        attn_probs = jnp.exp(scores - log_total[:, first_row : first_row + block_rows, None])
        grad_block = grad_mixed[first_row : first_row + block_rows].reshape(
            block_rows, head_count, HEAD_DIM
        )
        grad_probs = jnp.einsum(
            "qhd,khd->hqk", grad_block, value_heads, preferred_element_type=jnp.float32
        )
        grad_scores = (
            attn_probs * (grad_probs - jnp.sum(attn_probs * grad_probs, -1, keepdims=True))
        ).astype(jnp.bfloat16)
        grad_query = (
            jnp.einsum("hqk,khd->qhd", grad_scores, key_heads, preferred_element_type=jnp.float32)
            * score_scale
        )
        grad_query_parts.append(grad_query.reshape(block_rows, head_count * HEAD_DIM))
        grad_keys = (
            grad_keys
            + jnp.einsum(
                "hqk,qhd->khd", grad_scores, query_block, preferred_element_type=jnp.float32
            )
            * score_scale
        )
        grad_values = grad_values + jnp.einsum(
            "hqk,qhd->khd",
            attn_probs.astype(jnp.bfloat16),
            grad_block,
            preferred_element_type=jnp.float32,
        )
    return (
        jnp.concatenate(grad_query_parts, 0),
        grad_keys.reshape(seq_len, head_count * HEAD_DIM),
        grad_values.reshape(seq_len, head_count * HEAD_DIM),
    )


def activations(
    layernorm_rows,
    query_key_value_whole,
    first_linear_whole,
    bias_qkv,
    first_linear_bias,
    tables,
    slot_len,
):
    qkv_raw = (
        jnp.einsum(
            "mnv,voe->mnoe",
            layernorm_rows,
            query_key_value_whole,
            preferred_element_type=jnp.float32,
        )
        + bias_qkv
    )
    queries = rotate(qkv_raw[:, :, 0], tables).astype(jnp.bfloat16)
    key_rows = rotate(qkv_raw[:, :, 1], tables).astype(jnp.bfloat16)
    values = qkv_raw[:, :, 2].astype(jnp.bfloat16)
    attention_mixture, log_total = lax.map(attend_forward, (queries, key_rows, values, slot_len))
    pre_act = (
        jnp.einsum(
            "bjp,pv->bjv", layernorm_rows, first_linear_whole, preferred_element_type=jnp.float32
        )
        + first_linear_bias
    )
    hidden = jax.nn.gelu(pre_act, approximate=True).astype(jnp.bfloat16)
    return (queries, key_rows, values, attention_mixture, log_total, pre_act, hidden)


def shards(
    hidden_in,
    cotangent,
    lengths,
    slot_of_seq,
    seq_of_slot,
    qkv_weight,
    out_weight,
    fc1_weight,
    fc2_weight,
    ln_gain,
    ln_bias,
    qkv_bias,
    out_bias,
    fc1_bias,
    fc2_bias,
):
    per_index = hidden_in.shape[0]
    rows_here = hidden_in.shape[1]
    width = hidden_in.shape[2]
    tensor_count = lax.axis_size("tensor")
    tensor_index = lax.axis_index("tensor")
    data_index = lax.axis_index("dp")
    seq_len = rows_here * tensor_count
    heads_local = qkv_weight.shape[2]
    hidden_local = fc1_weight.shape[1]
    my_slots = data_index * per_index + jnp.arange(per_index, dtype=jnp.int32)
    sources = jnp.take(seq_of_slot, my_slots)
    slot_len = jnp.take(lengths, sources)
    targets = jnp.take(slot_of_seq, my_slots)
    routed = pick_rows(
        jnp.zeros_like(hidden_in), lax.all_gather(hidden_in, "dp", axis=0, tiled=True), sources
    )
    gain_full, shift_full, qkv_bias_full, out_bias_full, fc1_bias_full, fc2_bias_full = (
        lax.all_gather(ln_gain, ("dp", "tensor"), axis=0, tiled=True),
        lax.all_gather(ln_bias, ("dp", "tensor"), axis=0, tiled=True),
        lax.all_gather(qkv_bias, ("dp", "tensor"), axis=0, tiled=True),
        lax.all_gather(out_bias, ("dp", "tensor"), axis=0, tiled=True),
        lax.all_gather(fc1_bias, ("dp", "tensor"), axis=0, tiled=True),
        lax.all_gather(fc2_bias, ("dp", "tensor"), axis=0, tiled=True),
    )
    gain_full = gain_full.astype(jnp.float32)
    bias_qkv = lax.dynamic_slice_in_dim(
        qkv_bias_full.astype(jnp.float32).reshape(3, width),
        tensor_index * heads_local,
        heads_local,
        1,
    )
    first_linear_bias = lax.dynamic_slice_in_dim(
        fc1_bias_full.astype(jnp.float32), tensor_index * hidden_local, hidden_local, 0
    )
    slot_rows = routed.astype(jnp.float32)
    normed, inv_scale = normalize(slot_rows)
    ln_local = (normed * gain_full + shift_full.astype(jnp.float32)).astype(jnp.bfloat16)
    ln_full = lax.all_gather(ln_local, "tensor", axis=1, tiled=True)
    query_key_value_whole, output_whole, first_linear_whole, fc2_full = (
        lax.all_gather(qkv_weight, "dp", axis=0, tiled=True),
        lax.all_gather(out_weight, "dp", axis=0, tiled=True),
        lax.all_gather(fc1_weight, "dp", axis=0, tiled=True),
        lax.all_gather(fc2_weight, "dp", axis=0, tiled=True),
    )
    tables = rotary_tables(seq_len, heads_local)
    queries, key_rows, values, attention_mixture, log_total, pre_act, hidden = activations(
        ln_full,
        query_key_value_whole,
        first_linear_whole,
        bias_qkv,
        first_linear_bias,
        tables,
        slot_len,
    )
    partial_value = jnp.einsum(
        "xhj,zj->xhz", attention_mixture, output_whole, preferred_element_type=jnp.float32
    ) + jnp.einsum("slf,ef->sle", hidden, fc2_full, preferred_element_type=jnp.float32)
    summed = lax.psum_scatter(partial_value, "tensor", scatter_dimension=1, tiled=True)
    positions = tensor_index * rows_here + jnp.arange(rows_here, dtype=jnp.int32)
    valid = (positions[None, :] < slot_len[:, None])[:, :, None]
    branch = summed + out_bias_full.astype(jnp.float32) + fc2_bias_full.astype(jnp.float32)
    block_out = (slot_rows + jnp.where(valid, branch, 0.0)).astype(jnp.bfloat16)
    grad_rows = jnp.where(valid, cotangent.astype(jnp.float32), 0.0)
    grad_bias = jnp.sum(grad_rows, axis=(0, 1))
    grad_low = grad_rows.astype(jnp.bfloat16)
    whole_gradient = lax.all_gather(grad_low, "tensor", axis=1, tiled=True)
    grad_mixed = jnp.einsum(
        "wix,xa->wia", whole_gradient, output_whole, preferred_element_type=jnp.float32
    ).astype(jnp.bfloat16)
    output_weight_gradient = jnp.einsum(
        "rav,rac->vc", whole_gradient, attention_mixture, preferred_element_type=jnp.float32
    )
    grad_hidden = jnp.einsum(
        "sle,ef->slf", whole_gradient, fc2_full, preferred_element_type=jnp.float32
    )
    grad_fc2_w = jnp.einsum(
        "sle,slf->ef", whole_gradient, hidden, preferred_element_type=jnp.float32
    )
    _, gelu_pull = jax.vjp(lambda inputs: jax.nn.gelu(inputs, approximate=True), pre_act)
    preactivation_gradient = gelu_pull(grad_hidden)[0].astype(jnp.bfloat16)
    grad_fc1_b = jnp.sum(preactivation_gradient, axis=(0, 1), dtype=jnp.float32)
    first_linear_weight_gradient = jnp.einsum(
        "hwj,hwy->jy", ln_full, preactivation_gradient, preferred_element_type=jnp.float32
    )
    layernorm_gradient = jnp.einsum(
        "mig,qg->miq",
        preactivation_gradient,
        first_linear_whole,
        preferred_element_type=jnp.float32,
    )
    grad_query, grad_keys, grad_values = lax.map(
        attend_backward, (queries, key_rows, values, log_total, grad_mixed, slot_len)
    )
    _, rotate_pull = jax.vjp(lambda field: rotate(field, tables), grad_query)
    query_key_value_gradient = jnp.stack(
        [rotate_pull(grad_query)[0], rotate_pull(grad_keys)[0], grad_values], axis=2
    ).astype(jnp.bfloat16)
    grad_qkv_b = jnp.sum(query_key_value_gradient, axis=(0, 1), dtype=jnp.float32)
    query_key_value_weight_gradient = jnp.einsum(
        "jqm,jqnx->mnx", ln_full, query_key_value_gradient, preferred_element_type=jnp.float32
    )
    layernorm_gradient = layernorm_gradient + jnp.einsum(
        "zrhv,nhv->zrn",
        query_key_value_gradient,
        query_key_value_whole,
        preferred_element_type=jnp.float32,
    )
    grad_ln_rows = lax.psum_scatter(layernorm_gradient, "tensor", scatter_dimension=1, tiled=True)
    grad_gain = jnp.sum(grad_ln_rows * normed, axis=(0, 1))
    grad_shift = jnp.sum(grad_ln_rows, axis=(0, 1))
    grad_norm = grad_ln_rows * gain_full
    grad_from_norm = inv_scale * (
        grad_norm
        - jnp.mean(grad_norm, -1, keepdims=True)
        - normed * jnp.mean(grad_norm * normed, -1, keepdims=True)
    )
    grad_slot = (cotangent.astype(jnp.float32) + grad_from_norm).astype(jnp.bfloat16)
    grad_input = pick_rows(
        jnp.zeros_like(grad_slot), lax.all_gather(grad_slot, "dp", axis=0, tiled=True), targets
    )
    grad_qkv_weight, grad_out_weight, grad_fc1_weight, grad_fc2_weight = (
        lax.psum_scatter(query_key_value_weight_gradient, "dp", scatter_dimension=0, tiled=True),
        lax.psum_scatter(output_weight_gradient, "dp", scatter_dimension=0, tiled=True),
        lax.psum_scatter(first_linear_weight_gradient, "dp", scatter_dimension=0, tiled=True),
        lax.psum_scatter(grad_fc2_w, "dp", scatter_dimension=0, tiled=True),
    )
    full_qkv_b = lax.dynamic_update_slice_in_dim(
        jnp.zeros((3, width), jnp.float32), grad_qkv_b, tensor_index * heads_local, 1
    ).reshape(3 * width)
    full_fc1_b = lax.dynamic_update_slice_in_dim(
        jnp.zeros((hidden_local * tensor_count,), jnp.float32),
        grad_fc1_b,
        tensor_index * hidden_local,
        0,
    )
    small_sums = (
        lax.psum_scatter(grad_gain, ("dp", "tensor"), scatter_dimension=0, tiled=True),
        lax.psum_scatter(grad_shift, ("dp", "tensor"), scatter_dimension=0, tiled=True),
        lax.psum_scatter(full_qkv_b, ("dp", "tensor"), scatter_dimension=0, tiled=True),
        lax.psum_scatter(grad_bias, ("dp", "tensor"), scatter_dimension=0, tiled=True),
        lax.psum_scatter(full_fc1_b, ("dp", "tensor"), scatter_dimension=0, tiled=True),
        lax.psum_scatter(grad_bias, ("dp", "tensor"), scatter_dimension=0, tiled=True),
    )
    return (
        block_out,
        grad_input,
        grad_qkv_weight,
        grad_out_weight,
        grad_fc1_weight,
        grad_fc2_weight,
        small_sums[0],
        small_sums[1],
        small_sums[2],
        small_sums[3],
        small_sums[4],
        small_sums[5],
    )


def solution(mesh):
    in_specs = (
        P("dp", "tensor", None),
        P("dp", "tensor", None),
        P(),
        P(),
        P(),
        P("dp", None, "tensor"),
        P("dp", "tensor"),
        P("dp", "tensor"),
        P("dp", "tensor"),
        P(("dp", "tensor")),
        P(("dp", "tensor")),
        P(("dp", "tensor")),
        P(("dp", "tensor")),
        P(("dp", "tensor")),
        P(("dp", "tensor")),
    )
    out_specs = (
        P("dp", "tensor", None),
        P("dp", "tensor", None),
        P("dp", None, "tensor"),
        P("dp", "tensor"),
        P("dp", "tensor"),
        P("dp", "tensor"),
        P(("dp", "tensor")),
        P(("dp", "tensor")),
        P(("dp", "tensor")),
        P(("dp", "tensor")),
        P(("dp", "tensor")),
        P(("dp", "tensor")),
    )
    return jax.shard_map(shards, mesh=mesh, in_specs=in_specs, out_specs=out_specs, check_vma=False)
```

profile of v0, /device:TPU:0, one launch (start us, length us, event | category | flops | bytes accessed | tf_op | source)
XLA Modules:
  0.0 1403.2 jit_solution(5798299145258276597)
XLA Ops:
  18.2 43.2 %all-reduce.19 = (bf16[2048]{0:T(1024)(128)(2,1)S(1)}, bf16[2048]{0:T(1024)(128)(2,1)S(1)}, bf16[6144]{0:T(1024)(128)(2,1)S(1)}, bf16[2048]{0:T(1024)(128)(2,1)}, bf16[2048]{0:T(1024)(128)(2,1)}) all-reduce(bf16[2048]{0:T(1024)(128)(2,1)S(1)} %dynamic-update-slice.5, ...), channel_id=1, replica_groups=mesh['dp'=8,'tensor'=4] {'dp','tensor'}, use_global_device_ids=true, to_apply=%add.9 | all-reduce | flops 14336 | bytes 57344
  77.9 68.1 %all-gather = bf16[32,1,256]{2,1,0:T(2,128)(2,1)S(1)} all-gather(bf16[1,1,256]{2,1,0:T(2,128)(2,1)S(1)} %reshape.1348), channel_id=1, replica_groups=mesh['dp'=8,'tensor'=4] {'dp','tensor'}, dimensions={0}, use_global_device_ids=true | all-gather | bytes 16896 | tf_op jit(solution)/shard_map/all_gather | solution.py:210
  148.2 33.4 %all-gather.22.cloned.1.call-done = bf16[1,1024,2048]{2,1,0:T(8,128)(2,1)} async-done(((bf16[1,256,2048]{2,1,0:T(8,128)(2,1)}), bf16[1,1024,2048]{2,1,0:T(8,128)(2,1)}) %all-gather.22.cloned.1.call-update) | async-done | bytes 4194320 | tf_op jit(solution)/shard_map/all_gather | solution.py:254
  187.8 41.3 %all-gather.14.cloned.1.call-done = bf16[2048,3,512]{0,2,1:T(8,128)(2,1)} async-done(((bf16[256,3,512]{0,2,1:T(8,128)(2,1)}), bf16[2048,3,512]{0,2,1:T(8,128)(2,1)}) %all-gather.14.cloned.1.call-update) | async-done | bytes 6291472 | tf_op jit(solution)/shard_map/all_gather | solution.py:228
  229.1 82.8 %all-gather.12.cloned.1.call-done = bf16[1,1024,2048]{2,1,0:T(8,128)(2,1)} async-done(((bf16[1,256,2048]{2,1,0:T(8,128)(2,1)}), bf16[1,1024,2048]{2,1,0:T(8,128)(2,1)}) %all-gather.12.cloned.1.call-update) | async-done | bytes 4194320 | tf_op jit(solution)/shard_map/all_gather | solution.py:226
  311.9 10.5 add_bitcast_fusion.1
  325.0 9.3 fusion.70
  335.2 8.9 fusion.67
  358.9 7.8 fusion
  367.3 13.1 multiply_reduce_fusion.1
  380.4 11.9 multiply_convert_fusion.1
  405.4 9.5 multiply_reduce_fusion
  415.0 10.7 multiply_convert_fusion
  437.0 8.0 fusion.40
  446.0 9.4 fusion.81
  466.6 14.9 %fusion.32 = f32[1024,2048]{1,0:T(8,128)} fusion(bf16[2048,2048]{1,0:T(8,128)(2,1)} %all-gather.18.cloned.1.call-done, bf16[1,1024,2048]{2,1,0:T(8,128)(2,1)} %all-gather.12.cloned.1.call-done), kind=kOutput, calls=%fused_computation.50 | convolution fusion | flops 8589934592 | bytes 20971520 | tf_op jit(solution)/shard_map/bjp,pv->bjv/dot_general | solution.py:163
  481.5 19.9 %convert_reduce_fusion = (f32[2048]{0:T(1024)S(1)}, bf16[1024,2048]{1,0:T(8,128)(2,1)}) fusion(f32[1024,2048]{1,0:T(8,128)} %fusion.32, f32[2048]{0:T(1024)S(1)} %copy-done.31, bf16[2048,2048]{1,0:T(8,128)(2,1)} %all-gather.20.cloned.1.call-done, bf16[1,1024,2048]{2,1,0:T(8,128)(2,1)} %all-gather.22.cloned.1.call-done), kind=kOutput, calls=%fused_computation.29 | convolution fusion | flops 8638167040 | bytes 25182208 | tf_op jit(solution)/shard_map/sle,ef->slf/dot_general | solution.py:261
  501.5 11.0 fusion.137
  512.5 10.8 fusion.15
  523.4 17.7 %fusion.127 = f32[1024,2048]{1,0:T(8,128)} fusion(bf16[2048,2048]{1,0:T(8,128)(2,1)} %all-gather.20.cloned.1.call-done, f32[1024,2048]{1,0:T(8,128)} %fusion.32, f32[2048]{0:T(1024)S(1)} %copy-done.31), kind=kOutput, calls=%fused_computation.183 | convolution fusion | flops 8610906112 | bytes 25174016 | tf_op jit(solution)/shard_map/slf,ef->sle/dot_general | solution.py:245
  554.1 9.1 add_bitcast_fusion
  566.4 101.1 %reduce-scatter.9.cloned.1.call-done = f32[1,256,2048]{2,1,0:T(8,128)} async-done(((f32[1,1024,2048]{2,1,0:T(8,128)}), f32[1,256,2048]{2,1,0:T(8,128)}) %reduce-scatter.9.cloned.1.call-update) | async-done | bytes 2097168 | tf_op jit(solution)/shard_map/reduce_scatter | solution.py:296
  671.1 144.1 %reduce-scatter.7.cloned.1.call-done = f32[1,256,2048]{2,1,0:T(8,128)} async-done(((f32[1,1024,2048]{2,1,0:T(8,128)}), f32[1,256,2048]{2,1,0:T(8,128)}) %reduce-scatter.7.cloned.1.call-update) | async-done | bytes 2097168 | tf_op jit(solution)/shard_map/reduce_scatter | solution.py:246
  828.4 12.0 fusion.28
  840.5 16.5 %fusion.20 = f32[2048,2048]{1,0:T(8,128)} fusion(bf16[1,1024,2048]{2,1,0:T(8,128)(2,1)} %all-gather.22.cloned.1.call-done, f32[1024,2048]{1,0:T(8,128)} %fusion.32, f32[2048]{0:T(1024)S(1)} %copy-done.31), kind=kOutput, calls=%fused_computation.38 | convolution fusion | flops 8610906112 | bytes 29368320 | tf_op jit(solution)/shard_map/sle,slf->ef/dot_general | solution.py:264
  857.0 15.2 %fusion.34 = f32[2048,2048]{1,0:T(8,128)} fusion(bf16[1024,2048]{1,0:T(8,128)(2,1)} %get-tuple-element.159, bf16[1,1024,2048]{2,1,0:T(8,128)(2,1)} %all-gather.12.cloned.1.call-done), kind=kOutput, calls=%fused_computation.52 | convolution fusion | flops 8589934592 | bytes 25165824 | tf_op jit(solution)/shard_map/hwj,hwy->jy/dot_general | solution.py:270
  874.1 70.4 %all-reduce.22.cloned.1.call-done = (f32[2048]{0:T(1024)}, f32[2048]{0:T(1024)}, f32[6144]{0:T(1024)}, f32[2048]{0:T(1024)}, f32[8192]{0:T(1024)}) async-done(((f32[2048]{0:T(1024)}, f32[2048]{0:T(1024)}, f32[6144]{0:T(1024)}, f32[2048]{0:T(1024)}, f32[8192]{0:T(1024)}), (f32[2048]{0:T(1024)}, f32[2048]{0:T(1024)}, f32[6144]{0:T(1024)}, f32[2048]{0:T(1024)}, f32[8192]{0:T(1024)})) %all-reduce.22.cloned.1.call-update) | async-done | bytes 81936
  950.5 52.3 %all-gather.24.cloned.1.call-done = bf16[8,256,2048]{2,1,0:T(8,128)(2,1)} async-done(((bf16[1,256,2048]{2,1,0:T(8,128)(2,1)}), bf16[8,256,2048]{2,1,0:T(8,128)(2,1)}) %all-gather.24.cloned.1.call-update) | async-done | bytes 8388624 | tf_op jit(solution)/shard_map/all_gather | solution.py:307
  1005.1 52.9 %reduce-scatter.13.cloned.1.call-done = f32[256,512]{1,0:T(8,128)} async-done(((f32[2048,512]{1,0:T(8,128)}), f32[256,512]{1,0:T(8,128)}) %reduce-scatter.13.cloned.1.call-update) | async-done | bytes 524304 | tf_op jit(solution)/shard_map/reduce_scatter | solution.py:311
  1058.0 96.9 %reduce-scatter.11.cloned.1.call-done = f32[256,3,512]{2,0,1:T(8,128)} async-done(((f32[2048,3,512]{2,0,1:T(8,128)}), f32[256,3,512]{2,0,1:T(8,128)}) %reduce-scatter.11.cloned.1.call-update) | async-done | bytes 1572880 | tf_op jit(solution)/shard_map/reduce_scatter | solution.py:310
  1154.9 120.4 %reduce-scatter.17.cloned.1.call-done = f32[256,2048]{1,0:T(8,128)} async-done(((f32[2048,2048]{1,0:T(8,128)}), f32[256,2048]{1,0:T(8,128)}) %reduce-scatter.17.cloned.1.call-update) | async-done | bytes 2097168 | tf_op jit(solution)/shard_map/reduce_scatter | solution.py:313
  1275.3 120.4 %reduce-scatter.15.cloned.1.call-done = f32[256,2048]{1,0:T(8,128)} async-done(((f32[2048,2048]{1,0:T(8,128)}), f32[256,2048]{1,0:T(8,128)}) %reduce-scatter.15.cloned.1.call-update) | async-done | bytes 2097168 | tf_op jit(solution)/shard_map/reduce_scatter | solution.py:312
  (245 shorter events, 132.5 us)
Async XLA Ops:
  7.2 61.3 %all-gather.10.cloned.1.call-start = ((), (), s32[]{:S(2)}) async-start(), calls=%async_computation.6 | async-start | bytes 9437184 | tf_op jit(solution)/shard_map/all_gather | solution.py:203
  8.0 140.2 %all-gather.16.cloned.1.call-start = ((), (), s32[]{:S(2)}) async-start(), calls=%async_computation.9 | async-start | bytes 2359296 | tf_op jit(solution)/shard_map/all_gather | solution.py:229
  8.7 172.8 %all-gather.22.cloned.1.call-start = ((), (), s32[]{:S(2)}) async-start(), calls=%async_computation.13 | async-start | bytes 5242880 | tf_op jit(solution)/shard_map/all_gather | solution.py:254
  15.6 213.4 %all-gather.14.cloned.1.call-start = ((), (), s32[]{:S(2)}) async-start(), calls=%async_computation.8 | async-start | bytes 7077888 | tf_op jit(solution)/shard_map/all_gather | solution.py:228
  16.8 61.0 %copy-start.52 = (bf16[256]{0:T(256)(128)(2,1)S(1)}, bf16[256]{0:T(256)(128)(2,1)}, u32[]{:S(2)}) copy-start(bf16[256]{0:T(256)(128)(2,1)} %param.30) | copy-start | bytes 1540
  16.9 295.0 %all-gather.12.cloned.1.call-start = ((), (), s32[]{:S(2)}) async-start(), calls=%async_computation.7 | async-start | bytes 5242880 | tf_op jit(solution)/shard_map/all_gather | solution.py:226
  61.4 86.8 %copy-start.21 = (f32[2048]{0:T(1024)}, f32[2048]{0:T(1024)S(1)}, u32[]{:S(2)}) copy-start(f32[2048]{0:T(1024)S(1)} %convert_element_type.189) | copy-start | bytes 24580
  75.2 391.4 %all-gather.18.cloned.1.call-start = ((), (), s32[]{:S(2)}) async-start(), calls=%async_computation.10 | async-start | bytes 9437184 | tf_op jit(solution)/shard_map/all_gather | solution.py:230
  75.8 405.7 %all-gather.20.cloned.1.call-start = ((), (), s32[]{:S(2)}) async-start(), calls=%async_computation.11 | async-start | bytes 9437184 | tf_op jit(solution)/shard_map/all_gather | solution.py:231
  76.6 591.0 %reduce-scatter.9.cloned.1.call-start = ((), (), s32[]{:S(2)}) async-start(), calls=%async_computation.14 | async-start | bytes 10485760 | tf_op jit(solution)/shard_map/reduce_scatter | solution.py:296
  76.6 248.4 %copy-start.40 = (pred[512]{0:T(512)(128)(4,1)}, pred[512]{0:T(512)(128)(4,1)S(1)}, u32[]{:S(2)}) copy-start(pred[512]{0:T(512)(128)(4,1)S(1)} %fusion.121) | copy-start | bytes 1540
  77.2 247.8 %copy-start.38 = (pred[512]{0:T(512)(128)(4,1)}, pred[512]{0:T(512)(128)(4,1)S(1)}, u32[]{:S(2)}) copy-start(pred[512]{0:T(512)(128)(4,1)S(1)} %get-tuple-element.165) | copy-start | bytes 1540
  77.2 247.8 %copy-start.42 = (pred[512]{0:T(512)(128)(4,1)}, pred[512]{0:T(512)(128)(4,1)S(1)}, u32[]{:S(2)}) copy-start(pred[512]{0:T(512)(128)(4,1)S(1)} %get-tuple-element.164) | copy-start | bytes 1540
  347.4 108.1 %copy-start = (f32[8,512,1024]{2,1,0:T(8,128)}, f32[8,512,1024]{2,1,0:T(8,128)S(1)}, u32[]{:S(2)}) copy-start(f32[8,512,1024]{2,1,0:T(8,128)S(1)} %get-tuple-element.151) | copy-start | bytes 50331652
  481.5 20.0 %copy-start.45 = (bf16[2048,2048]{1,0:T(8,128)(2,1)S(1)}, bf16[2048,2048]{1,0:T(8,128)(2,1)}, u32[]{:S(2)}) copy-start(bf16[2048,2048]{1,0:T(8,128)(2,1)} %all-gather.18.cloned.1.call-done) | copy-start | bytes 25165828
  523.3 17.8 %copy-start.17 = (f32[8,512]{1,0:T(8,128)S(1)}, f32[8,512]{1,0:T(8,128)}, u32[]{:S(2)}) copy-start(f32[8,512]{1,0:T(8,128)} %copy-done.16) | copy-start | bytes 49156
  523.3 291.8 %reduce-scatter.7.cloned.1.call-start = ((), (), s32[]{:S(2)}) async-start(), calls=%async_computation.12 | async-start | bytes 10485760 | tf_op jit(solution)/shard_map/reduce_scatter | solution.py:246
  523.4 25.6 %slice-start = ((s8[16777216]{0:T(1024)(128)(4,1)}), s8[4194304]{0:T(1024)(128)(4,1)S(1)}, s32[]{:S(2)}) async-start(s8[16777216]{0:T(1024)(128)(4,1)} %bitcast.125), calls=%async_computation.21 | async-start | bytes 8388608
  523.4 25.6 %slice-start.1 = ((s8[16777216]{0:T(1024)(128)(4,1)}), s8[4194304]{0:T(1024)(128)(4,1)S(1)}, s32[]{:S(2)}) async-start(s8[16777216]{0:T(1024)(128)(4,1)} %bitcast.125), calls=%async_computation.22 | async-start | bytes 8388608
  523.4 25.6 %slice-start.2 = ((s8[16777216]{0:T(1024)(128)(4,1)}), s8[4194304]{0:T(1024)(128)(4,1)S(1)}, s32[]{:S(2)}) async-start(s8[16777216]{0:T(1024)(128)(4,1)} %bitcast.125), calls=%async_computation.23 | async-start | bytes 8388608
  563.1 104.4 %copy-start.22 = (f32[2048]{0:T(1024)S(1)}, f32[2048]{0:T(1024)}, u32[]{:S(2)}) copy-start(f32[2048]{0:T(1024)} %copy-done.21) | copy-start | bytes 24580
  563.1 104.4 %copy-start.28 = (f32[256]{0:T(256)S(1)}, f32[256]{0:T(256)}, u32[]{:S(2)}) copy-start(f32[256]{0:T(256)} %copy-done.27) | copy-start | bytes 3076
  563.1 104.4 %copy-start.30 = (f32[256]{0:T(256)S(1)}, f32[256]{0:T(256)}, u32[]{:S(2)}) copy-start(f32[256]{0:T(256)} %copy-done.29) | copy-start | bytes 3076
  563.2 252.0 %copy-start.37 = (pred[256]{0:T(512)(128)(4,1)S(1)}, pred[256]{0:T(512)(128)(4,1)}, u32[]{:S(2)}) copy-start(pred[256]{0:T(512)(128)(4,1)} %copy-done.36) | copy-start | bytes 772
  563.2 381.4 %all-reduce.22.cloned.1.call-start = ((), (), s32[]{:S(2)}) async-start(), calls=%async_computation.20 | async-start | bytes 163840
  566.4 254.3 %copy-start.20 = (f32[8192]{0:T(1024)}, f32[8192]{0:T(1024)S(1)}, u32[]{:S(2)}) copy-start(f32[8192]{0:T(1024)S(1)} %dynamic_update_slice.20) | copy-start | bytes 98308
  820.7 182.1 %all-gather.24.cloned.1.call-start = ((), (), s32[]{:S(2)}) async-start(), calls=%async_computation.15 | async-start | bytes 9437184 | tf_op jit(solution)/shard_map/all_gather | solution.py:307
  821.5 236.5 %reduce-scatter.13.cloned.1.call-start = ((), (), s32[]{:S(2)}) async-start(), calls=%async_computation.17 | async-start | bytes 4718592 | tf_op jit(solution)/shard_map/reduce_scatter | solution.py:311
  828.4 326.5 %reduce-scatter.11.cloned.1.call-start = ((), (), s32[]{:S(2)}) async-start(), calls=%async_computation.16 | async-start | bytes 14155776 | tf_op jit(solution)/shard_map/reduce_scatter | solution.py:310
  840.4 434.8 %reduce-scatter.17.cloned.1.call-start = ((), (), s32[]{:S(2)}) async-start(), calls=%async_computation.19 | async-start | bytes 18874368 | tf_op jit(solution)/shard_map/reduce_scatter | solution.py:313
  857.0 538.7 %reduce-scatter.15.cloned.1.call-start = ((), (), s32[]{:S(2)}) async-start(), calls=%async_computation.18 | async-start | bytes 18874368 | tf_op jit(solution)/shard_map/reduce_scatter | solution.py:312
  946.6 449.6 %copy-start.56 = (f32[64]{0:T(128)}, f32[64]{0:T(128)S(1)}, u32[]{:S(2)}) copy-start(f32[64]{0:T(128)S(1)} %dynamic-slice.20) | copy-start | bytes 772
  (44 other events, 272.0 us)
Sparse Core Ops, SparseCore 0:
  10.0 58.5 all-gather.9
  70.4 27.8 all-gather.15
  100.5 80.9 all-gather.21
  183.8 45.2 all-gather.13
  231.1 80.7 all-gather.11
  313.6 52.9 all-gather.17
  368.4 54.3 all-gather.19
  523.4 144.0 reduce-scatter.8
  669.9 145.1 reduce-scatter.6
  821.4 123.0 all-reduce.21
  947.0 55.7 all-gather.23
  1006.6 51.3 reduce-scatter.12
  1062.4 92.3 reduce-scatter.10
  1159.3 115.9 reduce-scatter.16
  1279.7 115.9 reduce-scatter.14
where the time goes:
time: 1410 us; the launch traced here: 1400 us
  waiting for transfers between devices  927 us (66%)
  matrix products  227 us (16%)
  blocking collectives  111 us (8%)
  other arithmetic  93.8 us (7%)
  local copies, waits for them, and re-layouts  26.1 us (2%)
  between operations  17.4 us (1%)
    reduce_scatter x1, waiting for transfers between devices, shards(): lax.psum_scatter(partial_value, 'tensor', scatter_dimension=1, tiled=True)  144 us
    reduce_scatter x1, waiting for transfers between devices, shards(): lax.psum_scatter(grad_fc2_w, 'dp', scatter_dimension=0, tiled=True)  120 us
    reduce_scatter x1, waiting for transfers between devices, shards(): lax.psum_scatter(first_linear_weight_gradient, 'dp', scatter_dimension=0,...  120 us
    reduce_scatter x1, waiting for transfers between devices, shards(): lax.psum_scatter(layernorm_gradient, 'tensor', scatter_dimension=1, tiled...  101 us
    reduce_scatter x1, waiting for transfers between devices, shards(): lax.psum_scatter(query_key_value_weight_gradient, 'dp', scatter_dimension...  96.9 us
    all_gather x1, waiting for transfers between devices, shards(): ln_full = lax.all_gather(ln_local, 'tensor', axis=1, tiled=True)  82.8 us
    unnamed x16, waiting for transfers between devices  73.9 us
    all_gather x1, blocking collectives, shards(): lax.all_gather(fc1_bias, ('dp', 'tensor'), axis=0, tiled=True)  68.1 us
  transfers between devices with their start and end apart: 15, of which 12 were waited for; matrix products, arithmetic and copies ran while one was open for 21% of the time, Pallas kernels for 0%

commit v1 on v0

v1 whole, which is shorter than its diff:
```python
import math

import jax
import jax.numpy as jnp
from jax import lax
from jax.sharding import PartitionSpec as P

HEAD_DIM = 64
ROT = 32


eps = 1e-05
masked_score = -1e30
f32 = jnp.float32
bf16 = jnp.bfloat16


def rotary_tables(row_count, col_count):
    half_rot = ROT // 2
    column = jnp.arange(col_count) % HEAD_DIM
    exponent = (2 * (column % half_rot)).astype(jnp.float32) / ROT
    frequency = jnp.exp(-math.log(10000.0) * exponent)
    angles = jnp.arange(row_count).astype(jnp.float32)[:, None] * frequency[None, :]
    inside = column < ROT
    cosine = jnp.where(inside, jnp.cos(angles), 1.0)
    sine_part = jnp.sin(angles)
    ahead_sin = jnp.where(column < half_rot, -sine_part, 0.0)
    behind_sin = jnp.where(inside & (column >= half_rot), sine_part, 0.0)
    return (cosine, ahead_sin, behind_sin)


def rotate(field, tables):
    cosine, ahead_sin, behind_sin = tables
    half_rot = ROT // 2
    return (
        field * cosine
        + jnp.roll(field, -half_rot, axis=-1) * ahead_sin
        + jnp.roll(field, half_rot, axis=-1) * behind_sin
    )


def normalize(rows_in):
    row_mean = jnp.mean(rows_in, -1, keepdims=True)
    centred = rows_in - row_mean
    variance = jnp.mean(centred * centred, -1, keepdims=True)
    inv_scale = lax.rsqrt(variance + eps)
    return (centred * inv_scale, inv_scale)


def block_scores(queries, key_heads, first_row, block_rows, length):
    head_count = key_heads.shape[1]
    query_block = queries[first_row : first_row + block_rows].reshape(
        block_rows, head_count, HEAD_DIM
    )
    scores = jnp.einsum(
        "qhd,khd->hqk", query_block, key_heads, preferred_element_type=jnp.float32
    ) * (1.0 / math.sqrt(HEAD_DIM))
    row_ids = first_row + jnp.arange(block_rows, dtype=jnp.int32)
    col_ids = jnp.arange(key_heads.shape[0], dtype=jnp.int32)
    allowed = (col_ids[None, :] <= row_ids[:, None]) & (col_ids[None, :] < length)
    return (jnp.where(allowed[None], scores, masked_score), query_block)


def attend_forward(queries, key_rows, values, length):
    seq_len = queries.shape[0]
    head_count = queries.shape[1] // HEAD_DIM
    key_heads = key_rows.reshape(seq_len, head_count, HEAD_DIM)
    value_heads = values.reshape(seq_len, head_count, HEAD_DIM)
    block_rows = min(512, seq_len)
    mixed_parts = []
    total_parts = []
    for first_row in range(0, seq_len, block_rows):
        scores, query_block = block_scores(queries, key_heads, first_row, block_rows, length)
        row_max = jnp.max(scores, -1, keepdims=True)
        exped = jnp.exp(scores - row_max)
        row_total = jnp.sum(exped, -1, keepdims=True)
        attn_probs = (exped / row_total).astype(jnp.bfloat16)
        attention_mixture = jnp.einsum(
            "hqk,khd->qhd", attn_probs, value_heads, preferred_element_type=jnp.float32
        )
        mixed_parts.append(attention_mixture.reshape(block_rows, head_count * HEAD_DIM))
        total_parts.append(row_max[..., 0] + jnp.log(row_total[..., 0]))
    return (jnp.concatenate(mixed_parts, 0).astype(jnp.bfloat16), jnp.concatenate(total_parts, 1))


def attend_backward(queries, key_rows, values, log_total, grad_mixed, length):
    seq_len = queries.shape[0]
    head_count = queries.shape[1] // HEAD_DIM
    key_heads = key_rows.reshape(seq_len, head_count, HEAD_DIM)
    value_heads = values.reshape(seq_len, head_count, HEAD_DIM)
    block_rows = min(512, seq_len)
    score_scale = 1.0 / math.sqrt(HEAD_DIM)
    grad_query_parts = []
    grad_keys = jnp.zeros((seq_len, head_count, HEAD_DIM), jnp.float32)
    grad_values = jnp.zeros((seq_len, head_count, HEAD_DIM), jnp.float32)
    for first_row in range(0, seq_len, block_rows):
        scores, query_block = block_scores(queries, key_heads, first_row, block_rows, length)
        attn_probs = jnp.exp(scores - log_total[:, first_row : first_row + block_rows, None])
        grad_block = grad_mixed[first_row : first_row + block_rows].reshape(
            block_rows, head_count, HEAD_DIM
        )
        grad_probs = jnp.einsum(
            "qhd,khd->hqk", grad_block, value_heads, preferred_element_type=jnp.float32
        )
        grad_scores = (
            attn_probs * (grad_probs - jnp.sum(attn_probs * grad_probs, -1, keepdims=True))
        ).astype(jnp.bfloat16)
        grad_query = (
            jnp.einsum("hqk,khd->qhd", grad_scores, key_heads, preferred_element_type=jnp.float32)
            * score_scale
        )
        grad_query_parts.append(grad_query.reshape(block_rows, head_count * HEAD_DIM))
        grad_keys = (
            grad_keys
            + jnp.einsum(
                "hqk,qhd->khd", grad_scores, query_block, preferred_element_type=jnp.float32
            )
            * score_scale
        )
        grad_values = grad_values + jnp.einsum(
            "hqk,qhd->khd",
            attn_probs.astype(jnp.bfloat16),
            grad_block,
            preferred_element_type=jnp.float32,
        )
    return (
        jnp.concatenate(grad_query_parts, 0),
        grad_keys.reshape(seq_len, head_count * HEAD_DIM),
        grad_values.reshape(seq_len, head_count * HEAD_DIM),
    )


def flip(array, axis_name, bit):
    size = lax.axis_size(axis_name)
    return lax.ppermute(array, axis_name, [(i, i ^ (1 << bit)) for i in range(size)])


def bits_of(size):
    return size.bit_length() - 1


def swap_blocks(array, index, axis, blocks):
    for bit in range(bits_of(blocks)):
        shape = array.shape
        parts = shape[:axis] + (blocks >> (bit + 1), 2, 1 << bit, shape[axis] // blocks)
        view = array.reshape(parts + shape[axis + 1 :])
        turned = jnp.flip(view, axis=axis + 1)
        array = jnp.where((index >> bit) & 1 == 1, turned, view).reshape(shape)
    return array


def reversed_bits(value, bits):
    return sum(((value >> k) & 1) << (bits - 1 - k) for k in range(bits))


def xor_columns(array, index, blocks):
    width = array.shape[-1] // blocks
    bits = bits_of(blocks)
    pieces = [
        lax.dynamic_slice_in_dim(
            array, (index ^ reversed_bits(p, bits)) * width, width, array.ndim - 1
        )
        for p in range(blocks)
    ]
    return jnp.concatenate(pieces, -1)


def plain_columns(array, index, blocks):
    width = array.shape[-1] // blocks
    bits = bits_of(blocks)
    pieces = []
    for q in range(blocks):
        mask = index ^ q
        place = sum(((mask >> k) & 1) << (bits - 1 - k) for k in range(bits))
        pieces.append(lax.dynamic_slice_in_dim(array, place * width, width, array.ndim - 1))
    return jnp.concatenate(pieces, -1)


def gather_blocks(shard, order):
    bits = len(order)
    stack = shard[None]
    masks = [0]
    for bit in order:
        stack = jnp.concatenate([stack, flip(stack, "dp", bit)], 0)
        masks = masks + [m | (1 << bit) for m in masks]
    pieces = [stack[masks.index(reversed_bits(p, bits))] for p in range(1 << bits)]
    return jnp.concatenate(pieces, 0)


def scatter_blocks(kept, order, rows):
    bits = len(order) + 1
    count = 1 << (bits - 1)
    blocks = {reversed_bits(p, bits): kept[p * rows : (p + 1) * rows] for p in range(count)}
    for step, bit in enumerate(order):
        sent = [m for m in blocks if (m >> bit) & 1]
        arrived = flip(jnp.concatenate([blocks[m] for m in sent], 0), "dp", bit)
        last = step == len(order) - 1
        fresh = {}
        for i, m in enumerate(sent):
            target = m ^ (1 << bit)
            total = blocks[target].astype(f32) + arrived[i * rows : (i + 1) * rows].astype(f32)
            fresh[target] = total if last else total.astype(bf16)
        blocks = fresh
    return blocks[0]


def weight_gradient(rows_by_feature, other, order, rows):
    half = rows_by_feature.shape[1] // 2
    sent = jnp.einsum(
        "rd,rc->dc", rows_by_feature[:, half:], other, preferred_element_type=f32
    ).astype(bf16)
    arrived = flip(sent, "dp", 0)
    kept = jnp.einsum("rd,rc->dc", rows_by_feature[:, :half], other, preferred_element_type=f32)
    kept = (kept + arrived.astype(f32)).astype(bf16)
    return scatter_blocks(kept, order, rows)


def route(block, wanted, index, last):
    bits = bits_of(lax.axis_size("dp"))
    order = [b for b in range(bits - 1, -1, -1) if b != last]
    stack = block[None]
    for bit in order:
        stack = jnp.concatenate([stack, flip(stack, "dp", bit)], 0)

    def place(mask):
        return sum(((mask >> bit) & 1) << k for k, bit in enumerate(order))

    mine = wanted[index]
    theirs = wanted[index ^ (1 << last)]
    given = lax.dynamic_index_in_dim(stack, place(index ^ theirs), 0, keepdims=False)
    held = lax.dynamic_index_in_dim(stack, place(index ^ mine), 0, keepdims=False)
    arrived = flip(given, "dp", last)
    return jnp.where(((index ^ mine) >> last) & 1 == 1, arrived, held)


def route_rows(rows, wanted, index):
    bits = bits_of(lax.axis_size("dp"))
    half = rows.shape[0] // 2
    return jnp.concatenate(
        [
            route(rows[:half], wanted, index, bits - 1),
            route(rows[half:], wanted, index, max(bits - 2, 0)),
        ],
        0,
    )


def gather_small(vector, data_index, tensor_index):
    data_count, tensor_count = lax.axis_size("dp"), lax.axis_size("tensor")
    stack = vector[None]
    for bit in range(bits_of(tensor_count)):
        stack = jnp.concatenate([stack, flip(stack, "tensor", bit)], 0)
    for bit in range(bits_of(data_count)):
        stack = jnp.concatenate([stack, flip(stack, "dp", bit)], 0)
    stack = swap_blocks(stack, data_index * tensor_count + tensor_index, 0, stack.shape[0])
    return stack.reshape(data_count, tensor_count, vector.shape[0])


def scatter_small(blocks, data_index, tensor_index):
    data_count, tensor_count = lax.axis_size("dp"), lax.axis_size("tensor")
    stack = swap_blocks(blocks, data_index * tensor_count + tensor_index, 0, blocks.shape[0])
    for bit in range(bits_of(data_count) - 1, -1, -1):
        half = stack.shape[0] // 2
        stack = stack[:half] + flip(stack[half:], "dp", bit)
    for bit in range(bits_of(tensor_count) - 1, -1, -1):
        half = stack.shape[0] // 2
        stack = stack[:half] + flip(stack[half:], "tensor", bit)
    return stack[0]


def shards(
    hidden_in,
    cotangent,
    lengths,
    slot_of_seq,
    seq_of_slot,
    qkv_weight,
    out_weight,
    fc1_weight,
    fc2_weight,
    ln_gain,
    ln_bias,
    qkv_bias,
    out_bias,
    fc1_bias,
    fc2_bias,
):
    rows_here = hidden_in.shape[1]
    width = hidden_in.shape[2]
    tensor_count = lax.axis_size("tensor")
    data_count = lax.axis_size("dp")
    tensor_index = lax.axis_index("tensor")
    data_index = lax.axis_index("dp")
    seq_len = rows_here * tensor_count
    heads_local = qkv_weight.shape[2]
    hidden_local = fc1_weight.shape[1]
    block = width // data_count
    length = lengths[seq_of_slot[data_index]]
    bits = bits_of(data_count)
    upper = list(range(1, bits))
    x_first = upper + [0]
    y_first = upper[::-1] + [0]

    positions = tensor_index * rows_here + jnp.arange(rows_here, dtype=jnp.int32)
    valid = (positions < length)[:, None]
    cot_rows = xor_columns(cotangent[0], data_index, data_count)
    grad_low = jnp.where(valid, cot_rows, jnp.zeros_like(cot_rows))
    halfway = width // 2
    grads_left = lax.all_gather(grad_low[:, :halfway], "tensor", axis=0, tiled=True)

    routed = route_rows(hidden_in[0], seq_of_slot, data_index)
    slot_rows = xor_columns(routed, data_index, data_count)
    rows_full = lax.all_gather(slot_rows, "tensor", axis=0, tiled=True)
    grads_right = lax.all_gather(grad_low[:, halfway:], "tensor", axis=0, tiled=True)
    grads = jnp.concatenate([grads_left, grads_right], 1)

    small = jnp.concatenate([ln_gain, ln_bias, out_bias, fc2_bias, qkv_bias, fc1_bias])
    gathered = gather_small(small, data_index, tensor_index)
    s = ln_gain.shape[0]
    vectors = [
        xor_columns(gathered[:, :, i * s : (i + 1) * s].reshape(width), data_index, data_count)
        for i in range(4)
    ]
    gain, shift, bias_a, bias_b = [v.astype(f32) for v in vectors]
    q = qkv_bias.shape[0]
    bias_qkv = lax.dynamic_slice_in_dim(
        gathered[:, :, 4 * s : 4 * s + q].reshape(3, width), tensor_index * heads_local, heads_local, 1
    ).astype(f32)
    bias_fc1 = lax.dynamic_slice_in_dim(
        gathered[:, :, 4 * s + q :].reshape(hidden_local * tensor_count),
        tensor_index * hidden_local,
        hidden_local,
        0,
    ).astype(f32)

    w_qk = gather_blocks(
        qkv_weight[:, :2].reshape(block, 2 * heads_local), x_first
    )
    w_vo = gather_blocks(jnp.concatenate([qkv_weight[:, 2], out_weight], 1), y_first)
    w_fc1 = gather_blocks(fc1_weight, x_first)
    w_fc2 = gather_blocks(fc2_weight, y_first)
    w_v, w_out = w_vo[:, :heads_local], w_vo[:, heads_local:]

    full_normed, _ = normalize(rows_full.astype(f32))
    ln = (full_normed * gain + shift).astype(bf16)
    tables = rotary_tables(seq_len, heads_local)
    qk_raw = jnp.einsum("rd,dc->rc", ln, w_qk, preferred_element_type=f32)
    v_raw = jnp.einsum("rd,dc->rc", ln, w_v, preferred_element_type=f32)
    queries = rotate(qk_raw[:, :heads_local] + bias_qkv[0], tables).astype(bf16)
    key_rows = rotate(qk_raw[:, heads_local:] + bias_qkv[1], tables).astype(bf16)
    values = (v_raw + bias_qkv[2]).astype(bf16)
    mixed, log_total = attend_forward(queries, key_rows, values, length)
    pre_act = jnp.einsum("rd,dc->rc", ln, w_fc1, preferred_element_type=f32) + bias_fc1
    hidden = jax.nn.gelu(pre_act, approximate=True).astype(bf16)
    branch_part = (
        jnp.einsum("rd,ed->re", mixed, w_out, preferred_element_type=f32)
        + jnp.einsum("rf,ef->re", hidden, w_fc2, preferred_element_type=f32)
    ).astype(bf16)
    branch_sum = lax.psum_scatter(branch_part, "tensor", scatter_dimension=0, tiled=True)
    slot_f32 = slot_rows.astype(f32)
    branch = branch_sum.astype(f32) + bias_a + bias_b
    block_out = (slot_f32 + jnp.where(valid, branch, 0.0)).astype(bf16)
    block_out = plain_columns(block_out, data_index, data_count)[None]

    grad_bias = jnp.sum(grad_low.astype(f32), axis=0)
    grad_mixed = jnp.einsum("re,ed->rd", grads, w_out, preferred_element_type=f32).astype(bf16)
    grad_hidden = jnp.einsum("re,ef->rf", grads, w_fc2, preferred_element_type=f32)
    _, gelu_pull = jax.vjp(lambda inputs: jax.nn.gelu(inputs, approximate=True), pre_act)
    grad_pre = gelu_pull(grad_hidden)[0].astype(bf16)
    grad_fc1_b = jnp.sum(grad_pre, axis=0, dtype=f32)
    grad_query, grad_keys, grad_values = attend_backward(
        queries, key_rows, values, log_total, grad_mixed, length
    )
    _, rotate_pull = jax.vjp(lambda field: rotate(field, tables), grad_query)
    grad_qk = jnp.concatenate(
        [rotate_pull(grad_query)[0].astype(bf16), rotate_pull(grad_keys)[0].astype(bf16)], 1
    )
    grad_v = grad_values.astype(bf16)
    grad_qkv_b = jnp.concatenate(
        [jnp.sum(grad_qk, 0, dtype=f32), jnp.sum(grad_v, 0, dtype=f32)]
    ).reshape(3, heads_local)
    ln_part = (
        jnp.einsum("rf,df->rd", grad_pre, w_fc1, preferred_element_type=f32)
        + jnp.einsum("rc,dc->rd", grad_qk, w_qk, preferred_element_type=f32)
        + jnp.einsum("rc,dc->rd", grad_v, w_v, preferred_element_type=f32)
    ).astype(bf16)
    grad_ln = lax.psum_scatter(ln_part, "tensor", scatter_dimension=0, tiled=True).astype(f32)

    grad_fc2_w = weight_gradient(grads, hidden, y_first[:-1], block)
    grad_out_w = weight_gradient(grads, mixed, y_first[:-1], block)
    grad_fc1_w = weight_gradient(ln, grad_pre, x_first[:-1], block)
    grad_qk_w = weight_gradient(ln, grad_qk, x_first[:-1], block)
    grad_v_w = weight_gradient(ln, grad_v, y_first[:-1], block)
    grad_qkv_w = jnp.stack(
        [grad_qk_w[:, :heads_local], grad_qk_w[:, heads_local:], grad_v_w], 1
    )

    normed, inv_scale = normalize(slot_f32)
    grad_gain = jnp.sum(grad_ln * normed, axis=0)
    grad_shift = jnp.sum(grad_ln, axis=0)
    grad_norm = grad_ln * gain
    grad_from_norm = inv_scale * (
        grad_norm
        - jnp.mean(grad_norm, -1, keepdims=True)
        - normed * jnp.mean(grad_norm * normed, -1, keepdims=True)
    )
    grad_slot = (cot_rows.astype(f32) + grad_from_norm).astype(bf16)
    grad_slot = plain_columns(grad_slot, data_index, data_count)
    grad_input = route_rows(grad_slot, slot_of_seq, data_index)[None]

    devices = data_count * tensor_count
    full_qkv_b = lax.dynamic_update_slice_in_dim(
        jnp.zeros((3, width), f32), grad_qkv_b, tensor_index * heads_local, 1
    )
    full_fc1_b = lax.dynamic_update_slice_in_dim(
        jnp.zeros((hidden_local * tensor_count,), f32), grad_fc1_b, tensor_index * hidden_local, 0
    )
    sums = jnp.concatenate(
        [plain_columns(v, data_index, data_count).reshape(devices, s) for v in (grad_gain, grad_shift, grad_bias)]
        + [full_qkv_b.reshape(devices, q), full_fc1_b.reshape(devices, -1)],
        1,
    )
    total = scatter_small(sums, data_index, tensor_index)
    return (
        block_out,
        grad_input,
        grad_qkv_w,
        grad_out_w,
        grad_fc1_w,
        grad_fc2_w,
        total[:s],
        total[s : 2 * s],
        total[3 * s : 3 * s + q],
        total[2 * s : 3 * s],
        total[3 * s + q :],
        total[2 * s : 3 * s],
    )


def solution(mesh):
    in_specs = (
        P("dp", "tensor", None),
        P("dp", "tensor", None),
        P(),
        P(),
        P(),
        P("dp", None, "tensor"),
        P("dp", "tensor"),
        P("dp", "tensor"),
        P("dp", "tensor"),
        P(("dp", "tensor")),
        P(("dp", "tensor")),
        P(("dp", "tensor")),
        P(("dp", "tensor")),
        P(("dp", "tensor")),
        P(("dp", "tensor")),
    )
    out_specs = (
        P("dp", "tensor", None),
        P("dp", "tensor", None),
        P("dp", None, "tensor"),
        P("dp", "tensor"),
        P("dp", "tensor"),
        P("dp", "tensor"),
        P(("dp", "tensor")),
        P(("dp", "tensor")),
        P(("dp", "tensor")),
        P(("dp", "tensor")),
        P(("dp", "tensor")),
        P(("dp", "tensor")),
    )
    return jax.shard_map(shards, mesh=mesh, in_specs=in_specs, out_specs=out_specs, check_vma=False)
```

time: 1410 us -> 760 us (0.54)
  waiting for transfers between devices: 927 us -> 186 us
  blocking collectives: 111 us -> 0 us
  local copies, waits for them, and re-layouts: 26.1 us -> 131 us
  other arithmetic: 93.8 us -> 141 us
  starting transfers between devices: 0.6 us -> 44.1 us
    reduce_scatter x6 -> x2, waiting for transfers between devices: 636 us -> 0.01 us  [the longest x1 0.01 us: shards(): lax.psum_scatter(ln_part, 'tensor', scatter_dimension=0, tiled=True)]
    all_gather x8 -> x3, waiting for transfers between devices: 217 us -> 7.12 us  [the longest x1 7.11 us: shards(): rows_full = lax.all_gather(slot_rows, 'tensor', axis=0, tiled=True)]
    ppermute x0 -> x49, waiting for transfers between devices: none -> 178 us  [flip(): lax.ppermute(array, axis_name, [(i, i ^ 1 << bit) for i in range(size)])]
    unnamed x16 -> x5, waiting for transfers between devices: 73.9 us -> 0.08 us
    unnamed x140 -> x260, local copies, waits for them, and re-layouts: 16.7 us -> 86.6 us
    all_gather x1 -> x0, blocking collectives: 68.1 us -> none  [shards(): lax.all_gather(fc1_bias, ('dp', 'tensor'), axis=0, tiled=True)]
    ppermute x0 -> x49, starting transfers between devices: none -> 43.7 us  [flip(): lax.ppermute(array, axis_name, [(i, i ^ 1 << bit) for i in range(size)])]
    unnamed x1 -> x0, blocking collectives: 43.2 us -> none
  transfers between devices with their start and end apart: 15 -> 54, of which waited for: 12 -> 20; matrix products, arithmetic and copies ran while one was open for 21% -> 33% of each run, Pallas kernels for 0% -> 0%
where the time goes in v1:
time: 760 us; the launch traced here: 753 us
  matrix products  230 us (30%)
  waiting for transfers between devices  186 us (24%)
  other arithmetic  141 us (19%)
  local copies, waits for them, and re-layouts  131 us (17%)
  starting transfers between devices  44.1 us (6%)
  between operations  22 us (3%)
    ppermute x49, waiting for transfers between devices, flip(): lax.ppermute(array, axis_name, [(i, i ^ 1 << bit) for i in range(size)])  178 us
    unnamed x260, local copies, waits for them, and re-layouts  86.6 us
    ppermute x49, starting transfers between devices, flip(): lax.ppermute(array, axis_name, [(i, i ^ 1 << bit) for i in range(size)])  43.7 us
    dot_general x5, matrix products, weight_gradient(): jnp.einsum('rd,rc->dc', rows_by_feature[:, half:], other, preferred_eleme...  30.1 us
    convert_element_type x2, other arithmetic, attend_backward(): grad_scores = (attn_probs * (grad_probs - jnp.sum(attn_probs * grad_probs...  25.4 us
    concatenate x8, other arithmetic, gather_blocks(): stack = jnp.concatenate([stack, flip(stack, 'dp', bit)], 0)  24.3 us
    dot_general x5, matrix products, weight_gradient(): jnp.einsum('rd,rc->dc', rows_by_feature[:, :half], other, preferred_eleme...  23.4 us
    dot_general x2, matrix products, attend_backward(): jnp.einsum('qhd,khd->hqk', grad_block, value_heads, preferred_element_typ...  21.7 us
  transfers between devices with their start and end apart: 54, of which 20 were waited for; matrix products, arithmetic and copies ran while one was open for 33% of the time, Pallas kernels for 0%

profile of v1, /device:TPU:0, one launch (start us, length us, event | category | flops | bytes accessed | tf_op | source)
XLA Modules:
  0.0 753.3 jit_solution(18086706272190248798)
XLA Ops:
  34.3 8.6 %collective-permute-done = bf16[1,128,2048]{2,1,0:T(8,128)(2,1)S(1)} collective-permute-done((bf16[1,128,2048]{2,1,0:T(8,128)(2,1)S(1)}, bf16[1,128,2048]{2,1,0:T(8,128)(2,1)S(1)}, u32[]{:S(2)}, u32[]{:S(2)}) %collective-permute-start) | collective-permute-done | bytes 524320 | tf_op jit(solution)/shard_map/ppermute | solution.py:135
  65.7 7.4 collective-permute-done.2
  91.1 15.5 %collective-permute-done.10 = bf16[16,704]{1,0:T(8,128)(2,1)S(1)} collective-permute-done((bf16[16,704]{1,0:T(8,128)(2,1)S(1)}, bf16[16,704]{1,0:T(8,128)(2,1)S(1)}, u32[]{:S(2)}, u32[]{:S(2)}) %collective-permute-start.10) | collective-permute-done | bytes 22560 | tf_op jit(solution)/shard_map/ppermute | solution.py:135
  135.1 10.0 %collective-permute-done.15 = bf16[2,256,1024]{1,2,0:T(8,128)(2,1)} collective-permute-done((bf16[2,256,1024]{1,2,0:T(8,128)(2,1)}, bf16[2,256,1024]{1,2,0:T(8,128)(2,1)}, u32[]{:S(2)}, u32[]{:S(2)}) %collective-permute-start.15) | collective-permute-done | bytes 1048608 | tf_op jit(solution)/shard_map/ppermute | solution.py:135
  169.6 18.9 %collective-permute-done.18 = bf16[2,256,2048]{2,1,0:T(8,128)(2,1)} collective-permute-done((bf16[2,256,2048]{2,1,0:T(8,128)(2,1)}, bf16[2,256,2048]{2,1,0:T(8,128)(2,1)}, u32[]{:S(2)}, u32[]{:S(2)}) %collective-permute-start.18) | collective-permute-done | bytes 2097184 | tf_op jit(solution)/shard_map/ppermute | solution.py:135
  254.9 7.1 all-gather.4.cloned.1.call-done
  268.6 7.9 %fusion.184 = f32[1024,1024]{0,1:T(8,128)S(1)} fusion(bf16[1024,2048]{1,0:T(8,128)(2,1)S(1)} %fusion.9, bf16[2048,1024]{0,1:T(8,128)(2,1)} %fusion.116), kind=kOutput, calls=%fused_computation.393 | convolution fusion | flops 4294967296 | bytes 12582912 | tf_op jit(solution)/shard_map/rd,dc->rc/dot_general | solution.py:347
  277.9 10.2 %fusion.46 = (bf16[1024,512]{0,1:T(8,128)(2,1)S(1)}, bf16[1024,512]{0,1:T(8,128)(2,1)S(1)}) fusion(f32[1024,512]{0,1:T(8,128)S(1)} %get-tuple-element.23, f32[1024,16]{0,1:T(8,128)S(1)} %get-tuple-element.30, f32[1024,496]{0,1:T(8,128)S(1)} %get-tuple-element.32, f32[1024,496]{0,1:T(8,128)S(1)} %get-tuple-element.31, f32[1024,16]{0,1:T(8,128)S(1)} %get-tuple-element.29, ...), kind=kLoop, calls=%fused_computation.80 | loop fusion | flops 11010048 | bytes 14687744 | tf_op jit(solution)/shard_map/convert_element_type | solution.py:350
  304.5 10.0 %multiply_reduce_fusion = (f32[8,512]{1,0:T(8,128)}, f32[8,512,1024]{2,1,0:T(8,128)}) fusion(f32[8,512,1024]{2,1,0:T(8,128)S(1)} %get-tuple-element.142, f32[8,512]{1,0:T(8,128)S(1)} %log_add_fusion, bf16[512,8,64]{0,2,1:T(8,128)(2,1)} %bitcast.305, bf16[1024,8,64]{0,2,1:T(8,128)(2,1)} %bitcast.307), kind=kOutput, calls=%fused_computation.1 | convolution fusion | flops 549449728 | bytes 35160064 | tf_op jit(solution)/shard_map/qhd,khd->hqk/dot_general | solution.py:102
  314.5 8.4 %fusion.182 = (f32[8,512]{1,0:T(8,128)S(1)}, f32[8,512,1024]{2,1,0:T(8,128)}) fusion(bf16[512,8,64]{0,2,1:T(8,128)(2,1)S(1)} %bitcast.301, bf16[1024,8,64]{0,2,1:T(8,128)(2,1)S(1)} %bitcast.287, pred[512,1024]{1,0:T(8,128)(4,1)} %get-tuple-element.129), kind=kOutput, calls=%fused_computation.391 | convolution fusion | flops 549449728 | bytes 18890752 | tf_op jit(solution)/shard_map/qhd,khd->hqk/dot_general | solution.py:55
  322.9 7.7 %fusion = f32[8,512]{1,0:T(8,128)S(1)} fusion(f32[8,512,1024]{2,1,0:T(8,128)} %get-tuple-element.138, f32[8,512]{1,0:T(8,128)S(1)} %get-tuple-element.137), kind=kLoop, calls=%fused_computation.12 | loop fusion | flops 8384512 | bytes 16809984 | tf_op jit(solution)/shard_map/reduce_sum | solution.py:76
  331.2 11.7 %multiply_reduce_fusion.1 = (f32[8,512]{1,0:T(8,128)S(1)}, f32[8,512,1024]{2,1,0:T(8,128)}) fusion(f32[8,512,1024]{2,1,0:T(8,128)} %get-tuple-element.138, f32[8,512]{1,0:T(8,128)S(1)} %log_add_fusion.1, bf16[512,8,64]{0,2,1:T(8,128)(2,1)S(1)} %bitcast.303, bf16[1024,8,64]{0,2,1:T(8,128)(2,1)} %bitcast.308), kind=kOutput, calls=%fused_computation.4 | convolution fusion | flops 549449728 | bytes 35160064 | tf_op jit(solution)/shard_map/qhd,khd->hqk/dot_general | solution.py:102
  342.9 15.2 %multiply_convert_fusion.1 = bf16[8,512,1024]{2,1,0:T(8,128)(2,1)} fusion(f32[8,512,1024]{2,1,0:T(8,128)} %get-tuple-element.140, f32[8,512,1024]{2,1,0:T(8,128)} %get-tuple-element.138, f32[8,512]{1,0:T(8,128)S(1)} %get-tuple-element.139, f32[8,512]{1,0:T(8,128)S(1)} %log_add_fusion.1), kind=kLoop, calls=%fused_computation.3 | loop fusion | flops 16777216 | bytes 41975808 | tf_op jit(solution)/shard_map/convert_element_type | solution.py:107
  370.5 10.2 %multiply_convert_fusion = bf16[8,512,1024]{2,1,0:T(8,128)(2,1)} fusion(f32[8,512,1024]{2,1,0:T(8,128)} %get-tuple-element.144, f32[8,512,1024]{2,1,0:T(8,128)S(1)} %get-tuple-element.142, f32[8,512]{1,0:T(8,128)S(1)} %copy-done.47, f32[8,512]{1,0:T(8,128)S(1)} %copy-done.40), kind=kLoop, calls=%fused_computation | loop fusion | flops 16777216 | bytes 41975808 | tf_op jit(solution)/shard_map/convert_element_type | solution.py:107
  388.7 8.2 %fusion.27 = (f32[1024,512]{0,1:T(8,128)S(1)}, f32[1024,512]{0,1:T(8,128)S(1)}, f32[1024,512]{0,1:T(8,128)S(1)}, f32[1024,512]{0,1:T(8,128)S(1)}) fusion(f32[8,64,1024]{2,1,0:T(8,128)S(1)} %add_multiply_fusion, f32[512]{0:T(512)S(1)} %fusion.147, f32[1024]{0:T(1024)S(1)} %iota_convert_fusion, pred[512]{0:T(512)(128)(4,1)S(1)} %copy-done.70, ...), kind=kLoop, calls=%fused_computation.61 | loop fusion | flops 4718592 | bytes 12590080 | tf_op jit(solution)/shard_map/transpose(jvp())/mul | solution.py:38
  403.5 13.5 %fusion.185 = f32[1024,2048]{1,0:T(8,128)} fusion(bf16[1024,2048]{1,0:T(8,128)(2,1)S(1)} %copy-done.19, bf16[2048,2048]{1,0:T(8,128)(2,1)} %fusion.110), kind=kOutput, calls=%fused_computation.394 | convolution fusion | flops 8589934592 | bytes 20971520 | tf_op jit(solution)/shard_map/rd,dc->rc/dot_general | solution.py:353
  417.0 19.7 %convert_reduce_fusion.1 = (f32[2048]{0:T(1024)}, bf16[1024,2048]{1,0:T(8,128)(2,1)S(1)}, bf16[1024,2048]{1,0:T(8,128)(2,1)}) fusion(f32[1024,2048]{1,0:T(8,128)} %fusion.185, f32[2048]{0:T(1024)S(1)} %copy-done.59, bf16[1024,2048]{1,0:T(8,128)(2,1)S(1)} %copy-done.36, bf16[2048,2048]{1,0:T(8,128)(2,1)} %fusion.104), kind=kOutput, calls=%fused_computation.35 | convolution fusion | flops 8642361344 | bytes 29376512 | tf_op jit(solution)/shard_map/re,ef->rf/dot_general | solution.py:367
  438.8 13.9 %fusion.187 = f32[1024,2048]{1,0:T(8,128)} fusion(bf16[1024,2048]{1,0:T(8,128)(2,1)S(1)} %get-tuple-element.17, bf16[2048,2048]{1,0:T(8,128)(2,1)} %fusion.110), kind=kOutput, calls=%fused_computation.396 | convolution fusion | flops 8589934592 | bytes 20971520 | tf_op jit(solution)/shard_map/rf,df->rd/dot_general | solution.py:383
  452.7 14.8 %fusion.186 = f32[1024,2048]{1,0:T(8,128)} fusion(bf16[1024,2048]{1,0:T(8,128)(2,1)} %get-tuple-element.20, bf16[2048,2048]{1,0:T(8,128)(2,1)} %fusion.104), kind=kOutput, calls=%fused_computation.395 | convolution fusion | flops 8589934592 | bytes 20971520 | tf_op jit(solution)/shard_map/rf,ef->re/dot_general | solution.py:357
  472.8 10.1 %fusion.60 = (bf16[1024,512]{0,1:T(8,128)(2,1)S(1)}, bf16[1024,512]{0,1:T(8,128)(2,1)S(1)}) fusion(f32[1024,496]{0,1:T(8,128)} %split.39, f32[1024,16]{0,1:T(8,128)S(1)} %split.38, f32[1024,16]{0,1:T(8,128)S(1)} %split.37, f32[1024,496]{0,1:T(8,128)} %split.36, f32[512,512]{0,1:T(8,128)S(1)} %bitcast.293, f32[512,512]{0,1:T(8,128)S(1)} %bitcast.291, ...), kind=kLoop, calls=%fused_computation.94 | loop fusion | flops 7864320 | bytes 14686720 | tf_op jit(solution)/shard_map/convert_element_type | solution.py:376
  483.0 7.4 fusion.158
  496.8 9.5 %convolution_convert_fusion = bf16[1024,2048]{1,0:T(8,128)(2,1)} fusion(bf16[1024,1024]{1,0:T(8,128)(2,1)} %all-gather.8.cloned.1.call-done, bf16[1024,2048]{1,0:T(8,128)(2,1)} %get-tuple-element.20), kind=kOutput, calls=%fused_computation.49 | convolution fusion | flops 4297064448 | bytes 10485760 | tf_op jit(solution)/shard_map/rd,rc->dc/dot_general | solution.py:209
  506.4 7.7 %fusion.102 = bf16[8,64,512]{2,1,0:T(8,128)(2,1)S(1)} fusion(bf16[1024,8,64]{0,2,1:T(8,128)(2,1)S(1)} %bitcast.309, f32[8,512,1024]{2,1,0:T(8,128)} %copy-done, f32[8,512]{1,0:T(8,128)S(1)} %copy-done.50, f32[8,512]{1,0:T(8,128)S(1)} %copy-done.42), kind=kOutput, calls=%fused_computation.169 | convolution fusion | flops 549715968 | bytes 18382848 | tf_op jit(solution)/shard_map/hqk,khd->qhd/dot_general | solution.py:78
  519.7 8.7 %convolution_convert_fusion.1 = bf16[1024,2048]{1,0:T(8,128)(2,1)} fusion(bf16[1024,2048]{1,0:T(8,128)(2,1)} %copy-done.78, bf16[1024,2048]{1,0:T(8,128)(2,1)S(1)} %copy-done.20), kind=kOutput, calls=%fused_computation.50 | convolution fusion | flops 4297064448 | bytes 10485760 | tf_op jit(solution)/shard_map/rd,rc->dc/dot_general | solution.py:209
  531.3 8.4 %add_convert_fusion.3 = bf16[1024,2048]{1,0:T(8,128)(2,1)} fusion(f32[1024,2048]{1,0:T(8,128)} %fusion.186, bf16[2048,1024]{1,0:T(8,128)(2,1)} %fusion.122, bf16[512,512]{0,1:T(8,128)(2,1)S(1)} %bitcast.330, bf16[512,512]{0,1:T(8,128)(2,1)S(1)} %bitcast.333), kind=kOutput, calls=%fused_computation.41 | convolution fusion | flops 2153775104 | bytes 15728640 | tf_op jit(solution)/shard_map/rd,ed->re/dot_general | solution.py:356
  559.3 7.0 add_convert_fusion
  571.9 6.6 add_convert_fusion.1
  592.9 64.3 %collective-permute-done.34 = bf16[256,512]{1,0:T(8,128)(2,1)S(1)} collective-permute-done((bf16[256,512]{1,0:T(8,128)(2,1)}, bf16[256,512]{1,0:T(8,128)(2,1)S(1)}, u32[]{:S(2)}, u32[]{:S(2)}) %collective-permute-start.34) | collective-permute-done | bytes 262176 | tf_op jit(solution)/shard_map/ppermute | solution.py:135
  670.8 7.6 %collective-permute-done.31 = bf16[256,1024]{1,0:T(8,128)(2,1)S(1)} collective-permute-done((bf16[256,1024]{1,0:T(8,128)(2,1)S(1)}, bf16[256,1024]{1,0:T(8,128)(2,1)S(1)}, u32[]{:S(2)}, u32[]{:S(2)}) %collective-permute-start.31) | collective-permute-done | bytes 524320 | tf_op jit(solution)/shard_map/ppermute | solution.py:135
  680.0 10.5 %collective-permute-done.43 = bf16[256,2048]{1,0:T(8,128)(2,1)S(1)} collective-permute-done((bf16[256,2048]{1,0:T(8,128)(2,1)S(1)}, bf16[256,2048]{1,0:T(8,128)(2,1)S(1)}, u32[]{:S(2)}, u32[]{:S(2)}) %collective-permute-start.43) | collective-permute-done | bytes 1048608 | tf_op jit(solution)/shard_map/ppermute | solution.py:135
  713.6 9.3 %collective-permute-done.45 = f32[8,640]{1,0:T(8,128)S(1)} collective-permute-done((f32[8,640]{1,0:T(8,128)S(1)}, f32[8,640]{1,0:T(8,128)S(1)}, u32[]{:S(2)}, u32[]{:S(2)}) %collective-permute-start.45) | collective-permute-done | bytes 20512 | tf_op jit(solution)/shard_map/ppermute | solution.py:135
  736.8 7.7 %collective-permute-done.25 = bf16[128,2048]{1,0:T(8,128)(2,1)S(1)} collective-permute-done((bf16[128,2048]{1,0:T(8,128)(2,1)S(1)}, bf16[128,2048]{1,0:T(8,128)(2,1)S(1)}, u32[]{:S(2)}, u32[]{:S(2)}) %collective-permute-start.25) | collective-permute-done | bytes 524320 | tf_op jit(solution)/shard_map/ppermute | solution.py:135
  (595 shorter events, 347.4 us)
Async XLA Ops:
  7.2 216.4 %all-gather.6.cloned.1.call-start = ((), (), s32[]{:S(2)}) async-start(), calls=%async_computation.4 | async-start | bytes 2621440 | tf_op jit(solution)/shard_map/all_gather | solution.py:309
  11.4 36.4 %collective-permute-start.6 = (bf16[1,704]{1,0:T(2,128)(2,1)S(1)}, bf16[1,704]{1,0:T(2,128)(2,1)S(1)}, u32[]{:S(2)}, u32[]{:S(2)}) collective-permute-start(bf16[1,704]{1,0:T(2,128)(2,1)S(1)} %broadcast_in_dim.155), channel_id=1, source_target_pairs={{0,1},{1,0},{2,3},{3,2},{4,5},{5,4},{6,7},{7,6},{8,9},{9,8},{10,11... | collective-permute-start | bytes 4232 | tf_op jit(solution)/shard_map/ppermute | solution.py:135
  16.6 99.8 %collective-permute-start.14 = (bf16[1,256,1024]{1,2,0:T(8,128)(2,1)}, bf16[1,256,1024]{1,2,0:T(8,128)(2,1)}, u32[]{:S(2)}, u32[]{:S(2)}) collective-permute-start(bf16[1,256,1024]{1,2,0:T(8,128)(2,1)} %bitcast.22), channel_id=1, source_target_pairs={{0,8},{4,12},{8,0},{12,4},{16,24},{20,28},{24,16},{28,20},{1,9},{5... | collective-permute-start | bytes 1572872 | tf_op jit(solution)/shard_map/ppermute | solution.py:135
  20.0 26.3 %collective-permute-start.3 = (bf16[1,128,2048]{2,1,0:T(8,128)(2,1)S(1)}, bf16[1,128,2048]{2,1,0:T(8,128)(2,1)S(1)}, u32[]{:S(2)}, u32[]{:S(2)}) collective-permute-start(bf16[1,128,2048]{2,1,0:T(8,128)(2,1)S(1)} %get-tuple-element.54), channel_id=1, source_target_pairs={{0,16},{4,20},{8,24},{12,28},{16,0},{20,4},{24,8},{28,12},{1,17},{... | collective-permute-start | bytes 1572872 | tf_op jit(solution)/shard_map/ppermute | solution.py:135
  21.5 103.4 %collective-permute-start.17 = (bf16[1,256,2048]{2,1,0:T(8,128)(2,1)S(1)}, bf16[1,256,2048]{2,1,0:T(8,128)(2,1)}, u32[]{:S(2)}, u32[]{:S(2)}) collective-permute-start(bf16[1,256,2048]{2,1,0:T(8,128)(2,1)S(1)} %bitcast.294), channel_id=1, source_target_pairs={{0,8},{4,12},{8,0},{12,4},{16,24},{20,28},{24,16},{28,20},{1,9},{5... | collective-permute-start | bytes 3145736 | tf_op jit(solution)/shard_map/ppermute | solution.py:135
  64.6 63.6 %collective-permute-start.20 = (bf16[1,256,2048]{2,1,0:T(8,128)(2,1)}, bf16[1,256,2048]{2,1,0:T(8,128)(2,1)}, u32[]{:S(2)}, u32[]{:S(2)}) collective-permute-start(bf16[1,256,2048]{2,1,0:T(8,128)(2,1)} %bitcast.47), channel_id=1, source_target_pairs={{0,16},{4,20},{8,24},{12,28},{16,0},{20,4},{24,8},{28,12},{1,17},{... | collective-permute-start | bytes 3145736 | tf_op jit(solution)/shard_map/ppermute | solution.py:135
  73.1 47.1 %collective-permute-start.11 = (bf16[1,256,1024]{2,1,0:T(8,128)(2,1)}, bf16[1,256,1024]{2,1,0:T(8,128)(2,1)}, u32[]{:S(2)}, u32[]{:S(2)}) collective-permute-start(bf16[1,256,1024]{2,1,0:T(8,128)(2,1)} %get-tuple-element.55), channel_id=1, source_target_pairs={{0,16},{4,20},{8,24},{12,28},{16,0},{20,4},{24,8},{28,12},{1,17},{... | collective-permute-start | bytes 1572872 | tf_op jit(solution)/shard_map/ppermute | solution.py:135
  76.6 30.0 %collective-permute-start.10 = (bf16[16,704]{1,0:T(8,128)(2,1)S(1)}, bf16[16,704]{1,0:T(8,128)(2,1)S(1)}, u32[]{:S(2)}, u32[]{:S(2)}) collective-permute-start(bf16[16,704]{1,0:T(8,128)(2,1)S(1)} %concatenate.268), channel_id=1, source_target_pairs={{0,16},{4,20},{8,24},{12,28},{16,0},{20,4},{24,8},{28,12},{1,17},{... | collective-permute-start | bytes 67592 | tf_op jit(solution)/shard_map/ppermute | solution.py:135
  88.1 138.6 %all-gather.8.cloned.1.call-start = ((), (), s32[]{:S(2)}) async-start(), calls=%async_computation.5 | async-start | bytes 2621440 | tf_op jit(solution)/shard_map/all_gather | solution.py:314
  118.7 26.4 %collective-permute-start.15 = (bf16[2,256,1024]{1,2,0:T(8,128)(2,1)}, bf16[2,256,1024]{1,2,0:T(8,128)(2,1)}, u32[]{:S(2)}, u32[]{:S(2)}) collective-permute-start(bf16[2,256,1024]{1,2,0:T(8,128)(2,1)} %pad_maximum_fusion.17), channel_id=1, source_target_pairs={{0,16},{4,20},{8,24},{12,28},{16,0},{20,4},{24,8},{28,12},{1,17},{... | collective-permute-start | bytes 3145736 | tf_op jit(solution)/shard_map/ppermute | solution.py:135
  122.5 26.4 %collective-permute-start.12 = (bf16[2,256,1024]{2,1,0:T(8,128)(2,1)}, bf16[2,256,1024]{2,1,0:T(8,128)(2,1)}, u32[]{:S(2)}, u32[]{:S(2)}) collective-permute-start(bf16[2,256,1024]{2,1,0:T(8,128)(2,1)} %pad_maximum_fusion.16), channel_id=1, source_target_pairs={{0,8},{4,12},{8,0},{12,4},{16,24},{20,28},{24,16},{28,20},{1,9},{5... | collective-permute-start | bytes 3145736 | tf_op jit(solution)/shard_map/ppermute | solution.py:135
  127.6 60.9 %collective-permute-start.18 = (bf16[2,256,2048]{2,1,0:T(8,128)(2,1)}, bf16[2,256,2048]{2,1,0:T(8,128)(2,1)}, u32[]{:S(2)}, u32[]{:S(2)}) collective-permute-start(bf16[2,256,2048]{2,1,0:T(8,128)(2,1)} %pad_maximum_fusion.6), channel_id=1, source_target_pairs={{0,16},{4,20},{8,24},{12,28},{16,0},{20,4},{24,8},{28,12},{1,17},{... | collective-permute-start | bytes 6291464 | tf_op jit(solution)/shard_map/ppermute | solution.py:135
  128.1 133.9 %all-gather.4.cloned.1.call-start = ((), (), s32[]{:S(2)}) async-start(), calls=%async_computation.2 | async-start | bytes 5242880 | tf_op jit(solution)/shard_map/all_gather | solution.py:313
  131.2 61.2 %collective-permute-start.21 = (bf16[2,256,2048]{2,1,0:T(8,128)(2,1)}, bf16[2,256,2048]{2,1,0:T(8,128)(2,1)}, u32[]{:S(2)}, u32[]{:S(2)}) collective-permute-start(bf16[2,256,2048]{2,1,0:T(8,128)(2,1)} %pad_maximum_fusion.7), channel_id=1, source_target_pairs={{0,8},{4,12},{8,0},{12,4},{16,24},{20,28},{24,16},{28,20},{1,9},{5... | collective-permute-start | bytes 6291464 | tf_op jit(solution)/shard_map/ppermute | solution.py:135
  148.1 60.3 %collective-permute-start.16 = (bf16[4,256,1024]{1,2,0:T(8,128)(2,1)}, bf16[4,256,1024]{1,2,0:T(8,128)(2,1)}, u32[]{:S(2)}, u32[]{:S(2)}) collective-permute-start(bf16[4,256,1024]{1,2,0:T(8,128)(2,1)} %pad_maximum_fusion.5), channel_id=1, source_target_pairs={{0,4},{4,0},{8,12},{12,8},{16,20},{20,16},{24,28},{28,24},{1,5},{5... | collective-permute-start | bytes 6291464 | tf_op jit(solution)/shard_map/ppermute | solution.py:135
  152.0 64.1 %collective-permute-start.13 = (bf16[4,256,1024]{2,1,0:T(8,128)(2,1)}, bf16[4,256,1024]{2,1,0:T(8,128)(2,1)}, u32[]{:S(2)}, u32[]{:S(2)}) collective-permute-start(bf16[4,256,1024]{2,1,0:T(8,128)(2,1)} %pad_maximum_fusion.4), channel_id=1, source_target_pairs={{0,4},{4,0},{8,12},{12,8},{16,20},{20,16},{24,28},{28,24},{1,5},{5... | collective-permute-start | bytes 6291464 | tf_op jit(solution)/shard_map/ppermute | solution.py:135
  163.4 537.9 %reduce-scatter.5.cloned.1.call-start = ((), (), s32[]{:S(2)}) async-start(), calls=%async_computation.6 | async-start | bytes 5242880 | tf_op jit(solution)/shard_map/reduce_scatter | solution.py:387
  192.4 43.6 %collective-permute-start.19 = (bf16[4,256,2048]{2,1,0:T(8,128)(2,1)}, bf16[4,256,2048]{2,1,0:T(8,128)(2,1)}, u32[]{:S(2)}, u32[]{:S(2)}) collective-permute-start(bf16[4,256,2048]{2,1,0:T(8,128)(2,1)} %pad_maximum_fusion), channel_id=1, source_target_pairs={{0,4},{4,0},{8,12},{12,8},{16,20},{20,16},{24,28},{28,24},{1,5},{5... | collective-permute-start | bytes 12582920 | tf_op jit(solution)/shard_map/ppermute | solution.py:135
  196.3 49.4 %collective-permute-start.22 = (bf16[4,256,2048]{2,1,0:T(8,128)(2,1)}, bf16[4,256,2048]{2,1,0:T(8,128)(2,1)}, u32[]{:S(2)}, u32[]{:S(2)}) collective-permute-start(bf16[4,256,2048]{2,1,0:T(8,128)(2,1)} %pad_maximum_fusion.1), channel_id=1, source_target_pairs={{0,4},{4,0},{8,12},{12,8},{16,20},{20,16},{24,28},{28,24},{1,5},{5... | collective-permute-start | bytes 12582920 | tf_op jit(solution)/shard_map/ppermute | solution.py:135
  496.7 211.2 %reduce-scatter.3.cloned.1.call-start = ((), (), s32[]{:S(2)}) async-start(), calls=%async_computation.3 | async-start | bytes 5242880 | tf_op jit(solution)/shard_map/reduce_scatter | solution.py:359
  506.3 52.9 %collective-permute-start.41 = (bf16[1024,2048]{1,0:T(8,128)(2,1)}, bf16[1024,2048]{1,0:T(8,128)(2,1)}, u32[]{:S(2)}, u32[]{:S(2)}) collective-permute-start(bf16[1024,2048]{1,0:T(8,128)(2,1)} %convolution_convert_fusion), channel_id=1, source_target_pairs={{0,4},{4,0},{8,12},{12,8},{16,20},{20,16},{24,28},{28,24},{1,5},{5... | collective-permute-start | bytes 12582920 | tf_op jit(solution)/shard_map/ppermute | solution.py:135
  528.5 41.8 %collective-permute-start.38 = (bf16[1024,2048]{1,0:T(8,128)(2,1)}, bf16[1024,2048]{1,0:T(8,128)(2,1)}, u32[]{:S(2)}, u32[]{:S(2)}) collective-permute-start(bf16[1024,2048]{1,0:T(8,128)(2,1)} %convolution_convert_fusion.1), channel_id=1, source_target_pairs={{0,4},{4,0},{8,12},{12,8},{16,20},{20,16},{24,28},{28,24},{1,5},{5... | collective-permute-start | bytes 12582920 | tf_op jit(solution)/shard_map/ppermute | solution.py:135
  549.8 32.1 %collective-permute-start.29 = (bf16[1024,1024]{1,0:T(8,128)(2,1)}, bf16[1024,1024]{1,0:T(8,128)(2,1)}, u32[]{:S(2)}, u32[]{:S(2)}) collective-permute-start(bf16[1024,1024]{1,0:T(8,128)(2,1)} %convolution_convert_fusion.2), channel_id=1, source_target_pairs={{0,4},{4,0},{8,12},{12,8},{16,20},{20,16},{24,28},{28,24},{1,5},{5... | collective-permute-start | bytes 6291464 | tf_op jit(solution)/shard_map/ppermute | solution.py:135
  553.8 34.8 %collective-permute-start.33 = (bf16[512,512]{1,0:T(8,128)(2,1)S(1)}, bf16[512,512]{1,0:T(8,128)(2,1)S(1)}, u32[]{:S(2)}, u32[]{:S(2)}) collective-permute-start(bf16[512,512]{1,0:T(8,128)(2,1)S(1)} %pad_maximum_fusion.22), channel_id=1, source_target_pairs={{0,16},{4,20},{8,24},{12,28},{16,0},{20,4},{24,8},{28,12},{1,17},{... | collective-permute-start | bytes 1572872 | tf_op jit(solution)/shard_map/ppermute | solution.py:135
  558.0 32.3 %collective-permute-start.36 = (bf16[512,512]{1,0:T(8,128)(2,1)S(1)}, bf16[512,512]{1,0:T(8,128)(2,1)S(1)}, u32[]{:S(2)}, u32[]{:S(2)}) collective-permute-start(bf16[512,512]{1,0:T(8,128)(2,1)S(1)} %pad_maximum_fusion.23), channel_id=1, source_target_pairs={{0,16},{4,20},{8,24},{12,28},{16,0},{20,4},{24,8},{28,12},{1,17},{... | collective-permute-start | bytes 1572872 | tf_op jit(solution)/shard_map/ppermute | solution.py:135
  569.4 95.4 %collective-permute-start.42 = (bf16[512,2048]{1,0:T(8,128)(2,1)}, bf16[512,2048]{1,0:T(8,128)(2,1)}, u32[]{:S(2)}, u32[]{:S(2)}) collective-permute-start(bf16[512,2048]{1,0:T(8,128)(2,1)} %pad_maximum_fusion.12), channel_id=1, source_target_pairs={{0,16},{4,20},{8,24},{12,28},{16,0},{20,4},{24,8},{28,12},{1,17},{... | collective-permute-start | bytes 6291464 | tf_op jit(solution)/shard_map/ppermute | solution.py:135
  580.3 88.0 %collective-permute-start.39 = (bf16[512,2048]{1,0:T(8,128)(2,1)}, bf16[512,2048]{1,0:T(8,128)(2,1)}, u32[]{:S(2)}, u32[]{:S(2)}) collective-permute-start(bf16[512,2048]{1,0:T(8,128)(2,1)} %concatenate.343), channel_id=1, source_target_pairs={{0,8},{4,12},{8,0},{12,4},{16,24},{20,28},{24,16},{28,20},{1,9},{5... | collective-permute-start | bytes 6291464 | tf_op jit(solution)/shard_map/ppermute | solution.py:135
  587.5 75.7 %collective-permute-start.30 = (bf16[512,1024]{1,0:T(8,128)(2,1)}, bf16[512,1024]{1,0:T(8,128)(2,1)S(1)}, u32[]{:S(2)}, u32[]{:S(2)}) collective-permute-start(bf16[512,1024]{1,0:T(8,128)(2,1)} %concatenate.342), channel_id=1, source_target_pairs={{0,8},{4,12},{8,0},{12,4},{16,24},{20,28},{24,16},{28,20},{1,9},{5... | collective-permute-start | bytes 3145736 | tf_op jit(solution)/shard_map/ppermute | solution.py:135
  589.3 67.9 %collective-permute-start.34 = (bf16[256,512]{1,0:T(8,128)(2,1)}, bf16[256,512]{1,0:T(8,128)(2,1)S(1)}, u32[]{:S(2)}, u32[]{:S(2)}) collective-permute-start(bf16[256,512]{1,0:T(8,128)(2,1)} %add_convert_fusion.17), channel_id=1, source_target_pairs={{0,8},{4,12},{8,0},{12,4},{16,24},{20,28},{24,16},{28,20},{1,9},{5... | collective-permute-start | bytes 786440 | tf_op jit(solution)/shard_map/ppermute | solution.py:135
  591.2 70.0 %collective-permute-start.37 = (bf16[256,512]{1,0:T(8,128)(2,1)}, bf16[256,512]{1,0:T(8,128)(2,1)}, u32[]{:S(2)}, u32[]{:S(2)}) collective-permute-start(bf16[256,512]{1,0:T(8,128)(2,1)} %add_convert_fusion.15), channel_id=1, source_target_pairs={{0,8},{4,12},{8,0},{12,4},{16,24},{20,28},{24,16},{28,20},{1,9},{5... | collective-permute-start | bytes 786440 | tf_op jit(solution)/shard_map/ppermute | solution.py:135
  666.7 23.7 %collective-permute-start.43 = (bf16[256,2048]{1,0:T(8,128)(2,1)S(1)}, bf16[256,2048]{1,0:T(8,128)(2,1)S(1)}, u32[]{:S(2)}, u32[]{:S(2)}) collective-permute-start(bf16[256,2048]{1,0:T(8,128)(2,1)S(1)} %add_convert_fusion.5), channel_id=1, source_target_pairs={{0,8},{4,12},{8,0},{12,4},{16,24},{20,28},{24,16},{28,20},{1,9},{5... | collective-permute-start | bytes 3145736 | tf_op jit(solution)/shard_map/ppermute | solution.py:135
  669.9 28.3 %collective-permute-start.40 = (bf16[256,2048]{1,0:T(8,128)(2,1)S(1)}, bf16[256,2048]{1,0:T(8,128)(2,1)S(1)}, u32[]{:S(2)}, u32[]{:S(2)}) collective-permute-start(bf16[256,2048]{1,0:T(8,128)(2,1)S(1)} %add_convert_fusion.7), channel_id=1, source_target_pairs={{0,16},{4,20},{8,24},{12,28},{16,0},{20,4},{24,8},{28,12},{1,17},{... | collective-permute-start | bytes 3145736 | tf_op jit(solution)/shard_map/ppermute | solution.py:135
  (112 other events, 2179.6 us)
Sparse Core Ops, SparseCore 0:
  88.2 45.2 all-gather.5
  135.7 44.6 all-gather.7
  182.5 79.4 all-gather.3
  496.8 75.2 reduce-scatter.4
  574.4 77.2 reduce-scatter.2

commit v2 on v1

v2 whole, which is shorter than its diff:
```python
import functools
import math

import jax
import jax.numpy as jnp
from jax import lax
from jax.experimental import pallas as pl
from jax.experimental.pallas import tpu as pltpu
from jax.sharding import PartitionSpec as P

HEAD_DIM = 64
ROT = 32
PAIR = 2 * HEAD_DIM


eps = 1e-05
masked_score = -1e30
f32 = jnp.float32
bf16 = jnp.bfloat16
NN = (((1,), (0,)), ((), ()))
NT = (((1,), (1,)), ((), ()))
TN = (((0,), (0,)), ((), ()))
once = pl.Buffered(1)


def dot(a, b, dims):
    return lax.dot_general(a, b, dims, preferred_element_type=f32)


def params(mib):
    return pltpu.CompilerParams(vmem_limit_bytes=mib * 1024 * 1024)


def cost(flops, nbytes, exps=0):
    return pl.CostEstimate(flops=int(flops), bytes_accessed=int(nbytes), transcendentals=int(exps))


def shape(dims, dtype):
    return jax.ShapeDtypeStruct(dims, dtype)


def turned(field, tables):
    cosine, ahead, behind = tables
    half = ROT // 2
    wide = field.shape[1]
    return (
        field * cosine
        + pltpu.roll(field, wide - half, 1) * ahead
        + pltpu.roll(field, half, 1) * behind
    )


def turned_back(grad, tables):
    cosine, ahead, behind = tables
    half = ROT // 2
    wide = grad.shape[1]
    return (
        grad * cosine
        + pltpu.roll(grad * ahead, half, 1)
        + pltpu.roll(grad * behind, wide - half, 1)
    )


def qkv_kernel(ln_ref, qka_ref, qkb_ref, va_ref, vb_ref, bias_ref, c_ref, a_ref, b_ref, out_ref):
    kind = pl.program_id(0)
    half = ln_ref.shape[1] // 2
    rows = ln_ref.shape[0]
    tile = min(512, rows)
    tables_of = lambda r: (c_ref[r, :], a_ref[r, :], b_ref[r, :])
    for start in range(0, rows, tile):
        r = slice(start, start + tile)

        @pl.when(kind < 2)
        def _():
            raw = dot(ln_ref[r, :half], qka_ref[...], NN) + dot(ln_ref[r, half:], qkb_ref[...], NN)
            raw = raw + bias_ref[0]
            for pair in range(raw.shape[1] // PAIR):
                cols = slice(pair * PAIR, (pair + 1) * PAIR)
                out_ref[0, r, cols] = turned(raw[:, cols], tables_of(r)).astype(bf16)

        @pl.when(kind == 2)
        def _():
            raw = dot(ln_ref[r, :half], va_ref[...], NN) + dot(ln_ref[r, half:], vb_ref[...], NN)
            out_ref[0, r, :] = (raw + bias_ref[0]).astype(bf16)


def project(ln, qk, vo, bias, tables):
    rows, width = ln.shape
    heads = bias.shape[1]
    half = width // 2
    qk_spec = pl.BlockSpec((half, heads), lambda i: (0, jnp.minimum(i, 1)))
    v_spec = pl.BlockSpec((half, heads), lambda i: (0, 0), pipeline_mode=once)
    table_spec = pl.BlockSpec((rows, PAIR), lambda i: (0, 0), pipeline_mode=once)
    return pl.pallas_call(
        qkv_kernel,
        grid=(3,),
        in_specs=[
            pl.BlockSpec((rows, width), lambda i: (0, 0), pipeline_mode=once),
            qk_spec,
            qk_spec,
            v_spec,
            v_spec,
            pl.BlockSpec((1, 1, heads), lambda i: (i, 0, 0)),
            table_spec,
            table_spec,
            table_spec,
        ],
        out_specs=pl.BlockSpec((1, rows, heads), lambda i: (i, 0, 0)),
        out_shape=shape((3, rows, heads), bf16),
        compiler_params=params(48),
        cost_estimate=cost(6 * rows * width * heads, 12 << 20),
        name="project",
    )(ln, qk[0], qk[1], vo[0], vo[1], bias[:, None, :], *tables)


def head_lanes(head):
    lane = lax.broadcasted_iota(jnp.int32, (1, PAIR), 1)
    return (lane // HEAD_DIM) == (head % 2)


def masked_scores(keys, queries, first, length):
    scores = dot(keys, queries, NT)
    key = lax.broadcasted_iota(jnp.int32, scores.shape, 0)
    row = first + lax.broadcasted_iota(jnp.int32, (1, scores.shape[1]), 1)
    return jnp.where(key <= jnp.minimum(row, length - 1), scores, masked_score)


def attend_kernel(block, len_ref, q_ref, k_ref, v_ref, out_ref, total_ref, q_mine, v_turned):
    head = pl.program_id(0)
    lanes = head_lanes(head)
    rows = q_ref.shape[1]
    zero = jnp.zeros((rows, PAIR), bf16)
    scale = jnp.asarray(1.0 / math.sqrt(HEAD_DIM), bf16)
    q_mine[...] = jnp.where(lanes, q_ref[0] * scale, zero)
    v_turned[...] = jnp.where(lanes, v_ref[0], zero).T
    length = len_ref[0]
    for first in range(0, rows, block):
        n = first + block
        r = slice(first, n)
        scores = masked_scores(k_ref[0, :n, :], q_mine[r, :], first, length)
        top = jnp.max(scores, 0, keepdims=True)
        exped = jnp.exp(scores - top)
        total = jnp.sum(exped, 0, keepdims=True)
        probs = (exped * (1.0 / total)).astype(bf16)
        mixed = dot(v_turned[:, :n], probs, NN).T.astype(bf16)
        total_ref[0, :, r] = top + jnp.log(total)

        @pl.when(head % 2 == 0)
        def _():
            out_ref[r, :] = mixed

        @pl.when(head % 2 == 1)
        def _():
            out_ref[r, :] = out_ref[r, :] + mixed


def attend(qkv, length):
    _, rows, width = qkv.shape
    heads = width // HEAD_DIM
    kind = lambda c: pl.BlockSpec((1, rows, PAIR), lambda h, n: (c, 0, h // 2))
    return pl.pallas_call(
        functools.partial(attend_kernel, min(512, rows)),
        grid_spec=pltpu.PrefetchScalarGridSpec(
            num_scalar_prefetch=1,
            grid=(heads,),
            in_specs=[kind(0), kind(1), kind(2)],
            out_specs=[
                pl.BlockSpec((rows, PAIR), lambda h, n: (0, h // 2)),
                pl.BlockSpec((1, 1, rows), lambda h, n: (h, 0, 0)),
            ],
            scratch_shapes=[pltpu.VMEM((rows, PAIR), bf16), pltpu.VMEM((PAIR, rows), bf16)],
        ),
        out_shape=[shape((rows, width), bf16), shape((heads, 1, rows), f32)],
        compiler_params=params(48),
        cost_estimate=cost(16 * rows * rows * width, 4 << 20, rows * rows * heads),
        name="attend",
    )(length, qkv, qkv, qkv)


def attend_back_kernel(
    block, len_ref, q_ref, k_ref, v_ref, do_ref, total_ref, c_ref, a_ref, b_ref,
    grad_ref, q_mine, do_mine, k_turned, key_sum, value_sum,
):
    head = pl.program_id(0)
    lanes = head_lanes(head)
    rows = q_ref.shape[1]
    zero = jnp.zeros((rows, PAIR), bf16)
    scale = 1.0 / math.sqrt(HEAD_DIM)
    q_mine[...] = jnp.where(lanes, q_ref[0] * jnp.asarray(scale, bf16), zero)
    do_mine[...] = jnp.where(lanes, do_ref[...], zero)
    k_turned[...] = jnp.where(lanes, k_ref[0], zero).T
    length = len_ref[0]

    def put(kind, r, value):
        value = value.astype(bf16)

        @pl.when(head % 2 == 0)
        def _():
            grad_ref[kind, r, :] = value

        @pl.when(head % 2 == 1)
        def _():
            grad_ref[kind, r, :] = grad_ref[kind, r, :] + value

    tables_of = lambda r: (c_ref[r, :], a_ref[r, :], b_ref[r, :])
    for first in range(rows - block, -1, -block):
        n = first + block
        r = slice(first, n)
        scores = masked_scores(k_ref[0, :n, :], q_mine[r, :], first, length)
        probs = jnp.exp(scores - total_ref[0, :, r])
        grad_probs = dot(v_ref[0, :n, :], do_mine[r, :], NT)
        product = probs * grad_probs
        delta = jnp.sum(product, 0, keepdims=True)
        grad_scores = (product - probs * delta).astype(bf16)
        keys = dot(grad_scores, q_mine[r, :], NN)
        vals = dot(probs.astype(bf16), do_mine[r, :], NN)
        if n == rows:
            key_sum[...] = keys
            value_sum[...] = vals
        else:
            key_sum[:n, :] += keys
            value_sum[:n, :] += vals
        grad_query = dot(k_turned[:, :n], grad_scores, NN).T * scale
        put(0, r, turned_back(grad_query, tables_of(r)))
    for first in range(0, rows, block):
        r = slice(first, first + block)
        put(1, r, turned_back(key_sum[r, :], tables_of(r)))
        put(2, r, value_sum[r, :])


def attend_back(qkv, grad_mixed, totals, length, tables):
    _, rows, width = qkv.shape
    heads = width // HEAD_DIM
    kind = lambda c: pl.BlockSpec((1, rows, PAIR), lambda h, n: (c, 0, h // 2))
    table_spec = pl.BlockSpec((rows, PAIR), lambda h, n: (0, 0))
    return pl.pallas_call(
        functools.partial(attend_back_kernel, min(512, rows)),
        grid_spec=pltpu.PrefetchScalarGridSpec(
            num_scalar_prefetch=1,
            grid=(heads,),
            in_specs=[
                kind(0),
                kind(1),
                kind(2),
                pl.BlockSpec((rows, PAIR), lambda h, n: (0, h // 2)),
                pl.BlockSpec((1, 1, rows), lambda h, n: (h, 0, 0)),
                table_spec,
                table_spec,
                table_spec,
            ],
            out_specs=pl.BlockSpec((3, rows, PAIR), lambda h, n: (0, 0, h // 2)),
            scratch_shapes=[
                pltpu.VMEM((rows, PAIR), bf16),
                pltpu.VMEM((rows, PAIR), bf16),
                pltpu.VMEM((PAIR, rows), bf16),
                pltpu.VMEM((rows, PAIR), f32),
                pltpu.VMEM((rows, PAIR), f32),
            ],
        ),
        out_shape=shape((3, rows, width), bf16),
        compiler_params=params(48),
        cost_estimate=cost(40 * rows * rows * width, 8 << 20, rows * rows * heads),
        name="attend_back",
    )(length, qkv, qkv, qkv, grad_mixed, totals, *tables)


def feed_kernel(
    tile, steps, ln_ref, mixed_ref, oa_ref, ob_ref, w1a_ref, w1b_ref, w2a_ref, w2b_ref, bias_ref,
    branch_ref, hidden_ref, slope_ref, acc,
):
    step = pl.program_id(0)
    rows = ln_ref.shape[0]
    half = ln_ref.shape[1] // 2
    c0 = math.sqrt(2.0 / math.pi)
    c1 = 0.044715

    @pl.loop(0, rows // tile)
    def _(m):
        r = pl.ds(pl.multiple_of(m * tile, tile), tile)
        pre = dot(ln_ref[r, :half], w1a_ref[...], NN) + dot(ln_ref[r, half:], w1b_ref[...], NN)
        pre = pre + bias_ref[...]
        square = pre * pre
        bent = jnp.tanh(c0 * (pre + c1 * (square * pre)))
        half_pre = 0.5 * pre
        hidden = (half_pre * (1.0 + bent)).astype(bf16)
        hidden_ref[r, :] = hidden
        slope_ref[r, :] = 0.5 * (1.0 + bent) + half_pre * (1.0 - bent * bent) * (
            c0 * (1.0 + (3.0 * c1) * square)
        )
        parts = (dot(hidden, w2a_ref[...], NT), dot(hidden, w2b_ref[...], NT))
        for side, part in enumerate(parts):
            cols = slice(side * half, (side + 1) * half)

            @pl.when(step == 0)
            def _():
                out_ref = (oa_ref, ob_ref)[side]
                acc[r, cols] = part + dot(mixed_ref[r, :], out_ref[...], NT)

            @pl.when((step > 0) & (step < steps - 1))
            def _():
                acc[r, cols] += part

            @pl.when(step == steps - 1)
            def _():
                branch_ref[r, cols] = (acc[r, cols] + part).astype(bf16)


def feed(ln, mixed, vo, w1, w2, bias, tile_f):
    rows, width = ln.shape
    half = width // 2
    hidden = bias.shape[1]
    heads = mixed.shape[1]
    steps = hidden // tile_f
    whole = lambda dims: pl.BlockSpec(dims, lambda i: (0, 0), pipeline_mode=once)
    out_spec = pl.BlockSpec((half, heads), lambda i: (0, 1), pipeline_mode=once)
    weight = pl.BlockSpec((half, tile_f), lambda i: (0, i))
    by_row = pl.BlockSpec((rows, tile_f), lambda i: (0, i))
    return pl.pallas_call(
        functools.partial(feed_kernel, min(512, rows), steps),
        grid=(steps,),
        in_specs=[whole((rows, width)), whole((rows, heads)), out_spec, out_spec]
        + [weight] * 4
        + [pl.BlockSpec((1, tile_f), lambda i: (0, i))],
        out_specs=[whole((rows, width)), by_row, by_row],
        out_shape=[
            shape((rows, width), bf16),
            shape((rows, hidden), bf16),
            shape((rows, hidden), f32),
        ],
        scratch_shapes=[pltpu.VMEM((rows, width), f32)],
        compiler_params=params(58),
        cost_estimate=cost(4 * rows * width * hidden, 40 << 20, rows * hidden),
        name="feed",
    )(ln, mixed, vo[0], vo[1], w1[0], w1[1], w2[0], w2[1], bias)


def feed_back_kernel(
    tile, tile_d, ln_ref, g_ref, w1a_ref, w1b_ref, w2a_ref, w2b_ref, hidden_ref, slope_ref,
    sum_ref, k1_ref, s1_ref, k2_ref, s2_ref, bias_ref, grad_pre,
):
    step = pl.program_id(0)
    rows, width = ln_ref.shape
    half = width // 2

    @pl.loop(0, rows // tile)
    def _(m):
        r = pl.ds(pl.multiple_of(m * tile, tile), tile)
        grad = dot(g_ref[r, :half], w2a_ref[...], NN) + dot(g_ref[r, half:], w2b_ref[...], NN)
        grad = (grad * slope_ref[r, :]).astype(bf16)
        grad_pre[r, :] = grad
        for side, weight_ref in enumerate((w1a_ref, w1b_ref)):
            cols = slice(side * half, (side + 1) * half)
            part = dot(grad, weight_ref[...], NT)

            @pl.when(step == 0)
            def _():
                sum_ref[r, cols] = part

            @pl.when(step > 0)
            def _():
                sum_ref[r, cols] += part

    bias_ref[...] = jnp.sum(grad_pre[...].astype(f32), axis=0, keepdims=True)

    @pl.loop(0, half // tile_d)
    def _(k):
        c = pl.ds(pl.multiple_of(k * tile_d, tile_d), tile_d)
        far = pl.ds(pl.multiple_of(half + k * tile_d, tile_d), tile_d)
        k2_ref[c, :] = dot(g_ref[:, c], hidden_ref[...], TN).astype(bf16)
        s2_ref[c, :] = dot(g_ref[:, far], hidden_ref[...], TN).astype(bf16)
        k1_ref[c, :] = dot(ln_ref[:, c], grad_pre[...], TN).astype(bf16)
        s1_ref[c, :] = dot(ln_ref[:, far], grad_pre[...], TN).astype(bf16)


def feed_back(ln, grads, w1, w2, hidden, slope, tile_f):
    rows, width = ln.shape
    half = width // 2
    units = hidden.shape[1]
    steps = units // tile_f
    whole = pl.BlockSpec((rows, width), lambda i: (0, 0), pipeline_mode=once)
    weight = pl.BlockSpec((half, tile_f), lambda i: (0, i))
    by_row = pl.BlockSpec((rows, tile_f), lambda i: (0, i))
    return pl.pallas_call(
        functools.partial(feed_back_kernel, min(512, rows), min(512, half)),
        grid=(steps,),
        in_specs=[whole, whole] + [weight] * 4 + [by_row, by_row],
        out_specs=[whole] + [weight] * 4 + [pl.BlockSpec((1, tile_f), lambda i: (0, i))],
        out_shape=[shape((rows, width), f32)]
        + [shape((half, units), bf16)] * 4
        + [shape((1, units), f32)],
        scratch_shapes=[pltpu.VMEM((rows, tile_f), bf16)],
        compiler_params=params(60),
        cost_estimate=cost(8 * rows * width * units, 60 << 20),
        name="feed_back",
    )(ln, grads, w1[0], w1[1], w2[0], w2[1], hidden, slope)


def mixed_grad_kernel(g_ref, oa_ref, ob_ref, out_ref):
    half = g_ref.shape[1] // 2
    out_ref[...] = (
        dot(g_ref[:, :half], oa_ref[...], NN) + dot(g_ref[:, half:], ob_ref[...], NN)
    ).astype(bf16)


def mixed_grad(grads, vo, heads):
    rows, width = grads.shape
    half = width // 2
    tile = min(512, rows)
    out_spec = pl.BlockSpec((half, heads), lambda i: (0, 1), pipeline_mode=once)
    return pl.pallas_call(
        mixed_grad_kernel,
        grid=(rows // tile,),
        in_specs=[pl.BlockSpec((tile, width), lambda i: (i, 0)), out_spec, out_spec],
        out_specs=pl.BlockSpec((tile, heads), lambda i: (i, 0)),
        out_shape=shape((rows, heads), bf16),
        compiler_params=params(40),
        cost_estimate=cost(2 * rows * width * heads, 7 << 20),
        name="mixed_grad",
    )(grads, vo[0], vo[1])


def ln_grad_kernel(grad_ref, qka_ref, qkb_ref, va_ref, vb_ref, sum_ref, out_ref):
    half = sum_ref.shape[1] // 2
    heads = grad_ref.shape[2]
    sides = ((qka_ref, va_ref), (qkb_ref, vb_ref))
    for side, (qk_ref, v_ref) in enumerate(sides):
        cols = slice(side * half, (side + 1) * half)
        total = sum_ref[:, cols]
        total += dot(grad_ref[0], qk_ref[:, :heads], NT)
        total += dot(grad_ref[1], qk_ref[:, heads:], NT)
        total += dot(grad_ref[2], v_ref[...], NT)
        out_ref[:, cols] = total.astype(bf16)


def ln_grad(grad_qkv, qk, vo, partial_sum):
    _, rows, heads = grad_qkv.shape
    width = partial_sum.shape[1]
    half = width // 2
    tile = min(512, rows)
    qk_spec = pl.BlockSpec((half, 2 * heads), lambda i: (0, 0), pipeline_mode=once)
    v_spec = pl.BlockSpec((half, heads), lambda i: (0, 0), pipeline_mode=once)
    return pl.pallas_call(
        ln_grad_kernel,
        grid=(rows // tile,),
        in_specs=[
            pl.BlockSpec((3, tile, heads), lambda i: (0, i, 0)),
            qk_spec,
            qk_spec,
            v_spec,
            v_spec,
            pl.BlockSpec((tile, width), lambda i: (i, 0)),
        ],
        out_specs=pl.BlockSpec((tile, width), lambda i: (i, 0)),
        out_shape=shape((rows, width), bf16),
        compiler_params=params(48),
        cost_estimate=cost(6 * rows * width * heads, 22 << 20),
        name="ln_grad",
    )(grad_qkv, qk[0], qk[1], vo[0], vo[1], partial_sum)


def weight_grad_kernel(ln_ref, g_ref, grad_ref, mixed_ref, kqk_ref, kvo_ref, sqk_ref, svo_ref, bias_ref):
    heads = mixed_ref.shape[1]
    step = pl.program_id(0)
    steps = pl.num_programs(0)
    for kind in range(3):
        @pl.when(step == 0)
        def _():
            bias_ref[kind] = jnp.sum(grad_ref[kind].astype(f32), axis=0, keepdims=True)

    for qk_ref, vo_ref, here in ((kqk_ref, kvo_ref, step < steps // 2), (sqk_ref, svo_ref, step >= steps // 2)):
        @pl.when(here)
        def _():
            qk_ref[:, :heads] = dot(ln_ref[...], grad_ref[0], TN).astype(bf16)
            qk_ref[:, heads:] = dot(ln_ref[...], grad_ref[1], TN).astype(bf16)
            vo_ref[:, :heads] = dot(ln_ref[...], grad_ref[2], TN).astype(bf16)
            vo_ref[:, heads:] = dot(g_ref[...], mixed_ref[...], TN).astype(bf16)


def weight_grad(ln, grads, grad_qkv, mixed):
    rows, width = ln.shape
    heads = mixed.shape[1]
    half = width // 2
    tile = min(512, half)
    near = half // tile
    column = pl.BlockSpec((rows, tile), lambda i: (0, i))
    kept = pl.BlockSpec((tile, 2 * heads), lambda i: (jnp.minimum(i, near - 1), 0))
    sent = pl.BlockSpec((tile, 2 * heads), lambda i: (jnp.maximum(i - near, 0), 0))
    return pl.pallas_call(
        weight_grad_kernel,
        grid=(2 * near,),
        in_specs=[
            column,
            column,
            pl.BlockSpec((3, rows, heads), lambda i: (0, 0, 0), pipeline_mode=once),
            pl.BlockSpec((rows, heads), lambda i: (0, 0), pipeline_mode=once),
        ],
        out_specs=[kept, kept, sent, sent, pl.BlockSpec((3, 1, heads), lambda i: (0, 0, 0))],
        out_shape=[shape((half, 2 * heads), bf16)] * 4 + [shape((3, 1, heads), f32)],
        compiler_params=params(48),
        cost_estimate=cost(8 * rows * width * heads, 20 << 20),
        name="weight_grad",
    )(ln, grads, grad_qkv, mixed)


def normalize(rows_in):
    row_mean = jnp.mean(rows_in, -1, keepdims=True)
    centred = rows_in - row_mean
    variance = jnp.mean(centred * centred, -1, keepdims=True)
    inv_scale = lax.rsqrt(variance + eps)
    return (centred * inv_scale, inv_scale)


def rotary_tables(row_count, col_count):
    half_rot = ROT // 2
    column = jnp.arange(col_count) % HEAD_DIM
    exponent = (2 * (column % half_rot)).astype(jnp.float32) / ROT
    frequency = jnp.exp(-math.log(10000.0) * exponent)
    angles = jnp.arange(row_count).astype(jnp.float32)[:, None] * frequency[None, :]
    inside = column < ROT
    cosine = jnp.where(inside, jnp.cos(angles), 1.0)
    sine_part = jnp.sin(angles)
    ahead_sin = jnp.where(column < half_rot, -sine_part, 0.0)
    behind_sin = jnp.where(inside & (column >= half_rot), sine_part, 0.0)
    return (cosine, ahead_sin, behind_sin)


def flip(array, axis_name, bit):
    size = lax.axis_size(axis_name)
    return lax.ppermute(array, axis_name, [(i, i ^ (1 << bit)) for i in range(size)])


def bits_of(size):
    return size.bit_length() - 1


def swap_blocks(array, index, axis, blocks):
    for bit in range(bits_of(blocks)):
        dims = array.shape
        parts = dims[:axis] + (blocks >> (bit + 1), 2, 1 << bit, dims[axis] // blocks)
        view = array.reshape(parts + dims[axis + 1 :])
        other = jnp.flip(view, axis=axis + 1)
        array = jnp.where((index >> bit) & 1 == 1, other, view).reshape(dims)
    return array


def reversed_bits(value, bits):
    return sum(((value >> k) & 1) << (bits - 1 - k) for k in range(bits))


def xor_columns(array, index, blocks):
    width = array.shape[-1] // blocks
    bits = bits_of(blocks)
    pieces = [
        lax.dynamic_slice_in_dim(
            array, (index ^ reversed_bits(p, bits)) * width, width, array.ndim - 1
        )
        for p in range(blocks)
    ]
    return jnp.concatenate(pieces, -1)


def plain_columns(array, index, blocks):
    width = array.shape[-1] // blocks
    bits = bits_of(blocks)
    pieces = []
    for q in range(blocks):
        place = reversed_bits(index ^ q, bits)
        pieces.append(lax.dynamic_slice_in_dim(array, place * width, width, array.ndim - 1))
    return jnp.concatenate(pieces, -1)


def gather_first(shard, order):
    return {0: shard, 1 << order[0]: flip(shard, "dp", order[0])}


def gather_second(blocks, order):
    masks = sorted(blocks)
    bit = order[len(bin(len(blocks))) - 3]
    return flip(jnp.concatenate([blocks[m] for m in masks], 0), "dp", bit)


def with_arrived(blocks, arrived, order):
    rows = blocks[0].shape[0]
    bit = order[len(bin(len(blocks))) - 3]
    fresh = dict(blocks)
    for i, m in enumerate(sorted(blocks)):
        fresh[m | (1 << bit)] = arrived[i * rows : (i + 1) * rows]
    return fresh


def gather_upper(blocks, order, arrived=None):
    while len(blocks) < (1 << len(order)):
        if arrived is None:
            arrived = gather_second(blocks, order)
        blocks = with_arrived(blocks, arrived, order)
        arrived = None
    return blocks


def gather_core(blocks, order):
    bits = len(order) + 1
    near = jnp.concatenate([blocks[reversed_bits(p, bits)] for p in range(1 << len(order))], 0)
    return near, flip(near, "dp", 0)


def by_position(kept, order, rows):
    bits = len(order) + 1
    count = 1 << (bits - 1)
    return {reversed_bits(p, bits): kept[p * rows : (p + 1) * rows] for p in range(count)}


def merge(kept, arrived):
    return (kept.astype(f32) + arrived.astype(f32)).astype(bf16)


def scatter_start(blocks, bit):
    given = [m for m in blocks if (m >> bit) & 1]
    return flip(jnp.concatenate([blocks[m] for m in given], 0), "dp", bit)


def scatter_end(blocks, arrived, bit, last):
    rows = blocks[0].shape[0]
    fresh = {}
    for i, m in enumerate([m for m in blocks if (m >> bit) & 1]):
        target = m ^ (1 << bit)
        total = blocks[target].astype(f32) + arrived[i * rows : (i + 1) * rows].astype(f32)
        fresh[target] = total if last else total.astype(bf16)
    return fresh


def route_order(last):
    return [b for b in range(bits_of(lax.axis_size("dp")) - 1, -1, -1) if b != last]


def route_first(block, last):
    return jnp.stack([block, flip(block, "dp", route_order(last)[0])], 0)


def route_rest(stack, wanted, index, last):
    order = route_order(last)
    for bit in order[1:]:
        stack = jnp.concatenate([stack, flip(stack, "dp", bit)], 0)

    def place(mask):
        return sum(((mask >> bit) & 1) << k for k, bit in enumerate(order))

    mine = wanted[index]
    theirs = wanted[index ^ (1 << last)]
    given = lax.dynamic_index_in_dim(stack, place(index ^ theirs), 0, keepdims=False)
    held = lax.dynamic_index_in_dim(stack, place(index ^ mine), 0, keepdims=False)
    arrived = flip(given, "dp", last)
    return jnp.where(((index ^ mine) >> last) & 1 == 1, arrived, held)


def gather_small(vector, data_index, tensor_index):
    data_count, tensor_count = lax.axis_size("dp"), lax.axis_size("tensor")
    stack = vector[None]
    for bit in range(bits_of(tensor_count)):
        stack = jnp.concatenate([stack, flip(stack, "tensor", bit)], 0)
    for bit in range(bits_of(data_count)):
        stack = jnp.concatenate([stack, flip(stack, "dp", bit)], 0)
    stack = swap_blocks(stack, data_index * tensor_count + tensor_index, 0, stack.shape[0])
    return stack.reshape(data_count, tensor_count, vector.shape[0])


def scatter_small(blocks, data_index, tensor_index):
    data_count, tensor_count = lax.axis_size("dp"), lax.axis_size("tensor")
    stack = swap_blocks(blocks, data_index * tensor_count + tensor_index, 0, blocks.shape[0])
    for bit in range(bits_of(data_count) - 1, -1, -1):
        half = stack.shape[0] // 2
        stack = stack[:half] + flip(stack[half:], "dp", bit)
    for bit in range(bits_of(tensor_count) - 1, -1, -1):
        half = stack.shape[0] // 2
        stack = stack[:half] + flip(stack[half:], "tensor", bit)
    return stack[0]


def after(values, *others):
    held = lax.optimization_barrier((tuple(values), tuple(others)))
    return held[0]


def shards(
    hidden_in,
    cotangent,
    lengths,
    slot_of_seq,
    seq_of_slot,
    qkv_weight,
    out_weight,
    fc1_weight,
    fc2_weight,
    ln_gain,
    ln_bias,
    qkv_bias,
    out_bias,
    fc1_bias,
    fc2_bias,
):
    rows_here = hidden_in.shape[1]
    width = hidden_in.shape[2]
    tensor_count = lax.axis_size("tensor")
    data_count = lax.axis_size("dp")
    tensor_index = lax.axis_index("tensor")
    data_index = lax.axis_index("dp")
    seq_len = rows_here * tensor_count
    heads_local = qkv_weight.shape[2]
    hidden_local = fc1_weight.shape[1]
    block = width // data_count
    length = lengths[seq_of_slot[data_index]]
    bits = bits_of(data_count)
    x_first = list(range(1, bits))
    y_first = x_first[::-1]
    tile_f = min(512, hidden_local)

    half_rows = rows_here // 2
    lasts = (bits - 1, bits - 2)
    halves = (hidden_in[0, :half_rows], hidden_in[0, half_rows:])
    firsts = [route_first(h, last) for h, last in zip(halves, lasts)]
    qk_shard = qkv_weight[:, :2].reshape(block, 2 * heads_local)
    vo_shard = jnp.concatenate([qkv_weight[:, 2], out_weight], 1)
    qk_shard, vo_shard = after((qk_shard, vo_shard), *firsts)
    qk_blocks = gather_first(qk_shard, x_first)
    vo_blocks = gather_first(vo_shard, y_first)
    routed = jnp.concatenate(
        [route_rest(f, seq_of_slot, data_index, last) for f, last in zip(firsts, lasts)], 0
    )
    slot_rows = xor_columns(routed, data_index, data_count)
    rows_full = lax.all_gather(slot_rows, "tensor", axis=0, tiled=True)

    positions = tensor_index * rows_here + jnp.arange(rows_here, dtype=jnp.int32)
    valid = (positions < length)[:, None]
    cot_plain, = after((cotangent[0],), routed)
    cot_rows = xor_columns(cot_plain, data_index, data_count)
    grad_low = jnp.where(valid, cot_rows, jnp.zeros_like(cot_rows))
    grads = lax.all_gather(grad_low, "tensor", axis=0, tiled=True)

    w_qk = gather_core(gather_upper(qk_blocks, x_first), x_first)
    w_vo = gather_core(gather_upper(vo_blocks, y_first), y_first)
    fc1_shard, fc2_shard = after(
        (fc1_weight, fc2_weight), routed, *qk_blocks.values(), *vo_blocks.values()
    )
    fc1_blocks = gather_first(fc1_shard, x_first)
    fc2_blocks = gather_first(fc2_shard, y_first)
    fc1_next = gather_second(fc1_blocks, x_first)
    fc2_next = gather_second(fc2_blocks, y_first)

    small = jnp.concatenate([ln_gain, ln_bias, out_bias, fc2_bias, qkv_bias, fc1_bias])
    gathered = gather_small(small, data_index, tensor_index)
    s = ln_gain.shape[0]
    vectors = [
        xor_columns(gathered[:, :, i * s : (i + 1) * s].reshape(width), data_index, data_count)
        for i in range(4)
    ]
    gain, shift, bias_a, bias_b = [v.astype(f32) for v in vectors]
    q = qkv_bias.shape[0]
    bias_qkv = lax.dynamic_slice_in_dim(
        gathered[:, :, 4 * s : 4 * s + q].reshape(3, width), tensor_index * heads_local, heads_local, 1
    ).astype(f32)
    bias_fc1 = lax.dynamic_slice_in_dim(
        gathered[:, :, 4 * s + q :].reshape(1, hidden_local * tensor_count),
        tensor_index * hidden_local,
        hidden_local,
        1,
    ).astype(f32)

    full_normed, _ = normalize(rows_full.astype(f32))
    ln = (full_normed * gain + shift).astype(bf16)
    tables = rotary_tables(seq_len, PAIR)
    size = length.reshape(1)
    qkv = project(ln, w_qk, w_vo, bias_qkv, tables)
    fc1_next, fc2_next = after((fc1_next, fc2_next), qkv)
    w_fc1 = gather_core(gather_upper(fc1_blocks, x_first, fc1_next), x_first)
    w_fc2 = gather_core(gather_upper(fc2_blocks, y_first, fc2_next), y_first)
    attend_in, = after((qkv,), w_fc1[0], w_fc2[0])
    mixed, totals = attend(attend_in, size)
    branch_part, hidden, slope = feed(ln, mixed, w_vo, w_fc1, w_fc2, bias_fc1, tile_f)
    branch_sum = lax.psum_scatter(branch_part, "tensor", scatter_dimension=0, tiled=True)

    feed_sum, k1, s1, k2, s2, grad_fc1_b = feed_back(ln, grads, w_fc1, w_fc2, hidden, slope, tile_f)
    c1, c2 = flip(s1, "dp", 0), flip(s2, "dp", 0)
    grads_again, = after((grads,), feed_sum)
    grad_mixed = mixed_grad(grads_again, w_vo, heads_local)
    grad_qkv = attend_back(qkv, grad_mixed, totals, size, tables)
    grad_qkv, = after((grad_qkv,), branch_sum)
    ln_part = ln_grad(grad_qkv, w_qk, w_vo, feed_sum)
    grad_ln = lax.psum_scatter(ln_part, "tensor", scatter_dimension=0, tiled=True).astype(f32)
    k1, k2 = after((k1, k2), ln_part)
    m1 = by_position(merge(k1, c1), x_first, block)
    m2 = by_position(merge(k2, c2), y_first, block)
    f1, f2 = scatter_start(m1, x_first[0]), scatter_start(m2, y_first[0])
    mixed_again, = after((mixed,), m1, m2)
    kqk, kvo, sqk, svo, grad_qkv_b = weight_grad(ln, grads, grad_qkv, mixed_again)
    cqk, cvo = flip(sqk, "dp", 0), flip(svo, "dp", 0)
    mqk = by_position(merge(kqk, cqk), x_first, block)
    mvo = by_position(merge(kvo, cvo), y_first, block)
    fqk, fvo = scatter_start(mqk, x_first[0]), scatter_start(mvo, y_first[0])
    m1, m2 = after((m1, m2), mqk, mvo)
    for step in range(len(x_first)):
        last = step == len(x_first) - 1
        m1 = scatter_end(m1, f1, x_first[step], last)
        m2 = scatter_end(m2, f2, y_first[step], last)
        if not last:
            f1, f2 = scatter_start(m1, x_first[step + 1]), scatter_start(m2, y_first[step + 1])
            grad_ln, = after((grad_ln,), m1, m2)

    grad_bias = jnp.sum(grad_low.astype(f32), axis=0)
    slot_f32 = slot_rows.astype(f32)
    normed, inv_scale = normalize(slot_f32)
    grad_gain = jnp.sum(grad_ln * normed, axis=0)
    grad_shift = jnp.sum(grad_ln, axis=0)
    grad_norm = grad_ln * gain
    grad_from_norm = inv_scale * (
        grad_norm
        - jnp.mean(grad_norm, -1, keepdims=True)
        - normed * jnp.mean(grad_norm * normed, -1, keepdims=True)
    )
    grad_slot = (cot_rows.astype(f32) + grad_from_norm).astype(bf16)
    grad_slot = plain_columns(grad_slot, data_index, data_count)
    out_firsts = [
        route_first(h, last)
        for h, last in zip((grad_slot[:half_rows], grad_slot[half_rows:]), lasts)
    ]
    mqk, mvo = after((mqk, mvo), *out_firsts)
    for step in range(len(x_first)):
        last = step == len(x_first) - 1
        mqk = scatter_end(mqk, fqk, x_first[step], last)
        mvo = scatter_end(mvo, fvo, y_first[step], last)
        if not last:
            fqk, fvo = scatter_start(mqk, x_first[step + 1]), scatter_start(mvo, y_first[step + 1])
    grad_fc1_w, grad_fc2_w, grad_qk_w, grad_vo_w = m1[0], m2[0], mqk[0], mvo[0]
    grad_out_w = grad_vo_w[:, heads_local:]
    grad_qkv_w = jnp.stack(
        [grad_qk_w[:, :heads_local], grad_qk_w[:, heads_local:], grad_vo_w[:, :heads_local]], 1
    )
    grad_input = jnp.concatenate(
        [route_rest(f, slot_of_seq, data_index, last) for f, last in zip(out_firsts, lasts)], 0
    )[None]

    branch = branch_sum.astype(f32) + bias_a + bias_b
    block_out = (slot_f32 + jnp.where(valid, branch, 0.0)).astype(bf16)
    block_out = plain_columns(block_out, data_index, data_count)[None]

    devices = data_count * tensor_count
    full_qkv_b = lax.dynamic_update_slice_in_dim(
        jnp.zeros((3, width), f32), grad_qkv_b[:, 0], tensor_index * heads_local, 1
    )
    full_fc1_b = lax.dynamic_update_slice_in_dim(
        jnp.zeros((hidden_local * tensor_count,), f32), grad_fc1_b[0], tensor_index * hidden_local, 0
    )
    sums = jnp.concatenate(
        [
            plain_columns(v, data_index, data_count).reshape(devices, s)
            for v in (grad_gain, grad_shift, grad_bias)
        ]
        + [full_qkv_b.reshape(devices, q), full_fc1_b.reshape(devices, -1)],
        1,
    )
    total = scatter_small(sums, data_index, tensor_index)
    return (
        block_out,
        grad_input,
        grad_qkv_w,
        grad_out_w,
        grad_fc1_w,
        grad_fc2_w,
        total[:s],
        total[s : 2 * s],
        total[3 * s : 3 * s + q],
        total[2 * s : 3 * s],
        total[3 * s + q :],
        total[2 * s : 3 * s],
    )


def solution(mesh):
    in_specs = (
        P("dp", "tensor", None),
        P("dp", "tensor", None),
        P(),
        P(),
        P(),
        P("dp", None, "tensor"),
        P("dp", "tensor"),
        P("dp", "tensor"),
        P("dp", "tensor"),
        P(("dp", "tensor")),
        P(("dp", "tensor")),
        P(("dp", "tensor")),
        P(("dp", "tensor")),
        P(("dp", "tensor")),
        P(("dp", "tensor")),
    )
    out_specs = (
        P("dp", "tensor", None),
        P("dp", "tensor", None),
        P("dp", None, "tensor"),
        P("dp", "tensor"),
        P("dp", "tensor"),
        P("dp", "tensor"),
        P(("dp", "tensor")),
        P(("dp", "tensor")),
        P(("dp", "tensor")),
        P(("dp", "tensor")),
        P(("dp", "tensor")),
        P(("dp", "tensor")),
    )
    return jax.shard_map(shards, mesh=mesh, in_specs=in_specs, out_specs=out_specs, check_vma=False)
```

time: 760 us -> 572 us (0.75)
  matrix products: 230 us -> 0 us
  Pallas kernels: 0 us -> 188 us
  local copies, waits for them, and re-layouts: 131 us -> 56.1 us
  other arithmetic: 141 us -> 81.6 us
  waiting for transfers between devices: 186 us -> 170 us
    dot_general x32 -> x0, matrix products: 230 us -> none  [the longest x5 30.1 us: weight_gradient(): jnp.einsum('rd,rc->dc', rows_by_feature[:, half:], other, preferred_eleme...]
    pallas_call x0 -> x8, Pallas kernels: none -> 188 us  [the longest x1 54.6 us: feed_back(): pl.pallas_call(functools.partial(feed_back_kernel, min(512, rows), min(51...]
    unnamed x260 -> x178, local copies, waits for them, and re-layouts: 86.6 us -> 26.9 us
    convert_element_type x11 -> x10, other arithmetic: 51.8 us -> 25.5 us  [the longest x4 16.8 us: merge(): return (kept.astype(f32) + arrived.astype(f32)).astype(bf16)]
    reduce_sum x3 -> x0, other arithmetic: 11.7 us -> none  [the longest x2 11.4 us: attend_forward(): row_total = jnp.sum(exped, -1, keepdims=True)]
    concatenate x20 -> x13, other arithmetic: 31.5 us -> 23 us  [the longest x2 9.01 us: gather_core(): jnp.concatenate([blocks[reversed_bits(p, bits)] for p in range(1 << len(o...]
    ppermute x49 -> x46, waiting for transfers between devices: 178 us -> 170 us  [flip(): lax.ppermute(array, axis_name, [(i, i ^ 1 << bit) for i in range(size)])]
    mul x1 -> x0, other arithmetic: 8.18 us -> none  [rotate(): jnp.roll(field, half_rot, axis=-1) * behind_sin]
  transfers between devices with their start and end apart: 54 -> 50, of which waited for: 20 -> 26; matrix products, arithmetic and copies ran while one was open for 33% -> 21% of each run, Pallas kernels for 0% -> 33%
where the time goes in v2:
time: 572 us; the launch traced here: 563 us
  Pallas kernels  188 us (33%)
  waiting for transfers between devices  170 us (30%)
  other arithmetic  81.6 us (14%)
  local copies, waits for them, and re-layouts  56.1 us (10%)
  starting transfers between devices  45.9 us (8%)
  between operations  21.3 us (4%)
    ppermute x46, waiting for transfers between devices, flip(): lax.ppermute(array, axis_name, [(i, i ^ 1 << bit) for i in range(size)])  170 us
    pallas_call x1, Pallas kernels, feed_back(): pl.pallas_call(functools.partial(feed_back_kernel, min(512, rows), min(51...  54.6 us
    ppermute x46, starting transfers between devices, flip(): lax.ppermute(array, axis_name, [(i, i ^ 1 << bit) for i in range(size)])  45.3 us
    pallas_call x1, Pallas kernels, feed(): pl.pallas_call(functools.partial(feed_kernel, min(512, rows), steps), gri...  37.2 us
    pallas_call x1, Pallas kernels, attend_back(): pl.pallas_call(functools.partial(attend_back_kernel, min(512, rows)), gri...  32.7 us
    unnamed x178, local copies, waits for them, and re-layouts  26.9 us
    pallas_call x1, Pallas kernels, attend(): pl.pallas_call(functools.partial(attend_kernel, min(512, rows)), grid_spe...  19 us
    convert_element_type x4, other arithmetic, merge(): return (kept.astype(f32) + arrived.astype(f32)).astype(bf16)  16.8 us
  transfers between devices with their start and end apart: 50, of which 26 were waited for; matrix products, arithmetic and copies ran while one was open for 21% of the time, Pallas kernels for 33%

profile of v2, /device:TPU:0, one launch (start us, length us, event | category | flops | bytes accessed | tf_op | source)
XLA Modules:
  0.0 563.3 jit_solution(4491733554440509970)
XLA Ops:
  13.2 10.4 %collective-permute-done = bf16[128,2048]{1,0:T(8,128)(2,1)S(1)} collective-permute-done((bf16[128,2048]{1,0:T(8,128)(2,1)S(1)}, bf16[128,2048]{1,0:T(8,128)(2,1)S(1)}, u32[]{:S(2)}, u32[]{:S(2)}) %collective-permute-start) | collective-permute-done | bytes 524320 | tf_op jit(solution)/shard_map/ppermute | solution.py:529
  36.6 8.4 %collective-permute-done.2 = bf16[128,2048]{1,0:T(8,128)(2,1)} collective-permute-done((bf16[128,2048]{1,0:T(8,128)(2,1)S(1)}, bf16[128,2048]{1,0:T(8,128)(2,1)}, u32[]{:S(2)}, u32[]{:S(2)}) %collective-permute-start.2) | collective-permute-done | bytes 524320 | tf_op jit(solution)/shard_map/ppermute | solution.py:529
  45.1 4.0 collective-permute-done.5
  55.0 3.0 fusion.19
  73.9 10.9 %collective-permute-done.14 = bf16[256,1024]{1,0:T(8,128)(2,1)S(1)} collective-permute-done((bf16[256,1024]{1,0:T(8,128)(2,1)S(1)}, bf16[256,1024]{1,0:T(8,128)(2,1)S(1)}, u32[]{:S(2)}, u32[]{:S(2)}) %collective-permute-start.14) | collective-permute-done | bytes 524320 | tf_op jit(solution)/shard_map/ppermute | solution.py:529
  97.2 15.1 %collective-permute-done.15 = bf16[512,1024]{1,0:T(8,128)(2,1)} collective-permute-done((bf16[512,1024]{1,0:T(8,128)(2,1)}, bf16[512,1024]{1,0:T(8,128)(2,1)}, u32[]{:S(2)}, u32[]{:S(2)}) %collective-permute-start.15) | collective-permute-done | bytes 1048608 | tf_op jit(solution)/shard_map/ppermute | solution.py:529
  123.1 8.6 %collective-permute-done.17 = bf16[256,2048]{1,0:T(8,128)(2,1)} collective-permute-done((bf16[256,2048]{1,0:T(8,128)(2,1)}, bf16[256,2048]{1,0:T(8,128)(2,1)}, u32[]{:S(2)}, u32[]{:S(2)}) %collective-permute-start.17) | collective-permute-done | bytes 1048608 | tf_op jit(solution)/shard_map/ppermute | solution.py:529
  141.9 3.2 convert_reduce_fusion
  147.1 3.3 fusion.5.ln_ref
  150.4 13.9 %project.1.q_ref.k_ref.v_ref = bf16[3,1024,512]{2,1,0:T(8,128)(2,1)} custom-call(bf16[1024,2048]{1,0:T(8,128)(2,1)} %fusion.5.ln_ref, bf16[1024,1024]{1,0:T(8,128)(2,1)} %pad_maximum_fusion.4.qka_ref, bf16[1024,1024]{1,0:T(8,128)(2,1)} %collective-permute-done.13.qkb_ref, bf16[1024,1024]{1,0:T(8,128)(2,1)} %copy-done, ...), custom_call_target="tpu_custom_call" | custom-call | flops 6442450944 | bytes 12582912 | tf_op jit(solution)/shard_map/project/pallas_call | solution.py:94
  164.3 15.1 %collective-permute-done.18 = bf16[512,2048]{1,0:T(8,128)(2,1)} collective-permute-done((bf16[512,2048]{1,0:T(8,128)(2,1)}, bf16[512,2048]{1,0:T(8,128)(2,1)}, u32[]{:S(2)}, u32[]{:S(2)}) %collective-permute-start.18) | collective-permute-done | bytes 2097184 | tf_op jit(solution)/shard_map/ppermute | solution.py:529
  179.4 3.3 collective-permute-done.20
  184.5 3.3 constant_dynamic-update-slice_fusion.3.w2a_ref
  187.9 7.5 %pad_maximum_fusion.w1a_ref = bf16[1024,2048]{1,0:T(8,128)(2,1)} fusion(bf16[256,2048]{1,0:T(8,128)(2,1)S(1)} %get-tuple-element.115, bf16[256,2048]{1,0:T(8,128)(2,1)} %collective-permute-done.17, bf16[256,2048]{1,0:T(8,128)(2,1)S(1)} %get-tuple-element.114, bf16[256,2048]{1,0:T(8,128)(2,1)S(1)} %copy-done.30), kind=kLoop, calls=%fused_computation.10 | loop fusion | flops 16777216 | bytes 8388608 | tf_op jit(solution)/shard_map/concatenate | solution.py:602
  198.4 19.0 %attend.1 = (bf16[1024,512]{1,0:T(8,128)(2,1)S(1)}, f32[8,1,1024]{2,1,0:T(1,128)S(1)}) custom-call(s32[1]{0:T(128)} %dynamic_slice.334.len_ref, bf16[3,1024,512]{2,1,0:T(8,128)(2,1)S(1)} %copy-done.8, bf16[3,1024,512]{2,1,0:T(8,128)(2,1)S(1)} %copy-done.8, bf16[3,1024,512]{2,1,0:T(8,128)(2,1)S(1)} %copy-done.8), custom_call_target="tpu_custom_call" | custom-call | flops 8589934592 | bytes 4194304 | tf_op jit(solution)/shard_map/attend/pallas_call | solution.py:161
  218.4 37.2 %feed.1 = (bf16[1024,2048]{1,0:T(8,128)(2,1)}, bf16[1024,2048]{1,0:T(8,128)(2,1)}, f32[1024,2048]{1,0:T(8,128)}) custom-call(bf16[1024,2048]{1,0:T(8,128)(2,1)} %fusion.5.ln_ref, bf16[1024,512]{1,0:T(8,128)(2,1)} %copy-done.9, bf16[1024,1024]{1,0:T(8,128)(2,1)} %copy-done, bf16[1024,1024]{1,0:T(8,128)(2,1)} %collective-permute-done.16.vb_ref.ob_ref, ...), custom_call_target="tpu_custom_call" | custom-call | flops 17179869184 | bytes 41943040 | tf_op jit(solution)/shard_map/feed/pallas_call | solution.py:318
  255.7 54.6 %feed_back.1 = (f32[1024,2048]{1,0:T(8,128)}, bf16[1024,2048]{1,0:T(8,128)(2,1)}, bf16[1024,2048]{1,0:T(8,128)(2,1)}, bf16[1024,2048]{1,0:T(8,128)(2,1)}, bf16[1024,2048]{1,0:T(8,128)(2,1)}, /*index=5*/f32[1,2048]{1,0:T(1,128)}) custom-call(bf16[1024,2048]{1,0:T(8,128)(2,1)} %fusion.5.ln_ref, bf16[1024,2048]{1,0:T(8,128)(2,1)} %all-gather.5.cloned.1.call-done.g_ref, ...), custom_call_target="tpu_custom_call" | custom-call | flops 34359738368 | bytes 62914560 | tf_op jit(solution)/shard_map/feed_back/pallas_call | solution.py:383
  313.1 3.9 mixed_grad.1.do_ref
  316.9 32.7 %attend_back.1.grad_ref = bf16[3,1024,512]{2,1,0:T(8,128)(2,1)S(1)} custom-call(s32[1]{0:T(128)} %dynamic_slice.334.len_ref, bf16[3,1024,512]{2,1,0:T(8,128)(2,1)} %project.1.q_ref.k_ref.v_ref, bf16[3,1024,512]{2,1,0:T(8,128)(2,1)} %project.1.q_ref.k_ref.v_ref, bf16[3,1024,512]{2,1,0:T(8,128)(2,1)} %project.1.q_ref.k_ref.v_ref, ...), custom_call_target="tpu_custom_call" | custom-call | flops 21474836480 | bytes 8388608 | tf_op jit(solution)/shard_map/attend_back/pallas_call | solution.py:236
  351.4 13.0 %ln_grad.1 = bf16[1024,2048]{1,0:T(8,128)(2,1)} custom-call(bf16[3,1024,512]{2,1,0:T(8,128)(2,1)} %copy-done.3, bf16[1024,1024]{1,0:T(8,128)(2,1)} %pad_maximum_fusion.4.qka_ref, bf16[1024,1024]{1,0:T(8,128)(2,1)} %collective-permute-done.13.qkb_ref, bf16[1024,1024]{1,0:T(8,128)(2,1)} %copy-done, bf16[1024,1024]{1,0:T(8,128)(2,1)} %collective-permute-done.16.vb_ref.ob_ref, ...), custom_call_target="tpu_custom_call" | custom-call | flops 6442450944 | bytes 23068672 | tf_op jit(solution)/shard_map/ln_grad/pallas_call | solution.py:442
  364.4 5.5 add_convert_fusion.1
  370.0 6.1 %add_convert_fusion = bf16[1024,2048]{1,0:T(8,128)(2,1)S(1)} fusion(bf16[1024,2048]{1,0:T(8,128)(2,1)} %collective-permute-done.24, bf16[1024,2048]{1,0:T(8,128)(2,1)S(1)} %copy-done.23), kind=kLoop, calls=%fused_computation.8 | loop fusion | flops 8388608 | bytes 12582912 | tf_op jit(solution)/shard_map/convert_element_type | solution.py:613
  379.5 14.0 %weight_grad.1 = (bf16[1024,1024]{1,0:T(8,128)(2,1)S(1)}, bf16[1024,1024]{1,0:T(8,128)(2,1)S(1)}, bf16[1024,1024]{1,0:T(8,128)(2,1)}, bf16[1024,1024]{1,0:T(8,128)(2,1)}, f32[3,1,512]{2,1,0:T(1,128)S(1)}) custom-call(bf16[1024,2048]{1,0:T(8,128)(2,1)} %fusion.5.ln_ref, bf16[1024,2048]{1,0:T(8,128)(2,1)} %all-gather.5.cloned.1.call-done.g_ref, ...), custom_call_target="tpu_custom_call" | custom-call | flops 8589934592 | bytes 20971520 | tf_op jit(solution)/shard_map/weight_grad/pallas_call | solution.py:488
  415.6 28.0 %collective-permute-done.28 = bf16[512,2048]{1,0:T(8,128)(2,1)} collective-permute-done((bf16[512,2048]{1,0:T(8,128)(2,1)}, bf16[512,2048]{1,0:T(8,128)(2,1)}, u32[]{:S(2)}, u32[]{:S(2)}) %collective-permute-start.28) | collective-permute-done | bytes 2097184 | tf_op jit(solution)/shard_map/ppermute | solution.py:529
  447.8 6.8 %collective-permute-done.27 = bf16[512,2048]{1,0:T(8,128)(2,1)S(1)} collective-permute-done((bf16[512,2048]{1,0:T(8,128)(2,1)S(1)}, bf16[512,2048]{1,0:T(8,128)(2,1)S(1)}, u32[]{:S(2)}, u32[]{:S(2)}) %collective-permute-start.27) | collective-permute-done | bytes 2097184 | tf_op jit(solution)/shard_map/ppermute | solution.py:529
  463.6 13.6 %collective-permute-done.40 = bf16[256,2048]{1,0:T(8,128)(2,1)} collective-permute-done((bf16[256,2048]{1,0:T(8,128)(2,1)}, bf16[256,2048]{1,0:T(8,128)(2,1)}, u32[]{:S(2)}, u32[]{:S(2)}) %collective-permute-start.40) | collective-permute-done | bytes 1048608 | tf_op jit(solution)/shard_map/ppermute | solution.py:529
  477.2 3.4 convert_add_fusion.1
  482.7 3.1 convert_add_fusion.2
  495.2 7.7 %collective-permute-done.41 = f32[16,640]{1,0:T(8,128)S(1)} collective-permute-done((f32[16,640]{1,0:T(8,128)S(1)}, f32[16,640]{1,0:T(8,128)S(1)}, u32[]{:S(2)}, u32[]{:S(2)}) %collective-permute-start.41) | collective-permute-done | bytes 40992 | tf_op jit(solution)/shard_map/ppermute | solution.py:529
  514.4 7.0 %collective-permute-done.29 = bf16[128,2048]{1,0:T(8,128)(2,1)S(1)} collective-permute-done((bf16[128,2048]{1,0:T(8,128)(2,1)S(1)}, bf16[128,2048]{1,0:T(8,128)(2,1)S(1)}, u32[]{:S(2)}, u32[]{:S(2)}) %collective-permute-start.29) | collective-permute-done | bytes 524320 | tf_op jit(solution)/shard_map/ppermute | solution.py:529
  530.6 6.4 %collective-permute-done.38 = bf16[256,1024]{1,0:T(8,128)(2,1)S(1)} collective-permute-done((bf16[256,1024]{1,0:T(8,128)(2,1)S(1)}, bf16[256,1024]{1,0:T(8,128)(2,1)S(1)}, u32[]{:S(2)}, u32[]{:S(2)}) %collective-permute-start.38) | collective-permute-done | bytes 524320 | tf_op jit(solution)/shard_map/ppermute | solution.py:529
  545.8 8.5 %collective-permute-done.34 = bf16[128,2048]{1,0:T(8,128)(2,1)S(1)} collective-permute-done((bf16[128,2048]{1,0:T(8,128)(2,1)S(1)}, bf16[128,2048]{1,0:T(8,128)(2,1)S(1)}, u32[]{:S(2)}, u32[]{:S(2)}) %collective-permute-start.34) | collective-permute-done | bytes 524320 | tf_op jit(solution)/shard_map/ppermute | solution.py:529
  (449 shorter events, 161.8 us)
Async XLA Ops:
  7.2 134.7 %all-gather.3.cloned.1.call-start = ((), (), s32[]{:S(2)}) async-start(), calls=%async_computation.2 | async-start | bytes 5242880 | tf_op jit(solution)/shard_map/all_gather | solution.py:729
  8.7 14.9 %collective-permute-start = (bf16[128,2048]{1,0:T(8,128)(2,1)S(1)}, bf16[128,2048]{1,0:T(8,128)(2,1)S(1)}, u32[]{:S(2)}, u32[]{:S(2)}) collective-permute-start(bf16[128,2048]{1,0:T(8,128)(2,1)S(1)} %get-tuple-element.129), channel_id=1, source_target_pairs={{0,8},{4,12},{8,0},{12,4},{16,24},{20,28},{24,16},{28,20},{1,9},{5... | collective-permute-start | bytes 1572872 | tf_op jit(solution)/shard_map/ppermute | solution.py:529
  11.7 13.4 %collective-permute-start.3 = (bf16[128,2048]{1,0:T(8,128)(2,1)S(1)}, bf16[128,2048]{1,0:T(8,128)(2,1)S(1)}, u32[]{:S(2)}, u32[]{:S(2)}) collective-permute-start(bf16[128,2048]{1,0:T(8,128)(2,1)S(1)} %get-tuple-element.130), channel_id=1, source_target_pairs={{0,16},{4,20},{8,24},{12,28},{16,0},{20,4},{24,8},{28,12},{1,17},{... | collective-permute-start | bytes 1572872 | tf_op jit(solution)/shard_map/ppermute | solution.py:529
  30.5 14.5 %collective-permute-start.2 = (bf16[128,2048]{1,0:T(8,128)(2,1)S(1)}, bf16[128,2048]{1,0:T(8,128)(2,1)}, u32[]{:S(2)}, u32[]{:S(2)}) collective-permute-start(bf16[128,2048]{1,0:T(8,128)(2,1)S(1)} %dynamic-slice_bitcast_fusion.3), channel_id=1, source_target_pairs={{0,16},{4,20},{8,24},{12,28},{16,0},{20,4},{24,8},{28,12},{1,17},{... | collective-permute-start | bytes 1572872 | tf_op jit(solution)/shard_map/ppermute | solution.py:529
  34.9 14.2 %collective-permute-start.5 = (bf16[128,2048]{1,0:T(8,128)(2,1)S(1)}, bf16[128,2048]{1,0:T(8,128)(2,1)}, u32[]{:S(2)}, u32[]{:S(2)}) collective-permute-start(bf16[128,2048]{1,0:T(8,128)(2,1)S(1)} %dynamic-slice_bitcast_fusion.2), channel_id=1, source_target_pairs={{0,8},{4,12},{8,0},{12,4},{16,24},{20,28},{24,16},{28,20},{1,9},{5... | collective-permute-start | bytes 1572872 | tf_op jit(solution)/shard_map/ppermute | solution.py:529
  53.1 202.5 %all-gather.5.cloned.1.call-start = ((), (), s32[]{:S(2)}) async-start(), calls=%async_computation.4 | async-start | bytes 5242880 | tf_op jit(solution)/shard_map/all_gather | solution.py:736
  72.8 14.6 %collective-permute-start.11 = (bf16[256,1024]{1,0:T(8,128)(2,1)S(1)}, bf16[256,1024]{1,0:T(8,128)(2,1)S(1)}, u32[]{:S(2)}, u32[]{:S(2)}) collective-permute-start(bf16[256,1024]{1,0:T(8,128)(2,1)S(1)} %bitcast.94), channel_id=1, source_target_pairs={{0,8},{4,12},{8,0},{12,4},{16,24},{20,28},{24,16},{28,20},{1,9},{5... | collective-permute-start | bytes 1572872 | tf_op jit(solution)/shard_map/ppermute | solution.py:529
  85.8 26.4 %collective-permute-start.15 = (bf16[512,1024]{1,0:T(8,128)(2,1)}, bf16[512,1024]{1,0:T(8,128)(2,1)}, u32[]{:S(2)}, u32[]{:S(2)}) collective-permute-start(bf16[512,1024]{1,0:T(8,128)(2,1)} %pad_maximum_fusion.14), channel_id=1, source_target_pairs={{0,8},{4,12},{8,0},{12,4},{16,24},{20,28},{24,16},{28,20},{1,9},{5... | collective-permute-start | bytes 3145736 | tf_op jit(solution)/shard_map/ppermute | solution.py:529
  88.6 26.4 %collective-permute-start.12 = (bf16[512,1024]{1,0:T(8,128)(2,1)}, bf16[512,1024]{1,0:T(8,128)(2,1)}, u32[]{:S(2)}, u32[]{:S(2)}) collective-permute-start(bf16[512,1024]{1,0:T(8,128)(2,1)} %pad_maximum_fusion.13), channel_id=1, source_target_pairs={{0,16},{4,20},{8,24},{12,28},{16,0},{20,4},{24,8},{28,12},{1,17},{... | collective-permute-start | bytes 3145736 | tf_op jit(solution)/shard_map/ppermute | solution.py:529
  94.9 36.7 %collective-permute-start.17 = (bf16[256,2048]{1,0:T(8,128)(2,1)}, bf16[256,2048]{1,0:T(8,128)(2,1)}, u32[]{:S(2)}, u32[]{:S(2)}) collective-permute-start(bf16[256,2048]{1,0:T(8,128)(2,1)} %param.22), channel_id=1, source_target_pairs={{0,8},{4,12},{8,0},{12,4},{16,24},{20,28},{24,16},{28,20},{1,9},{5... | collective-permute-start | bytes 3145736 | tf_op jit(solution)/shard_map/ppermute | solution.py:529
  95.7 39.2 %collective-permute-start.19 = (bf16[256,2048]{1,0:T(8,128)(2,1)}, bf16[256,2048]{1,0:T(8,128)(2,1)}, u32[]{:S(2)}, u32[]{:S(2)}) collective-permute-start(bf16[256,2048]{1,0:T(8,128)(2,1)} %param.23), channel_id=1, source_target_pairs={{0,16},{4,20},{8,24},{12,28},{16,0},{20,4},{24,8},{28,12},{1,17},{... | collective-permute-start | bytes 3145736 | tf_op jit(solution)/shard_map/ppermute | solution.py:529
  113.6 36.8 %collective-permute-start.16 = (bf16[1024,1024]{1,0:T(8,128)(2,1)S(1)}, bf16[1024,1024]{1,0:T(8,128)(2,1)}, u32[]{:S(2)}, u32[]{:S(2)}) collective-permute-start(bf16[1024,1024]{1,0:T(8,128)(2,1)S(1)} %constant_dynamic-update-slice_fusion.va_ref.oa_ref), channel_id=1, source_target_pairs={{0,4},{4,0},{8,12},{12,8},{16,20},{20,16},{24,28},{28,24},{1,5},{5... | collective-permute-start | bytes 6291464 | tf_op jit(solution)/shard_map/ppermute | solution.py:529
  117.8 32.6 %collective-permute-start.13 = (bf16[1024,1024]{1,0:T(8,128)(2,1)}, bf16[1024,1024]{1,0:T(8,128)(2,1)}, u32[]{:S(2)}, u32[]{:S(2)}) collective-permute-start(bf16[1024,1024]{1,0:T(8,128)(2,1)} %pad_maximum_fusion.4.qka_ref), channel_id=1, source_target_pairs={{0,4},{4,0},{8,12},{12,8},{16,20},{20,16},{24,28},{28,24},{1,5},{5... | collective-permute-start | bytes 6291464 | tf_op jit(solution)/shard_map/ppermute | solution.py:529
  120.1 231.2 %reduce-scatter.3.cloned.1.call-start = ((), (), s32[]{:S(2)}) async-start(), calls=%async_computation.3 | async-start | bytes 5242880 | tf_op jit(solution)/shard_map/reduce_scatter | solution.py:778
  134.4 45.0 %collective-permute-start.18 = (bf16[512,2048]{1,0:T(8,128)(2,1)}, bf16[512,2048]{1,0:T(8,128)(2,1)}, u32[]{:S(2)}, u32[]{:S(2)}) collective-permute-start(bf16[512,2048]{1,0:T(8,128)(2,1)} %pad_maximum_fusion.5), channel_id=1, source_target_pairs={{0,16},{4,20},{8,24},{12,28},{16,0},{20,4},{24,8},{28,12},{1,17},{... | collective-permute-start | bytes 6291464 | tf_op jit(solution)/shard_map/ppermute | solution.py:529
  137.8 45.0 %collective-permute-start.20 = (bf16[512,2048]{1,0:T(8,128)(2,1)}, bf16[512,2048]{1,0:T(8,128)(2,1)}, u32[]{:S(2)}, u32[]{:S(2)}) collective-permute-start(bf16[512,2048]{1,0:T(8,128)(2,1)} %pad_maximum_fusion.6), channel_id=1, source_target_pairs={{0,8},{4,12},{8,0},{12,4},{16,24},{20,28},{24,16},{28,20},{1,9},{5... | collective-permute-start | bytes 6291464 | tf_op jit(solution)/shard_map/ppermute | solution.py:529
  187.8 30.5 %collective-permute-start.22 = (bf16[1024,2048]{1,0:T(8,128)(2,1)}, bf16[1024,2048]{1,0:T(8,128)(2,1)}, u32[]{:S(2)}, u32[]{:S(2)}) collective-permute-start(bf16[1024,2048]{1,0:T(8,128)(2,1)} %constant_dynamic-update-slice_fusion.3.w2a_ref), channel_id=1, source_target_pairs={{0,4},{4,0},{8,12},{12,8},{16,20},{20,16},{24,28},{28,24},{1,5},{5... | collective-permute-start | bytes 12582920 | tf_op jit(solution)/shard_map/ppermute | solution.py:529
  195.4 23.0 %collective-permute-start.21 = (bf16[1024,2048]{1,0:T(8,128)(2,1)}, bf16[1024,2048]{1,0:T(8,128)(2,1)}, u32[]{:S(2)}, u32[]{:S(2)}) collective-permute-start(bf16[1024,2048]{1,0:T(8,128)(2,1)} %pad_maximum_fusion.w1a_ref), channel_id=1, source_target_pairs={{0,4},{4,0},{8,12},{12,8},{16,20},{20,16},{24,28},{28,24},{1,5},{5... | collective-permute-start | bytes 12582920 | tf_op jit(solution)/shard_map/ppermute | solution.py:529
  255.6 230.1 %reduce-scatter.5.cloned.1.call-start = ((), (), s32[]{:S(2)}) async-start(), calls=%async_computation.5 | async-start | bytes 5242880 | tf_op jit(solution)/shard_map/reduce_scatter | solution.py:787
  310.3 54.1 %collective-permute-start.23 = (bf16[1024,2048]{1,0:T(8,128)(2,1)}, bf16[1024,2048]{1,0:T(8,128)(2,1)}, u32[]{:S(2)}, u32[]{:S(2)}) collective-permute-start(bf16[1024,2048]{1,0:T(8,128)(2,1)} %get-tuple-element.69), channel_id=1, source_target_pairs={{0,4},{4,0},{8,12},{12,8},{16,20},{20,16},{24,28},{28,24},{1,5},{5... | collective-permute-start | bytes 12582920 | tf_op jit(solution)/shard_map/ppermute | solution.py:529
  310.4 59.6 %collective-permute-start.24 = (bf16[1024,2048]{1,0:T(8,128)(2,1)}, bf16[1024,2048]{1,0:T(8,128)(2,1)}, u32[]{:S(2)}, u32[]{:S(2)}) collective-permute-start(bf16[1024,2048]{1,0:T(8,128)(2,1)} %get-tuple-element.71), channel_id=1, source_target_pairs={{0,4},{4,0},{8,12},{12,8},{16,20},{20,16},{24,28},{28,24},{1,5},{5... | collective-permute-start | bytes 12582920 | tf_op jit(solution)/shard_map/ppermute | solution.py:529
  393.5 14.4 %collective-permute-start.25 = (bf16[1024,1024]{1,0:T(8,128)(2,1)}, bf16[1024,1024]{1,0:T(8,128)(2,1)}, u32[]{:S(2)}, u32[]{:S(2)}) collective-permute-start(bf16[1024,1024]{1,0:T(8,128)(2,1)} %get-tuple-element.74), channel_id=1, source_target_pairs={{0,4},{4,0},{8,12},{12,8},{16,20},{20,16},{24,28},{28,24},{1,5},{5... | collective-permute-start | bytes 6291464 | tf_op jit(solution)/shard_map/ppermute | solution.py:529
  393.5 18.1 %collective-permute-start.26 = (bf16[1024,1024]{1,0:T(8,128)(2,1)}, bf16[1024,1024]{1,0:T(8,128)(2,1)}, u32[]{:S(2)}, u32[]{:S(2)}) collective-permute-start(bf16[1024,1024]{1,0:T(8,128)(2,1)} %get-tuple-element.76), channel_id=1, source_target_pairs={{0,4},{4,0},{8,12},{12,8},{16,20},{20,16},{24,28},{28,24},{1,5},{5... | collective-permute-start | bytes 6291464 | tf_op jit(solution)/shard_map/ppermute | solution.py:529
  395.6 47.9 %collective-permute-start.28 = (bf16[512,2048]{1,0:T(8,128)(2,1)}, bf16[512,2048]{1,0:T(8,128)(2,1)}, u32[]{:S(2)}, u32[]{:S(2)}) collective-permute-start(bf16[512,2048]{1,0:T(8,128)(2,1)} %pad_maximum_fusion.7), channel_id=1, source_target_pairs={{0,16},{4,20},{8,24},{12,28},{16,0},{20,4},{24,8},{28,12},{1,17},{... | collective-permute-start | bytes 6291464 | tf_op jit(solution)/shard_map/ppermute | solution.py:529
  406.0 48.6 %collective-permute-start.27 = (bf16[512,2048]{1,0:T(8,128)(2,1)S(1)}, bf16[512,2048]{1,0:T(8,128)(2,1)S(1)}, u32[]{:S(2)}, u32[]{:S(2)}) collective-permute-start(bf16[512,2048]{1,0:T(8,128)(2,1)S(1)} %concatenate.263), channel_id=1, source_target_pairs={{0,8},{4,12},{8,0},{12,4},{16,24},{20,28},{24,16},{28,20},{1,9},{5... | collective-permute-start | bytes 6291464 | tf_op jit(solution)/shard_map/ppermute | solution.py:529
  446.1 31.0 %collective-permute-start.40 = (bf16[256,2048]{1,0:T(8,128)(2,1)}, bf16[256,2048]{1,0:T(8,128)(2,1)}, u32[]{:S(2)}, u32[]{:S(2)}) collective-permute-start(bf16[256,2048]{1,0:T(8,128)(2,1)} %add_convert_fusion.4), channel_id=1, source_target_pairs={{0,8},{4,12},{8,0},{12,4},{16,24},{20,28},{24,16},{28,20},{1,9},{5... | collective-permute-start | bytes 3145736 | tf_op jit(solution)/shard_map/ppermute | solution.py:529
  456.2 26.4 %collective-permute-start.39 = (bf16[256,2048]{1,0:T(8,128)(2,1)}, bf16[256,2048]{1,0:T(8,128)(2,1)}, u32[]{:S(2)}, u32[]{:S(2)}) collective-permute-start(bf16[256,2048]{1,0:T(8,128)(2,1)} %add_convert_fusion.6), channel_id=1, source_target_pairs={{0,16},{4,20},{8,24},{12,28},{16,0},{20,4},{24,8},{28,12},{1,17},{... | collective-permute-start | bytes 3145736 | tf_op jit(solution)/shard_map/ppermute | solution.py:529
  459.4 66.1 %collective-permute-start.35 = (bf16[512,1024]{1,0:T(8,128)(2,1)}, bf16[512,1024]{1,0:T(8,128)(2,1)}, u32[]{:S(2)}, u32[]{:S(2)}) collective-permute-start(bf16[512,1024]{1,0:T(8,128)(2,1)} %concatenate.264), channel_id=1, source_target_pairs={{0,8},{4,12},{8,0},{12,4},{16,24},{20,28},{24,16},{28,20},{1,9},{5... | collective-permute-start | bytes 3145736 | tf_op jit(solution)/shard_map/ppermute | solution.py:529
  462.1 59.6 %collective-permute-start.37 = (bf16[512,1024]{1,0:T(8,128)(2,1)}, bf16[512,1024]{1,0:T(8,128)(2,1)}, u32[]{:S(2)}, u32[]{:S(2)}) collective-permute-start(bf16[512,1024]{1,0:T(8,128)(2,1)} %pad_maximum_fusion.17), channel_id=1, source_target_pairs={{0,16},{4,20},{8,24},{12,28},{16,0},{20,4},{24,8},{28,12},{1,17},{... | collective-permute-start | bytes 3145736 | tf_op jit(solution)/shard_map/ppermute | solution.py:529
  506.8 14.7 %collective-permute-start.32 = (bf16[128,2048]{1,0:T(8,128)(2,1)S(1)}, bf16[128,2048]{1,0:T(8,128)(2,1)S(1)}, u32[]{:S(2)}, u32[]{:S(2)}) collective-permute-start(bf16[128,2048]{1,0:T(8,128)(2,1)S(1)} %get-tuple-element.122), channel_id=1, source_target_pairs={{0,16},{4,20},{8,24},{12,28},{16,0},{20,4},{24,8},{28,12},{1,17},{... | collective-permute-start | bytes 1572872 | tf_op jit(solution)/shard_map/ppermute | solution.py:529
  507.4 14.0 %collective-permute-start.29 = (bf16[128,2048]{1,0:T(8,128)(2,1)S(1)}, bf16[128,2048]{1,0:T(8,128)(2,1)S(1)}, u32[]{:S(2)}, u32[]{:S(2)}) collective-permute-start(bf16[128,2048]{1,0:T(8,128)(2,1)S(1)} %get-tuple-element.123), channel_id=1, source_target_pairs={{0,8},{4,12},{8,0},{12,4},{16,24},{20,28},{24,16},{28,20},{1,9},{5... | collective-permute-start | bytes 1572872 | tf_op jit(solution)/shard_map/ppermute | solution.py:529
  513.6 14.6 %collective-permute-start.45 = (f32[1,640]{1,0:T(1,128)S(1)}, f32[1,640]{1,0:T(1,128)S(1)}, u32[]{:S(2)}, u32[]{:S(2)}) collective-permute-start(f32[1,640]{1,0:T(1,128)S(1)} %slice.320), channel_id=1, source_target_pairs={{0,1},{1,0},{2,3},{3,2},{4,5},{5,4},{6,7},{7,6},{8,9},{9,8},{10,11... | collective-permute-start | bytes 7688 | tf_op jit(solution)/shard_map/ppermute | solution.py:529
  (80 other events, 714.9 us)
Sparse Core Ops, SparseCore 0:
  53.3 80.2 all-gather.2
  135.7 79.2 all-gather.4
  255.7 77.2 reduce-scatter.2
  364.5 77.2 reduce-scatter.4

commit v3 on v2

v3 whole, which is shorter than its diff:
```python
import functools
import math

import jax
import jax.numpy as jnp
from jax import lax
from jax.experimental import pallas as pl
from jax.experimental.pallas import tpu as pltpu
from jax.sharding import PartitionSpec as P

HEAD_DIM = 64
ROT = 32
PAIR = 2 * HEAD_DIM
VMEM = 63 * 1024 * 1024
SHARE = 0.4


eps = 1e-05
masked_score = -1e30
f32 = jnp.float32
bf16 = jnp.bfloat16
NN = (((1,), (0,)), ((), ()))
NT = (((1,), (1,)), ((), ()))
TN = (((0,), (0,)), ((), ()))
once = pl.Buffered(1)


def dot(a, b, dims):
    return lax.dot_general(a, b, dims, preferred_element_type=f32)


def params(mib):
    return pltpu.CompilerParams(vmem_limit_bytes=VMEM)


def cost(flops, nbytes, exps=0):
    return pl.CostEstimate(
        flops=int(flops * SHARE), bytes_accessed=int(nbytes * SHARE), transcendentals=int(exps * SHARE)
    )


def shape(dims, dtype):
    return jax.ShapeDtypeStruct(dims, dtype)


def turned(field, tables):
    cosine, ahead, behind = tables
    half = ROT // 2
    wide = field.shape[1]
    return (
        field * cosine
        + pltpu.roll(field, wide - half, 1) * ahead
        + pltpu.roll(field, half, 1) * behind
    )


def turned_back(grad, tables):
    cosine, ahead, behind = tables
    half = ROT // 2
    wide = grad.shape[1]
    return (
        grad * cosine
        + pltpu.roll(grad * ahead, half, 1)
        + pltpu.roll(grad * behind, wide - half, 1)
    )


def norm_kernel(x_ref, gain_ref, shift_ref, *rest):
    out_ref = rest[-1]
    rows = x_ref[...].astype(f32)
    centred = rows - jnp.mean(rows, -1, keepdims=True)
    scale = lax.rsqrt(jnp.mean(centred * centred, -1, keepdims=True) + eps)
    out_ref[...] = (centred * scale * gain_ref[...] + shift_ref[...]).astype(bf16)


def norm_wave(rows_in, gain, shift, wave, held):
    rows, width = rows_in.shape
    tile = min(128, rows)
    steps = rows // tile
    vector = pl.BlockSpec((1, width), lambda i: (0, 0))
    extra = [] if held is None else [held]
    return pl.pallas_call(
        norm_kernel,
        grid=(steps,),
        in_specs=[pl.BlockSpec((tile, width), lambda i: (i, 0)), vector, vector]
        + [pl.BlockSpec(memory_space=pl.ANY)] * len(extra),
        out_specs=pl.BlockSpec((tile, width), lambda i: (i + wave * steps, 0)),
        out_shape=shape((2 * rows, width), bf16),
        input_output_aliases={3: 0} if extra else {},
        compiler_params=params(32),
        cost_estimate=cost(10 * rows * width, 4 * rows * width),
        name="norm_wave",
    )(rows_in, gain, shift, *extra)


def project_rows(kind, ln_ref, weight, bias_ref, tables, out_ref):
    raw = dot(ln_ref[...], weight, NN) + bias_ref[0]

    @pl.when(kind < 2)
    def _():
        for pair in range(raw.shape[1] // PAIR):
            cols = slice(pair * PAIR, (pair + 1) * PAIR)
            out_ref[0, :, cols] = turned(raw[:, cols], [t[...] for t in tables]).astype(bf16)

    @pl.when(kind == 2)
    def _():
        out_ref[0] = raw.astype(bf16)


def assemble_start(refs, plan, column, size, buffer, sems):
    for j, (which, row, place, count) in enumerate(plan):
        pltpu.make_async_copy(
            refs[which].at[pl.ds(row, count), pl.ds(column, size)],
            buffer.at[pl.ds(place, count), :],
            sems.at[j],
        ).start()


def assemble_wait(refs, plan, column, size, buffer, sems):
    for j, (which, row, place, count) in enumerate(plan):
        pltpu.make_async_copy(
            refs[which].at[pl.ds(row, count), pl.ds(column, size)],
            buffer.at[pl.ds(place, count), :],
            sems.at[j],
        ).wait()


def project_first_kernel(qk_plan, vo_plan, ln_ref, bias_ref, c_ref, a_ref, b_ref, *rest):
    n = len({p[0] for p in qk_plan})
    qk_refs, vo_refs = rest[:n], rest[n : 2 * n]
    out_ref, w_ref, buffer, sems, out_sems = rest[2 * n :]
    kind = pl.program_id(0)
    heads = buffer.shape[2]
    sources = (
        (qk_refs, qk_plan, 0),
        (qk_refs, qk_plan, heads),
        (vo_refs, vo_plan, 0),
        (vo_refs, vo_plan, heads),
    )

    def drain(k):
        pltpu.make_async_copy(buffer.at[k % 2], w_ref.at[k], out_sems.at[k % 2]).wait()

    for k in range(4):
        refs, plan, column = sources[k]
        slot = k % 2

        @pl.when(kind == k)
        def _():
            if k == 0:
                assemble_start(refs, plan, column, heads, buffer.at[slot], sems.at[slot])
            assemble_wait(refs, plan, column, heads, buffer.at[slot], sems.at[slot])
            pltpu.make_async_copy(buffer.at[slot], w_ref.at[k], out_sems.at[slot]).start()
            if k >= 1:
                drain(k - 1)
            if k < 3:
                nrefs, nplan, ncolumn = sources[k + 1]
                assemble_start(
                    nrefs, nplan, ncolumn, heads, buffer.at[1 - slot], sems.at[1 - slot]
                )
            else:
                drain(k)

    @pl.when(kind < 3)
    def _():
        project_rows(kind, ln_ref, buffer[kind % 2], bias_ref, (c_ref, a_ref, b_ref), out_ref)


def project_first(ln, qk, vo, bias, tables):
    rows, width = ln.shape[0] // 2, ln.shape[1]
    heads = bias.shape[1]
    table = pl.BlockSpec((rows, PAIR), lambda i: (0, 0), pipeline_mode=once)
    hbm = pl.BlockSpec(memory_space=pl.ANY)
    last = lambda i: jnp.minimum(i, 2)
    return pl.pallas_call(
        functools.partial(project_first_kernel, qk[1], vo[1]),
        grid=(4,),
        in_specs=[
            pl.BlockSpec((rows, width), lambda i: (0, 0), pipeline_mode=once),
            pl.BlockSpec((1, 1, heads), lambda i: (last(i), 0, 0)),
            table,
            table,
            table,
        ]
        + [hbm] * (len(qk[0]) + len(vo[0])),
        out_specs=[pl.BlockSpec((1, rows, heads), lambda i: (last(i), 0, 0)), hbm],
        out_shape=[shape((3, 2 * rows, heads), bf16), shape((4, width, heads), bf16)],
        scratch_shapes=[
            pltpu.VMEM((2, width, heads), bf16),
            pltpu.SemaphoreType.DMA((2, len(qk[1]))),
            pltpu.SemaphoreType.DMA((2,)),
        ],
        compiler_params=params(48),
        cost_estimate=cost(6 * rows * width * heads, 22 << 20),
        name="project_first",
    )(ln, bias[:, None, :], *tables, *qk[0], *vo[0])


def project_second_kernel(ln_ref, w_ref, bias_ref, c_ref, a_ref, b_ref, held_ref, out_ref):
    project_rows(pl.program_id(0), ln_ref, w_ref[0], bias_ref, (c_ref, a_ref, b_ref), out_ref)


def project_second(ln, weights, bias, tables, held):
    rows, width = ln.shape[0] // 2, ln.shape[1]
    heads = bias.shape[1]
    table = pl.BlockSpec((rows, PAIR), lambda i: (1, 0), pipeline_mode=once)
    return pl.pallas_call(
        project_second_kernel,
        grid=(3,),
        in_specs=[
            pl.BlockSpec((rows, width), lambda i: (1, 0), pipeline_mode=once),
            pl.BlockSpec((1, width, heads), lambda i: (i, 0, 0)),
            pl.BlockSpec((1, 1, heads), lambda i: (i, 0, 0)),
            table,
            table,
            table,
            pl.BlockSpec(memory_space=pl.ANY),
        ],
        out_specs=pl.BlockSpec((1, rows, heads), lambda i: (i, 1, 0)),
        out_shape=shape(held.shape, bf16),
        input_output_aliases={6: 0},
        compiler_params=params(48),
        cost_estimate=cost(6 * rows * width * heads, 12 << 20),
        name="project_second",
    )(ln, weights, bias[:, None, :], *tables, held)


def head_lanes(head):
    lane = lax.broadcasted_iota(jnp.int32, (1, PAIR), 1)
    return (lane // HEAD_DIM) == (head % 2)


def masked_scores(keys, queries, first, length):
    scores = dot(keys, queries, NT)
    key = lax.broadcasted_iota(jnp.int32, scores.shape, 0)
    row = first + lax.broadcasted_iota(jnp.int32, (1, scores.shape[1]), 1)
    return jnp.where(key <= jnp.minimum(row, length - 1), scores, masked_score)


def chunk_places(rows, chunks):
    size = rows // chunks
    return [((c % 2) * (chunks // 2) + c // 2) * size for c in range(chunks)], size


def in_sequence(value, chunks):
    places, size = chunk_places(value.shape[0], chunks)
    return jnp.concatenate([value[p : p + size] for p in places], 0)


def attend_kernel(block, chunks, len_ref, q_ref, k_ref, v_ref, *rest):
    out_ref, total_ref, q_mine, k_all, v_turned = rest[-5:]
    head = pl.program_id(0)
    lanes = head_lanes(head)
    rows = q_ref.shape[1]
    zero = jnp.zeros((rows, PAIR), bf16)
    scale = jnp.asarray(1.0 / math.sqrt(HEAD_DIM), bf16)
    q_mine[...] = in_sequence(jnp.where(lanes, q_ref[0] * scale, zero), chunks)
    k_all[...] = in_sequence(k_ref[0], chunks)
    v_turned[...] = in_sequence(jnp.where(lanes, v_ref[0], zero), chunks).T
    length = len_ref[0]
    places, size = chunk_places(rows, chunks)
    for first in range(0, rows, block):
        n = first + block
        r = slice(first, n)
        scores = masked_scores(k_all[:n, :], q_mine[r, :], first, length)
        top = jnp.max(scores, 0, keepdims=True)
        exped = jnp.exp(scores - top)
        total = jnp.sum(exped, 0, keepdims=True)
        probs = (exped * (1.0 / total)).astype(bf16)
        mixed = dot(v_turned[:, :n], probs, NN).T.astype(bf16)
        total_ref[0, :, r] = top + jnp.log(total)

        @pl.when(head % 2 == 0)
        def _():
            for c in range(block // size):
                place = places[first // size + c]
                out_ref[place : place + size, :] = mixed[c * size : (c + 1) * size]

        @pl.when(head % 2 == 1)
        def _():
            for c in range(block // size):
                place = places[first // size + c]
                out_ref[place : place + size, :] += mixed[c * size : (c + 1) * size]


def attend(qkv, length, chunks, part, held):
    _, rows, width = qkv.shape
    heads = width // HEAD_DIM
    here = heads // 2
    off = part * here
    kind = lambda c: pl.BlockSpec((1, rows, PAIR), lambda h, n: (c, 0, (h + off) // 2))
    extra = [] if held is None else list(held)
    return pl.pallas_call(
        functools.partial(attend_kernel, min(512, rows), chunks),
        grid_spec=pltpu.PrefetchScalarGridSpec(
            num_scalar_prefetch=1,
            grid=(here,),
            in_specs=[kind(0), kind(1), kind(2)]
            + [pl.BlockSpec(memory_space=pl.ANY)] * len(extra),
            out_specs=[
                pl.BlockSpec((rows, PAIR), lambda h, n: (0, (h + off) // 2)),
                pl.BlockSpec((1, 1, rows), lambda h, n: (h + off, 0, 0)),
            ],
            scratch_shapes=[
                pltpu.VMEM((rows, PAIR), bf16),
                pltpu.VMEM((rows, PAIR), bf16),
                pltpu.VMEM((PAIR, rows), bf16),
            ],
        ),
        out_shape=[shape((rows, width), bf16), shape((heads, 1, rows), f32)],
        input_output_aliases={4 + k: k for k in range(len(extra))},
        compiler_params=params(48),
        cost_estimate=cost(8 * rows * rows * width, 2 << 20, rows * rows * here),
        name="attend",
    )(length, qkv, qkv, qkv, *extra)


def attend_back_kernel(
    block, chunks, len_ref, q_ref, k_ref, v_ref, do_ref, total_ref, c_ref, a_ref, b_ref, *rest
):
    grad_ref, q_mine, do_mine, k_all, v_all, k_turned, key_sum, value_sum = rest[-8:]
    head = pl.program_id(0)
    lanes = head_lanes(head)
    rows = q_ref.shape[1]
    zero = jnp.zeros((rows, PAIR), bf16)
    scale = 1.0 / math.sqrt(HEAD_DIM)
    q_mine[...] = in_sequence(jnp.where(lanes, q_ref[0] * jnp.asarray(scale, bf16), zero), chunks)
    do_mine[...] = in_sequence(jnp.where(lanes, do_ref[...], zero), chunks)
    keys = in_sequence(k_ref[0], chunks)
    k_all[...] = keys
    v_all[...] = in_sequence(v_ref[0], chunks)
    k_turned[...] = jnp.where(lanes, keys, zero).T
    length = len_ref[0]
    places, size = chunk_places(rows, chunks)

    def put(kind, first, value):
        value = value.astype(bf16)

        @pl.when(head % 2 == 0)
        def _():
            for c in range(block // size):
                place = places[first // size + c]
                grad_ref[kind, place : place + size, :] = value[c * size : (c + 1) * size]

        @pl.when(head % 2 == 1)
        def _():
            for c in range(block // size):
                place = places[first // size + c]
                grad_ref[kind, place : place + size, :] += value[c * size : (c + 1) * size]

    tables_of = lambda r: (c_ref[r, :], a_ref[r, :], b_ref[r, :])
    for first in range(rows - block, -1, -block):
        n = first + block
        r = slice(first, n)
        scores = masked_scores(k_all[:n, :], q_mine[r, :], first, length)
        probs = jnp.exp(scores - total_ref[0, :, r])
        grad_probs = dot(v_all[:n, :], do_mine[r, :], NT)
        product = probs * grad_probs
        delta = jnp.sum(product, 0, keepdims=True)
        grad_scores = (product - probs * delta).astype(bf16)
        grad_keys = dot(grad_scores, q_mine[r, :], NN)
        grad_values = dot(probs.astype(bf16), do_mine[r, :], NN)
        if n == rows:
            key_sum[...] = grad_keys
            value_sum[...] = grad_values
        else:
            key_sum[:n, :] += grad_keys
            value_sum[:n, :] += grad_values
        grad_query = dot(k_turned[:, :n], grad_scores, NN).T * scale
        put(0, first, turned_back(grad_query, tables_of(r)))
    for first in range(0, rows, block):
        r = slice(first, first + block)
        put(1, first, turned_back(key_sum[r, :], tables_of(r)))
        put(2, first, value_sum[r, :])


def attend_back(qkv, grad_mixed, totals, length, tables, chunks):
    _, rows, width = qkv.shape
    heads = width // HEAD_DIM
    kind = lambda c: pl.BlockSpec((1, rows, PAIR), lambda h, n: (c, 0, h // 2))
    table = pl.BlockSpec((rows, PAIR), lambda h, n: (0, 0))
    return pl.pallas_call(
        functools.partial(attend_back_kernel, min(512, rows), chunks),
        grid_spec=pltpu.PrefetchScalarGridSpec(
            num_scalar_prefetch=1,
            grid=(heads,),
            in_specs=[
                kind(0),
                kind(1),
                kind(2),
                pl.BlockSpec((rows, PAIR), lambda h, n: (0, h // 2)),
                pl.BlockSpec((1, 1, rows), lambda h, n: (h, 0, 0)),
                table,
                table,
                table,
            ],
            out_specs=pl.BlockSpec((3, rows, PAIR), lambda h, n: (0, 0, h // 2)),
            scratch_shapes=[pltpu.VMEM((rows, PAIR), bf16)] * 4
            + [pltpu.VMEM((PAIR, rows), bf16)]
            + [pltpu.VMEM((rows, PAIR), f32)] * 2,
        ),
        out_shape=shape((3, rows, width), bf16),
        compiler_params=params(48),
        cost_estimate=cost(40 * rows * rows * width, 8 << 20, rows * rows * heads),
        name="attend_back",
    )(length, qkv, qkv, qkv, grad_mixed, totals, *tables)


def feed_kernel(tile, tile_f, steps, plan1, plan2, ln_ref, mixed_ref, wo_ref, bias_ref, *rest):
    n1 = len({p[0] for p in plan1})
    w1_refs, w2_refs = rest[:n1], rest[n1 : 2 * n1]
    (first_ref, second_ref, hidden_ref, slope_ref, full1_ref, full2_ref, acc, buf1, buf2, sems1,
     sems2, out_sems) = rest[2 * n1 :]
    step = pl.program_id(0)
    slot = lax.rem(step, 2)
    rows = ln_ref.shape[0]
    c0 = math.sqrt(2.0 / math.pi)
    c1 = 0.044715

    def start(s, at):
        column = pl.multiple_of(s * tile_f, tile_f)
        assemble_start(w1_refs, plan1, column, tile_f, buf1.at[at], sems1.at[at])
        assemble_start(w2_refs, plan2, column, tile_f, buf2.at[at], sems2.at[at])

    def outward(s, at):
        column = pl.multiple_of(s * tile_f, tile_f)
        return (
            pltpu.make_async_copy(
                buf1.at[at], full1_ref.at[:, pl.ds(column, tile_f)], out_sems.at[at, 0]
            ),
            pltpu.make_async_copy(
                buf2.at[at], full2_ref.at[:, pl.ds(column, tile_f)], out_sems.at[at, 1]
            ),
        )

    @pl.when(step == 0)
    def _():
        start(0, 0)

    column = pl.multiple_of(step * tile_f, tile_f)
    assemble_wait(w1_refs, plan1, column, tile_f, buf1.at[slot], sems1.at[slot])
    assemble_wait(w2_refs, plan2, column, tile_f, buf2.at[slot], sems2.at[slot])
    for copy in outward(step, slot):
        copy.start()

    @pl.when(step > 0)
    def _():
        for copy in outward(step - 1, 1 - slot):
            copy.wait()

    @pl.when(step < steps - 1)
    def _():
        start(step + 1, 1 - slot)

    @pl.loop(0, rows // tile)
    def _(m):
        r = pl.ds(pl.multiple_of(m * tile, tile), tile)
        pre = dot(ln_ref[r, :], buf1[slot], NN) + bias_ref[...]
        square = pre * pre
        bent = jnp.tanh(c0 * (pre + c1 * (square * pre)))
        half_pre = 0.5 * pre
        hidden = (half_pre * (1.0 + bent)).astype(bf16)
        hidden_ref[r, :] = hidden
        slope_ref[r, :] = 0.5 * (1.0 + bent) + half_pre * (1.0 - bent * bent) * (
            c0 * (1.0 + (3.0 * c1) * square)
        )
        part = dot(hidden, buf2[slot], NT)

        @pl.when(step == 0)
        def _():
            acc[r, :] = part + dot(mixed_ref[r, :], wo_ref[0], NT)

        @pl.when((step > 0) & (step < steps - 1))
        def _():
            acc[r, :] += part

        for wave, wave_ref in enumerate((first_ref, second_ref)):
            @pl.when((step == steps - 1) & (m == wave))
            def _():
                wave_ref[...] = (acc[r, :] + part).astype(bf16)

    @pl.when(step == steps - 1)
    def _():
        for copy in outward(step, slot):
            copy.wait()


def feed(ln, mixed, weights, w1, w2, bias, tile_f):
    rows, width = ln.shape
    hidden = bias.shape[1]
    heads = mixed.shape[1]
    steps = hidden // tile_f
    whole = lambda dims: pl.BlockSpec(dims, lambda i: (0, 0), pipeline_mode=once)
    by_row = pl.BlockSpec((rows, tile_f), lambda i: (0, i))
    hbm = pl.BlockSpec(memory_space=pl.ANY)
    return pl.pallas_call(
        functools.partial(feed_kernel, rows // 2, tile_f, steps, w1[1], w2[1]),
        grid=(steps,),
        in_specs=[
            whole((rows, width)),
            whole((rows, heads)),
            pl.BlockSpec((1, width, heads), lambda i: (3, 0, 0), pipeline_mode=once),
            pl.BlockSpec((1, tile_f), lambda i: (0, i)),
        ]
        + [hbm] * (len(w1[0]) + len(w2[0])),
        out_specs=[whole((rows // 2, width))] * 2 + [by_row, by_row, hbm, hbm],
        out_shape=[
            shape((rows // 2, width), bf16),
            shape((rows // 2, width), bf16),
            shape((rows, hidden), bf16),
            shape((rows, hidden), f32),
            shape((width, hidden), bf16),
            shape((width, hidden), bf16),
        ],
        scratch_shapes=[
            pltpu.VMEM((rows, width), f32),
            pltpu.VMEM((2, width, tile_f), bf16),
            pltpu.VMEM((2, width, tile_f), bf16),
            pltpu.SemaphoreType.DMA((2, len(w1[1]))),
            pltpu.SemaphoreType.DMA((2, len(w2[1]))),
            pltpu.SemaphoreType.DMA((2, 2)),
        ],
        compiler_params=params(58),
        cost_estimate=cost(4 * rows * width * hidden, 56 << 20, rows * hidden),
        name="feed",
    )(ln, mixed, weights, bias, *w1[0], *w2[0])


def column_products(left_ref, right_ref, near_ref, far_ref, tile):
    half = left_ref.shape[1] // 2

    @pl.loop(0, half // tile)
    def _(k):
        c = pl.ds(pl.multiple_of(k * tile, tile), tile)
        far = pl.ds(pl.multiple_of(half + k * tile, tile), tile)
        near_ref[c, :] = dot(left_ref[:, c], right_ref[...], TN).astype(bf16)
        far_ref[c, :] = dot(left_ref[:, far], right_ref[...], TN).astype(bf16)


def back_rows_kernel(first, g_ref, w1_ref, w2_ref, slope_ref, wo_ref, *rest):
    sum_ref, pre_ref, mixed_ref, all_ref, bias_ref = rest[-5:]
    step = pl.program_id(0)

    @pl.when(step == 0)
    def _():
        all_ref[...] = g_ref[...]
        mixed_ref[...] = dot(g_ref[...], wo_ref[0], NN).astype(bf16)

    grad = (dot(g_ref[...], w2_ref[...], NN) * slope_ref[...]).astype(bf16)
    pre_ref[...] = grad
    bias_ref[...] = jnp.sum(grad.astype(f32), axis=0, keepdims=True)
    part = dot(grad, w1_ref[...], NT)

    @pl.when(step == 0)
    def _():
        sum_ref[...] = part

    @pl.when(step > 0)
    def _():
        sum_ref[...] += part


def back_rows(grads, w1, w2, slope, weights, tile_f, wave, held):
    rows, width = grads.shape
    units = slope.shape[1]
    heads = weights.shape[2]
    weight = pl.BlockSpec((width, tile_f), lambda i: (0, i))
    extra = [] if held is None else list(held)
    return pl.pallas_call(
        functools.partial(back_rows_kernel, wave == 0),
        grid=(units // tile_f,),
        in_specs=[
            pl.BlockSpec((rows, width), lambda i: (0, 0), pipeline_mode=once),
            weight,
            weight,
            pl.BlockSpec((rows, tile_f), lambda i: (wave, i)),
            pl.BlockSpec((1, width, heads), lambda i: (3, 0, 0), pipeline_mode=once),
        ]
        + [pl.BlockSpec(memory_space=pl.ANY)] * len(extra),
        out_specs=[
            pl.BlockSpec((rows, width), lambda i: (0, 0), pipeline_mode=once),
            pl.BlockSpec((rows, tile_f), lambda i: (wave, i)),
            pl.BlockSpec((rows, heads), lambda i: (wave, 0), pipeline_mode=once),
            pl.BlockSpec((rows, width), lambda i: (wave, 0), pipeline_mode=once),
            pl.BlockSpec((1, tile_f), lambda i: (0, i)),
        ],
        out_shape=[
            shape((rows, width), f32),
            shape((2 * rows, units), bf16),
            shape((2 * rows, heads), bf16),
            shape((2 * rows, width), bf16),
            shape((1, units), f32),
        ],
        input_output_aliases={5 + k: 1 + k for k in range(len(extra))},
        compiler_params=params(58),
        cost_estimate=cost(4 * rows * width * units, 30 << 20),
        name="back_rows",
    )(grads, w1, w2, slope, weights, *extra)


def feed_weight_kernel(tile, ln_ref, pre_ref, near_ref, far_ref):
    column_products(ln_ref, pre_ref, near_ref, far_ref, tile)


def feed_weight(ln, grad_pre, tile_f):
    rows, width = ln.shape
    units = grad_pre.shape[1]
    half = pl.BlockSpec((width // 2, tile_f), lambda i: (0, i))
    return pl.pallas_call(
        functools.partial(feed_weight_kernel, min(512, width // 2)),
        grid=(units // tile_f,),
        in_specs=[
            pl.BlockSpec((rows, width), lambda i: (0, 0), pipeline_mode=once),
            pl.BlockSpec((rows, tile_f), lambda i: (0, i)),
        ],
        out_specs=[half, half],
        out_shape=[shape((width // 2, units), bf16)] * 2,
        compiler_params=params(48),
        cost_estimate=cost(2 * rows * width * units, 16 << 20),
        name="feed_weight",
    )(ln, grad_pre)


def ln_grad_kernel(grad_ref, w_ref, sum_ref, out_ref):
    total = sum_ref[...]
    for kind in range(3):
        total += dot(grad_ref[kind], w_ref[kind], NT)
    out_ref[...] = total.astype(bf16)


def ln_grad(grad_qkv, weights, partial_sum, wave):
    _, rows, heads = grad_qkv.shape
    width = partial_sum.shape[1]
    tile = min(256, rows // 2)
    steps = rows // 2 // tile
    return pl.pallas_call(
        ln_grad_kernel,
        grid=(steps,),
        in_specs=[
            pl.BlockSpec((3, tile, heads), lambda i: (0, i + wave * steps, 0)),
            pl.BlockSpec((3, width, heads), lambda i: (0, 0, 0), pipeline_mode=once),
            pl.BlockSpec((tile, width), lambda i: (i, 0)),
        ],
        out_specs=pl.BlockSpec((tile, width), lambda i: (i, 0)),
        out_shape=shape((rows // 2, width), bf16),
        compiler_params=params(48),
        cost_estimate=cost(3 * rows * width * heads, 14 << 20),
        name="ln_grad",
    )(grad_qkv, weights, partial_sum)


def weight_grad_kernel(ln_ref, g_ref, grad_ref, mixed_ref, kqk_ref, kvo_ref, sqk_ref, svo_ref, bias_ref):
    heads = mixed_ref.shape[1]
    step = pl.program_id(0)
    steps = pl.num_programs(0)
    for kind in range(3):
        @pl.when(step == 0)
        def _():
            bias_ref[kind] = jnp.sum(grad_ref[kind].astype(f32), axis=0, keepdims=True)

    for qk_ref, vo_ref, here in ((kqk_ref, kvo_ref, step < steps // 2), (sqk_ref, svo_ref, step >= steps // 2)):
        @pl.when(here)
        def _():
            qk_ref[:, :heads] = dot(ln_ref[...], grad_ref[0], TN).astype(bf16)
            qk_ref[:, heads:] = dot(ln_ref[...], grad_ref[1], TN).astype(bf16)
            vo_ref[:, :heads] = dot(ln_ref[...], grad_ref[2], TN).astype(bf16)
            vo_ref[:, heads:] = dot(g_ref[...], mixed_ref[...], TN).astype(bf16)


def weight_grad(ln, grads, grad_qkv, mixed):
    rows, width = ln.shape
    heads = mixed.shape[1]
    half = width // 2
    tile = min(512, half)
    near = half // tile
    column = pl.BlockSpec((rows, tile), lambda i: (0, i))
    kept = pl.BlockSpec((tile, 2 * heads), lambda i: (jnp.minimum(i, near - 1), 0))
    sent = pl.BlockSpec((tile, 2 * heads), lambda i: (jnp.maximum(i - near, 0), 0))
    return pl.pallas_call(
        weight_grad_kernel,
        grid=(2 * near,),
        in_specs=[
            column,
            column,
            pl.BlockSpec((3, rows, heads), lambda i: (0, 0, 0), pipeline_mode=once),
            pl.BlockSpec((rows, heads), lambda i: (0, 0), pipeline_mode=once),
        ],
        out_specs=[kept, kept, sent, sent, pl.BlockSpec((3, 1, heads), lambda i: (0, 0, 0))],
        out_shape=[shape((half, 2 * heads), bf16)] * 4 + [shape((3, 1, heads), f32)],
        compiler_params=params(48),
        cost_estimate=cost(8 * rows * width * heads, 20 << 20),
        name="weight_grad",
    )(ln, grads, grad_qkv, mixed)


def merge_kernel(kept_give, kept_hold, come_give, come_hold, give_ref, hold_ref):
    give_ref[...] = (kept_give[...].astype(f32) + come_give[...].astype(f32)).astype(bf16)
    hold_ref[...] = (kept_hold[...].astype(f32) + come_hold[...].astype(f32)).astype(bf16)


def merge(kept, arrived, rule, part=(0, 1)):
    rows, width = kept.shape[0], kept.shape[1] // part[1]
    count, odd = rule
    block = rows // count
    half = count // 2
    wide = min(1024, width)
    off = part[0] * (width // wide)
    give = pl.BlockSpec((block, wide), lambda i, j: (2 * i + 1 if odd else i + half, j + off))
    hold = pl.BlockSpec((block, wide), lambda i, j: (2 * i if odd else i, j + off))
    out = pl.BlockSpec((block, wide), lambda i, j: (i, j))
    return pl.pallas_call(
        merge_kernel,
        grid=(half, width // wide),
        in_specs=[give, hold, give, hold],
        out_specs=[out, out],
        out_shape=[shape((rows // 2, width), bf16)] * 2,
        compiler_params=params(32),
        cost_estimate=cost(rows * width, 6 * rows * width),
        name="merge",
    )(kept, kept, arrived, arrived)


def norm_back_kernel(
    blocks, index_ref, sum_ref, rows_ref, cot_ref, gain_ref, out_ref, gain_sum_ref, shift_sum_ref, held
):
    grad_ln = sum_ref[...].astype(f32)
    rows = rows_ref[...].astype(f32)
    centred = rows - jnp.mean(rows, -1, keepdims=True)
    inv_scale = lax.rsqrt(jnp.mean(centred * centred, -1, keepdims=True) + eps)
    normed = centred * inv_scale
    grad_norm = grad_ln * gain_ref[...]
    product = grad_ln * normed
    back = inv_scale * (
        grad_norm
        - jnp.mean(grad_norm, -1, keepdims=True)
        - normed * jnp.mean(grad_norm * normed, -1, keepdims=True)
    )
    held[...] = (cot_ref[...].astype(f32) + back).astype(bf16)
    gain_sum_ref[...] = jnp.sum(product, 0, keepdims=True)
    shift_sum_ref[...] = jnp.sum(grad_ln, 0, keepdims=True)
    wide = rows.shape[1] // blocks
    bits = blocks.bit_length() - 1
    for q in range(blocks):
        place = reversed_bits(index_ref[0] ^ q, bits) * wide
        out_ref[:, q * wide : (q + 1) * wide] = held[:, pl.ds(pl.multiple_of(place, wide), wide)]


def norm_back(total, rows_in, cot, gain, index, blocks):
    rows, width = rows_in.shape
    whole = pl.BlockSpec((rows, width), lambda i, n: (0, 0))
    vector = pl.BlockSpec((1, width), lambda i, n: (0, 0))
    return pl.pallas_call(
        functools.partial(norm_back_kernel, blocks),
        grid_spec=pltpu.PrefetchScalarGridSpec(
            num_scalar_prefetch=1,
            grid=(1,),
            in_specs=[whole, whole, whole, vector],
            out_specs=[whole, vector, vector],
            scratch_shapes=[pltpu.VMEM((rows, width), bf16)],
        ),
        out_shape=[shape((rows, width), bf16), shape((1, width), f32), shape((1, width), f32)],
        compiler_params=params(32),
        cost_estimate=cost(20 * rows * width, 8 * rows * width),
        name="norm_back",
    )(index.reshape(1), total, rows_in, cot, gain)


def normalize(rows_in):
    row_mean = jnp.mean(rows_in, -1, keepdims=True)
    centred = rows_in - row_mean
    variance = jnp.mean(centred * centred, -1, keepdims=True)
    inv_scale = lax.rsqrt(variance + eps)
    return (centred * inv_scale, inv_scale)


def rotary_tables(rows, col_count):
    half_rot = ROT // 2
    column = jnp.arange(col_count) % HEAD_DIM
    exponent = (2 * (column % half_rot)).astype(jnp.float32) / ROT
    frequency = jnp.exp(-math.log(10000.0) * exponent)
    angles = rows.astype(jnp.float32)[:, None] * frequency[None, :]
    inside = column < ROT
    cosine = jnp.where(inside, jnp.cos(angles), 1.0)
    sine_part = jnp.sin(angles)
    ahead_sin = jnp.where(column < half_rot, -sine_part, 0.0)
    behind_sin = jnp.where(inside & (column >= half_rot), sine_part, 0.0)
    return (cosine, ahead_sin, behind_sin)


def flip(array, axis_name, bit):
    size = lax.axis_size(axis_name)
    return lax.ppermute(array, axis_name, [(i, i ^ (1 << bit)) for i in range(size)])


def bits_of(size):
    return size.bit_length() - 1


def swap_blocks(array, index, axis, blocks):
    for bit in range(bits_of(blocks)):
        dims = array.shape
        parts = dims[:axis] + (blocks >> (bit + 1), 2, 1 << bit, dims[axis] // blocks)
        view = array.reshape(parts + dims[axis + 1 :])
        other = jnp.flip(view, axis=axis + 1)
        array = jnp.where((index >> bit) & 1 == 1, other, view).reshape(dims)
    return array


def reversed_bits(value, bits):
    return sum(((value >> k) & 1) << (bits - 1 - k) for k in range(bits))


def xor_columns(array, index, blocks):
    width = array.shape[-1] // blocks
    bits = bits_of(blocks)
    pieces = [
        lax.dynamic_slice_in_dim(
            array, (index ^ reversed_bits(p, bits)) * width, width, array.ndim - 1
        )
        for p in range(blocks)
    ]
    return jnp.concatenate(pieces, -1)


def plain_columns(array, index, blocks):
    width = array.shape[-1] // blocks
    bits = bits_of(blocks)
    pieces = []
    for q in range(blocks):
        place = reversed_bits(index ^ q, bits)
        pieces.append(lax.dynamic_slice_in_dim(array, place * width, width, array.ndim - 1))
    return jnp.concatenate(pieces, -1)


def gather_step(stacks, bit):
    return stacks + [(flip(rows, "dp", bit), [m | (1 << bit) for m in masks]) for rows, masks in stacks]


def gather_plan(stacks, block, bits):
    plan = []
    for which, (_, masks) in enumerate(stacks):
        for i, m in enumerate(masks):
            plan.append((which, i * block, reversed_bits(m, bits) * block, block))
    return [s[0] for s in stacks], tuple(plan)


def core_copies(stacks):
    return [(flip(rows, "dp", 0), [m | 1 for m in masks]) for rows, masks in stacks]


def route_order(last):
    return [b for b in range(bits_of(lax.axis_size("dp")) - 1, -1, -1) if b != last]


def route_first(block, last):
    return jnp.stack([block, flip(block, "dp", route_order(last)[0])], 0)


def route_rest(stack, wanted, index, last):
    order = route_order(last)
    for bit in order[1:]:
        stack = jnp.concatenate([stack, flip(stack, "dp", bit)], 0)

    def place(mask):
        return sum(((mask >> bit) & 1) << k for k, bit in enumerate(order))

    mine = wanted[index]
    theirs = wanted[index ^ (1 << last)]
    given = lax.dynamic_index_in_dim(stack, place(index ^ theirs), 0, keepdims=False)
    held = lax.dynamic_index_in_dim(stack, place(index ^ mine), 0, keepdims=False)
    arrived = flip(given, "dp", last)
    return jnp.where(((index ^ mine) >> last) & 1 == 1, arrived, held)


def gather_small(stack, axis_name):
    for bit in range(bits_of(lax.axis_size(axis_name))):
        stack = jnp.concatenate([stack, flip(stack, axis_name, bit)], 0)
    return stack


def scatter_small(blocks, data_index, tensor_index):
    data_count, tensor_count = lax.axis_size("dp"), lax.axis_size("tensor")
    stack = swap_blocks(blocks, data_index * tensor_count + tensor_index, 0, blocks.shape[0])
    for bit in range(bits_of(data_count) - 1, -1, -1):
        half = stack.shape[0] // 2
        stack = stack[:half] + flip(stack[half:], "dp", bit)
    for bit in range(bits_of(tensor_count) - 1, -1, -1):
        half = stack.shape[0] // 2
        stack = stack[:half] + flip(stack[half:], "tensor", bit)
    return stack[0]


def after(values, *others):
    held = lax.optimization_barrier((tuple(values), tuple(others)))
    return held[0]


def shards(
    hidden_in,
    cotangent,
    lengths,
    slot_of_seq,
    seq_of_slot,
    qkv_weight,
    out_weight,
    fc1_weight,
    fc2_weight,
    ln_gain,
    ln_bias,
    qkv_bias,
    out_bias,
    fc1_bias,
    fc2_bias,
):
    rows_here = hidden_in.shape[1]
    width = hidden_in.shape[2]
    tensor_count = lax.axis_size("tensor")
    data_count = lax.axis_size("dp")
    tensor_index = lax.axis_index("tensor")
    data_index = lax.axis_index("dp")
    seq_len = rows_here * tensor_count
    heads_local = qkv_weight.shape[2]
    hidden_local = fc1_weight.shape[1]
    block = width // data_count
    length = lengths[seq_of_slot[data_index]]
    bits = bits_of(data_count)
    x_first = list(range(1, bits))
    y_first = x_first[::-1]
    tile_f = min(512, hidden_local)

    chunks = 2 * tensor_count
    lasts = (bits - 1, bits - 2)
    wave_rows = rows_here // 2
    quarter = wave_rows // 2

    def send(rows):
        half = rows.shape[0] // 2
        return [route_first(h, last) for h, last in zip((rows[:half], rows[half:]), lasts)]

    def receive(firsts, wanted):
        return jnp.concatenate(
            [route_rest(f, wanted, data_index, last) for f, last in zip(firsts, lasts)], 0
        )

    firsts = send(hidden_in[0])
    vectors = [ln_gain, ln_bias, out_bias, fc2_bias, qkv_bias, fc1_bias]
    s = ln_gain.shape[0]
    vectors = after(vectors, *firsts)
    small = jnp.concatenate([v.reshape(-1, s) for v in vectors], 0)
    stack = gather_small(gather_small(small[None], "tensor"), "dp")
    routed = receive(firsts, seq_of_slot)
    routed, stack = after((routed, stack))
    gathered = swap_blocks(stack, data_index * tensor_count + tensor_index, 0, stack.shape[0])
    gathered = gathered.reshape(data_count, tensor_count, -1)
    rows_here_all = xor_columns(routed, data_index, data_count)
    rows_a, rows_b = rows_here_all[:wave_rows], rows_here_all[wave_rows:]
    full_a = lax.all_gather(rows_a, "tensor", axis=0, tiled=True)
    full_b = lax.all_gather(rows_b, "tensor", axis=0, tiled=True)

    qk_shard = qkv_weight[:, :2].reshape(block, 2 * heads_local)
    vo_shard = jnp.concatenate([qkv_weight[:, 2], out_weight], 1)
    qk_shard, vo_shard = after((qk_shard, vo_shard), routed)
    qk_stacks = gather_step([(qk_shard, [0])], x_first[0])
    vo_stacks = gather_step([(vo_shard, [0])], y_first[0])
    for step in range(1, len(x_first)):
        qk_stacks = gather_step(qk_stacks, x_first[step])
        vo_stacks = gather_step(vo_stacks, y_first[step])

    def held_back(groups, *values):
        flat = [rows for stacks in groups for rows, _ in stacks]
        out = list(after(tuple(flat) + values))
        fresh = [[(out.pop(0), masks) for _, masks in stacks] for stacks in groups]
        return fresh, out

    (qk_stacks, vo_stacks), (fc1_shard, fc2_shard, row_ids) = held_back(
        (qk_stacks, vo_stacks), fc1_weight, fc2_weight, jnp.arange(seq_len, dtype=jnp.int32)
    )
    qk = gather_plan(qk_stacks + core_copies(qk_stacks), block, bits)
    vo = gather_plan(vo_stacks + core_copies(vo_stacks), block, bits)
    fc1_stacks = gather_step([(fc1_shard, [0])], x_first[0])
    fc2_stacks = gather_step([(fc2_shard, [0])], y_first[0])

    positions = tensor_index * rows_here + jnp.arange(rows_here, dtype=jnp.int32)
    valid = (positions < length)[:, None]
    cot_plain, = after((cotangent[0],), routed)
    cot_rows = xor_columns(cot_plain, data_index, data_count)
    cot_a, cot_b = cot_rows[:wave_rows], cot_rows[wave_rows:]
    low = jnp.where(valid, cot_rows, jnp.zeros_like(cot_rows))
    low_a, low_b = low[:wave_rows], low[wave_rows:]
    grads_a, grads_b = after((low_a, low_b), rows_b)
    grads_a = lax.all_gather(grads_a, "tensor", axis=0, tiled=True)
    grads_b = lax.all_gather(grads_b, "tensor", axis=0, tiled=True)

    vectors = [
        xor_columns(gathered[:, :, i * s : (i + 1) * s].reshape(1, width), data_index, data_count)
        for i in range(4)
    ]
    gain, shift, bias_a, bias_b = [v.astype(f32) for v in vectors]
    q = qkv_bias.shape[0]
    bias_qkv = lax.dynamic_slice_in_dim(
        gathered[:, :, 4 * s : 4 * s + q].reshape(3, width), tensor_index * heads_local, heads_local, 1
    ).astype(f32)
    bias_fc1 = lax.dynamic_slice_in_dim(
        gathered[:, :, 4 * s + q :].reshape(1, hidden_local * tensor_count),
        tensor_index * hidden_local,
        hidden_local,
        1,
    ).astype(f32)

    tables = rotary_tables(row_ids, PAIR)
    wave_tables = [
        v.reshape(tensor_count, 2, wave_rows, PAIR).swapaxes(0, 1).reshape(seq_len, PAIR) for v in tables
    ]
    size = length.reshape(1)
    ln_a = norm_wave(full_a, gain, shift, 0, None)
    qkv_a, weights = project_first(ln_a, qk, vo, bias_qkv, wave_tables)
    (fc1_stacks, fc2_stacks), (weights,) = held_back((fc1_stacks, fc2_stacks), weights)
    fc1_far, fc2_far = core_copies(fc1_stacks), core_copies(fc2_stacks)
    for step in range(1, len(x_first)):
        fc1_stacks = gather_step(fc1_stacks, x_first[step])
        fc2_stacks = gather_step(fc2_stacks, y_first[step])
    (fc1_far, fc2_far), (ln_a, full_b, weights) = held_back(
        (fc1_far, fc2_far), ln_a, full_b, weights
    )
    ln = norm_wave(full_b, gain, shift, 1, ln_a)
    qkv = project_second(ln, weights, bias_qkv, wave_tables, qkv_a)
    attended = attend(qkv, size, chunks, 0, None)
    (fc1_stacks, fc2_stacks), attended = held_back((fc1_stacks, fc2_stacks), *attended)
    fc1_far = fc1_far + core_copies(fc1_stacks[2:])
    fc2_far = fc2_far + core_copies(fc2_stacks[2:])
    mixed, totals = attend(qkv, size, chunks, 1, attended)
    w1 = gather_plan(fc1_stacks + fc1_far, block, bits)
    w2 = gather_plan(fc2_stacks + fc2_far, block, bits)
    branch_a, branch_b, hidden, slope, full1, full2 = feed(
        ln, mixed, weights, w1, w2, bias_fc1, tile_f
    )

    count = data_count // 2
    steps = len(x_first)
    x_rule = lambda step: (1 << (steps - step), False)
    y_rule = lambda step: (1 << (steps - step), True)
    feed_a, *waves, bias_a1 = back_rows(grads_a, full1, full2, slope, weights, tile_f, 0, None)
    waves, grads_b, branch_a, branch_b = after((waves, grads_b, branch_a, branch_b))
    branch_a = lax.psum_scatter(branch_a, "tensor", scatter_dimension=0, tiled=True)
    branch_b = lax.psum_scatter(branch_b, "tensor", scatter_dimension=0, tiled=True)
    feed_b, grad_pre, grad_mixed, grads, bias_b1 = back_rows(
        grads_b, full1, full2, slope, weights, tile_f, 1, waves
    )
    grad_fc1_b = bias_a1 + bias_b1
    k2, s2 = feed_weight(grads, hidden, tile_f)
    f2 = flip(s2, "dp", 0)
    grad_pre, = after((grad_pre,), s2)
    k1, s1 = feed_weight(ln, grad_pre, tile_f)
    f1 = flip(s1, "dp", 0)
    k2, f2 = after((k2, f2), s1)
    give2, hold2 = merge(k2, f2, y_rule(0))
    f2 = flip(give2, "dp", y_first[0])
    k1, f1 = after((k1, f1), give2)
    give1, hold1 = merge(k1, f1, x_rule(0))
    f1 = flip(give1, "dp", x_first[0])
    grad_mixed, = after((grad_mixed,), give1)
    grad_qkv = attend_back(qkv, grad_mixed, totals, size, tables, chunks)
    kqk, kvo, sqk, svo, grad_qkv_b = weight_grad(ln, grads, grad_qkv, mixed)
    fq, fv = flip(sqk, "dp", 0), flip(svo, "dp", 0)
    grad_qkv, branch_a, branch_b, f2, f1 = after((grad_qkv, branch_a, branch_b, f2, f1), sqk)
    part_a = ln_grad(grad_qkv, weights, feed_a, 0)
    sum_a = lax.psum_scatter(part_a, "tensor", scatter_dimension=0, tiled=True)
    later_sum, = after((feed_b,), part_a)
    part_b = ln_grad(grad_qkv, weights, later_sum, 1)
    sum_b = lax.psum_scatter(part_b, "tensor", scatter_dimension=0, tiled=True)
    hold2, f2, hold1, f1, fq, fv = after((hold2, f2, hold1, f1, fq, fv), part_b)

    def all_steps(held, arrived, rule, order):
        give = held
        for step in range(1, steps):
            give, held = merge(held, arrived, rule(step))
            arrived = flip(give, "dp", order[step])
        return held, arrived, give

    hold2, f2, give2 = all_steps(hold2, f2, y_rule, y_first)
    hold1, f1, give1 = all_steps(hold1, f1, x_rule, x_first)
    kqk, kvo = after((kqk, kvo), give2, give1)
    giveq, holdq = merge(kqk, fq, x_rule(0))
    givev, holdv = merge(kvo, fv, y_rule(0))
    fq, fv = flip(giveq, "dp", x_first[0]), flip(givev, "dp", y_first[0])
    sum_a, f2, f1 = after((sum_a, f2, f1), giveq, givev)

    slots_f32 = [r.astype(f32) for r in (rows_a, rows_b)]
    slot_a, gain_a, shift_a = norm_back(sum_a, rows_a, cot_a, gain, data_index, data_count)
    back_a = send(slot_a)
    holdq, fq, holdv, fv = after((holdq, fq, holdv, fv), slot_a)
    holdq, fq, giveq = all_steps(holdq, fq, x_rule, x_first)
    holdv, fv, givev = all_steps(holdv, fv, y_rule, y_first)
    input_a = receive(back_a, slot_of_seq)
    sum_b, input_a = after((sum_b, input_a), giveq, givev)
    slot_b, gain_b, shift_b = norm_back(sum_b, rows_b, cot_b, gain, data_index, data_count)
    back_b = send(slot_b)
    hold1, f1, hold2, f2, holdq, fq, holdv, fv, back_b, gain_b, shift_b = after(
        (hold1, f1, hold2, f2, holdq, fq, holdv, fv, back_b, gain_b, shift_b)
    )
    input_b = receive(back_b, slot_of_seq)
    grad_input = jnp.concatenate([input_a, input_b], 0)[None]
    grad_gain, grad_shift = (gain_a + gain_b)[0], (shift_a + shift_b)[0]

    def final(held, arrived):
        return held.astype(f32) + arrived.astype(f32)

    grad_fc1_w, grad_fc2_w = final(hold1, f1), final(hold2, f2)
    grad_qk_w, grad_vo_w = final(holdq, fq), final(holdv, fv)
    grad_out_w = grad_vo_w[:, heads_local:]
    grad_qkv_w = jnp.stack(
        [grad_qk_w[:, :heads_local], grad_qk_w[:, heads_local:], grad_vo_w[:, :heads_local]], 1
    )
    branch = jnp.concatenate([branch_a, branch_b], 0).astype(f32) + bias_a + bias_b
    block_out = jnp.concatenate(slots_f32, 0) + jnp.where(valid, branch, 0.0)
    block_out = plain_columns(block_out.astype(bf16), data_index, data_count)[None]
    grad_bias = jnp.sum(low_a.astype(f32), axis=0) + jnp.sum(low_b.astype(f32), axis=0)

    devices = data_count * tensor_count
    full_qkv_b = lax.dynamic_update_slice_in_dim(
        jnp.zeros((3, width), f32), grad_qkv_b[:, 0], tensor_index * heads_local, 1
    )
    full_fc1_b = lax.dynamic_update_slice_in_dim(
        jnp.zeros((hidden_local * tensor_count,), f32), grad_fc1_b[0], tensor_index * hidden_local, 0
    )
    sums = jnp.concatenate(
        [
            plain_columns(v, data_index, data_count).reshape(devices, s)
            for v in (grad_gain, grad_shift, grad_bias)
        ]
        + [full_qkv_b.reshape(devices, q), full_fc1_b.reshape(devices, -1)],
        1,
    )
    total = scatter_small(sums, data_index, tensor_index)
    return (
        block_out,
        grad_input,
        grad_qkv_w,
        grad_out_w,
        grad_fc1_w,
        grad_fc2_w,
        total[:s],
        total[s : 2 * s],
        total[3 * s : 3 * s + q],
        total[2 * s : 3 * s],
        total[3 * s + q :],
        total[2 * s : 3 * s],
    )


def solution(mesh):
    in_specs = (
        P("dp", "tensor", None),
        P("dp", "tensor", None),
        P(),
        P(),
        P(),
        P("dp", None, "tensor"),
        P("dp", "tensor"),
        P("dp", "tensor"),
        P("dp", "tensor"),
        P(("dp", "tensor")),
        P(("dp", "tensor")),
        P(("dp", "tensor")),
        P(("dp", "tensor")),
        P(("dp", "tensor")),
        P(("dp", "tensor")),
    )
    out_specs = (
        P("dp", "tensor", None),
        P("dp", "tensor", None),
        P("dp", None, "tensor"),
        P("dp", "tensor"),
        P("dp", "tensor"),
        P("dp", "tensor"),
        P(("dp", "tensor")),
        P(("dp", "tensor")),
        P(("dp", "tensor")),
        P(("dp", "tensor")),
        P(("dp", "tensor")),
        P(("dp", "tensor")),
    )
    return jax.shard_map(shards, mesh=mesh, in_specs=in_specs, out_specs=out_specs, check_vma=False)
```

time: 572 us -> 541 us (0.946)
  Pallas kernels: 188 us -> 262 us
  other arithmetic: 81.6 us -> 28 us
  waiting for transfers between devices: 170 us -> 134 us
  local copies, waits for them, and re-layouts: 56.1 us -> 29.6 us
  starting transfers between devices: 45.9 us -> 57.2 us
    pallas_call x7 -> x24, Pallas kernels: 174 us -> 247 us  [the longest x2 40 us: back_rows(): pl.pallas_call(functools.partial(back_rows_kernel, wave == 0), grid=(unit...]
    ppermute x46 -> x68, waiting for transfers between devices: 170 us -> 115 us  [flip(): lax.ppermute(array, axis_name, [(i, i ^ 1 << bit) for i in range(size)])]
    convert_element_type x12 -> x2, other arithmetic: 31 us -> 1.72 us  [the longest x1 1.71 us: shards(): block_out.astype(bf16)]
    concatenate x12 -> x5, other arithmetic: 19.6 us -> 0.17 us  [the longest x2 0.14 us: receive(): jnp.concatenate([route_rest(f, wanted, data_index, last) for f, last in z...]
    all_gather x2 -> x4, waiting for transfers between devices: 0.02 us -> 18.5 us  [the longest x1 18.4 us: shards(): full_b = lax.all_gather(rows_b, 'tensor', axis=0, tiled=True)]
    unnamed x178 -> x147, local copies, waits for them, and re-layouts: 26.9 us -> 10.9 us
    ppermute x46 -> x68, starting transfers between devices: 45.3 us -> 56.3 us  [flip(): lax.ppermute(array, axis_name, [(i, i ^ 1 << bit) for i in range(size)])]
    concatenate x7 -> x5, local copies, waits for them, and re-layouts: 7.69 us -> 0.23 us  [the longest x1 0.12 us: shards(): small = jnp.concatenate([v.reshape(-1, s) for v in vectors], 0)]
  transfers between devices with their start and end apart: 50 -> 76, of which waited for: 26 -> 34; matrix products, arithmetic and copies ran while one was open for 21% -> 9% of each run, Pallas kernels for 33% -> 47%
where the time goes in v3:
time: 541 us; the launch traced here: 534 us
  Pallas kernels  262 us (48%)
  waiting for transfers between devices  134 us (25%)
  starting transfers between devices  57.2 us (11%)
  local copies, waits for them, and re-layouts  29.6 us (5%)
  other arithmetic  28 us (5%)
  between operations  22.1 us (4%)
    ppermute x68, waiting for transfers between devices, flip(): lax.ppermute(array, axis_name, [(i, i ^ 1 << bit) for i in range(size)])  115 us
    ppermute x68, starting transfers between devices, flip(): lax.ppermute(array, axis_name, [(i, i ^ 1 << bit) for i in range(size)])  56.3 us
    pallas_call x2, Pallas kernels, back_rows(): pl.pallas_call(functools.partial(back_rows_kernel, wave == 0), grid=(unit...  40 us
    pallas_call x1, Pallas kernels, feed(): pl.pallas_call(functools.partial(feed_kernel, rows // 2, tile_f, steps, w...  37.5 us
    pallas_call x1, Pallas kernels, attend_back(): pl.pallas_call(functools.partial(attend_back_kernel, min(512, rows), chun...  34.3 us
    pallas_call x8, Pallas kernels, merge(): pl.pallas_call(merge_kernel, grid=(half, width // wide), in_specs=[give,...  30.8 us
    pallas_call x2, Pallas kernels, feed_weight(): pl.pallas_call(functools.partial(feed_weight_kernel, min(512, width // 2)...  28.6 us
    pallas_call x2, Pallas kernels, attend(): pl.pallas_call(functools.partial(attend_kernel, min(512, rows), chunks),...  22.9 us
  transfers between devices with their start and end apart: 76, of which 34 were waited for; matrix products, arithmetic and copies ran while one was open for 9% of the time, Pallas kernels for 47%

profile of v3, /device:TPU:0, one launch (start us, length us, event | category | flops | bytes accessed | tf_op | source)
XLA Modules:
  0.0 533.5 jit_solution(13612503719728321704)
XLA Ops:
  15.8 7.8 %collective-permute-done = bf16[128,2048]{1,0:T(8,128)(2,1)S(1)} collective-permute-done((bf16[128,2048]{1,0:T(8,128)(2,1)S(1)}, bf16[128,2048]{1,0:T(8,128)(2,1)S(1)}, u32[]{:S(2)}, u32[]{:S(2)}) %collective-permute-start) | collective-permute-done | bytes 524320 | tf_op jit(solution)/shard_map/ppermute | solution.py:792
  44.4 10.3 %collective-permute-done.2 = bf16[128,2048]{1,0:T(8,128)(2,1)S(1)} collective-permute-done((bf16[128,2048]{1,0:T(8,128)(2,1)S(1)}, bf16[128,2048]{1,0:T(8,128)(2,1)S(1)}, u32[]{:S(2)}, u32[]{:S(2)}) %collective-permute-start.2) | collective-permute-done | bytes 524320 | tf_op jit(solution)/shard_map/ppermute | solution.py:792
  69.6 8.5 %collective-permute-done.11.rest_1_ = bf16[256,1024]{1,0:T(8,128)(2,1)} collective-permute-done((bf16[256,1024]{1,0:T(8,128)(2,1)S(1)}, bf16[256,1024]{1,0:T(8,128)(2,1)}, u32[]{:S(2)}, u32[]{:S(2)}) %collective-permute-start.11) | collective-permute-done | bytes 524320 | tf_op jit(solution)/shard_map/ppermute | solution.py:792
  78.5 9.2 %collective-permute-done.14.rest_9_ = bf16[256,1024]{1,0:T(8,128)(2,1)} collective-permute-done((bf16[256,1024]{1,0:T(8,128)(2,1)S(1)}, bf16[256,1024]{1,0:T(8,128)(2,1)}, u32[]{:S(2)}, u32[]{:S(2)}) %collective-permute-start.14) | collective-permute-done | bytes 524320 | tf_op jit(solution)/shard_map/ppermute | solution.py:792
  89.2 6.2 %collective-permute-done.13.rest_3_ = bf16[256,1024]{1,0:T(8,128)(2,1)S(1)} collective-permute-done((bf16[256,1024]{1,0:T(8,128)(2,1)}, bf16[256,1024]{1,0:T(8,128)(2,1)S(1)}, u32[]{:S(2)}, u32[]{:S(2)}) %collective-permute-start.13) | collective-permute-done | bytes 524320 | tf_op jit(solution)/shard_map/ppermute | solution.py:792
  103.6 5.6 %fusion = (f32[1024,128]{1,0:T(8,128)}, f32[1024,128]{1,0:T(8,128)}, f32[1024,128]{1,0:T(8,128)}, f32[1024,128]{1,0:T(8,128)}, f32[1024,128]{1,0:T(8,128)}, /*index=5*/f32[1024,128]{1,0:T(8,128)}) fusion(f32[128]{0:T(128)S(1)} %fusion.47, f32[1024]{0:T(1024)S(1)} %bitcast.152, pred[128]{0:T(512)(128)(4,1)S(1)} %get-tuple-element.400, ...), kind=kLoop, calls=%fused_computation.21 | loop fusion | flops 1310720 | bytes 3154816 | tf_op jit(solution)/shard_map/jit(_where)/select_n | solution.py:786
  109.3 4.6 norm_wave.2.ln_ref.rest_0_
  113.9 12.5 %project_first.1 = (bf16[3,1024,512]{2,1,0:T(8,128)(2,1)}, bf16[4,2048,512]{2,1,0:T(8,128)(2,1)}) custom-call(bf16[1024,2048]{1,0:T(8,128)(2,1)} %norm_wave.2.ln_ref.rest_0_, f32[3,1,512]{2,1,0:T(1,128)} %reshape.577.bias_ref, f32[1024,128]{1,0:T(8,128)} %get-tuple-element.383.c_ref, f32[1024,128]{1,0:T(8,128)} %get-tuple-element.382.a_ref, ...), custom_call_target="tpu_custom_call" | custom-call | flops 1288490240 | bytes 9227468 | tf_op jit(solution)/shard_map/project_first/pallas_call | solution.py:175
  133.5 18.4 %all-gather.7.cloned.1.call-done.x_ref = bf16[512,2048]{1,0:T(8,128)(2,1)} async-done(((bf16[128,2048]{1,0:T(8,128)(2,1)}), bf16[512,2048]{1,0:T(8,128)(2,1)}) %all-gather.7.cloned.1.call-update) | async-done | bytes 2097168 | tf_op jit(solution)/shard_map/all_gather | solution.py:958
  151.9 4.5 norm_wave.3.ln_ref
  156.4 8.3 %project_second.1.q_ref.k_ref.v_ref = bf16[3,1024,512]{2,1,0:T(8,128)(2,1)} custom-call(bf16[1024,2048]{1,0:T(8,128)(2,1)} %norm_wave.3.ln_ref, bf16[4,2048,512]{2,1,0:T(8,128)(2,1)} %get-tuple-element.187.w_ref.wo_ref, f32[3,1,512]{2,1,0:T(1,128)} %reshape.577.bias_ref, f32[1024,128]{1,0:T(8,128)} %get-tuple-element.383.c_ref, ...), custom_call_target="tpu_custom_call", output_to_operand_aliasing={{}: (6, {})} | custom-call | flops 1288490240 | bytes 5033164 | tf_op jit(solution)/shard_map/project_second/pallas_call | solution.py:207
  164.8 11.4 %attend.2 = (bf16[1024,512]{1,0:T(8,128)(2,1)}, f32[8,1,1024]{2,1,0:T(1,128)}) custom-call(s32[1]{0:T(128)} %dynamic_slice.327.len_ref, bf16[3,1024,512]{2,1,0:T(8,128)(2,1)} %project_second.1.q_ref.k_ref.v_ref, bf16[3,1024,512]{2,1,0:T(8,128)(2,1)} %project_second.1.q_ref.k_ref.v_ref, bf16[3,1024,512]{2,1,0:T(8,128)(2,1)} %project_second.1.q_ref.k_ref.v_ref), custom_call_target="tpu_custom_call" | custom-call | flops 1717986944 | bytes 838860 | tf_op jit(solution)/shard_map/attend/pallas_call | solution.py:293
  181.1 11.4 %attend.3 = (bf16[1024,512]{1,0:T(8,128)(2,1)}, f32[8,1,1024]{2,1,0:T(1,128)}) custom-call(s32[1]{0:T(128)} %dynamic_slice.327.len_ref, bf16[3,1024,512]{2,1,0:T(8,128)(2,1)} %project_second.1.q_ref.k_ref.v_ref, bf16[3,1024,512]{2,1,0:T(8,128)(2,1)} %project_second.1.q_ref.k_ref.v_ref, ...), custom_call_target="tpu_custom_call", output_to_operand_aliasing={{0}: (4, {}), {1}: (5, {})} | custom-call | flops 1717986944 | bytes 838860 | tf_op jit(solution)/shard_map/attend/pallas_call | solution.py:293
  192.5 37.5 %feed.1 = (bf16[512,2048]{1,0:T(8,128)(2,1)}, bf16[512,2048]{1,0:T(8,128)(2,1)}, bf16[1024,2048]{1,0:T(8,128)(2,1)}, f32[1024,2048]{1,0:T(8,128)}, bf16[2048,204...) custom-call(bf16[1024,2048]{1,0:T(8,128)(2,1)} %norm_wave.3.ln_ref, bf16[1024,512]{1,0:T(8,128)(2,1)} %get-tuple-element.195.mixed_ref, ...), custom_call_target="tpu_custom_call" | custom-call | flops 6871947776 | bytes 23488102 | tf_op jit(solution)/shard_map/feed/pallas_call | solution.py:496
  230.1 20.1 %back_rows.2 = (f32[512,2048]{1,0:T(8,128)}, bf16[1024,2048]{1,0:T(8,128)(2,1)}, bf16[1024,512]{1,0:T(8,128)(2,1)}, bf16[1024,2048]{1,0:T(8,128)(2,1)}, f32[1,2048]{1,0:T(1,128)}) custom-call(bf16[512,2048]{1,0:T(8,128)(2,1)} %all-gather.9.cloned.1.call-done.g_ref, bf16[2048,2048]{1,0:T(8,128)(2,1)} %get-tuple-element.208.w1_ref, ...), custom_call_target="tpu_custom_call" | custom-call | flops 3435973888 | bytes 12582912 | tf_op jit(solution)/shard_map/back_rows/pallas_call | solution.py:569
  250.3 19.9 %back_rows.3 = (f32[512,2048]{1,0:T(8,128)}, bf16[1024,2048]{1,0:T(8,128)(2,1)}, bf16[1024,512]{1,0:T(8,128)(2,1)}, bf16[1024,2048]{1,0:T(8,128)(2,1)}, f32[1,2048]{1,0:T(1,128)}) custom-call(bf16[512,2048]{1,0:T(8,128)(2,1)} %all-gather.11.cloned.1.call-done.g_ref, ...), custom_call_target="tpu_custom_call", output_to_operand_aliasing={{1}: (5, {}), {2}: (6, {}), {3}: (7, {})} | custom-call | flops 3435973888 | bytes 12582912 | tf_op jit(solution)/shard_map/back_rows/pallas_call | solution.py:569
  270.2 14.3 %feed_weight.2 = (bf16[1024,2048]{1,0:T(8,128)(2,1)}, bf16[1024,2048]{1,0:T(8,128)(2,1)}) custom-call(bf16[1024,2048]{1,0:T(8,128)(2,1)} %get-tuple-element.223.ln_ref.g_ref, bf16[1024,2048]{1,0:T(8,128)(2,1)} %get-tuple-element.224.pre_ref), custom_call_target="tpu_custom_call" | custom-call | flops 3435973888 | bytes 6710886 | tf_op jit(solution)/shard_map/feed_weight/pallas_call | solution.py:609
  284.5 14.3 %feed_weight.3 = (bf16[1024,2048]{1,0:T(8,128)(2,1)}, bf16[1024,2048]{1,0:T(8,128)(2,1)}) custom-call(bf16[1024,2048]{1,0:T(8,128)(2,1)} %norm_wave.3.ln_ref, bf16[1024,2048]{1,0:T(8,128)(2,1)} %get-tuple-element.226.pre_ref), custom_call_target="tpu_custom_call" | custom-call | flops 3435973888 | bytes 6710886 | tf_op jit(solution)/shard_map/feed_weight/pallas_call | solution.py:609
  299.4 6.1 %merge.8 = (bf16[512,2048]{1,0:T(8,128)(2,1)}, bf16[512,2048]{1,0:T(8,128)(2,1)}) custom-call(bf16[1024,2048]{1,0:T(8,128)(2,1)} %get-tuple-element.230.kept_give.kept_hold, bf16[1024,2048]{1,0:T(8,128)(2,1)} %get-tuple-element.230.kept_give.kept_hold, bf16[1024,2048]{1,0:T(8,128)(2,1)} %collective-permute-done.40.come_give.come_hold, ...), custom_call_target="tpu_custom_call" | custom-call | flops 838860 | bytes 5033164 | tf_op jit(solution)/shard_map/merge/pallas_call | solution.py:711
  306.5 5.9 %merge.9 = (bf16[512,2048]{1,0:T(8,128)(2,1)}, bf16[512,2048]{1,0:T(8,128)(2,1)}) custom-call(bf16[1024,2048]{1,0:T(8,128)(2,1)} %get-tuple-element.233.kept_give.kept_hold, bf16[1024,2048]{1,0:T(8,128)(2,1)} %get-tuple-element.233.kept_give.kept_hold, bf16[1024,2048]{1,0:T(8,128)(2,1)} %collective-permute-done.39.come_give.come_hold, ...), custom_call_target="tpu_custom_call" | custom-call | flops 838860 | bytes 5033164 | tf_op jit(solution)/shard_map/merge/pallas_call | solution.py:711
  314.7 34.3 %attend_back.1.grad_ref = bf16[3,1024,512]{2,1,0:T(8,128)(2,1)} custom-call(s32[1]{0:T(128)} %dynamic_slice.327.len_ref, bf16[3,1024,512]{2,1,0:T(8,128)(2,1)} %project_second.1.q_ref.k_ref.v_ref, bf16[3,1024,512]{2,1,0:T(8,128)(2,1)} %project_second.1.q_ref.k_ref.v_ref, bf16[3,1024,512]{2,1,0:T(8,128)(2,1)} %project_second.1.q_ref.k_ref.v_ref, ...), custom_call_target="tpu_custom_call" | custom-call | flops 8589934592 | bytes 3355443 | tf_op jit(solution)/shard_map/attend_back/pallas_call | solution.py:382
  349.0 15.0 %weight_grad.1 = (bf16[1024,1024]{1,0:T(8,128)(2,1)}, bf16[1024,1024]{1,0:T(8,128)(2,1)}, bf16[1024,1024]{1,0:T(8,128)(2,1)}, bf16[1024,1024]{1,0:T(8,128)(2,1)}, f32[3,1,512]{2,1,0:T(1,128)}) custom-call(bf16[1024,2048]{1,0:T(8,128)(2,1)} %norm_wave.3.ln_ref, bf16[1024,2048]{1,0:T(8,128)(2,1)} %get-tuple-element.223.ln_ref.g_ref, ...), custom_call_target="tpu_custom_call" | custom-call | flops 3435973888 | bytes 8388608 | tf_op jit(solution)/shard_map/weight_grad/pallas_call | solution.py:679
  364.1 8.3 %ln_grad.2 = bf16[512,2048]{1,0:T(8,128)(2,1)} custom-call(bf16[3,1024,512]{2,1,0:T(8,128)(2,1)} %attend_back.1.grad_ref, bf16[4,2048,512]{2,1,0:T(8,128)(2,1)} %get-tuple-element.187.w_ref.wo_ref, f32[512,2048]{1,0:T(8,128)} %get-tuple-element.245.sum_ref), custom_call_target="tpu_custom_call" | custom-call | flops 1288490240 | bytes 5872025 | tf_op jit(solution)/shard_map/ln_grad/pallas_call | solution.py:636
  373.1 8.6 %ln_grad.3 = bf16[512,2048]{1,0:T(8,128)(2,1)} custom-call(bf16[3,1024,512]{2,1,0:T(8,128)(2,1)} %attend_back.1.grad_ref, bf16[4,2048,512]{2,1,0:T(8,128)(2,1)} %get-tuple-element.187.w_ref.wo_ref, f32[512,2048]{1,0:T(8,128)} %get-tuple-element.246.sum_ref), custom_call_target="tpu_custom_call" | custom-call | flops 1288490240 | bytes 5872025 | tf_op jit(solution)/shard_map/ln_grad/pallas_call | solution.py:636
  381.7 3.3 merge.10
  399.5 3.3 merge.13
  403.8 3.6 merge.12
  411.3 4.2 collective-permute-done.46
  425.6 16.6 %collective-permute-done.50 = bf16[64,2048]{1,0:T(8,128)(2,1)S(1)} collective-permute-done((bf16[64,2048]{1,0:T(8,128)(2,1)S(1)}, bf16[64,2048]{1,0:T(8,128)(2,1)S(1)}, u32[]{:S(2)}, u32[]{:S(2)}) %collective-permute-start.50) | collective-permute-done | bytes 262176 | tf_op jit(solution)/shard_map/ppermute | solution.py:792
  455.5 4.8 collective-permute-done.52
  476.2 14.6 %collective-permute-done.57 = bf16[64,2048]{1,0:T(8,128)(2,1)S(1)} collective-permute-done((bf16[64,2048]{1,0:T(8,128)(2,1)S(1)}, bf16[64,2048]{1,0:T(8,128)(2,1)S(1)}, u32[]{:S(2)}, u32[]{:S(2)}) %collective-permute-start.57) | collective-permute-done | bytes 262176 | tf_op jit(solution)/shard_map/ppermute | solution.py:792
  519.7 4.2 collective-permute-done.60
  (459 shorter events, 153.6 us)
Async XLA Ops:
  7.2 102.1 %all-gather.5.cloned.1.call-start = ((), (), s32[]{:S(2)}) async-start(), calls=%async_computation.4 | async-start | bytes 2621440 | tf_op jit(solution)/shard_map/all_gather | solution.py:957
  24.7 15.9 %collective-permute-start.1 = (bf16[2,128,2048]{2,1,0:T(8,128)(2,1)}, bf16[2,128,2048]{2,1,0:T(8,128)(2,1)}, u32[]{:S(2)}, u32[]{:S(2)}) collective-permute-start(bf16[2,128,2048]{2,1,0:T(8,128)(2,1)} %pad_maximum_fusion.3), channel_id=1, source_target_pairs={{0,4},{4,0},{8,12},{12,8},{16,20},{20,16},{24,28},{28,24},{1,5},{5... | collective-permute-start | bytes 3145736 | tf_op jit(solution)/shard_map/ppermute | solution.py:792
  57.8 94.1 %all-gather.7.cloned.1.call-start = ((), (), s32[]{:S(2)}) async-start(), calls=%async_computation.5 | async-start | bytes 2621440 | tf_op jit(solution)/shard_map/all_gather | solution.py:958
  61.5 27.7 %collective-permute-start.12 = (bf16[256,1024]{1,0:T(8,128)(2,1)S(1)}, bf16[256,1024]{1,0:T(8,128)(2,1)S(1)}, u32[]{:S(2)}, u32[]{:S(2)}) collective-permute-start(bf16[256,1024]{1,0:T(8,128)(2,1)S(1)} %bitcast.113), channel_id=1, source_target_pairs={{0,16},{4,20},{8,24},{12,28},{16,0},{20,4},{24,8},{28,12},{1,17},{... | collective-permute-start | bytes 1572872 | tf_op jit(solution)/shard_map/ppermute | solution.py:792
  64.5 24.8 %collective-permute-start.15 = (bf16[256,1024]{1,0:T(8,128)(2,1)S(1)}, bf16[256,1024]{1,0:T(8,128)(2,1)}, u32[]{:S(2)}, u32[]{:S(2)}) collective-permute-start(bf16[256,1024]{1,0:T(8,128)(2,1)S(1)} %pad_maximum_fusion.8.rest_8_), channel_id=1, source_target_pairs={{0,8},{4,12},{8,0},{12,4},{16,24},{20,28},{24,16},{28,20},{1,9},{5... | collective-permute-start | bytes 1572872 | tf_op jit(solution)/shard_map/ppermute | solution.py:792
  65.1 22.7 %collective-permute-start.14 = (bf16[256,1024]{1,0:T(8,128)(2,1)S(1)}, bf16[256,1024]{1,0:T(8,128)(2,1)}, u32[]{:S(2)}, u32[]{:S(2)}) collective-permute-start(bf16[256,1024]{1,0:T(8,128)(2,1)S(1)} %pad_maximum_fusion.8.rest_8_), channel_id=1, source_target_pairs={{0,16},{4,20},{8,24},{12,28},{16,0},{20,4},{24,8},{28,12},{1,17},{... | collective-permute-start | bytes 1572872 | tf_op jit(solution)/shard_map/ppermute | solution.py:792
  65.7 164.4 %all-gather.9.cloned.1.call-start = ((), (), s32[]{:S(2)}) async-start(), calls=%async_computation.6 | async-start | bytes 2621440 | tf_op jit(solution)/shard_map/all_gather | solution.py:991
  69.5 180.7 %all-gather.11.cloned.1.call-start = ((), (), s32[]{:S(2)}) async-start(), calls=%async_computation.7 | async-start | bytes 2621440 | tf_op jit(solution)/shard_map/all_gather | solution.py:992
  78.0 17.3 %collective-permute-start.13 = (bf16[256,1024]{1,0:T(8,128)(2,1)}, bf16[256,1024]{1,0:T(8,128)(2,1)S(1)}, u32[]{:S(2)}, u32[]{:S(2)}) collective-permute-start(bf16[256,1024]{1,0:T(8,128)(2,1)} %collective-permute-done.11.rest_1_), channel_id=1, source_target_pairs={{0,16},{4,20},{8,24},{12,28},{16,0},{20,4},{24,8},{28,12},{1,17},{... | collective-permute-start | bytes 1572872 | tf_op jit(solution)/shard_map/ppermute | solution.py:792
  99.2 27.2 %collective-permute-start.17 = (bf16[256,2048]{1,0:T(8,128)(2,1)}, bf16[256,2048]{1,0:T(8,128)(2,1)}, u32[]{:S(2)}, u32[]{:S(2)}) collective-permute-start(bf16[256,2048]{1,0:T(8,128)(2,1)} %rest_0_), channel_id=1, source_target_pairs={{0,8},{4,12},{8,0},{12,4},{16,24},{20,28},{24,16},{28,20},{1,9},{5... | collective-permute-start | bytes 3145736 | tf_op jit(solution)/shard_map/ppermute | solution.py:792
  100.6 25.9 %collective-permute-start.18 = (bf16[256,2048]{1,0:T(8,128)(2,1)}, bf16[256,2048]{1,0:T(8,128)(2,1)}, u32[]{:S(2)}, u32[]{:S(2)}) collective-permute-start(bf16[256,2048]{1,0:T(8,128)(2,1)} %rest_8_), channel_id=1, source_target_pairs={{0,16},{4,20},{8,24},{12,28},{16,0},{20,4},{24,8},{28,12},{1,17},{... | collective-permute-start | bytes 3145736 | tf_op jit(solution)/shard_map/ppermute | solution.py:792
  127.5 24.4 %collective-permute-start.30 = (bf16[256,2048]{1,0:T(8,128)(2,1)}, bf16[256,2048]{1,0:T(8,128)(2,1)}, u32[]{:S(2)}, u32[]{:S(2)}) collective-permute-start(bf16[256,2048]{1,0:T(8,128)(2,1)} %collective-permute-done.18.rest_9_), channel_id=1, source_target_pairs={{0,4},{4,0},{8,12},{12,8},{16,20},{20,16},{24,28},{28,24},{1,5},{5... | collective-permute-start | bytes 3145736 | tf_op jit(solution)/shard_map/ppermute | solution.py:792
  127.6 236.4 %reduce-scatter.5.cloned.1.call-start = ((), (), s32[]{:S(2)}) async-start(), calls=%async_computation.8 | async-start | bytes 2621440 | tf_op jit(solution)/shard_map/reduce_scatter | solution.py:1044
  128.2 48.0 %collective-permute-start.31 = (bf16[256,2048]{1,0:T(8,128)(2,1)}, bf16[256,2048]{1,0:T(8,128)(2,1)}, u32[]{:S(2)}, u32[]{:S(2)}) collective-permute-start(bf16[256,2048]{1,0:T(8,128)(2,1)} %rest_0_), channel_id=1, source_target_pairs={{0,16},{4,20},{8,24},{12,28},{16,0},{20,4},{24,8},{28,12},{1,17},{... | collective-permute-start | bytes 3145736 | tf_op jit(solution)/shard_map/ppermute | solution.py:792
  129.6 46.9 %collective-permute-start.32 = (bf16[256,2048]{1,0:T(8,128)(2,1)}, bf16[256,2048]{1,0:T(8,128)(2,1)}, u32[]{:S(2)}, u32[]{:S(2)}) collective-permute-start(bf16[256,2048]{1,0:T(8,128)(2,1)} %collective-permute-done.17.rest_1_), channel_id=1, source_target_pairs={{0,16},{4,20},{8,24},{12,28},{16,0},{20,4},{24,8},{28,12},{1,17},{... | collective-permute-start | bytes 3145736 | tf_op jit(solution)/shard_map/ppermute | solution.py:792
  131.1 45.4 %collective-permute-start.33 = (bf16[256,2048]{1,0:T(8,128)(2,1)}, bf16[256,2048]{1,0:T(8,128)(2,1)}, u32[]{:S(2)}, u32[]{:S(2)}) collective-permute-start(bf16[256,2048]{1,0:T(8,128)(2,1)} %rest_8_), channel_id=1, source_target_pairs={{0,8},{4,12},{8,0},{12,4},{16,24},{20,28},{24,16},{28,20},{1,9},{5... | collective-permute-start | bytes 3145736 | tf_op jit(solution)/shard_map/ppermute | solution.py:792
  132.6 46.7 %collective-permute-start.34 = (bf16[256,2048]{1,0:T(8,128)(2,1)}, bf16[256,2048]{1,0:T(8,128)(2,1)}, u32[]{:S(2)}, u32[]{:S(2)}) collective-permute-start(bf16[256,2048]{1,0:T(8,128)(2,1)} %collective-permute-done.18.rest_9_), channel_id=1, source_target_pairs={{0,8},{4,12},{8,0},{12,4},{16,24},{20,28},{24,16},{28,20},{1,9},{5... | collective-permute-start | bytes 3145736 | tf_op jit(solution)/shard_map/ppermute | solution.py:792
  250.2 113.8 %reduce-scatter.7.cloned.1.call-start = ((), (), s32[]{:S(2)}) async-start(), calls=%async_computation.9 | async-start | bytes 2621440 | tf_op jit(solution)/shard_map/reduce_scatter | solution.py:1045
  299.4 117.0 %reduce-scatter.11.cloned.1.call-start = ((), (), s32[]{:S(2)}) async-start(), calls=%async_computation.11 | async-start | bytes 2621440 | tf_op jit(solution)/shard_map/reduce_scatter | solution.py:1067
  312.3 51.7 %collective-permute-start.42 = (bf16[512,2048]{1,0:T(8,128)(2,1)}, bf16[512,2048]{1,0:T(8,128)(2,1)}, u32[]{:S(2)}, u32[]{:S(2)}) collective-permute-start(bf16[512,2048]{1,0:T(8,128)(2,1)} %get-tuple-element.235), channel_id=1, source_target_pairs={{0,8},{4,12},{8,0},{12,4},{16,24},{20,28},{24,16},{28,20},{1,9},{5... | collective-permute-start | bytes 6291464 | tf_op jit(solution)/shard_map/ppermute | solution.py:792
  313.3 50.7 %collective-permute-start.41 = (bf16[512,2048]{1,0:T(8,128)(2,1)}, bf16[512,2048]{1,0:T(8,128)(2,1)}, u32[]{:S(2)}, u32[]{:S(2)}) collective-permute-start(bf16[512,2048]{1,0:T(8,128)(2,1)} %get-tuple-element.232), channel_id=1, source_target_pairs={{0,16},{4,20},{8,24},{12,28},{16,0},{20,4},{24,8},{28,12},{1,17},{... | collective-permute-start | bytes 6291464 | tf_op jit(solution)/shard_map/ppermute | solution.py:792
  372.4 90.3 %reduce-scatter.9.cloned.1.call-start = ((), (), s32[]{:S(2)}) async-start(), calls=%async_computation.10 | async-start | bytes 2621440 | tf_op jit(solution)/shard_map/reduce_scatter | solution.py:1070
  385.0 26.2 %collective-permute-start.45 = (bf16[256,2048]{1,0:T(8,128)(2,1)}, bf16[256,2048]{1,0:T(8,128)(2,1)}, u32[]{:S(2)}, u32[]{:S(2)}) collective-permute-start(bf16[256,2048]{1,0:T(8,128)(2,1)} %get-tuple-element.254), channel_id=1, source_target_pairs={{0,8},{4,12},{8,0},{12,4},{16,24},{20,28},{24,16},{28,20},{1,9},{5... | collective-permute-start | bytes 3145736 | tf_op jit(solution)/shard_map/ppermute | solution.py:792
  389.0 26.4 %collective-permute-start.46 = (bf16[256,2048]{1,0:T(8,128)(2,1)}, bf16[256,2048]{1,0:T(8,128)(2,1)}, u32[]{:S(2)}, u32[]{:S(2)}) collective-permute-start(bf16[256,2048]{1,0:T(8,128)(2,1)} %get-tuple-element.257), channel_id=1, source_target_pairs={{0,16},{4,20},{8,24},{12,28},{16,0},{20,4},{24,8},{28,12},{1,17},{... | collective-permute-start | bytes 3145736 | tf_op jit(solution)/shard_map/ppermute | solution.py:792
  402.8 41.8 %collective-permute-start.54 = (bf16[512,1024]{1,0:T(8,128)(2,1)}, bf16[512,1024]{1,0:T(8,128)(2,1)}, u32[]{:S(2)}, u32[]{:S(2)}) collective-permute-start(bf16[512,1024]{1,0:T(8,128)(2,1)} %get-tuple-element.265), channel_id=1, source_target_pairs={{0,16},{4,20},{8,24},{12,28},{16,0},{20,4},{24,8},{28,12},{1,17},{... | collective-permute-start | bytes 3145736 | tf_op jit(solution)/shard_map/ppermute | solution.py:792
  407.4 38.2 %collective-permute-start.53 = (bf16[512,1024]{1,0:T(8,128)(2,1)}, bf16[512,1024]{1,0:T(8,128)(2,1)}, u32[]{:S(2)}, u32[]{:S(2)}) collective-permute-start(bf16[512,1024]{1,0:T(8,128)(2,1)} %get-tuple-element.262), channel_id=1, source_target_pairs={{0,8},{4,12},{8,0},{12,4},{16,24},{20,28},{24,16},{28,20},{1,9},{5... | collective-permute-start | bytes 3145736 | tf_op jit(solution)/shard_map/ppermute | solution.py:792
  420.6 21.6 %collective-permute-start.50 = (bf16[64,2048]{1,0:T(8,128)(2,1)S(1)}, bf16[64,2048]{1,0:T(8,128)(2,1)S(1)}, u32[]{:S(2)}, u32[]{:S(2)}) collective-permute-start(bf16[64,2048]{1,0:T(8,128)(2,1)S(1)} %get-tuple-element.358), channel_id=1, source_target_pairs={{0,16},{4,20},{8,24},{12,28},{16,0},{20,4},{24,8},{28,12},{1,17},{... | collective-permute-start | bytes 786440 | tf_op jit(solution)/shard_map/ppermute | solution.py:792
  424.1 19.0 %collective-permute-start.47 = (bf16[64,2048]{1,0:T(8,128)(2,1)S(1)}, bf16[64,2048]{1,0:T(8,128)(2,1)S(1)}, u32[]{:S(2)}, u32[]{:S(2)}) collective-permute-start(bf16[64,2048]{1,0:T(8,128)(2,1)S(1)} %get-tuple-element.359), channel_id=1, source_target_pairs={{0,8},{4,12},{8,0},{12,4},{16,24},{20,28},{24,16},{28,20},{1,9},{5... | collective-permute-start | bytes 786440 | tf_op jit(solution)/shard_map/ppermute | solution.py:792
  471.7 19.2 %collective-permute-start.55 = (bf16[256,1024]{1,0:T(8,128)(2,1)S(1)}, bf16[256,1024]{1,0:T(8,128)(2,1)S(1)}, u32[]{:S(2)}, u32[]{:S(2)}) collective-permute-start(bf16[256,1024]{1,0:T(8,128)(2,1)S(1)} %copy-done.40), channel_id=1, source_target_pairs={{0,16},{4,20},{8,24},{12,28},{16,0},{20,4},{24,8},{28,12},{1,17},{... | collective-permute-start | bytes 1572872 | tf_op jit(solution)/shard_map/ppermute | solution.py:792
  472.4 18.4 %collective-permute-start.56 = (bf16[256,1024]{1,0:T(8,128)(2,1)S(1)}, bf16[256,1024]{1,0:T(8,128)(2,1)S(1)}, u32[]{:S(2)}, u32[]{:S(2)}) collective-permute-start(bf16[256,1024]{1,0:T(8,128)(2,1)S(1)} %copy-done.41), channel_id=1, source_target_pairs={{0,8},{4,12},{8,0},{12,4},{16,24},{20,28},{24,16},{28,20},{1,9},{5... | collective-permute-start | bytes 1572872 | tf_op jit(solution)/shard_map/ppermute | solution.py:792
  473.7 17.1 %collective-permute-start.57 = (bf16[64,2048]{1,0:T(8,128)(2,1)S(1)}, bf16[64,2048]{1,0:T(8,128)(2,1)S(1)}, u32[]{:S(2)}, u32[]{:S(2)}) collective-permute-start(bf16[64,2048]{1,0:T(8,128)(2,1)S(1)} %get-tuple-element.355), channel_id=1, source_target_pairs={{0,8},{4,12},{8,0},{12,4},{16,24},{20,28},{24,16},{28,20},{1,9},{5... | collective-permute-start | bytes 786440 | tf_op jit(solution)/shard_map/ppermute | solution.py:792
  495.7 21.6 %collective-permute-start.59 = (bf16[2,64,2048]{2,1,0:T(8,128)(2,1)S(1)}, bf16[2,64,2048]{2,1,0:T(8,128)(2,1)S(1)}, u32[]{:S(2)}, u32[]{:S(2)}) collective-permute-start(bf16[2,64,2048]{2,1,0:T(8,128)(2,1)S(1)} %pad_maximum_fusion.12), channel_id=1, source_target_pairs={{0,4},{4,0},{8,12},{12,8},{16,20},{20,16},{24,28},{28,24},{1,5},{5... | collective-permute-start | bytes 1572872 | tf_op jit(solution)/shard_map/ppermute | solution.py:792
  (89 other events, 774.8 us)
Sparse Core Ops, SparseCore 0:
  57.9 47.3 all-gather.4
  107.5 44.3 all-gather.6
  153.5 44.6 all-gather.8
  199.6 44.6 all-gather.10
  250.4 44.3 reduce-scatter.4
  299.5 44.2 reduce-scatter.6
  372.6 43.7 reduce-scatter.10
  419.3 43.2 reduce-scatter.8

commit v4 on v3

v4 whole, which is shorter than its diff:
```python
import functools
import math

import jax
import jax.numpy as jnp
from jax import lax
from jax.experimental import pallas as pl
from jax.experimental.pallas import tpu as pltpu
from jax.sharding import PartitionSpec as P

HEAD_DIM = 64
ROT = 32
PAIR = 2 * HEAD_DIM
VMEM = 63 * 1024 * 1024
SHARE = 0.4


eps = 1e-05
masked_score = -1e30
f32 = jnp.float32
bf16 = jnp.bfloat16
NN = (((1,), (0,)), ((), ()))
NT = (((1,), (1,)), ((), ()))
TN = (((0,), (0,)), ((), ()))
once = pl.Buffered(1)


def dot(a, b, dims):
    return lax.dot_general(a, b, dims, preferred_element_type=f32)


def params(mib):
    return pltpu.CompilerParams(vmem_limit_bytes=VMEM)


def cost(flops, nbytes, exps=0):
    return pl.CostEstimate(
        flops=int(flops * SHARE), bytes_accessed=int(nbytes * SHARE), transcendentals=int(exps * SHARE)
    )


def shape(dims, dtype):
    return jax.ShapeDtypeStruct(dims, dtype)


def turned(field, tables):
    cosine, ahead, behind = tables
    half = ROT // 2
    wide = field.shape[1]
    return (
        field * cosine
        + pltpu.roll(field, wide - half, 1) * ahead
        + pltpu.roll(field, half, 1) * behind
    )


def turned_back(grad, tables):
    cosine, ahead, behind = tables
    half = ROT // 2
    wide = grad.shape[1]
    return (
        grad * cosine
        + pltpu.roll(grad * ahead, half, 1)
        + pltpu.roll(grad * behind, wide - half, 1)
    )


def norm_kernel(blocks, at_ref, x_ref, gain_ref, shift_ref, *rest):
    out_ref, plain = rest[-2:]
    rows = x_ref[...].astype(f32)
    centred = rows - jnp.mean(rows, -1, keepdims=True)
    scale = lax.rsqrt(jnp.mean(centred * centred, -1, keepdims=True) + eps)
    plain[...] = (centred * scale * gain_ref[...] + shift_ref[...]).astype(bf16)
    wide = plain.shape[1] // blocks
    bits = blocks.bit_length() - 1
    for p in range(blocks):
        place = (at_ref[1] ^ reversed_bits(p, bits)) * wide
        out_ref[0, 0, :, p * wide : (p + 1) * wide] = plain[:, pl.ds(pl.multiple_of(place, wide), wide)]


def norm_wave(rows_in, count, at, gain, shift, blocks, wave, held):
    rows, width = rows_in.shape[0] // count, rows_in.shape[1]
    vector = pl.BlockSpec((1, width), lambda j, n: (0, 0))
    extra = [] if held is None else [held]
    return pl.pallas_call(
        functools.partial(norm_kernel, blocks),
        grid_spec=pltpu.PrefetchScalarGridSpec(
            num_scalar_prefetch=1,
            grid=(count,),
            in_specs=[pl.BlockSpec((rows, width), lambda j, n: (j, 0)), vector, vector]
            + [pl.BlockSpec(memory_space=pl.ANY)] * len(extra),
            out_specs=pl.BlockSpec((1, 1, rows, width), lambda j, n: (j, wave, 0, 0)),
            scratch_shapes=[pltpu.VMEM((rows, width), bf16)],
        ),
        out_shape=shape((count, 2, rows, width), bf16),
        input_output_aliases={4: 0} if extra else {},
        compiler_params=params(32),
        cost_estimate=cost(10 * count * rows * width, 4 * count * rows * width),
        name="norm_wave",
    )(at, rows_in, gain, shift, *extra)


def project_rows(kind, ln_ref, weight, bias_ref, tables, out_ref):
    rows = ln_ref.shape[0] * ln_ref.shape[2]
    many, size = ln_ref.shape[0], ln_ref.shape[2]
    raw = dot(ln_ref[...].reshape(rows, ln_ref.shape[3]), weight, NN) + bias_ref[0]

    @pl.when(kind < 2)
    def _():
        here = [t[...].reshape(rows, PAIR) for t in tables]
        for pair in range(raw.shape[1] // PAIR):
            cols = slice(pair * PAIR, (pair + 1) * PAIR)
            out_ref[0, :, 0, :, cols] = (
                turned(raw[:, cols], here).astype(bf16).reshape(many, size, PAIR)
            )

    @pl.when(kind == 2)
    def _():
        out_ref[0, :, 0] = raw.astype(bf16).reshape(many, size, raw.shape[1])


def assemble_start(refs, plan, column, size, buffer, sems):
    for j, (which, row, place, count) in enumerate(plan):
        pltpu.make_async_copy(
            refs[which].at[pl.ds(row, count), pl.ds(column, size)],
            buffer.at[pl.ds(place, count), :],
            sems.at[j],
        ).start()


def assemble_wait(refs, plan, column, size, buffer, sems):
    for j, (which, row, place, count) in enumerate(plan):
        pltpu.make_async_copy(
            refs[which].at[pl.ds(row, count), pl.ds(column, size)],
            buffer.at[pl.ds(place, count), :],
            sems.at[j],
        ).wait()


def project_first_kernel(qk_plan, vo_plan, ln_ref, bias_ref, c_ref, a_ref, b_ref, *rest):
    n = len({p[0] for p in qk_plan})
    qk_refs, vo_refs = rest[:n], rest[n : 2 * n]
    out_ref, w_ref, buffer, sems, out_sems = rest[2 * n :]
    kind = pl.program_id(0)
    heads = buffer.shape[2]
    sources = (
        (qk_refs, qk_plan, 0),
        (qk_refs, qk_plan, heads),
        (vo_refs, vo_plan, 0),
        (vo_refs, vo_plan, heads),
    )

    def drain(k):
        pltpu.make_async_copy(buffer.at[k % 2], w_ref.at[k], out_sems.at[k % 2]).wait()

    for k in range(4):
        refs, plan, column = sources[k]
        slot = k % 2

        @pl.when(kind == k)
        def _():
            if k == 0:
                assemble_start(refs, plan, column, heads, buffer.at[slot], sems.at[slot])
            assemble_wait(refs, plan, column, heads, buffer.at[slot], sems.at[slot])
            pltpu.make_async_copy(buffer.at[slot], w_ref.at[k], out_sems.at[slot]).start()
            if k >= 1:
                drain(k - 1)
            if k < 3:
                nrefs, nplan, ncolumn = sources[k + 1]
                assemble_start(
                    nrefs, nplan, ncolumn, heads, buffer.at[1 - slot], sems.at[1 - slot]
                )
            else:
                drain(k)

    @pl.when(kind < 3)
    def _():
        project_rows(kind, ln_ref, buffer[kind % 2], bias_ref, (c_ref, a_ref, b_ref), out_ref)


def project_first(ln, qk, vo, bias, tables):
    many, _, size, width = ln.shape
    heads = bias.shape[1]
    table = pl.BlockSpec((many, 1, size, PAIR), lambda i: (0, 0, 0, 0), pipeline_mode=once)
    hbm = pl.BlockSpec(memory_space=pl.ANY)
    last = lambda i: jnp.minimum(i, 2)
    return pl.pallas_call(
        functools.partial(project_first_kernel, qk[1], vo[1]),
        grid=(4,),
        in_specs=[
            pl.BlockSpec((many, 1, size, width), lambda i: (0, 0, 0, 0), pipeline_mode=once),
            pl.BlockSpec((1, 1, heads), lambda i: (last(i), 0, 0)),
            table,
            table,
            table,
        ]
        + [hbm] * (len(qk[0]) + len(vo[0])),
        out_specs=[
            pl.BlockSpec((1, many, 1, size, heads), lambda i: (last(i), 0, 0, 0, 0)),
            hbm,
        ],
        out_shape=[shape((3, many, 2, size, heads), bf16), shape((4, width, heads), bf16)],
        scratch_shapes=[
            pltpu.VMEM((2, width, heads), bf16),
            pltpu.SemaphoreType.DMA((2, len(qk[1]))),
            pltpu.SemaphoreType.DMA((2,)),
        ],
        compiler_params=params(48),
        cost_estimate=cost(6 * many * size * width * heads, 22 << 20),
        name="project_first",
    )(ln, bias[:, None, :], *tables, *qk[0], *vo[0])


def project_second_kernel(ln_ref, w_ref, bias_ref, c_ref, a_ref, b_ref, held_ref, out_ref):
    project_rows(pl.program_id(0), ln_ref, w_ref[0], bias_ref, (c_ref, a_ref, b_ref), out_ref)


def project_second(ln, weights, bias, tables, held):
    many, _, size, width = ln.shape
    heads = bias.shape[1]
    table = pl.BlockSpec((many, 1, size, PAIR), lambda i: (0, 1, 0, 0), pipeline_mode=once)
    return pl.pallas_call(
        project_second_kernel,
        grid=(3,),
        in_specs=[
            pl.BlockSpec((many, 1, size, width), lambda i: (0, 1, 0, 0), pipeline_mode=once),
            pl.BlockSpec((1, width, heads), lambda i: (i, 0, 0)),
            pl.BlockSpec((1, 1, heads), lambda i: (i, 0, 0)),
            table,
            table,
            table,
            pl.BlockSpec(memory_space=pl.ANY),
        ],
        out_specs=pl.BlockSpec((1, many, 1, size, heads), lambda i: (i, 0, 1, 0, 0)),
        out_shape=shape(held.shape, bf16),
        input_output_aliases={6: 0},
        compiler_params=params(48),
        cost_estimate=cost(6 * many * size * width * heads, 12 << 20),
        name="project_second",
    )(ln, weights, bias[:, None, :], *tables, held)


def head_lanes(head):
    lane = lax.broadcasted_iota(jnp.int32, (1, PAIR), 1)
    return (lane // HEAD_DIM) == (head % 2)


def masked_scores(keys, queries, first, length):
    scores = dot(keys, queries, NT)
    key = lax.broadcasted_iota(jnp.int32, scores.shape, 0)
    row = first + lax.broadcasted_iota(jnp.int32, (1, scores.shape[1]), 1)
    return jnp.where(key <= jnp.minimum(row, length - 1), scores, masked_score)


def attend_kernel(block, len_ref, q_ref, k_ref, v_ref, out_ref, total_ref, q_mine, v_turned):
    head = pl.program_id(0)
    lanes = head_lanes(head)
    rows = q_ref.shape[1]
    zero = jnp.zeros((rows, PAIR), bf16)
    scale = jnp.asarray(1.0 / math.sqrt(HEAD_DIM), bf16)
    q_mine[...] = jnp.where(lanes, q_ref[0] * scale, zero)
    v_turned[...] = jnp.where(lanes, v_ref[0], zero).T
    length = len_ref[0]
    for first in range(0, rows, block):
        n = first + block
        r = slice(first, n)
        scores = masked_scores(k_ref[0, :n, :], q_mine[r, :], first, length)
        top = jnp.max(scores, 0, keepdims=True)
        exped = jnp.exp(scores - top)
        total = jnp.sum(exped, 0, keepdims=True)
        mixed = dot(v_turned[:, :n], exped.astype(bf16), NN) * (1.0 / total)
        mixed = mixed.T.astype(bf16)
        total_ref[0, :, r] = top + jnp.log(total)

        @pl.when(head % 2 == 0)
        def _():
            out_ref[r, :] = mixed

        @pl.when(head % 2 == 1)
        def _():
            out_ref[r, :] = out_ref[r, :] + mixed


def attend(qkv, length):
    _, rows, width = qkv.shape
    heads = width // HEAD_DIM
    kind = lambda c: pl.BlockSpec((1, rows, PAIR), lambda h, n: (c, 0, h // 2))
    return pl.pallas_call(
        functools.partial(attend_kernel, min(512, rows)),
        grid_spec=pltpu.PrefetchScalarGridSpec(
            num_scalar_prefetch=1,
            grid=(heads,),
            in_specs=[kind(0), kind(1), kind(2)],
            out_specs=[
                pl.BlockSpec((rows, PAIR), lambda h, n: (0, h // 2)),
                pl.BlockSpec((1, 1, rows), lambda h, n: (h, 0, 0)),
            ],
            scratch_shapes=[pltpu.VMEM((rows, PAIR), bf16), pltpu.VMEM((PAIR, rows), bf16)],
        ),
        out_shape=[shape((rows, width), bf16), shape((heads, 1, rows), f32)],
        compiler_params=params(48),
        cost_estimate=cost(16 * rows * rows * width, 4 << 20, rows * rows * heads),
        name="attend",
    )(length, qkv, qkv, qkv)


def attend_back_kernel(
    block, len_ref, q_ref, k_ref, v_ref, do_ref, total_ref, c_ref, a_ref, b_ref,
    grad_ref, q_mine, do_mine, k_turned, key_sum, value_sum,
):
    head = pl.program_id(0)
    lanes = head_lanes(head)
    rows = q_ref.shape[1]
    zero = jnp.zeros((rows, PAIR), bf16)
    scale = 1.0 / math.sqrt(HEAD_DIM)
    q_mine[...] = jnp.where(lanes, q_ref[0] * jnp.asarray(scale, bf16), zero)
    do_mine[...] = jnp.where(lanes, do_ref[...], zero)
    k_turned[...] = jnp.where(lanes, k_ref[0], zero).T
    length = len_ref[0]

    def put(kind, r, value):
        value = value.astype(bf16)

        @pl.when(head % 2 == 0)
        def _():
            grad_ref[kind, r, :] = value

        @pl.when(head % 2 == 1)
        def _():
            grad_ref[kind, r, :] = grad_ref[kind, r, :] + value

    tables_of = lambda r: (c_ref[r, :], a_ref[r, :], b_ref[r, :])
    for first in range(rows - block, -1, -block):
        n = first + block
        r = slice(first, n)
        scores = masked_scores(k_ref[0, :n, :], q_mine[r, :], first, length)
        probs = jnp.exp(scores - total_ref[0, :, r])
        grad_probs = dot(v_ref[0, :n, :], do_mine[r, :], NT)
        product = probs * grad_probs
        delta = jnp.sum(product, 0, keepdims=True)
        grad_scores = (product - probs * delta).astype(bf16)
        keys = dot(grad_scores, q_mine[r, :], NN)
        vals = dot(probs.astype(bf16), do_mine[r, :], NN)
        if n == rows:
            key_sum[...] = keys
            value_sum[...] = vals
        else:
            key_sum[:n, :] += keys
            value_sum[:n, :] += vals
        grad_query = dot(k_turned[:, :n], grad_scores, NN).T * scale
        put(0, r, turned_back(grad_query, tables_of(r)))
    for first in range(0, rows, block):
        r = slice(first, first + block)
        put(1, r, turned_back(key_sum[r, :], tables_of(r)))
        put(2, r, value_sum[r, :])


def attend_back(qkv, grad_mixed, totals, length, tables):
    _, rows, width = qkv.shape
    heads = width // HEAD_DIM
    kind = lambda c: pl.BlockSpec((1, rows, PAIR), lambda h, n: (c, 0, h // 2))
    table_spec = pl.BlockSpec((rows, PAIR), lambda h, n: (0, 0))
    return pl.pallas_call(
        functools.partial(attend_back_kernel, min(512, rows)),
        grid_spec=pltpu.PrefetchScalarGridSpec(
            num_scalar_prefetch=1,
            grid=(heads,),
            in_specs=[
                kind(0),
                kind(1),
                kind(2),
                pl.BlockSpec((rows, PAIR), lambda h, n: (0, h // 2)),
                pl.BlockSpec((1, 1, rows), lambda h, n: (h, 0, 0)),
                table_spec,
                table_spec,
                table_spec,
            ],
            out_specs=pl.BlockSpec((3, rows, PAIR), lambda h, n: (0, 0, h // 2)),
            scratch_shapes=[
                pltpu.VMEM((rows, PAIR), bf16),
                pltpu.VMEM((rows, PAIR), bf16),
                pltpu.VMEM((PAIR, rows), bf16),
                pltpu.VMEM((rows, PAIR), f32),
                pltpu.VMEM((rows, PAIR), f32),
            ],
        ),
        out_shape=shape((3, rows, width), bf16),
        compiler_params=params(48),
        cost_estimate=cost(40 * rows * rows * width, 8 << 20, rows * rows * heads),
        name="attend_back",
    )(length, qkv, qkv, qkv, grad_mixed, totals, *tables)


def feed_kernel(tile, tile_f, steps, plan1, plan2, ln_ref, mixed_ref, wo_ref, bias_ref, *rest):
    n1 = len({p[0] for p in plan1})
    w1_refs, w2_refs = rest[:n1], rest[n1 : 2 * n1]
    (branch_ref, hidden_ref, slope_ref, full1_ref, full2_ref, acc, buf1, buf2, sems1, sems2,
     out_sems) = rest[2 * n1 :]
    step = pl.program_id(0)
    slot = lax.rem(step, 2)
    rows = ln_ref.shape[0]
    c0 = math.sqrt(2.0 / math.pi)
    c1 = 0.044715

    def start(s, at):
        column = pl.multiple_of(s * tile_f, tile_f)
        assemble_start(w1_refs, plan1, column, tile_f, buf1.at[at], sems1.at[at])
        assemble_start(w2_refs, plan2, column, tile_f, buf2.at[at], sems2.at[at])

    def outward(s, at):
        column = pl.multiple_of(s * tile_f, tile_f)
        return (
            pltpu.make_async_copy(
                buf1.at[at], full1_ref.at[:, pl.ds(column, tile_f)], out_sems.at[at, 0]
            ),
            pltpu.make_async_copy(
                buf2.at[at], full2_ref.at[:, pl.ds(column, tile_f)], out_sems.at[at, 1]
            ),
        )

    @pl.when(step == 0)
    def _():
        start(0, 0)

    column = pl.multiple_of(step * tile_f, tile_f)
    assemble_wait(w1_refs, plan1, column, tile_f, buf1.at[slot], sems1.at[slot])
    assemble_wait(w2_refs, plan2, column, tile_f, buf2.at[slot], sems2.at[slot])
    for copy in outward(step, slot):
        copy.start()

    @pl.when(step > 0)
    def _():
        for copy in outward(step - 1, 1 - slot):
            copy.wait()

    @pl.when(step < steps - 1)
    def _():
        start(step + 1, 1 - slot)

    for first in range(0, rows, tile):
        r = slice(first, first + tile)
        pre = dot(ln_ref[r, :], buf1[slot], NN) + bias_ref[...]
        square = pre * pre
        bent = jnp.tanh(c0 * (pre + c1 * (square * pre)))
        half_pre = 0.5 * pre
        hidden = (half_pre * (1.0 + bent)).astype(bf16)
        hidden_ref[r, :] = hidden
        slope_ref[r, :] = 0.5 * (1.0 + bent) + half_pre * (1.0 - bent * bent) * (
            c0 * (1.0 + (3.0 * c1) * square)
        )

    for first in range(0, rows, tile):
        r = slice(first, first + tile)
        part = dot(hidden_ref[r, :], buf2[slot], NT)

        @pl.when(step == 0)
        def _():
            acc[r, :] = part + dot(mixed_ref[r, :], wo_ref[0], NT)

        @pl.when((step > 0) & (step < steps - 1))
        def _():
            acc[r, :] += part

        @pl.when(step == steps - 1)
        def _():
            branch_ref[r, :] = (acc[r, :] + part).astype(bf16)

    @pl.when(step == steps - 1)
    def _():
        for copy in outward(step, slot):
            copy.wait()


def feed(ln, mixed, weights, w1, w2, bias, tile_f):
    rows, width = ln.shape
    hidden = bias.shape[1]
    heads = mixed.shape[1]
    steps = hidden // tile_f
    whole = lambda dims: pl.BlockSpec(dims, lambda i: (0, 0), pipeline_mode=once)
    by_row = pl.BlockSpec((rows, tile_f), lambda i: (0, i))
    hbm = pl.BlockSpec(memory_space=pl.ANY)
    return pl.pallas_call(
        functools.partial(feed_kernel, rows // 2, tile_f, steps, w1[1], w2[1]),
        grid=(steps,),
        in_specs=[
            whole((rows, width)),
            whole((rows, heads)),
            pl.BlockSpec((1, width, heads), lambda i: (3, 0, 0), pipeline_mode=once),
            pl.BlockSpec((1, tile_f), lambda i: (0, i)),
        ]
        + [hbm] * (len(w1[0]) + len(w2[0])),
        out_specs=[whole((rows, width)), by_row, by_row, hbm, hbm],
        out_shape=[
            shape((rows, width), bf16),
            shape((rows, hidden), bf16),
            shape((rows, hidden), f32),
            shape((width, hidden), bf16),
            shape((width, hidden), bf16),
        ],
        scratch_shapes=[
            pltpu.VMEM((rows, width), f32),
            pltpu.VMEM((2, width, tile_f), bf16),
            pltpu.VMEM((2, width, tile_f), bf16),
            pltpu.SemaphoreType.DMA((2, len(w1[1]))),
            pltpu.SemaphoreType.DMA((2, len(w2[1]))),
            pltpu.SemaphoreType.DMA((2, 2)),
        ],
        compiler_params=params(58),
        cost_estimate=cost(4 * rows * width * hidden, 56 << 20, rows * hidden),
        name="feed",
    )(ln, mixed, weights, bias, *w1[0], *w2[0])


def back_kernel(tile, g_ref, w1_ref, w2_ref, slope_ref, wo_ref, sum_ref, pre_ref, mixed_ref, bias_ref):
    step = pl.program_id(0)
    rows = g_ref.shape[0]

    @pl.when(step == 0)
    def _():
        mixed_ref[...] = dot(g_ref[...], wo_ref[0], NN).astype(bf16)

    for first in range(0, rows, tile):
        r = slice(first, first + tile)
        pre_ref[r, :] = (dot(g_ref[r, :], w2_ref[...], NN) * slope_ref[r, :]).astype(bf16)

    bias_ref[...] = jnp.sum(pre_ref[...].astype(f32), axis=0, keepdims=True)
    for first in range(0, rows, tile):
        r = slice(first, first + tile)
        part = dot(pre_ref[r, :], w1_ref[...], NT)

        @pl.when(step == 0)
        def _():
            sum_ref[r, :] = part

        @pl.when(step > 0)
        def _():
            sum_ref[r, :] += part


def back(grads, w1, w2, slope, weights, tile_f):
    rows, width = grads.shape
    units = slope.shape[1]
    heads = weights.shape[2]
    weight = pl.BlockSpec((width, tile_f), lambda i: (0, i))
    whole = lambda dims: pl.BlockSpec(dims, lambda i: (0, 0), pipeline_mode=once)
    by_row = pl.BlockSpec((rows, tile_f), lambda i: (0, i))
    return pl.pallas_call(
        functools.partial(back_kernel, min(512, rows)),
        grid=(units // tile_f,),
        in_specs=[
            whole((rows, width)),
            weight,
            weight,
            by_row,
            pl.BlockSpec((1, width, heads), lambda i: (3, 0, 0), pipeline_mode=once),
        ],
        out_specs=[
            whole((rows, width)),
            by_row,
            whole((rows, heads)),
            pl.BlockSpec((1, tile_f), lambda i: (0, i)),
        ],
        out_shape=[
            shape((rows, width), f32),
            shape((rows, units), bf16),
            shape((rows, heads), bf16),
            shape((1, units), f32),
        ],
        compiler_params=params(58),
        cost_estimate=cost(4 * rows * width * units, 40 << 20),
        name="back",
    )(grads, w1, w2, slope, weights)


def feed_weight_kernel(left_ref, right_ref, near_ref, far_ref):
    half = left_ref.shape[1] // 2
    far_ref[...] = dot(left_ref[:, half:], right_ref[...], TN).astype(bf16)
    near_ref[...] = dot(left_ref[:, :half], right_ref[...], TN).astype(bf16)


def feed_weight(left, right, tile_f):
    rows, width = left.shape
    units = right.shape[1]
    half = pl.BlockSpec((width // 2, tile_f), lambda i: (0, i))
    return pl.pallas_call(
        feed_weight_kernel,
        grid=(units // tile_f,),
        in_specs=[
            pl.BlockSpec((rows, width), lambda i: (0, 0), pipeline_mode=once),
            pl.BlockSpec((rows, tile_f), lambda i: (0, i)),
        ],
        out_specs=[half, half],
        out_shape=[shape((width // 2, units), bf16)] * 2,
        compiler_params=params(48),
        cost_estimate=cost(2 * rows * width * units, 16 << 20),
        name="feed_weight",
    )(left, right)


def ln_grad_kernel(grad_ref, w_ref, sum_ref, out_ref):
    total = sum_ref[...]
    for kind in range(3):
        total += dot(grad_ref[kind], w_ref[kind], NT)
    out_ref[...] = total.astype(bf16)


def ln_grad(grad_qkv, weights, partial_sum):
    _, rows, heads = grad_qkv.shape
    width = partial_sum.shape[1]
    tile = min(512, rows)
    return pl.pallas_call(
        ln_grad_kernel,
        grid=(rows // tile,),
        in_specs=[
            pl.BlockSpec((3, tile, heads), lambda i: (0, i, 0)),
            pl.BlockSpec((3, width, heads), lambda i: (0, 0, 0), pipeline_mode=once),
            pl.BlockSpec((tile, width), lambda i: (i, 0)),
        ],
        out_specs=pl.BlockSpec((tile, width), lambda i: (i, 0)),
        out_shape=shape((rows, width), bf16),
        compiler_params=params(48),
        cost_estimate=cost(6 * rows * width * heads, 22 << 20),
        name="ln_grad",
    )(grad_qkv, weights, partial_sum)


def weight_grad_kernel(ln_ref, g_ref, grad_ref, mixed_ref, kqk_ref, kvo_ref, sqk_ref, svo_ref, bias_ref):
    heads = mixed_ref.shape[1]
    step = pl.program_id(0)
    steps = pl.num_programs(0)
    for kind in range(3):
        @pl.when(step == 0)
        def _():
            bias_ref[kind] = jnp.sum(grad_ref[kind].astype(f32), axis=0, keepdims=True)

    for qk_ref, vo_ref, here in ((kqk_ref, kvo_ref, step < steps // 2), (sqk_ref, svo_ref, step >= steps // 2)):
        @pl.when(here)
        def _():
            qk_ref[:, :heads] = dot(ln_ref[...], grad_ref[0], TN).astype(bf16)
            qk_ref[:, heads:] = dot(ln_ref[...], grad_ref[1], TN).astype(bf16)
            vo_ref[:, :heads] = dot(ln_ref[...], grad_ref[2], TN).astype(bf16)
            vo_ref[:, heads:] = dot(g_ref[...], mixed_ref[...], TN).astype(bf16)


def weight_grad(ln, grads, grad_qkv, mixed):
    rows, width = ln.shape
    heads = mixed.shape[1]
    half = width // 2
    tile = min(512, half)
    near = half // tile
    column = pl.BlockSpec((rows, tile), lambda i: (0, i))
    kept = pl.BlockSpec((tile, 2 * heads), lambda i: (jnp.minimum(i, near - 1), 0))
    sent = pl.BlockSpec((tile, 2 * heads), lambda i: (jnp.maximum(i - near, 0), 0))
    return pl.pallas_call(
        weight_grad_kernel,
        grid=(2 * near,),
        in_specs=[
            column,
            column,
            pl.BlockSpec((3, rows, heads), lambda i: (0, 0, 0), pipeline_mode=once),
            pl.BlockSpec((rows, heads), lambda i: (0, 0), pipeline_mode=once),
        ],
        out_specs=[kept, kept, sent, sent, pl.BlockSpec((3, 1, heads), lambda i: (0, 0, 0))],
        out_shape=[shape((half, 2 * heads), bf16)] * 4 + [shape((3, 1, heads), f32)],
        compiler_params=params(48),
        cost_estimate=cost(8 * rows * width * heads, 20 << 20),
        name="weight_grad",
    )(ln, grads, grad_qkv, mixed)


def give_kernel(*refs):
    total = refs[0][...].astype(f32)
    for ref in refs[1:-1]:
        total += ref[...].astype(f32)
    refs[-1][...] = total.astype(bf16)


def give(full, partial_sums, count, low, part=(0, 1)):
    rows, width = full[0].shape[0], full[0].shape[1] // part[1]
    block = rows // count
    level = len(partial_sums) + 1
    out_count = count >> level
    wide = min(1024, width)
    off = part[0] * (width // wide)
    place = (lambda i: (2 * i + 1) << (level - 1)) if low else (lambda i: out_count + i)
    spec = lambda k, o: pl.BlockSpec(
        (block, wide), lambda i, j: (place(i) >> k if low else place(i), j + o)
    )
    return pl.pallas_call(
        give_kernel,
        grid=(out_count, width // wide),
        in_specs=[spec(0, off) for _ in full] + [spec(k + 1, 0) for k in range(level - 1)],
        out_specs=pl.BlockSpec((block, wide), lambda i, j: (i, j)),
        out_shape=shape((out_count * block, width), bf16),
        compiler_params=params(32),
        cost_estimate=cost(out_count * block * width * 2, 6 * out_count * block * width),
        name="give",
    )(*full, *partial_sums)


def norm_back_kernel(
    blocks, at_ref, sum_ref, rows_ref, cot_ref, gain_ref, out_ref, gain_sum_ref, shift_sum_ref, held
):
    wide = rows_ref.shape[1] // blocks
    bits = blocks.bit_length() - 1
    for q in range(blocks):
        place = pl.multiple_of(reversed_bits(at_ref[1] ^ q, bits) * wide, wide)
        held[:, q * wide : (q + 1) * wide] = sum_ref[:, pl.ds(place, wide)]
    grad_ln = held[...].astype(f32)
    rows = rows_ref[...].astype(f32)
    centred = rows - jnp.mean(rows, -1, keepdims=True)
    inv_scale = lax.rsqrt(jnp.mean(centred * centred, -1, keepdims=True) + eps)
    normed = centred * inv_scale
    grad_norm = grad_ln * gain_ref[...]
    back = inv_scale * (
        grad_norm
        - jnp.mean(grad_norm, -1, keepdims=True)
        - normed * jnp.mean(grad_norm * normed, -1, keepdims=True)
    )
    out_ref[...] = (cot_ref[...].astype(f32) + back).astype(bf16)
    gain_sum_ref[...] = jnp.sum(grad_ln * normed, 0, keepdims=True)
    shift_sum_ref[...] = jnp.sum(grad_ln, 0, keepdims=True)


def norm_back(total, rows_in, cot, gain, at, blocks):
    rows, width = rows_in.shape
    whole = pl.BlockSpec((rows, width), lambda i, n: (0, 0))
    vector = pl.BlockSpec((1, width), lambda i, n: (0, 0))
    return pl.pallas_call(
        functools.partial(norm_back_kernel, blocks),
        grid_spec=pltpu.PrefetchScalarGridSpec(
            num_scalar_prefetch=1,
            grid=(1,),
            in_specs=[whole, whole, whole, vector],
            out_specs=[whole, vector, vector],
            scratch_shapes=[pltpu.VMEM((rows, width), bf16)],
        ),
        out_shape=[shape((rows, width), bf16), shape((1, width), f32), shape((1, width), f32)],
        compiler_params=params(32),
        cost_estimate=cost(20 * rows * width, 8 * rows * width),
        name="norm_back",
    )(at, total, rows_in, cot, gain)


def final_kernel(parts, levels, *refs):
    full, rest, out_ref = refs[:2], refs[2:-1], refs[-1]
    base = full[0][...].astype(f32) + full[1][...].astype(f32)
    for part in range(parts):
        @pl.when(pl.program_id(0) == part)
        def _():
            total = base
            for ref in rest[part * levels : (part + 1) * levels]:
                total += ref[...].astype(f32)
            out_ref[...] = total


def final(full, sums, block):
    parts, levels = len(sums), len(sums[0])
    width = full[0].shape[1]
    wide = width // parts
    piece = pl.BlockSpec((block, wide), lambda i: (0, i))
    held = pl.BlockSpec((block, wide), lambda i: (0, 0))
    return pl.pallas_call(
        functools.partial(final_kernel, parts, levels),
        grid=(parts,),
        in_specs=[piece, piece] + [held] * (parts * levels),
        out_specs=piece,
        out_shape=shape((block, width), f32),
        compiler_params=params(32),
        cost_estimate=cost(4 * block * width, 12 * block * width),
        name="final",
    )(*full, *[f for s in sums for f in s])


def finish_kernel(blocks, at_ref, sum_ref, rows_ref, bias_a_ref, bias_b_ref, out_ref, held):
    rows, width = rows_ref.shape
    wide = width // blocks
    bits = blocks.bit_length() - 1
    for q in range(blocks):
        place = pl.multiple_of(reversed_bits(at_ref[1] ^ q, bits) * wide, wide)
        held[:, q * wide : (q + 1) * wide] = sum_ref[:, pl.ds(place, wide)]
    branch = held[...].astype(f32) + bias_a_ref[...] + bias_b_ref[...]
    position = at_ref[0] * rows + lax.broadcasted_iota(jnp.int32, (rows, 1), 0)
    branch = jnp.where(position < at_ref[2], branch, 0.0)
    out_ref[...] = (rows_ref[...].astype(f32) + branch).astype(bf16)


def finish(branch_sum, rows_in, bias_a, bias_b, at, blocks):
    rows, width = rows_in.shape
    whole = pl.BlockSpec((rows, width), lambda i, n: (0, 0))
    vector = pl.BlockSpec((1, width), lambda i, n: (0, 0))
    return pl.pallas_call(
        functools.partial(finish_kernel, blocks),
        grid_spec=pltpu.PrefetchScalarGridSpec(
            num_scalar_prefetch=1,
            grid=(1,),
            in_specs=[whole, whole, vector, vector],
            out_specs=whole,
            scratch_shapes=[pltpu.VMEM((rows, width), bf16)],
        ),
        out_shape=shape((rows, width), bf16),
        compiler_params=params(32),
        cost_estimate=cost(8 * rows * width, 6 * rows * width),
        name="finish",
    )(at, branch_sum, rows_in, bias_a, bias_b)


def rotary_tables(rows, col_count):
    half_rot = ROT // 2
    column = jnp.arange(col_count) % HEAD_DIM
    exponent = (2 * (column % half_rot)).astype(jnp.float32) / ROT
    frequency = jnp.exp(-math.log(10000.0) * exponent)
    angles = rows.astype(jnp.float32)[:, None] * frequency[None, :]
    inside = column < ROT
    cosine = jnp.where(inside, jnp.cos(angles), 1.0)
    sine_part = jnp.sin(angles)
    ahead_sin = jnp.where(column < half_rot, -sine_part, 0.0)
    behind_sin = jnp.where(inside & (column >= half_rot), sine_part, 0.0)
    return (cosine, ahead_sin, behind_sin)


def flip(array, axis_name, bit):
    size = lax.axis_size(axis_name)
    return lax.ppermute(array, axis_name, [(i, i ^ (1 << bit)) for i in range(size)])


def bits_of(size):
    return size.bit_length() - 1


def swap_blocks(array, index, axis, blocks):
    for bit in range(bits_of(blocks)):
        dims = array.shape
        parts = dims[:axis] + (blocks >> (bit + 1), 2, 1 << bit, dims[axis] // blocks)
        view = array.reshape(parts + dims[axis + 1 :])
        other = jnp.flip(view, axis=axis + 1)
        array = jnp.where((index >> bit) & 1 == 1, other, view).reshape(dims)
    return array


def reversed_bits(value, bits):
    return sum(((value >> k) & 1) << (bits - 1 - k) for k in range(bits))


def xor_columns(array, index, blocks):
    width = array.shape[-1] // blocks
    bits = bits_of(blocks)
    pieces = [
        lax.dynamic_slice_in_dim(
            array, (index ^ reversed_bits(p, bits)) * width, width, array.ndim - 1
        )
        for p in range(blocks)
    ]
    return jnp.concatenate(pieces, -1)


def plain_columns(array, index, blocks):
    width = array.shape[-1] // blocks
    bits = bits_of(blocks)
    pieces = []
    for q in range(blocks):
        place = reversed_bits(index ^ q, bits)
        pieces.append(lax.dynamic_slice_in_dim(array, place * width, width, array.ndim - 1))
    return jnp.concatenate(pieces, -1)


def gather_step(stacks, bit):
    return stacks + [(flip(rows, "dp", bit), [m | (1 << bit) for m in masks]) for rows, masks in stacks]


def gather_plan(stacks, block, bits):
    plan = []
    for which, (_, masks) in enumerate(stacks):
        for i, m in enumerate(masks):
            plan.append((which, i * block, reversed_bits(m, bits) * block, block))
    return [s[0] for s in stacks], tuple(plan)


def core_copies(stacks):
    return [(flip(rows, "dp", 0), [m | 1 for m in masks]) for rows, masks in stacks]


def route_order(last):
    return [b for b in range(bits_of(lax.axis_size("dp")) - 1, -1, -1) if b != last]


def route_first(block, last):
    return jnp.stack([block, flip(block, "dp", route_order(last)[0])], 0)


def route_more(stack, last):
    for bit in route_order(last)[1:]:
        stack = jnp.concatenate([stack, flip(stack, "dp", bit)], 0)
    return stack


def route_last(stack, wanted, index, last):
    order = route_order(last)

    def place(mask):
        return sum(((mask >> bit) & 1) << k for k, bit in enumerate(order))

    mine = wanted[index]
    theirs = wanted[index ^ (1 << last)]
    given = lax.dynamic_index_in_dim(stack, place(index ^ theirs), 0, keepdims=False)
    held = lax.dynamic_index_in_dim(stack, place(index ^ mine), 0, keepdims=False)
    arrived = flip(given, "dp", last)
    return jnp.where(((index ^ mine) >> last) & 1 == 1, arrived, held)


def gather_small(stack, axis_name):
    for bit in range(bits_of(lax.axis_size(axis_name))):
        stack = jnp.concatenate([stack, flip(stack, axis_name, bit)], 0)
    return stack


def scatter_first(blocks, data_index, tensor_index):
    stack = swap_blocks(
        blocks, data_index * lax.axis_size("tensor") + tensor_index, 0, blocks.shape[0]
    )
    half = stack.shape[0] // 2
    return stack[:half], flip(stack[half:], "dp", bits_of(lax.axis_size("dp")) - 1)


def scatter_rest(kept, arrived):
    stack = kept + arrived
    for bit in range(bits_of(lax.axis_size("dp")) - 2, -1, -1):
        half = stack.shape[0] // 2
        stack = stack[:half] + flip(stack[half:], "dp", bit)
    for bit in range(bits_of(lax.axis_size("tensor")) - 1, -1, -1):
        half = stack.shape[0] // 2
        stack = stack[:half] + flip(stack[half:], "tensor", bit)
    return stack[0]


def after(values, *others):
    held = lax.optimization_barrier((tuple(values), tuple(others)))
    return held[0]


def shards(
    hidden_in,
    cotangent,
    lengths,
    slot_of_seq,
    seq_of_slot,
    qkv_weight,
    out_weight,
    fc1_weight,
    fc2_weight,
    ln_gain,
    ln_bias,
    qkv_bias,
    out_bias,
    fc1_bias,
    fc2_bias,
):
    rows_here = hidden_in.shape[1]
    width = hidden_in.shape[2]
    tensor_count = lax.axis_size("tensor")
    data_count = lax.axis_size("dp")
    tensor_index = lax.axis_index("tensor")
    data_index = lax.axis_index("dp")
    seq_len = rows_here * tensor_count
    heads_local = qkv_weight.shape[2]
    hidden_local = fc1_weight.shape[1]
    block = width // data_count
    length = lengths[seq_of_slot[data_index]]
    bits = bits_of(data_count)
    x_first = list(range(1, bits))
    y_first = x_first[::-1]
    tile_f = min(512, hidden_local)

    lasts = (bits - 1, bits - 2)
    wave_rows = rows_here // 2
    at = jnp.stack([tensor_index, data_index, length]).astype(jnp.int32)

    def send(rows):
        half = rows.shape[0] // 2
        return [route_first(h, last) for h, last in zip((rows[:half], rows[half:]), lasts)]

    def receive(firsts, wanted):
        return finish_route([route_more(f, last) for f, last in zip(firsts, lasts)], wanted)

    def finish_route(stacks, wanted):
        return jnp.concatenate(
            [route_last(f, wanted, data_index, last) for f, last in zip(stacks, lasts)], 0
        )

    firsts = send(hidden_in[0])
    vectors = [ln_gain, ln_bias, out_bias, fc2_bias, qkv_bias, fc1_bias]
    s = ln_gain.shape[0]
    vectors = after(vectors, *firsts)
    small = jnp.concatenate([v.reshape(-1, s) for v in vectors], 0)
    stack = gather_small(small[None], "tensor")
    routed = receive(firsts, seq_of_slot)
    routed, stack = after((routed, stack))
    stack = gather_small(stack, "dp")
    gathered = swap_blocks(stack, data_index * tensor_count + tensor_index, 0, stack.shape[0])
    gathered = gathered.reshape(data_count, tensor_count, -1)

    rows_a, rows_b = routed[:wave_rows], routed[wave_rows:]
    full_a = lax.all_gather(rows_a, "tensor", axis=0, tiled=True)
    full_b = lax.all_gather(rows_b, "tensor", axis=0, tiled=True)

    qk_shard = qkv_weight[:, :2].reshape(block, 2 * heads_local)
    vo_shard = jnp.concatenate([qkv_weight[:, 2], out_weight], 1)
    qk_shard, vo_shard = after((qk_shard, vo_shard), routed)
    qk_stacks = gather_step([(qk_shard, [0])], x_first[0])
    vo_stacks = gather_step([(vo_shard, [0])], y_first[0])
    for step in range(1, len(x_first)):
        qk_stacks = gather_step(qk_stacks, x_first[step])
        vo_stacks = gather_step(vo_stacks, y_first[step])

    def held_back(groups, *values):
        flat = [rows for stacks in groups for rows, _ in stacks]
        out = list(after(tuple(flat) + values))
        fresh = [[(out.pop(0), masks) for _, masks in stacks] for stacks in groups]
        return fresh, out

    (qk_stacks, vo_stacks), (fc1_shard, fc2_shard, row_ids) = held_back(
        (qk_stacks, vo_stacks), fc1_weight, fc2_weight, jnp.arange(seq_len, dtype=jnp.int32)
    )
    qk = gather_plan(qk_stacks + core_copies(qk_stacks), block, bits)
    vo = gather_plan(vo_stacks + core_copies(vo_stacks), block, bits)
    fc1_stacks = gather_step([(fc1_shard, [0])], x_first[0])
    fc2_stacks = gather_step([(fc2_shard, [0])], y_first[0])

    positions = tensor_index * rows_here + jnp.arange(rows_here, dtype=jnp.int32)
    valid = (positions < length)[:, None]
    cot_rows = cotangent[0]
    low_plain = jnp.where(valid, cot_rows, jnp.zeros_like(cot_rows))
    low, = after((low_plain,), routed)
    low = xor_columns(low, data_index, data_count)
    grads = lax.all_gather(low, "tensor", axis=0, tiled=True)

    gain, shift, bias_a, bias_b = [
        gathered[:, :, i * s : (i + 1) * s].reshape(1, width).astype(f32) for i in range(4)
    ]
    q = qkv_bias.shape[0]
    bias_qkv = lax.dynamic_slice_in_dim(
        gathered[:, :, 4 * s : 4 * s + q].reshape(3, width), tensor_index * heads_local, heads_local, 1
    ).astype(f32)
    bias_fc1 = lax.dynamic_slice_in_dim(
        gathered[:, :, 4 * s + q :].reshape(1, hidden_local * tensor_count),
        tensor_index * hidden_local,
        hidden_local,
        1,
    ).astype(f32)

    tables = after(rotary_tables(row_ids, PAIR))
    wave_tables = [v.reshape(tensor_count, 2, wave_rows, PAIR) for v in tables]
    size = length.reshape(1)
    ln_a = norm_wave(full_a, tensor_count, at, gain, shift, data_count, 0, None)
    qkv_a, weights = project_first(ln_a, qk, vo, bias_qkv, wave_tables)
    (fc1_stacks, fc2_stacks), (weights,) = held_back((fc1_stacks, fc2_stacks), weights)
    fc1_far, fc2_far = core_copies(fc1_stacks), core_copies(fc2_stacks)
    for step in range(1, len(x_first)):
        fc1_stacks = gather_step(fc1_stacks, x_first[step])
        fc2_stacks = gather_step(fc2_stacks, y_first[step])
    (fc1_far, fc2_far), (full_b,) = held_back((fc1_far, fc2_far), full_b)
    ln = norm_wave(full_b, tensor_count, at, gain, shift, data_count, 1, ln_a)
    qkv = project_second(ln, weights, bias_qkv, wave_tables, qkv_a)
    ln, qkv = ln.reshape(seq_len, width), qkv.reshape(3, seq_len, heads_local)
    mixed, totals = attend(qkv, size)
    (fc1_stacks, fc2_stacks), (mixed,) = held_back((fc1_stacks, fc2_stacks), mixed)
    fc1_far = fc1_far + core_copies(fc1_stacks[2:])
    fc2_far = fc2_far + core_copies(fc2_stacks[2:])
    w1 = gather_plan(fc1_stacks + fc1_far, block, bits)
    w2 = gather_plan(fc2_stacks + fc2_far, block, bits)
    branch, hidden, slope, full1, full2 = feed(ln, mixed, weights, w1, w2, bias_fc1, tile_f)
    branch, grads = after((branch, grads))
    branch = lax.psum_scatter(branch, "tensor", scatter_dimension=0, tiled=True)

    count = data_count // 2
    steps = len(x_first)
    feed_sum, grad_pre, grad_mixed, grad_fc1_b = back(grads, full1, full2, slope, weights, tile_f)
    hidden, = after((hidden,), grad_pre)
    k2, s2 = feed_weight(grads, hidden, tile_f)
    c2 = flip(s2, "dp", 0)
    grad_pre, = after((grad_pre,), s2)
    k1, s1 = feed_weight(ln, grad_pre, tile_f)
    c1 = flip(s1, "dp", 0)

    pair = ((0, 2), (1, 2))
    both = (x_first, y_first)

    def first_gives(full):
        return [give(full, [], count, low, part) for part, low in zip(pair, (False, True))]

    def next_gives(full, sums, step):
        return [give(full, s, count, low, p) for s, low, p in zip(sums, (False, True), pair)]

    def send_on(gives, step):
        return [flip(g, "dp", order[step]) for g, order in zip(gives, both)]

    k2, c2 = after((k2, c2), s1)
    gives2 = first_gives([k2, c2])
    sums2 = [[f] for f in send_on(gives2, 0)]
    k1, c1 = after((k1, c1), *gives2)
    gives1 = first_gives([k1, c1])
    sums1 = [[f] for f in send_on(gives1, 0)]
    grad_mixed, = after((grad_mixed,), *gives1)
    grad_qkv = attend_back(qkv, grad_mixed, totals, size, tables)
    grad_qkv, branch, sums2, sums1 = after((grad_qkv, branch, sums2, sums1))
    ln_part = ln_grad(grad_qkv, weights, feed_sum)
    total = lax.psum_scatter(ln_part, "tensor", scatter_dimension=0, tiled=True)
    mixed, = after((mixed,), ln_part)
    kqk, kvo, sqk, svo, grad_qkv_b = weight_grad(ln, grads, grad_qkv, mixed)
    cq, cv = flip(sqk, "dp", 0), flip(svo, "dp", 0)
    k2, = after((k2,), sqk)
    for step in range(1, steps):
        gives2 = next_gives([k2, c2], sums2, step)
        sums2 = [s + [f] for s, f in zip(sums2, send_on(gives2, step))]
    k1, = after((k1,), *gives2)
    for step in range(1, steps):
        gives1 = next_gives([k1, c1], sums1, step)
        sums1 = [s + [f] for s, f in zip(sums1, send_on(gives1, step))]
    kqk, cq, kvo, cv = after((kqk, cq, kvo, cv), *gives1)
    giveq, givev = give([kqk, cq], [], count, False), give([kvo, cv], [], count, True)
    sumsq, sumsv = [flip(giveq, "dp", x_first[0])], [flip(givev, "dp", y_first[0])]
    branch, = after((branch,), giveq, givev)
    block_out = finish(branch, routed, bias_a, bias_b, at, data_count)[None]
    grad_bias = jnp.sum(low_plain.astype(f32), axis=0)
    devices = data_count * tensor_count
    full_qkv_b = lax.dynamic_update_slice_in_dim(
        jnp.zeros((3, width), f32), grad_qkv_b[:, 0], tensor_index * heads_local, 1
    )
    full_fc1_b = lax.dynamic_update_slice_in_dim(
        jnp.zeros((hidden_local * tensor_count,), f32), grad_fc1_b[0], tensor_index * hidden_local, 0
    )
    known = jnp.concatenate(
        [grad_bias.reshape(devices, s), full_qkv_b.reshape(devices, q), full_fc1_b.reshape(devices, -1)],
        1,
    )
    total, known, sumsq, sumsv, sums2, sums1 = after(
        (total, known, sumsq, sumsv, sums2, sums1), block_out
    )
    slot, grad_gain, grad_shift = norm_back(total, routed, cotangent[0], gain, at, data_count)
    firsts = send(slot)
    kqk, kvo = after((kqk, kvo), slot)
    for step in range(1, steps):
        giveq = give([kqk, cq], sumsq, count, False)
        givev = give([kvo, cv], sumsv, count, True)
        sumsq = sumsq + [flip(giveq, "dp", x_first[step])]
        sumsv = sumsv + [flip(givev, "dp", y_first[step])]
    k2, k1 = after((k2, k1), giveq, givev)
    grad_fc2_w, grad_fc1_w = final([k2, c2], sums2, block), final([k1, c1], sums1, block)
    grad_gain, grad_shift, known, firsts = after(
        (grad_gain, grad_shift, known, firsts), grad_fc2_w, grad_fc1_w
    )
    stacks = [route_more(f, last) for f, last in zip(firsts, lasts)]
    sums = jnp.concatenate(
        [v.reshape(devices, s) for v in (grad_gain[0], grad_shift[0])] + [known], 1
    )
    kept, arrived = scatter_first(sums, data_index, tensor_index)
    stacks, kept, arrived = after((stacks, kept, arrived))
    grad_input = finish_route(stacks, slot_of_seq)[None]
    total = scatter_rest(kept, arrived)
    sumsq, sumsv = after((sumsq, sumsv), *stacks)
    grad_qk_w, grad_vo_w = final([kqk, cq], [sumsq], block), final([kvo, cv], [sumsv], block)
    grad_out_w = grad_vo_w[:, heads_local:]
    grad_qkv_w = jnp.stack(
        [grad_qk_w[:, :heads_local], grad_qk_w[:, heads_local:], grad_vo_w[:, :heads_local]], 1
    )
    return (
        block_out,
        grad_input,
        grad_qkv_w,
        grad_out_w,
        grad_fc1_w,
        grad_fc2_w,
        total[:s],
        total[s : 2 * s],
        total[3 * s : 3 * s + q],
        total[2 * s : 3 * s],
        total[3 * s + q :],
        total[2 * s : 3 * s],
    )


def solution(mesh):
    in_specs = (
        P("dp", "tensor", None),
        P("dp", "tensor", None),
        P(),
        P(),
        P(),
        P("dp", None, "tensor"),
        P("dp", "tensor"),
        P("dp", "tensor"),
        P("dp", "tensor"),
        P(("dp", "tensor")),
        P(("dp", "tensor")),
        P(("dp", "tensor")),
        P(("dp", "tensor")),
        P(("dp", "tensor")),
        P(("dp", "tensor")),
    )
    out_specs = (
        P("dp", "tensor", None),
        P("dp", "tensor", None),
        P("dp", None, "tensor"),
        P("dp", "tensor"),
        P("dp", "tensor"),
        P("dp", "tensor"),
        P(("dp", "tensor")),
        P(("dp", "tensor")),
        P(("dp", "tensor")),
        P(("dp", "tensor")),
        P(("dp", "tensor")),
        P(("dp", "tensor")),
    )
    return jax.shard_map(shards, mesh=mesh, in_specs=in_specs, out_specs=out_specs, check_vma=False)
```

time: 541 us -> 510 us (0.943)
  local copies, waits for them, and re-layouts: 29.6 us -> 22.5 us
  waiting for transfers between devices: 134 us -> 127 us
  other arithmetic: 28 us -> 21.2 us
    unnamed x147 -> x69, local copies, waits for them, and re-layouts: 10.9 us -> 2.78 us
    all_gather x1, waiting for transfers between devices: 18.4 us -> 11.7 us  [shards(): full_b = lax.all_gather(rows_b, 'tensor', axis=0, tiled=True)]
    add x13 -> x5, other arithmetic: 6.61 us -> 0.02 us  [the longest x2 0.01 us: scatter_rest(): stack = stack[:half] + flip(stack[half:], 'tensor', bit)]
    ppermute x68 -> x66, starting transfers between devices: 56.3 us -> 53.1 us  [flip(): lax.ppermute(array, axis_name, [(i, i ^ 1 << bit) for i in range(size)])]
    ppermute x68 -> x66, waiting for transfers between devices: 115 us -> 112 us  [flip(): lax.ppermute(array, axis_name, [(i, i ^ 1 << bit) for i in range(size)])]
    pallas_call x19 -> x25, Pallas kernels: 183 us -> 182 us  [the longest x1 34 us: attend_back(): pl.pallas_call(functools.partial(attend_back_kernel, min(512, rows)), gri...]
  transfers between devices with their start and end apart: 76 -> 71, of which waited for: 34 -> 29; matrix products, arithmetic and copies ran while one was open for 9% -> 7% of each run, Pallas kernels for 47% -> 48%
where the time goes in v4:
time: 510 us; the launch traced here: 506 us
  Pallas kernels  261 us (51%)
  waiting for transfers between devices  127 us (25%)
  starting transfers between devices  53.5 us (10%)
  local copies, waits for them, and re-layouts  22.5 us (4%)
  other arithmetic  21.2 us (4%)
  between operations  20.8 us (4%)
    ppermute x66, waiting for transfers between devices, flip(): lax.ppermute(array, axis_name, [(i, i ^ 1 << bit) for i in range(size)])  112 us
    ppermute x66, starting transfers between devices, flip(): lax.ppermute(array, axis_name, [(i, i ^ 1 << bit) for i in range(size)])  53.1 us
    pallas_call x1, Pallas kernels, feed(): pl.pallas_call(functools.partial(feed_kernel, rows // 2, tile_f, steps, w...  37.7 us
    pallas_call x1, Pallas kernels, attend_back(): pl.pallas_call(functools.partial(attend_back_kernel, min(512, rows)), gri...  34 us
    pallas_call x1, Pallas kernels, back(): pl.pallas_call(functools.partial(back_kernel, min(512, rows)), grid=(unit...  33.7 us
    pallas_call x12, Pallas kernels, give(): pl.pallas_call(give_kernel, grid=(out_count, width // wide), in_specs=[sp...  28.8 us
    pallas_call x2, Pallas kernels, feed_weight(): pl.pallas_call(feed_weight_kernel, grid=(units // tile_f,), in_specs=[pl....  26.3 us
    pallas_call x1, Pallas kernels, attend(): pl.pallas_call(functools.partial(attend_kernel, min(512, rows)), grid_spe...  19.2 us
  transfers between devices with their start and end apart: 71, of which 29 were waited for; matrix products, arithmetic and copies ran while one was open for 7% of the time, Pallas kernels for 48%

profile of v4, /device:TPU:0, one launch (start us, length us, event | category | flops | bytes accessed | tf_op | source)
XLA Modules:
  0.0 505.8 jit_solution(8067327496671745052)
XLA Ops:
  8.6 3.0 collective-permute-start.3
  13.1 10.4 %collective-permute-done.3 = bf16[128,2048]{1,0:T(8,128)(2,1)S(1)} collective-permute-done((bf16[128,2048]{1,0:T(8,128)(2,1)S(1)}, bf16[128,2048]{1,0:T(8,128)(2,1)S(1)}, u32[]{:S(2)}, u32[]{:S(2)}) %collective-permute-start.3) | collective-permute-done | bytes 524320 | tf_op jit(solution)/shard_map/ppermute | solution.py:824
  31.2 2.9 collective-permute-start.7
  40.2 7.9 %collective-permute-done.5 = bf16[128,2048]{1,0:T(8,128)(2,1)S(1)} collective-permute-done((bf16[128,2048]{1,0:T(8,128)(2,1)S(1)}, bf16[128,2048]{1,0:T(8,128)(2,1)S(1)}, u32[]{:S(2)}, u32[]{:S(2)}) %collective-permute-start.5) | collective-permute-done | bytes 524320 | tf_op jit(solution)/shard_map/ppermute | solution.py:824
  48.2 2.7 collective-permute-done.2
  63.6 9.1 %collective-permute-done.8.rest_1_ = bf16[256,1024]{1,0:T(8,128)(2,1)S(1)} collective-permute-done((bf16[256,1024]{1,0:T(8,128)(2,1)S(1)}, bf16[256,1024]{1,0:T(8,128)(2,1)S(1)}, u32[]{:S(2)}, u32[]{:S(2)}) %collective-permute-start.8) | collective-permute-done | bytes 524320 | tf_op jit(solution)/shard_map/ppermute | solution.py:824
  76.3 16.0 %collective-permute-done.17 = bf16[8,11,64]{2,1,0:T(8,128)(2,1)S(1)} collective-permute-done((bf16[8,11,64]{2,1,0:T(8,128)(2,1)S(1)}, bf16[8,11,64]{2,1,0:T(8,128)(2,1)S(1)}, u32[]{:S(2)}, u32[]{:S(2)}) %collective-permute-start.17) | collective-permute-done | bytes 11296 | tf_op jit(solution)/shard_map/ppermute | solution.py:824
  104.8 3.2 fusion
  108.0 5.4 %norm_wave.2.ln_ref.rest_0_ = bf16[4,2,128,2048]{3,2,1,0:T(8,128)(2,1)} custom-call(s32[3]{0:T(128)} %pad_add_fusion.at_ref, bf16[512,2048]{1,0:T(8,128)(2,1)} %all-gather.4.cloned.1.call-done.x_ref, f32[1,2048]{1,0:T(1,128)} %reshape.204.gain_ref, f32[1,2048]{1,0:T(1,128)} %reshape.205.shift_ref), custom_call_target="tpu_custom_call" | custom-call | flops 4194304 | bytes 1677721 | tf_op jit(solution)/shard_map/norm_wave/pallas_call | solution.py:85
  113.5 12.5 %project_first.1 = (bf16[3,4,2,128,512]{4,3,2,1,0:T(8,128)(2,1)}, bf16[4,2048,512]{2,1,0:T(8,128)(2,1)}) custom-call(bf16[4,2,128,2048]{3,2,1,0:T(8,128)(2,1)} %norm_wave.2.ln_ref.rest_0_, f32[3,1,512]{2,1,0:T(1,128)} %reshape.206.bias_ref, f32[4,2,128,128]{3,2,1,0:T(8,128)} %bitcast.100, f32[4,2,128,128]{3,2,1,0:T(8,128)} %bitcast.98, ...), custom_call_target="tpu_custom_call" | custom-call | flops 1288490240 | bytes 9227468 | tf_op jit(solution)/shard_map/project_first/pallas_call | solution.py:187
  132.7 11.7 %all-gather.6.cloned.1.call-done.x_ref = bf16[512,2048]{1,0:T(8,128)(2,1)} async-done(((bf16[128,2048]{1,0:T(8,128)(2,1)}), bf16[512,2048]{1,0:T(8,128)(2,1)}) %all-gather.6.cloned.1.call-update) | async-done | bytes 2097168 | tf_op jit(solution)/shard_map/all_gather | solution.py:1004
  144.4 5.3 %norm_wave.3.ln_ref = bf16[4,2,128,2048]{3,2,1,0:T(8,128)(2,1)} custom-call(s32[3]{0:T(128)} %pad_add_fusion.at_ref, bf16[512,2048]{1,0:T(8,128)(2,1)} %all-gather.6.cloned.1.call-done.x_ref, f32[1,2048]{1,0:T(1,128)} %reshape.204.gain_ref, f32[1,2048]{1,0:T(1,128)} %reshape.205.shift_ref, ...), custom_call_target="tpu_custom_call", output_to_operand_aliasing={{}: (4, {})} | custom-call | flops 4194304 | bytes 1677721 | tf_op jit(solution)/shard_map/norm_wave/pallas_call | solution.py:85
  149.8 8.6 %project_second.1 = bf16[3,4,2,128,512]{4,3,2,1,0:T(8,128)(2,1)} custom-call(bf16[4,2,128,2048]{3,2,1,0:T(8,128)(2,1)} %norm_wave.3.ln_ref, bf16[4,2048,512]{2,1,0:T(8,128)(2,1)} %get-tuple-element.163.w_ref.wo_ref, f32[3,1,512]{2,1,0:T(1,128)} %reshape.206.bias_ref, f32[4,2,128,128]{3,2,1,0:T(8,128)} %bitcast.101, ...), custom_call_target="tpu_custom_call", output_to_operand_aliasing={{}: (6, {})} | custom-call | flops 1288490240 | bytes 5033164 | tf_op jit(solution)/shard_map/project_second/pallas_call | solution.py:222
  158.3 19.2 %attend.1 = (bf16[1024,512]{1,0:T(8,128)(2,1)}, f32[8,1,1024]{2,1,0:T(1,128)}) custom-call(s32[1]{0:T(128)} %dynamic_slice.80.len_ref, bf16[3,1024,512]{2,1,0:T(8,128)(2,1)} %bitcast.103, bf16[3,1024,512]{2,1,0:T(8,128)(2,1)} %bitcast.104, bf16[3,1024,512]{2,1,0:T(8,128)(2,1)} %bitcast.105), custom_call_target="tpu_custom_call" | custom-call | flops 3435973888 | bytes 1677721 | tf_op jit(solution)/shard_map/attend/pallas_call | solution.py:288
  186.3 37.7 %feed.1 = (bf16[1024,2048]{1,0:T(8,128)(2,1)}, bf16[1024,2048]{1,0:T(8,128)(2,1)}, f32[1024,2048]{1,0:T(8,128)}, bf16[2048,2048]{1,0:T(8,128)(2,1)}, bf16[2048,2048]{1,0:T(8,128)(2,1)}) custom-call(bf16[1024,2048]{1,0:T(8,128)(2,1)} %bitcast.93, bf16[1024,512]{1,0:T(8,128)(2,1)} %get-tuple-element.204.mixed_ref, ...), custom_call_target="tpu_custom_call" | custom-call | flops 6871947776 | bytes 23488102 | tf_op jit(solution)/shard_map/feed/pallas_call | solution.py:482
  226.1 33.7 %back.1 = (f32[1024,2048]{1,0:T(8,128)}, bf16[1024,2048]{1,0:T(8,128)(2,1)}, bf16[1024,512]{1,0:T(8,128)(2,1)}, f32[1,2048]{1,0:T(1,128)}) custom-call(bf16[1024,2048]{1,0:T(8,128)(2,1)} %all-gather.8.cloned.1.call-done.g_ref.left_ref, bf16[2048,2048]{1,0:T(8,128)(2,1)} %get-tuple-element.182.w1_ref, bf16[2048,2048]{1,0:T(8,128)(2,1)} %get-tuple-element.183.w2_ref, ...), custom_call_target="tpu_custom_call" | custom-call | flops 6871947776 | bytes 16777216 | tf_op jit(solution)/shard_map/back/pallas_call | solution.py:547
  259.7 13.1 %feed_weight.2 = (bf16[1024,2048]{1,0:T(8,128)(2,1)}, bf16[1024,2048]{1,0:T(8,128)(2,1)}) custom-call(bf16[1024,2048]{1,0:T(8,128)(2,1)} %all-gather.8.cloned.1.call-done.g_ref.left_ref, bf16[1024,2048]{1,0:T(8,128)(2,1)} %get-tuple-element.188.right_ref), custom_call_target="tpu_custom_call" | custom-call | flops 3435973888 | bytes 6710886 | tf_op jit(solution)/shard_map/feed_weight/pallas_call | solution.py:585
  272.9 13.1 %feed_weight.3 = (bf16[1024,2048]{1,0:T(8,128)(2,1)}, bf16[1024,2048]{1,0:T(8,128)(2,1)}) custom-call(bf16[1024,2048]{1,0:T(8,128)(2,1)} %bitcast.94, bf16[1024,2048]{1,0:T(8,128)(2,1)} %get-tuple-element.190.right_ref), custom_call_target="tpu_custom_call" | custom-call | flops 3435973888 | bytes 6710886 | tf_op jit(solution)/shard_map/feed_weight/pallas_call | solution.py:585
  297.5 2.5 give.15
  301.5 34.0 %attend_back.1.grad_ref = bf16[3,1024,512]{2,1,0:T(8,128)(2,1)} custom-call(s32[1]{0:T(128)} %dynamic_slice.80.len_ref, bf16[3,1024,512]{2,1,0:T(8,128)(2,1)} %bitcast.106, bf16[3,1024,512]{2,1,0:T(8,128)(2,1)} %bitcast.107, bf16[3,1024,512]{2,1,0:T(8,128)(2,1)} %bitcast.108, bf16[1024,512]{1,0:T(8,128)(2,1)} %get-tuple-element.198.do_ref, ...), custom_call_target="tpu_custom_call" | custom-call | flops 8589934592 | bytes 3355443 | tf_op jit(solution)/shard_map/attend_back/pallas_call | solution.py:363
  335.5 3.7 collective-permute-done.43.refs_2_
  340.5 12.8 %ln_grad.1 = bf16[1024,2048]{1,0:T(8,128)(2,1)} custom-call(bf16[3,1024,512]{2,1,0:T(8,128)(2,1)} %attend_back.1.grad_ref, bf16[4,2048,512]{2,1,0:T(8,128)(2,1)} %get-tuple-element.163.w_ref.wo_ref, f32[1024,2048]{1,0:T(8,128)} %get-tuple-element.203.sum_ref), custom_call_target="tpu_custom_call" | custom-call | flops 2576980480 | bytes 9227468 | tf_op jit(solution)/shard_map/ln_grad/pallas_call | solution.py:611
  353.2 15.0 %weight_grad.1 = (bf16[1024,1024]{1,0:T(8,128)(2,1)}, bf16[1024,1024]{1,0:T(8,128)(2,1)}, bf16[1024,1024]{1,0:T(8,128)(2,1)}, bf16[1024,1024]{1,0:T(8,128)(2,1)}, f32[3,1,512]{2,1,0:T(1,128)}) custom-call(bf16[1024,2048]{1,0:T(8,128)(2,1)} %bitcast.95, bf16[1024,2048]{1,0:T(8,128)(2,1)} %all-gather.8.cloned.1.call-done.g_ref.left_ref, ...), custom_call_target="tpu_custom_call" | custom-call | flops 3435973888 | bytes 8388608 | tf_op jit(solution)/shard_map/weight_grad/pallas_call | solution.py:654
  391.5 3.7 finish.1
  395.2 24.7 %collective-permute-done.50.refs_5_ = bf16[256,1024]{1,0:T(8,128)(2,1)} collective-permute-done((bf16[256,1024]{1,0:T(8,128)(2,1)}, bf16[256,1024]{1,0:T(8,128)(2,1)}, u32[]{:S(2)}, u32[]{:S(2)}) %collective-permute-start.50) | collective-permute-done | bytes 524320 | tf_op jit(solution)/shard_map/ppermute | solution.py:824
  421.5 8.4 %collective-permute-done.52.refs_5_ = bf16[256,1024]{1,0:T(8,128)(2,1)} collective-permute-done((bf16[256,1024]{1,0:T(8,128)(2,1)S(1)}, bf16[256,1024]{1,0:T(8,128)(2,1)}, u32[]{:S(2)}, u32[]{:S(2)}) %collective-permute-start.52) | collective-permute-done | bytes 524320 | tf_op jit(solution)/shard_map/ppermute | solution.py:824
  429.9 5.4 %norm_back.1 = (bf16[256,2048]{1,0:T(8,128)(2,1)}, f32[1,2048]{1,0:T(1,128)}, f32[1,2048]{1,0:T(1,128)}) custom-call(s32[3]{0:T(128)} %pad_add_fusion.at_ref, bf16[256,2048]{1,0:T(8,128)(2,1)} %reduce-scatter.5.cloned.1.call-done.sum_ref, bf16[256,2048]{1,0:T(8,128)(2,1)} %copy-done, bf16[256,2048]{1,0:T(8,128)(2,1)} %bitcast.102, f32[1,2048]{1,0:T(1,128)} %reshape.204.gain_ref), custom_call_target="tpu_custom_call" | custom-call | flops 4194304 | bytes 1677721 | tf_op jit(solution)/shard_map/norm_back/pallas_call | solution.py:729
  448.5 3.6 final.4
  452.1 3.6 final.5
  470.2 2.7 final.6
  472.9 7.2 %collective-permute-done.62 = f32[8,640]{1,0:T(8,128)S(1)} collective-permute-done((f32[8,640]{1,0:T(8,128)S(1)}, f32[8,640]{1,0:T(8,128)S(1)}, u32[]{:S(2)}, u32[]{:S(2)}) %collective-permute-start.62) | collective-permute-done | bytes 20512 | tf_op jit(solution)/shard_map/ppermute | solution.py:824
  482.3 2.7 final.7
  (315 shorter events, 139.3 us)
Async XLA Ops:
  7.2 100.9 %all-gather.4.cloned.1.call-start = ((), (), s32[]{:S(2)}) async-start(), calls=%async_computation.2 | async-start | bytes 2621440 | tf_op jit(solution)/shard_map/all_gather | solution.py:1003
  53.2 91.2 %all-gather.6.cloned.1.call-start = ((), (), s32[]{:S(2)}) async-start(), calls=%async_computation.3 | async-start | bytes 2621440 | tf_op jit(solution)/shard_map/all_gather | solution.py:1004
  53.9 172.1 %all-gather.8.cloned.1.call-start = ((), (), s32[]{:S(2)}) async-start(), calls=%async_computation.4 | async-start | bytes 5242880 | tf_op jit(solution)/shard_map/all_gather | solution.py:1035
  61.2 279.3 %reduce-scatter.3.cloned.1.call-start = ((), (), s32[]{:S(2)}) async-start(), calls=%async_computation.5 | async-start | bytes 5242880 | tf_op jit(solution)/shard_map/reduce_scatter | solution.py:1073
  61.5 35.3 %collective-permute-start.9 = (bf16[256,1024]{1,0:T(8,128)(2,1)S(1)}, bf16[256,1024]{1,0:T(8,128)(2,1)S(1)}, u32[]{:S(2)}, u32[]{:S(2)}) collective-permute-start(bf16[256,1024]{1,0:T(8,128)(2,1)S(1)} %bitcast.110), channel_id=1, source_target_pairs={{0,16},{4,20},{8,24},{12,28},{16,0},{20,4},{24,8},{28,12},{1,17},{... | collective-permute-start | bytes 1572872 | tf_op jit(solution)/shard_map/ppermute | solution.py:824
  62.1 34.7 %collective-permute-start.12 = (bf16[256,1024]{1,0:T(8,128)(2,1)S(1)}, bf16[256,1024]{1,0:T(8,128)(2,1)}, u32[]{:S(2)}, u32[]{:S(2)}) collective-permute-start(bf16[256,1024]{1,0:T(8,128)(2,1)S(1)} %pad_maximum_fusion.10.rest_8_), channel_id=1, source_target_pairs={{0,8},{4,12},{8,0},{12,4},{16,24},{20,28},{24,16},{28,20},{1,9},{5... | collective-permute-start | bytes 1572872 | tf_op jit(solution)/shard_map/ppermute | solution.py:824
  72.8 24.1 %collective-permute-start.10 = (bf16[256,1024]{1,0:T(8,128)(2,1)S(1)}, bf16[256,1024]{1,0:T(8,128)(2,1)S(1)}, u32[]{:S(2)}, u32[]{:S(2)}) collective-permute-start(bf16[256,1024]{1,0:T(8,128)(2,1)S(1)} %collective-permute-done.8.rest_1_), channel_id=1, source_target_pairs={{0,16},{4,20},{8,24},{12,28},{16,0},{20,4},{24,8},{28,12},{1,17},{... | collective-permute-start | bytes 1572872 | tf_op jit(solution)/shard_map/ppermute | solution.py:824
  74.2 22.6 %collective-permute-start.13 = (bf16[256,1024]{1,0:T(8,128)(2,1)}, bf16[256,1024]{1,0:T(8,128)(2,1)}, u32[]{:S(2)}, u32[]{:S(2)}) collective-permute-start(bf16[256,1024]{1,0:T(8,128)(2,1)} %collective-permute-done.11.rest_9_), channel_id=1, source_target_pairs={{0,8},{4,12},{8,0},{12,4},{16,24},{20,28},{24,16},{28,20},{1,9},{5... | collective-permute-start | bytes 1572872 | tf_op jit(solution)/shard_map/ppermute | solution.py:824
  74.9 17.5 %collective-permute-start.17 = (bf16[8,11,64]{2,1,0:T(8,128)(2,1)S(1)}, bf16[8,11,64]{2,1,0:T(8,128)(2,1)S(1)}, u32[]{:S(2)}, u32[]{:S(2)}) collective-permute-start(bf16[8,11,64]{2,1,0:T(8,128)(2,1)S(1)} %pad_maximum_fusion.15), channel_id=1, source_target_pairs={{0,8},{4,12},{8,0},{12,4},{16,24},{20,28},{24,16},{28,20},{1,9},{5... | collective-permute-start | bytes 33800 | tf_op jit(solution)/shard_map/ppermute | solution.py:824
  98.8 27.1 %collective-permute-start.14 = (bf16[256,2048]{1,0:T(8,128)(2,1)}, bf16[256,2048]{1,0:T(8,128)(2,1)}, u32[]{:S(2)}, u32[]{:S(2)}) collective-permute-start(bf16[256,2048]{1,0:T(8,128)(2,1)} %rest_0_), channel_id=1, source_target_pairs={{0,8},{4,12},{8,0},{12,4},{16,24},{20,28},{24,16},{28,20},{1,9},{5... | collective-permute-start | bytes 3145736 | tf_op jit(solution)/shard_map/ppermute | solution.py:824
  100.3 25.7 %collective-permute-start.15 = (bf16[256,2048]{1,0:T(8,128)(2,1)}, bf16[256,2048]{1,0:T(8,128)(2,1)}, u32[]{:S(2)}, u32[]{:S(2)}) collective-permute-start(bf16[256,2048]{1,0:T(8,128)(2,1)} %rest_8_), channel_id=1, source_target_pairs={{0,16},{4,20},{8,24},{12,28},{16,0},{20,4},{24,8},{28,12},{1,17},{... | collective-permute-start | bytes 3145736 | tf_op jit(solution)/shard_map/ppermute | solution.py:824
  127.0 17.5 %collective-permute-start.30 = (bf16[256,2048]{1,0:T(8,128)(2,1)}, bf16[256,2048]{1,0:T(8,128)(2,1)}, u32[]{:S(2)}, u32[]{:S(2)}) collective-permute-start(bf16[256,2048]{1,0:T(8,128)(2,1)} %collective-permute-done.15.rest_9_), channel_id=1, source_target_pairs={{0,4},{4,0},{8,12},{12,8},{16,20},{20,16},{24,28},{28,24},{1,5},{5... | collective-permute-start | bytes 3145736 | tf_op jit(solution)/shard_map/ppermute | solution.py:824
  127.1 50.5 %collective-permute-start.31 = (bf16[256,2048]{1,0:T(8,128)(2,1)}, bf16[256,2048]{1,0:T(8,128)(2,1)}, u32[]{:S(2)}, u32[]{:S(2)}) collective-permute-start(bf16[256,2048]{1,0:T(8,128)(2,1)} %rest_0_), channel_id=1, source_target_pairs={{0,16},{4,20},{8,24},{12,28},{16,0},{20,4},{24,8},{28,12},{1,17},{... | collective-permute-start | bytes 3145736 | tf_op jit(solution)/shard_map/ppermute | solution.py:824
  129.1 48.5 %collective-permute-start.32 = (bf16[256,2048]{1,0:T(8,128)(2,1)}, bf16[256,2048]{1,0:T(8,128)(2,1)}, u32[]{:S(2)}, u32[]{:S(2)}) collective-permute-start(bf16[256,2048]{1,0:T(8,128)(2,1)} %collective-permute-done.14.rest_1_), channel_id=1, source_target_pairs={{0,16},{4,20},{8,24},{12,28},{16,0},{20,4},{24,8},{28,12},{1,17},{... | collective-permute-start | bytes 3145736 | tf_op jit(solution)/shard_map/ppermute | solution.py:824
  130.6 47.0 %collective-permute-start.33 = (bf16[256,2048]{1,0:T(8,128)(2,1)}, bf16[256,2048]{1,0:T(8,128)(2,1)}, u32[]{:S(2)}, u32[]{:S(2)}) collective-permute-start(bf16[256,2048]{1,0:T(8,128)(2,1)} %rest_8_), channel_id=1, source_target_pairs={{0,8},{4,12},{8,0},{12,4},{16,24},{20,28},{24,16},{28,20},{1,9},{5... | collective-permute-start | bytes 3145736 | tf_op jit(solution)/shard_map/ppermute | solution.py:824
  132.1 46.7 %collective-permute-start.34 = (bf16[256,2048]{1,0:T(8,128)(2,1)}, bf16[256,2048]{1,0:T(8,128)(2,1)}, u32[]{:S(2)}, u32[]{:S(2)}) collective-permute-start(bf16[256,2048]{1,0:T(8,128)(2,1)} %collective-permute-done.15.rest_9_), channel_id=1, source_target_pairs={{0,8},{4,12},{8,0},{12,4},{16,24},{20,28},{24,16},{28,20},{1,9},{5... | collective-permute-start | bytes 3145736 | tf_op jit(solution)/shard_map/ppermute | solution.py:824
  226.0 203.9 %reduce-scatter.5.cloned.1.call-start = ((), (), s32[]{:S(2)}) async-start(), calls=%async_computation.6 | async-start | bytes 5242880 | tf_op jit(solution)/shard_map/reduce_scatter | solution.py:1107
  291.4 44.1 %collective-permute-start.41 = (bf16[512,1024]{1,0:T(8,128)(2,1)}, bf16[512,1024]{1,0:T(8,128)(2,1)}, u32[]{:S(2)}, u32[]{:S(2)}) collective-permute-start(bf16[512,1024]{1,0:T(8,128)(2,1)} %give.12), channel_id=1, source_target_pairs={{0,8},{4,12},{8,0},{12,4},{16,24},{20,28},{24,16},{28,20},{1,9},{5... | collective-permute-start | bytes 3145736 | tf_op jit(solution)/shard_map/ppermute | solution.py:824
  292.8 42.7 %collective-permute-start.42 = (bf16[512,1024]{1,0:T(8,128)(2,1)}, bf16[512,1024]{1,0:T(8,128)(2,1)}, u32[]{:S(2)}, u32[]{:S(2)}) collective-permute-start(bf16[512,1024]{1,0:T(8,128)(2,1)} %give.13), channel_id=1, source_target_pairs={{0,16},{4,20},{8,24},{12,28},{16,0},{20,4},{24,8},{28,12},{1,17},{... | collective-permute-start | bytes 3145736 | tf_op jit(solution)/shard_map/ppermute | solution.py:824
  296.7 42.5 %collective-permute-start.43 = (bf16[512,1024]{1,0:T(8,128)(2,1)}, bf16[512,1024]{1,0:T(8,128)(2,1)}, u32[]{:S(2)}, u32[]{:S(2)}) collective-permute-start(bf16[512,1024]{1,0:T(8,128)(2,1)} %give.14), channel_id=1, source_target_pairs={{0,8},{4,12},{8,0},{12,4},{16,24},{20,28},{24,16},{28,20},{1,9},{5... | collective-permute-start | bytes 3145736 | tf_op jit(solution)/shard_map/ppermute | solution.py:824
  300.0 40.5 %collective-permute-start.44 = (bf16[512,1024]{1,0:T(8,128)(2,1)}, bf16[512,1024]{1,0:T(8,128)(2,1)}, u32[]{:S(2)}, u32[]{:S(2)}) collective-permute-start(bf16[512,1024]{1,0:T(8,128)(2,1)} %give.15), channel_id=1, source_target_pairs={{0,16},{4,20},{8,24},{12,28},{16,0},{20,4},{24,8},{28,12},{1,17},{... | collective-permute-start | bytes 3145736 | tf_op jit(solution)/shard_map/ppermute | solution.py:824
  382.2 47.7 %collective-permute-start.47 = (bf16[512,1024]{1,0:T(8,128)(2,1)}, bf16[512,1024]{1,0:T(8,128)(2,1)}, u32[]{:S(2)}, u32[]{:S(2)}) collective-permute-start(bf16[512,1024]{1,0:T(8,128)(2,1)} %give.20), channel_id=1, source_target_pairs={{0,8},{4,12},{8,0},{12,4},{16,24},{20,28},{24,16},{28,20},{1,9},{5... | collective-permute-start | bytes 3145736 | tf_op jit(solution)/shard_map/ppermute | solution.py:824
  385.3 44.7 %collective-permute-start.48 = (bf16[512,1024]{1,0:T(8,128)(2,1)}, bf16[512,1024]{1,0:T(8,128)(2,1)}, u32[]{:S(2)}, u32[]{:S(2)}) collective-permute-start(bf16[512,1024]{1,0:T(8,128)(2,1)} %give.21), channel_id=1, source_target_pairs={{0,16},{4,20},{8,24},{12,28},{16,0},{20,4},{24,8},{28,12},{1,17},{... | collective-permute-start | bytes 3145736 | tf_op jit(solution)/shard_map/ppermute | solution.py:824
  385.7 34.2 %collective-permute-start.50 = (bf16[256,1024]{1,0:T(8,128)(2,1)}, bf16[256,1024]{1,0:T(8,128)(2,1)}, u32[]{:S(2)}, u32[]{:S(2)}) collective-permute-start(bf16[256,1024]{1,0:T(8,128)(2,1)} %give.17), channel_id=1, source_target_pairs={{0,8},{4,12},{8,0},{12,4},{16,24},{20,28},{24,16},{28,20},{1,9},{5... | collective-permute-start | bytes 1572872 | tf_op jit(solution)/shard_map/ppermute | solution.py:824
  387.3 34.2 %collective-permute-start.51 = (bf16[256,1024]{1,0:T(8,128)(2,1)}, bf16[256,1024]{1,0:T(8,128)(2,1)}, u32[]{:S(2)}, u32[]{:S(2)}) collective-permute-start(bf16[256,1024]{1,0:T(8,128)(2,1)} %give.18), channel_id=1, source_target_pairs={{0,16},{4,20},{8,24},{12,28},{16,0},{20,4},{24,8},{28,12},{1,17},{... | collective-permute-start | bytes 1572872 | tf_op jit(solution)/shard_map/ppermute | solution.py:824
  388.8 41.1 %collective-permute-start.52 = (bf16[256,1024]{1,0:T(8,128)(2,1)S(1)}, bf16[256,1024]{1,0:T(8,128)(2,1)}, u32[]{:S(2)}, u32[]{:S(2)}) collective-permute-start(bf16[256,1024]{1,0:T(8,128)(2,1)S(1)} %copy-done.14), channel_id=1, source_target_pairs={{0,8},{4,12},{8,0},{12,4},{16,24},{20,28},{24,16},{28,20},{1,9},{5... | collective-permute-start | bytes 1572872 | tf_op jit(solution)/shard_map/ppermute | solution.py:824
  437.8 17.8 %collective-permute-start.53 = (bf16[128,2048]{1,0:T(8,128)(2,1)}, bf16[128,2048]{1,0:T(8,128)(2,1)}, u32[]{:S(2)}, u32[]{:S(2)}) collective-permute-start(bf16[128,2048]{1,0:T(8,128)(2,1)} %get-tuple-element.263), channel_id=1, source_target_pairs={{0,8},{4,12},{8,0},{12,4},{16,24},{20,28},{24,16},{28,20},{1,9},{5... | collective-permute-start | bytes 1572872 | tf_op jit(solution)/shard_map/ppermute | solution.py:824
  438.4 18.6 %collective-permute-start.54 = (bf16[128,2048]{1,0:T(8,128)(2,1)}, bf16[128,2048]{1,0:T(8,128)(2,1)}, u32[]{:S(2)}, u32[]{:S(2)}) collective-permute-start(bf16[128,2048]{1,0:T(8,128)(2,1)} %get-tuple-element.262), channel_id=1, source_target_pairs={{0,16},{4,20},{8,24},{12,28},{16,0},{20,4},{24,8},{28,12},{1,17},{... | collective-permute-start | bytes 1572872 | tf_op jit(solution)/shard_map/ppermute | solution.py:824
  443.2 27.1 %collective-permute-start.60 = (bf16[256,1024]{1,0:T(8,128)(2,1)}, bf16[256,1024]{1,0:T(8,128)(2,1)}, u32[]{:S(2)}, u32[]{:S(2)}) collective-permute-start(bf16[256,1024]{1,0:T(8,128)(2,1)} %give.22), channel_id=1, source_target_pairs={{0,16},{4,20},{8,24},{12,28},{16,0},{20,4},{24,8},{28,12},{1,17},{... | collective-permute-start | bytes 1572872 | tf_op jit(solution)/shard_map/ppermute | solution.py:824
  447.1 23.1 %collective-permute-start.61 = (bf16[256,1024]{1,0:T(8,128)(2,1)}, bf16[256,1024]{1,0:T(8,128)(2,1)}, u32[]{:S(2)}, u32[]{:S(2)}) collective-permute-start(bf16[256,1024]{1,0:T(8,128)(2,1)} %give.23), channel_id=1, source_target_pairs={{0,8},{4,12},{8,0},{12,4},{16,24},{20,28},{24,16},{28,20},{1,9},{5... | collective-permute-start | bytes 1572872 | tf_op jit(solution)/shard_map/ppermute | solution.py:824
  466.5 28.6 %collective-permute-start.59 = (bf16[128,2048]{1,0:T(8,128)(2,1)}, bf16[128,2048]{1,0:T(8,128)(2,1)}, u32[]{:S(2)}, u32[]{:S(2)}) collective-permute-start(bf16[128,2048]{1,0:T(8,128)(2,1)} %dynamic-slice_bitcast_fusion), channel_id=1, source_target_pairs={{0,8},{4,12},{8,0},{12,4},{16,24},{20,28},{24,16},{28,20},{1,9},{5... | collective-permute-start | bytes 1572872 | tf_op jit(solution)/shard_map/ppermute | solution.py:824
  469.4 26.8 %collective-permute-start.58 = (bf16[128,2048]{1,0:T(8,128)(2,1)}, bf16[128,2048]{1,0:T(8,128)(2,1)}, u32[]{:S(2)}, u32[]{:S(2)}) collective-permute-start(bf16[128,2048]{1,0:T(8,128)(2,1)} %dynamic-slice_bitcast_fusion.1), channel_id=1, source_target_pairs={{0,16},{4,20},{8,24},{12,28},{16,0},{20,4},{24,8},{28,12},{1,17},{... | collective-permute-start | bytes 1572872 | tf_op jit(solution)/shard_map/ppermute | solution.py:824
  (69 other events, 554.9 us)
Sparse Core Ops, SparseCore 0:
  53.3 44.1 all-gather.3
  99.7 44.7 all-gather.5
  146.6 79.3 all-gather.7
  228.1 75.2 reduce-scatter.2
  353.4 74.3 reduce-scatter.4

commit v5 on v4

--- a/solution.py
+++ b/solution.py
@@ -240,9 +240,9 @@
     )(ln, weights, bias[:, None, :], *tables, held)
 
 
-def head_lanes(head):
+def side_lanes(side):
     lane = lax.broadcasted_iota(jnp.int32, (1, PAIR), 1)
-    return (lane // HEAD_DIM) == (head % 2)
+    return (lane // HEAD_DIM) == side
 
 
 def masked_scores(keys, queries, first, length):
@@ -253,142 +253,100 @@
 
 
 def attend_kernel(block, len_ref, q_ref, k_ref, v_ref, out_ref, total_ref, q_mine, v_turned):
-    head = pl.program_id(0)
-    lanes = head_lanes(head)
     rows = q_ref.shape[1]
     zero = jnp.zeros((rows, PAIR), bf16)
     scale = jnp.asarray(1.0 / math.sqrt(HEAD_DIM), bf16)
-    q_mine[...] = jnp.where(lanes, q_ref[0] * scale, zero)
-    v_turned[...] = jnp.where(lanes, v_ref[0], zero).T
     length = len_ref[0]
+    for side in range(2):
+        lanes = side_lanes(side)
+        q_mine[side] = jnp.where(lanes, q_ref[0] * scale, zero)
+    v_turned[...] = v_ref[0].T
     for first in range(0, rows, block):
         n = first + block
         r = slice(first, n)
-        scores = masked_scores(k_ref[0, :n, :], q_mine[r, :], first, length)
-        top = jnp.max(scores, 0, keepdims=True)
-        exped = jnp.exp(scores - top)
-        total = jnp.sum(exped, 0, keepdims=True)
-        mixed = dot(v_turned[:, :n], exped.astype(bf16), NN) * (1.0 / total)
-        mixed = mixed.T.astype(bf16)
-        total_ref[0, :, r] = top + jnp.log(total)
-
-        @pl.when(head % 2 == 0)
-        def _():
-            out_ref[r, :] = mixed
-
-        @pl.when(head % 2 == 1)
-        def _():
-            out_ref[r, :] = out_ref[r, :] + mixed
-
-
-def attend(qkv, length):
+        mixed = []
+        for side in range(2):
+            scores = masked_scores(k_ref[0, :n, :], q_mine[side, r, :], first, length)
+            top = jnp.max(scores, 0, keepdims=True)
+            exped = jnp.exp(scores - top)
+            total = jnp.sum(exped, 0, keepdims=True)
+            part = v_turned[side*HEAD_DIM:(side+1)*HEAD_DIM, :n]
+            mixed.append(dot(part, exped.astype(bf16), NN) * (1.0 / total))
+            total_ref[0, side:side+1, r] = top + jnp.log(total)
+        out_ref[r, :] = jnp.concatenate(mixed, 0).T.astype(bf16)
+
+
+def attend(qkv, length, block=512):
     _, rows, width = qkv.shape
-    heads = width // HEAD_DIM
-    kind = lambda c: pl.BlockSpec((1, rows, PAIR), lambda h, n: (c, 0, h // 2))
-    return pl.pallas_call(
-        functools.partial(attend_kernel, min(512, rows)),
-        grid_spec=pltpu.PrefetchScalarGridSpec(
-            num_scalar_prefetch=1,
-            grid=(heads,),
+    pairs = width // PAIR
+    kind = lambda c: pl.BlockSpec((1, rows, PAIR), lambda h, n: (c, 0, h))
+    return pl.pallas_call(functools.partial(attend_kernel, min(block, rows)),
+        grid_spec=pltpu.PrefetchScalarGridSpec(num_scalar_prefetch=1, grid=(pairs,),
             in_specs=[kind(0), kind(1), kind(2)],
-            out_specs=[
-                pl.BlockSpec((rows, PAIR), lambda h, n: (0, h // 2)),
-                pl.BlockSpec((1, 1, rows), lambda h, n: (h, 0, 0)),
-            ],
-            scratch_shapes=[pltpu.VMEM((rows, PAIR), bf16), pltpu.VMEM((PAIR, rows), bf16)],
-        ),
-        out_shape=[shape((rows, width), bf16), shape((heads, 1, rows), f32)],
+            out_specs=[pl.BlockSpec((rows, PAIR), lambda h, n: (0, h)), pl.BlockSpec((1, 2, rows), lambda h, n: (h, 0, 0))],
+            scratch_shapes=[pltpu.VMEM((2, rows, PAIR), bf16), pltpu.VMEM((PAIR, rows), bf16)]),
+        out_shape=[shape((rows, width), bf16), shape((pairs, 2, rows), f32)],
         compiler_params=params(48),
-        cost_estimate=cost(16 * rows * rows * width, 4 << 20, rows * rows * heads),
-        name="attend",
-    )(length, qkv, qkv, qkv)
-
-
-def attend_back_kernel(
-    block, len_ref, q_ref, k_ref, v_ref, do_ref, total_ref, c_ref, a_ref, b_ref,
-    grad_ref, q_mine, do_mine, k_turned, key_sum, value_sum,
-):
-    head = pl.program_id(0)
-    lanes = head_lanes(head)
+        cost_estimate=cost(16 * rows * rows * width, 4 << 20, rows * rows * 2 * pairs),
+        name="attend")(length, qkv, qkv, qkv)
+
+
+def attend_back_kernel(block, len_ref, q_ref, k_ref, v_ref, do_ref, total_ref, c_ref, a_ref, b_ref, grad_ref, q_mine, do_mine, k_turned, key_sum, value_sum):
     rows = q_ref.shape[1]
     zero = jnp.zeros((rows, PAIR), bf16)
     scale = 1.0 / math.sqrt(HEAD_DIM)
-    q_mine[...] = jnp.where(lanes, q_ref[0] * jnp.asarray(scale, bf16), zero)
-    do_mine[...] = jnp.where(lanes, do_ref[...], zero)
-    k_turned[...] = jnp.where(lanes, k_ref[0], zero).T
+    for side in range(2):
+        lanes = side_lanes(side)
+        q_mine[side] = jnp.where(lanes, q_ref[0] * jnp.asarray(scale, bf16), zero)
+        do_mine[side] = jnp.where(lanes, do_ref[...], zero)
+    k_turned[...] = k_ref[0].T
     length = len_ref[0]
-
-    def put(kind, r, value):
-        value = value.astype(bf16)
-
-        @pl.when(head % 2 == 0)
-        def _():
-            grad_ref[kind, r, :] = value
-
-        @pl.when(head % 2 == 1)
-        def _():
-            grad_ref[kind, r, :] = grad_ref[kind, r, :] + value
-
     tables_of = lambda r: (c_ref[r, :], a_ref[r, :], b_ref[r, :])
     for first in range(rows - block, -1, -block):
         n = first + block
         r = slice(first, n)
-        scores = masked_scores(k_ref[0, :n, :], q_mine[r, :], first, length)
-        probs = jnp.exp(scores - total_ref[0, :, r])
-        grad_probs = dot(v_ref[0, :n, :], do_mine[r, :], NT)
-        product = probs * grad_probs
-        delta = jnp.sum(product, 0, keepdims=True)
-        grad_scores = (product - probs * delta).astype(bf16)
-        keys = dot(grad_scores, q_mine[r, :], NN)
-        vals = dot(probs.astype(bf16), do_mine[r, :], NN)
+        gk = gv = None
+        gq = []
+        for side in range(2):
+            scores = masked_scores(k_ref[0, :n, :], q_mine[side, r, :], first, length)
+            probs = jnp.exp(scores - total_ref[0, side:side+1, r])
+            grad_probs = dot(v_ref[0, :n, :], do_mine[side, r, :], NT)
+            product = probs * grad_probs
+            delta = jnp.sum(product, 0, keepdims=True)
+            grad_scores = (product - probs * delta).astype(bf16)
+            a = dot(grad_scores, q_mine[side, r, :], NN)
+            b = dot(probs.astype(bf16), do_mine[side, r, :], NN)
+            gk = a if gk is None else gk + a
+            gv = b if gv is None else gv + b
+            gq.append(dot(k_turned[side*HEAD_DIM:(side+1)*HEAD_DIM, :n], grad_scores, NN))
         if n == rows:
-            key_sum[...] = keys
-            value_sum[...] = vals
+            key_sum[...] = gk
+            value_sum[...] = gv
         else:
-            key_sum[:n, :] += keys
-            value_sum[:n, :] += vals
-        grad_query = dot(k_turned[:, :n], grad_scores, NN).T * scale
-        put(0, r, turned_back(grad_query, tables_of(r)))
+            key_sum[:n, :] += gk
+            value_sum[:n, :] += gv
+        grad_query = jnp.concatenate(gq, 0).T * scale
+        grad_ref[0, r, :] = turned_back(grad_query, tables_of(r)).astype(bf16)
     for first in range(0, rows, block):
         r = slice(first, first + block)
-        put(1, r, turned_back(key_sum[r, :], tables_of(r)))
-        put(2, r, value_sum[r, :])
-
-
-def attend_back(qkv, grad_mixed, totals, length, tables):
+        grad_ref[1, r, :] = turned_back(key_sum[r, :], tables_of(r)).astype(bf16)
+        grad_ref[2, r, :] = value_sum[r, :].astype(bf16)
+
+
+def attend_back(qkv, grad_mixed, totals, length, tables, block=512):
     _, rows, width = qkv.shape
-    heads = width // HEAD_DIM
-    kind = lambda c: pl.BlockSpec((1, rows, PAIR), lambda h, n: (c, 0, h // 2))
-    table_spec = pl.BlockSpec((rows, PAIR), lambda h, n: (0, 0))
-    return pl.pallas_call(
-        functools.partial(attend_back_kernel, min(512, rows)),
-        grid_spec=pltpu.PrefetchScalarGridSpec(
-            num_scalar_prefetch=1,
-            grid=(heads,),
-            in_specs=[
-                kind(0),
-                kind(1),
-                kind(2),
-                pl.BlockSpec((rows, PAIR), lambda h, n: (0, h // 2)),
-                pl.BlockSpec((1, 1, rows), lambda h, n: (h, 0, 0)),
-                table_spec,
-                table_spec,
-                table_spec,
-            ],
-            out_specs=pl.BlockSpec((3, rows, PAIR), lambda h, n: (0, 0, h // 2)),
-            scratch_shapes=[
-                pltpu.VMEM((rows, PAIR), bf16),
-                pltpu.VMEM((rows, PAIR), bf16),
-                pltpu.VMEM((PAIR, rows), bf16),
-                pltpu.VMEM((rows, PAIR), f32),
-                pltpu.VMEM((rows, PAIR), f32),
-            ],
-        ),
+    pairs = width // PAIR
+    kind = lambda c: pl.BlockSpec((1, rows, PAIR), lambda h, n: (c, 0, h))
+    table = pl.BlockSpec((rows, PAIR), lambda h, n: (0, 0))
+    return pl.pallas_call(functools.partial(attend_back_kernel, min(block, rows)),
+        grid_spec=pltpu.PrefetchScalarGridSpec(num_scalar_prefetch=1, grid=(pairs,),
+            in_specs=[kind(0), kind(1), kind(2), pl.BlockSpec((rows, PAIR), lambda h, n: (0, h)), pl.BlockSpec((1, 2, rows), lambda h, n: (h, 0, 0)), table, table, table],
+            out_specs=pl.BlockSpec((3, rows, PAIR), lambda h, n: (0, 0, h)),
+            scratch_shapes=[pltpu.VMEM((2, rows, PAIR), bf16)]*2+[pltpu.VMEM((PAIR, rows), bf16)]+[pltpu.VMEM((rows, PAIR), f32)]*2),
         out_shape=shape((3, rows, width), bf16),
         compiler_params=params(48),
-        cost_estimate=cost(40 * rows * rows * width, 8 << 20, rows * rows * heads),
-        name="attend_back",
-    )(length, qkv, qkv, qkv, grad_mixed, totals, *tables)
+        cost_estimate=cost(40 * rows * rows * width, 8 << 20, rows * rows * 2 * pairs),
+        name="attend_back")(length, qkv, qkv, qkv, grad_mixed, totals, *tables)
 
 
 def feed_kernel(tile, tile_f, steps, plan1, plan2, ln_ref, mixed_ref, wo_ref, bias_ref, *rest):
@@ -480,7 +438,7 @@
     by_row = pl.BlockSpec((rows, tile_f), lambda i: (0, i))
     hbm = pl.BlockSpec(memory_space=pl.ANY)
     return pl.pallas_call(
-        functools.partial(feed_kernel, rows // 2, tile_f, steps, w1[1], w2[1]),
+        functools.partial(feed_kernel, rows, tile_f, steps, w1[1], w2[1]),
         grid=(steps,),
         in_specs=[
             whole((rows, width)),
@@ -545,7 +503,7 @@
     whole = lambda dims: pl.BlockSpec(dims, lambda i: (0, 0), pipeline_mode=once)
     by_row = pl.BlockSpec((rows, tile_f), lambda i: (0, i))
     return pl.pallas_call(
-        functools.partial(back_kernel, min(512, rows)),
+        functools.partial(back_kernel, rows),
         grid=(units // tile_f,),
         in_specs=[
             whole((rows, width)),
@@ -607,16 +565,16 @@
 def ln_grad(grad_qkv, weights, partial_sum):
     _, rows, heads = grad_qkv.shape
     width = partial_sum.shape[1]
-    tile = min(512, rows)
+    tile = 512
     return pl.pallas_call(
         ln_grad_kernel,
-        grid=(rows // tile,),
+        grid=(width // tile,),
         in_specs=[
+            pl.BlockSpec((3, rows, heads), lambda i: (0, 0, 0), pipeline_mode=once),
             pl.BlockSpec((3, tile, heads), lambda i: (0, i, 0)),
-            pl.BlockSpec((3, width, heads), lambda i: (0, 0, 0), pipeline_mode=once),
-            pl.BlockSpec((tile, width), lambda i: (i, 0)),
+            pl.BlockSpec((rows, tile), lambda i: (0, i)),
         ],
-        out_specs=pl.BlockSpec((tile, width), lambda i: (i, 0)),
+        out_specs=pl.BlockSpec((rows, tile), lambda i: (0, i)),
         out_shape=shape((rows, width), bf16),
         compiler_params=params(48),
         cost_estimate=cost(6 * rows * width * heads, 22 << 20),
@@ -668,38 +626,55 @@
     )(ln, grads, grad_qkv, mixed)
 
 
-def give_kernel(*refs):
-    total = refs[0][...].astype(f32)
-    for ref in refs[1:-1]:
-        total += ref[...].astype(f32)
-    refs[-1][...] = total.astype(bf16)
-
-
-def give(full, partial_sums, count, low, part=(0, 1)):
-    rows, width = full[0].shape[0], full[0].shape[1] // part[1]
-    block = rows // count
-    level = len(partial_sums) + 1
-    out_count = count >> level
-    wide = min(1024, width)
-    off = part[0] * (width // wide)
-    place = (lambda i: (2 * i + 1) << (level - 1)) if low else (lambda i: out_count + i)
-    spec = lambda k, o: pl.BlockSpec(
-        (block, wide), lambda i, j: (place(i) >> k if low else place(i), j + o)
-    )
+def give_kernel(counts, *refs):
+    outs = refs[sum(counts) :]
+    start = 0
+    for number, out_ref in zip(counts, outs):
+        total = refs[start][...].astype(f32)
+        for ref in refs[start + 1 : start + number]:
+            total += ref[...].astype(f32)
+        out_ref[...] = total.astype(bf16)
+        start += number
+
+
+def give(items, count):
+    specs, operands, numbers, outs = [], [], [], []
+    for full, arrivals, low, part in items:
+        rows, width = full[0].shape[0], full[0].shape[1] // part[1]
+        block = rows // count
+        level = len(arrivals) + 1
+        out_count = count >> level
+        place = (lambda i: (2 * i + 1) << (level - 1)) if low else (lambda i: out_count + i)
+        for k in range(level):
+            for array in full if k == 0 else [arrivals[k - 1]]:
+                off = part[0] if k == 0 else 0
+                specs.append(
+                    pl.BlockSpec(
+                        (block, width),
+                        lambda i, k=k, off=off, low=low, place=place: (
+                            place(i) >> k if low else place(i),
+                            off,
+                        ),
+                    )
+                )
+                operands.append(array)
+        numbers.append(len(full) + level - 1)
+        outs.append(shape((out_count * block, width), bf16))
+    moved = sum(o.shape[0] * o.shape[1] for o in outs)
     return pl.pallas_call(
-        give_kernel,
-        grid=(out_count, width // wide),
-        in_specs=[spec(0, off) for _ in full] + [spec(k + 1, 0) for k in range(level - 1)],
-        out_specs=pl.BlockSpec((block, wide), lambda i, j: (i, j)),
-        out_shape=shape((out_count * block, width), bf16),
+        functools.partial(give_kernel, tuple(numbers)),
+        grid=(out_count,),
+        in_specs=specs,
+        out_specs=[pl.BlockSpec((block, o.shape[1]), lambda i: (i, 0)) for o in outs],
+        out_shape=outs,
         compiler_params=params(32),
-        cost_estimate=cost(out_count * block * width * 2, 6 * out_count * block * width),
+        cost_estimate=cost(moved * 2, 6 * moved),
         name="give",
-    )(*full, *partial_sums)
+    )(*operands)
 
 
 def norm_back_kernel(
-    blocks, at_ref, sum_ref, rows_ref, cot_ref, gain_ref, out_ref, gain_sum_ref, shift_sum_ref, held
+    blocks, at_ref, sum_ref, rows_ref, cot_ref, gain_ref, first_ref, second_ref, vector_ref, held
 ):
     wide = rows_ref.shape[1] // blocks
     bits = blocks.bit_length() - 1
@@ -717,9 +692,12 @@
         - jnp.mean(grad_norm, -1, keepdims=True)
         - normed * jnp.mean(grad_norm * normed, -1, keepdims=True)
     )
-    out_ref[...] = (cot_ref[...].astype(f32) + back).astype(bf16)
-    gain_sum_ref[...] = jnp.sum(grad_ln * normed, 0, keepdims=True)
-    shift_sum_ref[...] = jnp.sum(grad_ln, 0, keepdims=True)
+    slot = (cot_ref[...].astype(f32) + back).astype(bf16)
+    half = first_ref.shape[0]
+    first_ref[...] = slot[:half]
+    second_ref[...] = slot[half:]
+    vector_ref[0:1] = jnp.sum(grad_ln * normed, 0, keepdims=True)
+    vector_ref[1:2] = jnp.sum(grad_ln, 0, keepdims=True)
 
 
 def norm_back(total, rows_in, cot, gain, at, blocks):
@@ -732,10 +710,11 @@
             num_scalar_prefetch=1,
             grid=(1,),
             in_specs=[whole, whole, whole, vector],
-            out_specs=[whole, vector, vector],
+            out_specs=[pl.BlockSpec((rows // 2, width), lambda i, n: (0, 0))] * 2
+            + [pl.BlockSpec((2, width), lambda i, n: (0, 0))],
             scratch_shapes=[pltpu.VMEM((rows, width), bf16)],
         ),
-        out_shape=[shape((rows, width), bf16), shape((1, width), f32), shape((1, width), f32)],
+        out_shape=[shape((rows // 2, width), bf16)] * 2 + [shape((2, width), f32)],
         compiler_params=params(32),
         cost_estimate=cost(20 * rows * width, 8 * rows * width),
         name="norm_back",
@@ -805,6 +784,40 @@
     )(at, branch_sum, rows_in, bias_a, bias_b)
 
 
+def final_attention_kernel(levels, *refs):
+    heads = refs[0].shape[1] // 2
+    grad_ref, out_ref = refs[-2:]
+    totals = []
+    for start in (0, levels + 2):
+        total = refs[start][...].astype(f32)
+        for ref in refs[start + 1 : start + levels + 2]:
+            total += ref[...].astype(f32)
+        totals.append(total)
+    grad_ref[0] = totals[0][:, :heads]
+    grad_ref[1] = totals[0][:, heads:]
+    grad_ref[2] = totals[1][:, :heads]
+    out_ref[...] = totals[1][:, heads:]
+
+
+def final_attention(qk, vo, block):
+    levels = len(qk) - 2
+    width = qk[0].shape[1]
+    piece = pl.BlockSpec((block, width), lambda i: (0, 0))
+    return pl.pallas_call(
+        functools.partial(final_attention_kernel, levels),
+        grid=(1,),
+        in_specs=[piece] * (2 * levels + 4),
+        out_specs=[
+            pl.BlockSpec((3, block, width // 2), lambda i: (0, 0, 0)),
+            pl.BlockSpec((block, width // 2), lambda i: (0, 0)),
+        ],
+        out_shape=[shape((3, block, width // 2), f32), shape((block, width // 2), f32)],
+        compiler_params=params(32),
+        cost_estimate=cost(8 * block * width, 24 * block * width),
+        name="final_attention",
+    )(*qk, *vo)
+
+
 def rotary_tables(rows, col_count):
     half_rot = ROT // 2
     column = jnp.arange(col_count) % HEAD_DIM
@@ -889,23 +902,28 @@
 
 
 def route_more(stack, last):
-    for bit in route_order(last)[1:]:
+    order = route_order(last)[1:]
+    for bit in order[:-1]:
         stack = jnp.concatenate([stack, flip(stack, "dp", bit)], 0)
-    return stack
-
-
-def route_last(stack, wanted, index, last):
+    return (stack, flip(stack, "dp", order[-1]))
+
+
+def route_picks(halves, wanted, index, last):
     order = route_order(last)
-
-    def place(mask):
-        return sum(((mask >> bit) & 1) << k for k, bit in enumerate(order))
-
-    mine = wanted[index]
-    theirs = wanted[index ^ (1 << last)]
-    given = lax.dynamic_index_in_dim(stack, place(index ^ theirs), 0, keepdims=False)
-    held = lax.dynamic_index_in_dim(stack, place(index ^ mine), 0, keepdims=False)
+    count = halves[0].shape[0]
+
+    def pick(want):
+        mask = index ^ want
+        at = sum(((mask >> bit) & 1) << k for k, bit in enumerate(order))
+        found = [lax.dynamic_index_in_dim(h, at % count, 0, keepdims=False) for h in halves]
+        return found[0] if len(found) == 1 else jnp.where(at < count, found[0], found[1])
+
+    return pick(wanted[index ^ (1 << last)]), pick(wanted[index])
+
+
+def route_end(given, held, wanted, index, last):
     arrived = flip(given, "dp", last)
-    return jnp.where(((index ^ mine) >> last) & 1 == 1, arrived, held)
+    return jnp.where(((index ^ wanted[index]) >> last) & 1 == 1, arrived, held)
 
 
 def gather_small(stack, axis_name):
@@ -914,23 +932,13 @@
     return stack
 
 
-def scatter_first(blocks, data_index, tensor_index):
-    stack = swap_blocks(
-        blocks, data_index * lax.axis_size("tensor") + tensor_index, 0, blocks.shape[0]
-    )
-    half = stack.shape[0] // 2
-    return stack[:half], flip(stack[half:], "dp", bits_of(lax.axis_size("dp")) - 1)
-
-
-def scatter_rest(kept, arrived):
-    stack = kept + arrived
-    for bit in range(bits_of(lax.axis_size("dp")) - 2, -1, -1):
-        half = stack.shape[0] // 2
-        stack = stack[:half] + flip(stack[half:], "dp", bit)
-    for bit in range(bits_of(lax.axis_size("tensor")) - 1, -1, -1):
-        half = stack.shape[0] // 2
-        stack = stack[:half] + flip(stack[half:], "tensor", bit)
-    return stack[0]
+def scatter_along(stack, axis_name):
+    bits = bits_of(lax.axis_size(axis_name))
+    stack = stack.reshape((2,) * bits + stack.shape[1:])
+    stack = stack.transpose(tuple(range(bits - 1, -1, -1)) + tuple(range(bits, stack.ndim)))
+    for bit in range(bits):
+        stack = stack[0] + flip(stack[1], axis_name, bit)
+    return stack
 
 
 def after(values, *others):
@@ -975,19 +983,23 @@
     wave_rows = rows_here // 2
     at = jnp.stack([tensor_index, data_index, length]).astype(jnp.int32)
 
-    def send(rows):
-        half = rows.shape[0] // 2
-        return [route_first(h, last) for h, last in zip((rows[:half], rows[half:]), lasts)]
+    def send(parts):
+        return [route_first(h, last) for h, last in zip(parts, lasts)]
+
+    def picks_of(stacks, wanted):
+        return [route_picks(f, wanted, data_index, last) for f, last in zip(stacks, lasts)]
+
+    def route_ends(picks, wanted):
+        return jnp.concatenate(
+            [route_end(g, k, wanted, data_index, last) for (g, k), last in zip(picks, lasts)], 0
+        )
 
     def receive(firsts, wanted):
-        return finish_route([route_more(f, last) for f, last in zip(firsts, lasts)], wanted)
-
-    def finish_route(stacks, wanted):
-        return jnp.concatenate(
-            [route_last(f, wanted, data_index, last) for f, last in zip(stacks, lasts)], 0
-        )
-
-    firsts = send(hidden_in[0])
+        stacks = [route_more(f, last) for f, last in zip(firsts, lasts)]
+        stacks = [(jnp.concatenate(halves, 0),) for halves in stacks]
+        return route_ends(picks_of(stacks, wanted), wanted)
+
+    firsts = send((hidden_in[0, :wave_rows], hidden_in[0, wave_rows:]))
     vectors = [ln_gain, ln_bias, out_bias, fc2_bias, qkv_bias, fc1_bias]
     s = ln_gain.shape[0]
     vectors = after(vectors, *firsts)
@@ -995,15 +1007,16 @@
     stack = gather_small(small[None], "tensor")
     routed = receive(firsts, seq_of_slot)
     routed, stack = after((routed, stack))
-    stack = gather_small(stack, "dp")
-    gathered = swap_blocks(stack, data_index * tensor_count + tensor_index, 0, stack.shape[0])
-    gathered = gathered.reshape(data_count, tensor_count, -1)
-
+    extra_rows = 16
     rows_a, rows_b = routed[:wave_rows], routed[wave_rows:]
     full_a = lax.all_gather(rows_a, "tensor", axis=0, tiled=True)
     full_b = lax.all_gather(rows_b, "tensor", axis=0, tiled=True)
 
-    qk_shard = qkv_weight[:, :2].reshape(block, 2 * heads_local)
+    stack = swap_blocks(stack, tensor_index, 0, tensor_count).reshape(-1)
+    extra = jnp.pad(stack, (0, extra_rows * 2 * heads_local - stack.shape[0]))
+    qk_shard = jnp.concatenate(
+        [qkv_weight[:, :2].reshape(block, 2 * heads_local), extra.reshape(extra_rows, 2 * heads_local)], 0
+    )
     vo_shard = jnp.concatenate([qkv_weight[:, 2], out_weight], 1)
     qk_shard, vo_shard = after((qk_shard, vo_shard), routed)
     qk_stacks = gather_step([(qk_shard, [0])], x_first[0])
@@ -1021,7 +1034,12 @@
     (qk_stacks, vo_stacks), (fc1_shard, fc2_shard, row_ids) = held_back(
         (qk_stacks, vo_stacks), fc1_weight, fc2_weight, jnp.arange(seq_len, dtype=jnp.int32)
     )
-    qk = gather_plan(qk_stacks + core_copies(qk_stacks), block, bits)
+    qk_stacks = qk_stacks + core_copies(qk_stacks)
+    qk = gather_plan(qk_stacks, block, bits)
+    by_mask = sorted(qk_stacks, key=lambda st: st[1][0])
+    gathered = jnp.stack([rows[block:].reshape(-1)[: stack.shape[0]] for rows, _ in by_mask], 0)
+    gathered = swap_blocks(gathered, data_index, 0, data_count)
+    gathered = gathered.reshape(data_count, tensor_count, -1)
     vo = gather_plan(vo_stacks + core_copies(vo_stacks), block, bits)
     fc1_stacks = gather_step([(fc1_shard, [0])], x_first[0])
     fc2_stacks = gather_step([(fc2_shard, [0])], y_first[0])
@@ -1085,41 +1103,39 @@
     pair = ((0, 2), (1, 2))
     both = (x_first, y_first)
 
-    def first_gives(full):
-        return [give(full, [], count, low, part) for part, low in zip(pair, (False, True))]
-
-    def next_gives(full, sums, step):
-        return [give(full, s, count, low, p) for s, low, p in zip(sums, (False, True), pair)]
+    def gives_of(full, sums):
+        return give([(full, s, low, p) for s, low, p in zip(sums, (False, True), pair)], count)
 
     def send_on(gives, step):
         return [flip(g, "dp", order[step]) for g, order in zip(gives, both)]
 
     k2, c2 = after((k2, c2), s1)
-    gives2 = first_gives([k2, c2])
+    gives2 = gives_of([k2, c2], ([], []))
     sums2 = [[f] for f in send_on(gives2, 0)]
     k1, c1 = after((k1, c1), *gives2)
-    gives1 = first_gives([k1, c1])
+    gives1 = gives_of([k1, c1], ([], []))
     sums1 = [[f] for f in send_on(gives1, 0)]
     grad_mixed, = after((grad_mixed,), *gives1)
     grad_qkv = attend_back(qkv, grad_mixed, totals, size, tables)
-    grad_qkv, branch, sums2, sums1 = after((grad_qkv, branch, sums2, sums1))
+    kqk, kvo, sqk, svo, grad_qkv_b = weight_grad(ln, grads, grad_qkv, mixed)
+    cq, cv = flip(sqk, "dp", 0), flip(svo, "dp", 0)
+    grad_qkv, branch, sums2, sums1 = after((grad_qkv, branch, sums2, sums1), sqk)
     ln_part = ln_grad(grad_qkv, weights, feed_sum)
     total = lax.psum_scatter(ln_part, "tensor", scatter_dimension=0, tiled=True)
-    mixed, = after((mixed,), ln_part)
-    kqk, kvo, sqk, svo, grad_qkv_b = weight_grad(ln, grads, grad_qkv, mixed)
-    cq, cv = flip(sqk, "dp", 0), flip(svo, "dp", 0)
-    k2, = after((k2,), sqk)
+    kqk, kvo, cq, cv = after((kqk, kvo, cq, cv), ln_part)
+    giveq, givev = give(
+        [([kqk, cq], [], False, (0, 1)), ([kvo, cv], [], True, (0, 1))], count
+    )
+    sumsq, sumsv = [flip(giveq, "dp", x_first[0])], [flip(givev, "dp", y_first[0])]
+    k2, = after((k2,), giveq, givev)
     for step in range(1, steps):
-        gives2 = next_gives([k2, c2], sums2, step)
+        gives2 = gives_of([k2, c2], sums2)
         sums2 = [s + [f] for s, f in zip(sums2, send_on(gives2, step))]
     k1, = after((k1,), *gives2)
     for step in range(1, steps):
-        gives1 = next_gives([k1, c1], sums1, step)
+        gives1 = gives_of([k1, c1], sums1)
         sums1 = [s + [f] for s, f in zip(sums1, send_on(gives1, step))]
-    kqk, cq, kvo, cv = after((kqk, cq, kvo, cv), *gives1)
-    giveq, givev = give([kqk, cq], [], count, False), give([kvo, cv], [], count, True)
-    sumsq, sumsv = [flip(giveq, "dp", x_first[0])], [flip(givev, "dp", y_first[0])]
-    branch, = after((branch,), giveq, givev)
+    branch, = after((branch,), *gives1)
     block_out = finish(branch, routed, bias_a, bias_b, at, data_count)[None]
     grad_bias = jnp.sum(low_plain.astype(f32), axis=0)
     devices = data_count * tensor_count
@@ -1133,36 +1149,32 @@
         [grad_bias.reshape(devices, s), full_qkv_b.reshape(devices, q), full_fc1_b.reshape(devices, -1)],
         1,
     )
-    total, known, sumsq, sumsv, sums2, sums1 = after(
-        (total, known, sumsq, sumsv, sums2, sums1), block_out
-    )
-    slot, grad_gain, grad_shift = norm_back(total, routed, cotangent[0], gain, at, data_count)
-    firsts = send(slot)
-    kqk, kvo = after((kqk, kvo), slot)
+    kqk, kvo, sumsq, sumsv = after((kqk, kvo, sumsq, sumsv), block_out)
     for step in range(1, steps):
-        giveq = give([kqk, cq], sumsq, count, False)
-        givev = give([kvo, cv], sumsv, count, True)
+        giveq, givev = give(
+            [([kqk, cq], sumsq, False, (0, 1)), ([kvo, cv], sumsv, True, (0, 1))], count
+        )
         sumsq = sumsq + [flip(giveq, "dp", x_first[step])]
         sumsv = sumsv + [flip(givev, "dp", y_first[step])]
-    k2, k1 = after((k2, k1), giveq, givev)
+    k2, k1, sums2, sums1 = after((k2, k1, sums2, sums1), giveq, givev)
     grad_fc2_w, grad_fc1_w = final([k2, c2], sums2, block), final([k1, c1], sums1, block)
-    grad_gain, grad_shift, known, firsts = after(
-        (grad_gain, grad_shift, known, firsts), grad_fc2_w, grad_fc1_w
-    )
+    sumsq, sumsv = after((sumsq, sumsv), grad_fc2_w, grad_fc1_w)
+    grad_qkv_w, grad_out_w = final_attention([kqk, cq] + sumsq, [kvo, cv] + sumsv, block)
+    grad_qkv_w = grad_qkv_w.swapaxes(0, 1)
+    total, known = after((total, known), grad_out_w)
+    *slot, vector_sums = norm_back(total, routed, cotangent[0], gain, at, data_count)
+    firsts = send(slot)
+    vector_sums = vector_sums.reshape(2, devices, s)
+    sums = jnp.concatenate([vector_sums[0], vector_sums[1], known], 1)
+    sums = swap_blocks(sums, data_index * tensor_count + tensor_index, 0, devices)
+    sums = sums.reshape(data_count, tensor_count, -1).swapaxes(0, 1)
+    sums = scatter_along(sums, "tensor")
+    firsts, sums = after((firsts, sums))
     stacks = [route_more(f, last) for f, last in zip(firsts, lasts)]
-    sums = jnp.concatenate(
-        [v.reshape(devices, s) for v in (grad_gain[0], grad_shift[0])] + [known], 1
-    )
-    kept, arrived = scatter_first(sums, data_index, tensor_index)
-    stacks, kept, arrived = after((stacks, kept, arrived))
-    grad_input = finish_route(stacks, slot_of_seq)[None]
-    total = scatter_rest(kept, arrived)
-    sumsq, sumsv = after((sumsq, sumsv), *stacks)
-    grad_qk_w, grad_vo_w = final([kqk, cq], [sumsq], block), final([kvo, cv], [sumsv], block)
-    grad_out_w = grad_vo_w[:, heads_local:]
-    grad_qkv_w = jnp.stack(
-        [grad_qk_w[:, :heads_local], grad_qk_w[:, heads_local:], grad_vo_w[:, :heads_local]], 1
-    )
+    picks = picks_of(stacks, slot_of_seq)
+    picks, sums = after((picks, sums))
+    grad_input = route_ends(picks, slot_of_seq)[None]
+    total = scatter_along(sums, "dp")
     return (
         block_out,
         grad_input,

time: 510 us -> 489 us (0.959)
  Pallas kernels: 261 us -> 237 us
  other arithmetic: 21.2 us -> 14.9 us
    pallas_call x17 -> x12, Pallas kernels: 166 us -> 148 us  [the longest x1 36.4 us: feed(): pl.pallas_call(functools.partial(feed_kernel, rows, tile_f, steps, w1[1],...]
    unnamed x69 -> x85, local copies, waits for them, and re-layouts: 2.78 us -> 10.9 us
    pallas_call x4 -> x2, Pallas kernels: 12.6 us -> 7.14 us  [final(): pl.pallas_call(functools.partial(final_kernel, parts, levels), grid=(part...]
    ppermute x66 -> x63, waiting for transfers between devices: 112 us -> 117 us  [flip(): lax.ppermute(array, axis_name, [(i, i ^ 1 << bit) for i in range(size)])]
    ppermute x66 -> x63, starting transfers between devices: 53.1 us -> 54.3 us  [flip(): lax.ppermute(array, axis_name, [(i, i ^ 1 << bit) for i in range(size)])]
  transfers between devices with their start and end apart: 71 -> 68, of which waited for: 29 -> 40; matrix products, arithmetic and copies ran while one was open for 7% -> 6% of each run, Pallas kernels for 48% -> 45%
where the time goes in v5:
time: 489 us; the launch traced here: 485 us
  Pallas kernels  237 us (48%)
  waiting for transfers between devices  132 us (27%)
  starting transfers between devices  54.8 us (11%)
  local copies, waits for them, and re-layouts  24.5 us (5%)
  between operations  21 us (4%)
  other arithmetic  14.9 us (3%)
    ppermute x63, waiting for transfers between devices, flip(): lax.ppermute(array, axis_name, [(i, i ^ 1 << bit) for i in range(size)])  117 us
    ppermute x63, starting transfers between devices, flip(): lax.ppermute(array, axis_name, [(i, i ^ 1 << bit) for i in range(size)])  54.3 us
    pallas_call x1, Pallas kernels, feed(): pl.pallas_call(functools.partial(feed_kernel, rows, tile_f, steps, w1[1],...  36.4 us
    pallas_call x1, Pallas kernels, back(): pl.pallas_call(functools.partial(back_kernel, rows), grid=(units // tile_...  32.9 us
    pallas_call x1, Pallas kernels, attend_back(): pl.pallas_call(functools.partial(attend_back_kernel, min(block, rows)), g...  26.8 us
    pallas_call x2, Pallas kernels, feed_weight(): pl.pallas_call(feed_weight_kernel, grid=(units // tile_f,), in_specs=[pl....  26.3 us
    pallas_call x6, Pallas kernels, give(): pl.pallas_call(functools.partial(give_kernel, tuple(numbers)), grid=(out_...  19.4 us
    pallas_call x1, Pallas kernels, attend(): pl.pallas_call(functools.partial(attend_kernel, min(block, rows)), grid_s...  16.6 us
  transfers between devices with their start and end apart: 68, of which 40 were waited for; matrix products, arithmetic and copies ran while one was open for 6% of the time, Pallas kernels for 45%

profile of v5, /device:TPU:0, one launch (start us, length us, event | category | flops | bytes accessed | tf_op | source)
XLA Modules:
  0.0 484.5 jit_solution(13477097218593575541)
XLA Ops:
  13.1 10.4 %collective-permute-done.3 = bf16[128,2048]{1,0:T(8,128)(2,1)S(1)} collective-permute-done((bf16[128,2048]{1,0:T(8,128)(2,1)S(1)}, bf16[128,2048]{1,0:T(8,128)(2,1)S(1)}, u32[]{:S(2)}, u32[]{:S(2)}) %collective-permute-start.3) | collective-permute-done | bytes 524320 | tf_op jit(solution)/shard_map/ppermute | solution.py:837
  40.9 7.9 %collective-permute-done.5 = bf16[128,2048]{1,0:T(8,128)(2,1)S(1)} collective-permute-done((bf16[128,2048]{1,0:T(8,128)(2,1)S(1)}, bf16[128,2048]{1,0:T(8,128)(2,1)S(1)}, u32[]{:S(2)}, u32[]{:S(2)}) %collective-permute-start.5) | collective-permute-done | bytes 524320 | tf_op jit(solution)/shard_map/ppermute | solution.py:837
  66.1 8.2 %collective-permute-done.11.rest_9_ = bf16[256,1024]{1,0:T(8,128)(2,1)} collective-permute-done((bf16[256,1024]{1,0:T(8,128)(2,1)S(1)}, bf16[256,1024]{1,0:T(8,128)(2,1)}, u32[]{:S(2)}, u32[]{:S(2)}) %collective-permute-start.11) | collective-permute-done | bytes 524320 | tf_op jit(solution)/shard_map/ppermute | solution.py:837
  81.0 4.7 collective-permute-done.12.rest_10_
  86.3 7.2 %collective-permute-done.13.rest_11_ = bf16[256,1024]{1,0:T(8,128)(2,1)} collective-permute-done((bf16[256,1024]{1,0:T(8,128)(2,1)}, bf16[256,1024]{1,0:T(8,128)(2,1)}, u32[]{:S(2)}, u32[]{:S(2)}) %collective-permute-start.13) | collective-permute-done | bytes 524320 | tf_op jit(solution)/shard_map/ppermute | solution.py:837
  108.4 5.4 %norm_wave.2.ln_ref.rest_0_ = bf16[4,2,128,2048]{3,2,1,0:T(8,128)(2,1)} custom-call(s32[3]{0:T(128)} %pad_add_fusion.at_ref, bf16[512,2048]{1,0:T(8,128)(2,1)} %all-gather.4.cloned.1.call-done.x_ref, f32[1,2048]{1,0:T(1,128)} %reshape.253.gain_ref, f32[1,2048]{1,0:T(1,128)} %reshape.254.shift_ref), custom_call_target="tpu_custom_call" | custom-call | flops 4194304 | bytes 1677721 | tf_op jit(solution)/shard_map/norm_wave/pallas_call | solution.py:85
  113.8 12.5 %project_first.1 = (bf16[3,4,2,128,512]{4,3,2,1,0:T(8,128)(2,1)}, bf16[4,2048,512]{2,1,0:T(8,128)(2,1)}) custom-call(bf16[4,2,128,2048]{3,2,1,0:T(8,128)(2,1)} %norm_wave.2.ln_ref.rest_0_, f32[3,1,512]{2,1,0:T(1,128)} %reshape.255.bias_ref, f32[4,2,128,128]{3,2,1,0:T(8,128)} %bitcast.148, f32[4,2,128,128]{3,2,1,0:T(8,128)} %bitcast.146, ...), custom_call_target="tpu_custom_call" | custom-call | flops 1288490240 | bytes 9227468 | tf_op jit(solution)/shard_map/project_first/pallas_call | solution.py:187
  133.9 11.3 %all-gather.6.cloned.1.call-done.x_ref = bf16[512,2048]{1,0:T(8,128)(2,1)} async-done(((bf16[128,2048]{1,0:T(8,128)(2,1)}), bf16[512,2048]{1,0:T(8,128)(2,1)}) %all-gather.6.cloned.1.call-update) | async-done | bytes 2097168 | tf_op jit(solution)/shard_map/all_gather | solution.py:1013
  145.1 5.3 %norm_wave.3.ln_ref = bf16[4,2,128,2048]{3,2,1,0:T(8,128)(2,1)} custom-call(s32[3]{0:T(128)} %pad_add_fusion.at_ref, bf16[512,2048]{1,0:T(8,128)(2,1)} %all-gather.6.cloned.1.call-done.x_ref, f32[1,2048]{1,0:T(1,128)} %reshape.253.gain_ref, f32[1,2048]{1,0:T(1,128)} %reshape.254.shift_ref, ...), custom_call_target="tpu_custom_call", output_to_operand_aliasing={{}: (4, {})} | custom-call | flops 4194304 | bytes 1677721 | tf_op jit(solution)/shard_map/norm_wave/pallas_call | solution.py:85
  150.5 8.5 %project_second.1 = bf16[3,4,2,128,512]{4,3,2,1,0:T(8,128)(2,1)} custom-call(bf16[4,2,128,2048]{3,2,1,0:T(8,128)(2,1)} %norm_wave.3.ln_ref, bf16[4,2048,512]{2,1,0:T(8,128)(2,1)} %get-tuple-element.175.w_ref.wo_ref, f32[3,1,512]{2,1,0:T(1,128)} %reshape.255.bias_ref, f32[4,2,128,128]{3,2,1,0:T(8,128)} %bitcast.149, ...), custom_call_target="tpu_custom_call", output_to_operand_aliasing={{}: (6, {})} | custom-call | flops 1288490240 | bytes 5033164 | tf_op jit(solution)/shard_map/project_second/pallas_call | solution.py:222
  159.0 16.6 %attend.1 = (bf16[1024,512]{1,0:T(8,128)(2,1)}, f32[4,2,1024]{2,1,0:T(2,128)}) custom-call(s32[1]{0:T(128)} %dynamic_slice.97.len_ref, bf16[3,1024,512]{2,1,0:T(8,128)(2,1)} %bitcast.151, bf16[3,1024,512]{2,1,0:T(8,128)(2,1)} %bitcast.152, bf16[3,1024,512]{2,1,0:T(8,128)(2,1)} %bitcast.153), custom_call_target="tpu_custom_call" | custom-call | flops 3435973888 | bytes 1677721 | tf_op jit(solution)/shard_map/attend/pallas_call | solution.py:283
  176.2 3.6 collective-permute-done.31.rest_11_
  187.3 36.4 %feed.1 = (bf16[1024,2048]{1,0:T(8,128)(2,1)}, bf16[1024,2048]{1,0:T(8,128)(2,1)}, f32[1024,2048]{1,0:T(8,128)}, bf16[2048,2048]{1,0:T(8,128)(2,1)}, bf16[2048,2048]{1,0:T(8,128)(2,1)}) custom-call(bf16[1024,2048]{1,0:T(8,128)(2,1)} %bitcast.141, bf16[1024,512]{1,0:T(8,128)(2,1)} %get-tuple-element.178.mixed_ref, ...), custom_call_target="tpu_custom_call" | custom-call | flops 6871947776 | bytes 23488102 | tf_op jit(solution)/shard_map/feed/pallas_call | solution.py:440
  226.8 32.9 %back.1 = (f32[1024,2048]{1,0:T(8,128)}, bf16[1024,2048]{1,0:T(8,128)(2,1)}, bf16[1024,512]{1,0:T(8,128)(2,1)}, f32[1,2048]{1,0:T(1,128)}) custom-call(bf16[1024,2048]{1,0:T(8,128)(2,1)} %all-gather.8.cloned.1.call-done.g_ref.left_ref, bf16[2048,2048]{1,0:T(8,128)(2,1)} %get-tuple-element.194.w1_ref, bf16[2048,2048]{1,0:T(8,128)(2,1)} %get-tuple-element.195.w2_ref, ...), custom_call_target="tpu_custom_call" | custom-call | flops 6871947776 | bytes 16777216 | tf_op jit(solution)/shard_map/back/pallas_call | solution.py:505
  259.7 13.1 %feed_weight.2 = (bf16[1024,2048]{1,0:T(8,128)(2,1)}, bf16[1024,2048]{1,0:T(8,128)(2,1)}) custom-call(bf16[1024,2048]{1,0:T(8,128)(2,1)} %all-gather.8.cloned.1.call-done.g_ref.left_ref, bf16[1024,2048]{1,0:T(8,128)(2,1)} %get-tuple-element.200.right_ref), custom_call_target="tpu_custom_call" | custom-call | flops 3435973888 | bytes 6710886 | tf_op jit(solution)/shard_map/feed_weight/pallas_call | solution.py:543
  272.8 13.2 %feed_weight.3 = (bf16[1024,2048]{1,0:T(8,128)(2,1)}, bf16[1024,2048]{1,0:T(8,128)(2,1)}) custom-call(bf16[1024,2048]{1,0:T(8,128)(2,1)} %bitcast.142, bf16[1024,2048]{1,0:T(8,128)(2,1)} %get-tuple-element.202.right_ref), custom_call_target="tpu_custom_call" | custom-call | flops 3435973888 | bytes 6710886 | tf_op jit(solution)/shard_map/feed_weight/pallas_call | solution.py:543
  286.4 3.4 give.6
  299.9 26.8 %attend_back.1.grad_ref = bf16[3,1024,512]{2,1,0:T(8,128)(2,1)} custom-call(s32[1]{0:T(128)} %dynamic_slice.97.len_ref, bf16[3,1024,512]{2,1,0:T(8,128)(2,1)} %bitcast.154, bf16[3,1024,512]{2,1,0:T(8,128)(2,1)} %bitcast.155, bf16[3,1024,512]{2,1,0:T(8,128)(2,1)} %bitcast.156, bf16[1024,512]{1,0:T(8,128)(2,1)} %get-tuple-element.214.do_ref, ...), custom_call_target="tpu_custom_call" | custom-call | flops 8589934592 | bytes 3355443 | tf_op jit(solution)/shard_map/attend_back/pallas_call | solution.py:341
  326.7 15.0 %weight_grad.1 = (bf16[1024,1024]{1,0:T(8,128)(2,1)}, bf16[1024,1024]{1,0:T(8,128)(2,1)}, bf16[1024,1024]{1,0:T(8,128)(2,1)}, bf16[1024,1024]{1,0:T(8,128)(2,1)}, f32[3,1,512]{2,1,0:T(1,128)}) custom-call(bf16[1024,2048]{1,0:T(8,128)(2,1)} %bitcast.143, bf16[1024,2048]{1,0:T(8,128)(2,1)} %all-gather.8.cloned.1.call-done.g_ref.left_ref, ...), custom_call_target="tpu_custom_call" | custom-call | flops 3435973888 | bytes 8388608 | tf_op jit(solution)/shard_map/weight_grad/pallas_call | solution.py:612
  341.7 12.2 %ln_grad.1 = bf16[1024,2048]{1,0:T(8,128)(2,1)} custom-call(bf16[3,1024,512]{2,1,0:T(8,128)(2,1)} %attend_back.1.grad_ref, bf16[4,2048,512]{2,1,0:T(8,128)(2,1)} %get-tuple-element.175.w_ref.wo_ref, f32[1024,2048]{1,0:T(8,128)} %get-tuple-element.223.sum_ref), custom_call_target="tpu_custom_call" | custom-call | flops 2576980480 | bytes 9227468 | tf_op jit(solution)/shard_map/ln_grad/pallas_call | solution.py:569
  361.3 3.5 give.8
  377.0 14.3 %collective-permute-done.44.refs_2_ = bf16[512,1024]{1,0:T(8,128)(2,1)} collective-permute-done((bf16[512,1024]{1,0:T(8,128)(2,1)}, bf16[512,1024]{1,0:T(8,128)(2,1)}, u32[]{:S(2)}, u32[]{:S(2)}) %collective-permute-start.44) | collective-permute-done | bytes 1048608 | tf_op jit(solution)/shard_map/ppermute | solution.py:837
  391.8 3.7 finish.1
  399.0 4.0 collective-permute-done.48.refs_3_
  405.1 9.1 %collective-permute-done.50.refs_3_ = bf16[256,1024]{1,0:T(8,128)(2,1)} collective-permute-done((bf16[256,1024]{1,0:T(8,128)(2,1)}, bf16[256,1024]{1,0:T(8,128)(2,1)}, u32[]{:S(2)}, u32[]{:S(2)}) %collective-permute-start.50) | collective-permute-done | bytes 524320 | tf_op jit(solution)/shard_map/ppermute | solution.py:837
  414.3 3.6 final.2
  417.9 3.6 final.3
  425.1 3.8 final_attention.1
  429.0 5.2 %norm_back.1 = (bf16[128,2048]{1,0:T(8,128)(2,1)}, bf16[128,2048]{1,0:T(8,128)(2,1)}, f32[2,2048]{1,0:T(2,128)}) custom-call(s32[3]{0:T(128)} %pad_add_fusion.at_ref, bf16[256,2048]{1,0:T(8,128)(2,1)} %reduce-scatter.5.cloned.1.call-done.sum_ref, bf16[256,2048]{1,0:T(8,128)(2,1)} %copy-done, bf16[256,2048]{1,0:T(8,128)(2,1)} %bitcast.150, ...), custom_call_target="tpu_custom_call" | custom-call | flops 4194304 | bytes 1677721 | tf_op jit(solution)/shard_map/norm_back/pallas_call | solution.py:707
  445.1 4.9 %collective-permute-done.52 = bf16[128,2048]{1,0:T(8,128)(2,1)S(1)} collective-permute-done((bf16[128,2048]{1,0:T(8,128)(2,1)S(1)}, bf16[128,2048]{1,0:T(8,128)(2,1)S(1)}, u32[]{:S(2)}, u32[]{:S(2)}) %collective-permute-start.52) | collective-permute-done | bytes 524320 | tf_op jit(solution)/shard_map/ppermute | solution.py:837
  467.5 5.2 %collective-permute-done.59 = bf16[128,2048]{1,0:T(8,128)(2,1)S(1)} collective-permute-done((bf16[128,2048]{1,0:T(8,128)(2,1)S(1)}, bf16[128,2048]{1,0:T(8,128)(2,1)S(1)}, u32[]{:S(2)}, u32[]{:S(2)}) %collective-permute-start.59) | collective-permute-done | bytes 524320 | tf_op jit(solution)/shard_map/ppermute | solution.py:837
  472.7 3.4 collective-permute-done.58
  (334 shorter events, 144.7 us)
Async XLA Ops:
  7.2 101.2 %all-gather.4.cloned.1.call-start = ((), (), s32[]{:S(2)}) async-start(), calls=%async_computation.2 | async-start | bytes 2621440 | tf_op jit(solution)/shard_map/all_gather | solution.py:1012
  8.6 15.0 %collective-permute-start.3 = (bf16[128,2048]{1,0:T(8,128)(2,1)S(1)}, bf16[128,2048]{1,0:T(8,128)(2,1)S(1)}, u32[]{:S(2)}, u32[]{:S(2)}) collective-permute-start(bf16[128,2048]{1,0:T(8,128)(2,1)S(1)} %get-tuple-element.292), channel_id=1, source_target_pairs={{0,16},{4,20},{8,24},{12,28},{16,0},{20,4},{24,8},{28,12},{1,17},{... | collective-permute-start | bytes 1572872 | tf_op jit(solution)/shard_map/ppermute | solution.py:837
  53.9 91.2 %all-gather.6.cloned.1.call-start = ((), (), s32[]{:S(2)}) async-start(), calls=%async_computation.3 | async-start | bytes 2621440 | tf_op jit(solution)/shard_map/all_gather | solution.py:1013
  54.7 172.1 %all-gather.8.cloned.1.call-start = ((), (), s32[]{:S(2)}) async-start(), calls=%async_computation.4 | async-start | bytes 5242880 | tf_op jit(solution)/shard_map/all_gather | solution.py:1053
  58.8 17.1 %collective-permute-start.8 = (bf16[272,1024]{1,0:T(8,128)(2,1)S(1)}, bf16[272,1024]{1,0:T(8,128)(2,1)S(1)}, u32[]{:S(2)}, u32[]{:S(2)}) collective-permute-start(bf16[272,1024]{1,0:T(8,128)(2,1)S(1)} %pad_maximum_fusion.7.rest_0_), channel_id=1, source_target_pairs={{0,8},{4,12},{8,0},{12,4},{16,24},{20,28},{24,16},{28,20},{1,9},{5... | collective-permute-start | bytes 1671176 | tf_op jit(solution)/shard_map/ppermute | solution.py:837
  59.4 15.0 %collective-permute-start.11 = (bf16[256,1024]{1,0:T(8,128)(2,1)S(1)}, bf16[256,1024]{1,0:T(8,128)(2,1)}, u32[]{:S(2)}, u32[]{:S(2)}) collective-permute-start(bf16[256,1024]{1,0:T(8,128)(2,1)S(1)} %pad_maximum_fusion.8.rest_8_), channel_id=1, source_target_pairs={{0,16},{4,20},{8,24},{12,28},{16,0},{20,4},{24,8},{28,12},{1,17},{... | collective-permute-start | bytes 1572872 | tf_op jit(solution)/shard_map/ppermute | solution.py:837
  62.1 24.2 %collective-permute-start.9 = (bf16[272,1024]{1,0:T(8,128)(2,1)S(1)}, bf16[272,1024]{1,0:T(8,128)(2,1)}, u32[]{:S(2)}, u32[]{:S(2)}) collective-permute-start(bf16[272,1024]{1,0:T(8,128)(2,1)S(1)} %pad_maximum_fusion.7.rest_0_), channel_id=1, source_target_pairs={{0,16},{4,20},{8,24},{12,28},{16,0},{20,4},{24,8},{28,12},{1,17},{... | collective-permute-start | bytes 1671176 | tf_op jit(solution)/shard_map/ppermute | solution.py:837
  62.6 23.1 %collective-permute-start.12 = (bf16[256,1024]{1,0:T(8,128)(2,1)S(1)}, bf16[256,1024]{1,0:T(8,128)(2,1)}, u32[]{:S(2)}, u32[]{:S(2)}) collective-permute-start(bf16[256,1024]{1,0:T(8,128)(2,1)S(1)} %pad_maximum_fusion.8.rest_8_), channel_id=1, source_target_pairs={{0,8},{4,12},{8,0},{12,4},{16,24},{20,28},{24,16},{28,20},{1,9},{5... | collective-permute-start | bytes 1572872 | tf_op jit(solution)/shard_map/ppermute | solution.py:837
  74.3 19.1 %collective-permute-start.13 = (bf16[256,1024]{1,0:T(8,128)(2,1)}, bf16[256,1024]{1,0:T(8,128)(2,1)}, u32[]{:S(2)}, u32[]{:S(2)}) collective-permute-start(bf16[256,1024]{1,0:T(8,128)(2,1)} %collective-permute-done.11.rest_9_), channel_id=1, source_target_pairs={{0,8},{4,12},{8,0},{12,4},{16,24},{20,28},{24,16},{28,20},{1,9},{5... | collective-permute-start | bytes 1572872 | tf_op jit(solution)/shard_map/ppermute | solution.py:837
  75.8 18.5 %collective-permute-start.10 = (bf16[272,1024]{1,0:T(8,128)(2,1)S(1)}, bf16[272,1024]{1,0:T(8,128)(2,1)}, u32[]{:S(2)}, u32[]{:S(2)}) collective-permute-start(bf16[272,1024]{1,0:T(8,128)(2,1)S(1)} %collective-permute-done.8.rest_1_), channel_id=1, source_target_pairs={{0,16},{4,20},{8,24},{12,28},{16,0},{20,4},{24,8},{28,12},{1,17},{... | collective-permute-start | bytes 1671176 | tf_op jit(solution)/shard_map/ppermute | solution.py:837
  80.7 261.0 %reduce-scatter.3.cloned.1.call-start = ((), (), s32[]{:S(2)}) async-start(), calls=%async_computation.5 | async-start | bytes 5242880 | tf_op jit(solution)/shard_map/reduce_scatter | solution.py:1091
  95.1 31.2 %collective-permute-start.14 = (bf16[256,2048]{1,0:T(8,128)(2,1)}, bf16[256,2048]{1,0:T(8,128)(2,1)}, u32[]{:S(2)}, u32[]{:S(2)}) collective-permute-start(bf16[256,2048]{1,0:T(8,128)(2,1)} %rest_0_), channel_id=1, source_target_pairs={{0,8},{4,12},{8,0},{12,4},{16,24},{20,28},{24,16},{28,20},{1,9},{5... | collective-permute-start | bytes 3145736 | tf_op jit(solution)/shard_map/ppermute | solution.py:837
  101.6 25.7 %collective-permute-start.15 = (bf16[256,2048]{1,0:T(8,128)(2,1)}, bf16[256,2048]{1,0:T(8,128)(2,1)}, u32[]{:S(2)}, u32[]{:S(2)}) collective-permute-start(bf16[256,2048]{1,0:T(8,128)(2,1)} %rest_8_), channel_id=1, source_target_pairs={{0,16},{4,20},{8,24},{12,28},{16,0},{20,4},{24,8},{28,12},{1,17},{... | collective-permute-start | bytes 3145736 | tf_op jit(solution)/shard_map/ppermute | solution.py:837
  127.8 17.3 %collective-permute-start.27 = (bf16[256,2048]{1,0:T(8,128)(2,1)}, bf16[256,2048]{1,0:T(8,128)(2,1)}, u32[]{:S(2)}, u32[]{:S(2)}) collective-permute-start(bf16[256,2048]{1,0:T(8,128)(2,1)} %collective-permute-done.15.rest_9_), channel_id=1, source_target_pairs={{0,4},{4,0},{8,12},{12,8},{16,20},{20,16},{24,28},{28,24},{1,5},{5... | collective-permute-start | bytes 3145736 | tf_op jit(solution)/shard_map/ppermute | solution.py:837
  128.3 47.2 %collective-permute-start.28 = (bf16[256,2048]{1,0:T(8,128)(2,1)}, bf16[256,2048]{1,0:T(8,128)(2,1)}, u32[]{:S(2)}, u32[]{:S(2)}) collective-permute-start(bf16[256,2048]{1,0:T(8,128)(2,1)} %rest_0_), channel_id=1, source_target_pairs={{0,16},{4,20},{8,24},{12,28},{16,0},{20,4},{24,8},{28,12},{1,17},{... | collective-permute-start | bytes 3145736 | tf_op jit(solution)/shard_map/ppermute | solution.py:837
  130.3 45.9 %collective-permute-start.29 = (bf16[256,2048]{1,0:T(8,128)(2,1)}, bf16[256,2048]{1,0:T(8,128)(2,1)}, u32[]{:S(2)}, u32[]{:S(2)}) collective-permute-start(bf16[256,2048]{1,0:T(8,128)(2,1)} %collective-permute-done.14.rest_1_), channel_id=1, source_target_pairs={{0,16},{4,20},{8,24},{12,28},{16,0},{20,4},{24,8},{28,12},{1,17},{... | collective-permute-start | bytes 3145736 | tf_op jit(solution)/shard_map/ppermute | solution.py:837
  131.8 44.4 %collective-permute-start.30 = (bf16[256,2048]{1,0:T(8,128)(2,1)}, bf16[256,2048]{1,0:T(8,128)(2,1)}, u32[]{:S(2)}, u32[]{:S(2)}) collective-permute-start(bf16[256,2048]{1,0:T(8,128)(2,1)} %rest_8_), channel_id=1, source_target_pairs={{0,8},{4,12},{8,0},{12,4},{16,24},{20,28},{24,16},{28,20},{1,9},{5... | collective-permute-start | bytes 3145736 | tf_op jit(solution)/shard_map/ppermute | solution.py:837
  133.3 46.5 %collective-permute-start.31 = (bf16[256,2048]{1,0:T(8,128)(2,1)}, bf16[256,2048]{1,0:T(8,128)(2,1)}, u32[]{:S(2)}, u32[]{:S(2)}) collective-permute-start(bf16[256,2048]{1,0:T(8,128)(2,1)} %collective-permute-done.15.rest_9_), channel_id=1, source_target_pairs={{0,8},{4,12},{8,0},{12,4},{16,24},{20,28},{24,16},{28,20},{1,9},{5... | collective-permute-start | bytes 3145736 | tf_op jit(solution)/shard_map/ppermute | solution.py:837
  226.8 202.1 %reduce-scatter.5.cloned.1.call-start = ((), (), s32[]{:S(2)}) async-start(), calls=%async_computation.6 | async-start | bytes 5242880 | tf_op jit(solution)/shard_map/reduce_scatter | solution.py:1124
  289.9 51.8 %collective-permute-start.38 = (bf16[512,1024]{1,0:T(8,128)(2,1)}, bf16[512,1024]{1,0:T(8,128)(2,1)}, u32[]{:S(2)}, u32[]{:S(2)}) collective-permute-start(bf16[512,1024]{1,0:T(8,128)(2,1)} %get-tuple-element.208), channel_id=1, source_target_pairs={{0,8},{4,12},{8,0},{12,4},{16,24},{20,28},{24,16},{28,20},{1,9},{5... | collective-permute-start | bytes 3145736 | tf_op jit(solution)/shard_map/ppermute | solution.py:837
  291.4 50.3 %collective-permute-start.39 = (bf16[512,1024]{1,0:T(8,128)(2,1)}, bf16[512,1024]{1,0:T(8,128)(2,1)}, u32[]{:S(2)}, u32[]{:S(2)}) collective-permute-start(bf16[512,1024]{1,0:T(8,128)(2,1)} %get-tuple-element.209), channel_id=1, source_target_pairs={{0,16},{4,20},{8,24},{12,28},{16,0},{20,4},{24,8},{28,12},{1,17},{... | collective-permute-start | bytes 3145736 | tf_op jit(solution)/shard_map/ppermute | solution.py:837
  296.9 44.8 %collective-permute-start.40 = (bf16[512,1024]{1,0:T(8,128)(2,1)}, bf16[512,1024]{1,0:T(8,128)(2,1)}, u32[]{:S(2)}, u32[]{:S(2)}) collective-permute-start(bf16[512,1024]{1,0:T(8,128)(2,1)} %get-tuple-element.212), channel_id=1, source_target_pairs={{0,8},{4,12},{8,0},{12,4},{16,24},{20,28},{24,16},{28,20},{1,9},{5... | collective-permute-start | bytes 3145736 | tf_op jit(solution)/shard_map/ppermute | solution.py:837
  298.4 43.3 %collective-permute-start.41 = (bf16[512,1024]{1,0:T(8,128)(2,1)}, bf16[512,1024]{1,0:T(8,128)(2,1)}, u32[]{:S(2)}, u32[]{:S(2)}) collective-permute-start(bf16[512,1024]{1,0:T(8,128)(2,1)} %get-tuple-element.213), channel_id=1, source_target_pairs={{0,16},{4,20},{8,24},{12,28},{16,0},{20,4},{24,8},{28,12},{1,17},{... | collective-permute-start | bytes 3145736 | tf_op jit(solution)/shard_map/ppermute | solution.py:837
  364.8 26.4 %collective-permute-start.44 = (bf16[512,1024]{1,0:T(8,128)(2,1)}, bf16[512,1024]{1,0:T(8,128)(2,1)}, u32[]{:S(2)}, u32[]{:S(2)}) collective-permute-start(bf16[512,1024]{1,0:T(8,128)(2,1)} %get-tuple-element.228), channel_id=1, source_target_pairs={{0,8},{4,12},{8,0},{12,4},{16,24},{20,28},{24,16},{28,20},{1,9},{5... | collective-permute-start | bytes 3145736 | tf_op jit(solution)/shard_map/ppermute | solution.py:837
  365.5 30.0 %collective-permute-start.45 = (bf16[512,1024]{1,0:T(8,128)(2,1)}, bf16[512,1024]{1,0:T(8,128)(2,1)}, u32[]{:S(2)}, u32[]{:S(2)}) collective-permute-start(bf16[512,1024]{1,0:T(8,128)(2,1)} %get-tuple-element.229), channel_id=1, source_target_pairs={{0,16},{4,20},{8,24},{12,28},{16,0},{20,4},{24,8},{28,12},{1,17},{... | collective-permute-start | bytes 3145736 | tf_op jit(solution)/shard_map/ppermute | solution.py:837
  369.1 34.0 %collective-permute-start.48 = (bf16[256,1024]{1,0:T(8,128)(2,1)}, bf16[256,1024]{1,0:T(8,128)(2,1)}, u32[]{:S(2)}, u32[]{:S(2)}) collective-permute-start(bf16[256,1024]{1,0:T(8,128)(2,1)} %get-tuple-element.233), channel_id=1, source_target_pairs={{0,16},{4,20},{8,24},{12,28},{16,0},{20,4},{24,8},{28,12},{1,17},{... | collective-permute-start | bytes 1572872 | tf_op jit(solution)/shard_map/ppermute | solution.py:837
  371.9 33.2 %collective-permute-start.49 = (bf16[256,1024]{1,0:T(8,128)(2,1)}, bf16[256,1024]{1,0:T(8,128)(2,1)}, u32[]{:S(2)}, u32[]{:S(2)}) collective-permute-start(bf16[256,1024]{1,0:T(8,128)(2,1)} %get-tuple-element.234), channel_id=1, source_target_pairs={{0,8},{4,12},{8,0},{12,4},{16,24},{20,28},{24,16},{28,20},{1,9},{5... | collective-permute-start | bytes 1572872 | tf_op jit(solution)/shard_map/ppermute | solution.py:837
  376.4 37.9 %collective-permute-start.50 = (bf16[256,1024]{1,0:T(8,128)(2,1)}, bf16[256,1024]{1,0:T(8,128)(2,1)}, u32[]{:S(2)}, u32[]{:S(2)}) collective-permute-start(bf16[256,1024]{1,0:T(8,128)(2,1)} %get-tuple-element.238), channel_id=1, source_target_pairs={{0,16},{4,20},{8,24},{12,28},{16,0},{20,4},{24,8},{28,12},{1,17},{... | collective-permute-start | bytes 1572872 | tf_op jit(solution)/shard_map/ppermute | solution.py:837
  391.2 23.1 %collective-permute-start.51 = (bf16[256,1024]{1,0:T(8,128)(2,1)}, bf16[256,1024]{1,0:T(8,128)(2,1)}, u32[]{:S(2)}, u32[]{:S(2)}) collective-permute-start(bf16[256,1024]{1,0:T(8,128)(2,1)} %get-tuple-element.239), channel_id=1, source_target_pairs={{0,8},{4,12},{8,0},{12,4},{16,24},{20,28},{24,16},{28,20},{1,9},{5... | collective-permute-start | bytes 1572872 | tf_op jit(solution)/shard_map/ppermute | solution.py:837
  398.5 25.8 %collective-permute-start.46 = (bf16[256,1024]{1,0:T(8,128)(2,1)}, bf16[256,1024]{1,0:T(8,128)(2,1)S(1)}, u32[]{:S(2)}, u32[]{:S(2)}) collective-permute-start(bf16[256,1024]{1,0:T(8,128)(2,1)} %get-tuple-element.247), channel_id=1, source_target_pairs={{0,16},{4,20},{8,24},{12,28},{16,0},{20,4},{24,8},{28,12},{1,17},{... | collective-permute-start | bytes 1572872 | tf_op jit(solution)/shard_map/ppermute | solution.py:837
  403.1 21.2 %collective-permute-start.47 = (bf16[256,1024]{1,0:T(8,128)(2,1)}, bf16[256,1024]{1,0:T(8,128)(2,1)}, u32[]{:S(2)}, u32[]{:S(2)}) collective-permute-start(bf16[256,1024]{1,0:T(8,128)(2,1)} %get-tuple-element.248), channel_id=1, source_target_pairs={{0,8},{4,12},{8,0},{12,4},{16,24},{20,28},{24,16},{28,20},{1,9},{5... | collective-permute-start | bytes 1572872 | tf_op jit(solution)/shard_map/ppermute | solution.py:837
  458.9 13.8 %collective-permute-start.59 = (bf16[128,2048]{1,0:T(8,128)(2,1)S(1)}, bf16[128,2048]{1,0:T(8,128)(2,1)S(1)}, u32[]{:S(2)}, u32[]{:S(2)}) collective-permute-start(bf16[128,2048]{1,0:T(8,128)(2,1)S(1)} %get-tuple-element.274), channel_id=1, source_target_pairs={{0,8},{4,12},{8,0},{12,4},{16,24},{20,28},{24,16},{28,20},{1,9},{5... | collective-permute-start | bytes 1572872 | tf_op jit(solution)/shard_map/ppermute | solution.py:837
  (64 other events, 468.7 us)
Sparse Core Ops, SparseCore 0:
  54.0 44.1 all-gather.3
  100.4 44.6 all-gather.5
  147.3 79.4 all-gather.7
  228.9 75.2 reduce-scatter.2
  354.1 73.5 reduce-scatter.4

commit v6 on v5

--- a/solution.py
+++ b/solution.py
@@ -78,26 +78,23 @@
         out_ref[0, 0, :, p * wide : (p + 1) * wide] = plain[:, pl.ds(pl.multiple_of(place, wide), wide)]
 
 
-def norm_wave(rows_in, count, at, gain, shift, blocks, wave, held):
+def norm(rows_in, count, at, gain, shift, blocks):
     rows, width = rows_in.shape[0] // count, rows_in.shape[1]
     vector = pl.BlockSpec((1, width), lambda j, n: (0, 0))
-    extra = [] if held is None else [held]
     return pl.pallas_call(
         functools.partial(norm_kernel, blocks),
         grid_spec=pltpu.PrefetchScalarGridSpec(
             num_scalar_prefetch=1,
             grid=(count,),
-            in_specs=[pl.BlockSpec((rows, width), lambda j, n: (j, 0)), vector, vector]
-            + [pl.BlockSpec(memory_space=pl.ANY)] * len(extra),
-            out_specs=pl.BlockSpec((1, 1, rows, width), lambda j, n: (j, wave, 0, 0)),
+            in_specs=[pl.BlockSpec((rows, width), lambda j, n: (j, 0)), vector, vector],
+            out_specs=pl.BlockSpec((1, 1, rows, width), lambda j, n: (j, 0, 0, 0)),
             scratch_shapes=[pltpu.VMEM((rows, width), bf16)],
         ),
-        out_shape=shape((count, 2, rows, width), bf16),
-        input_output_aliases={4: 0} if extra else {},
+        out_shape=shape((count, 1, rows, width), bf16),
         compiler_params=params(32),
         cost_estimate=cost(10 * count * rows * width, 4 * count * rows * width),
-        name="norm_wave",
-    )(at, rows_in, gain, shift, *extra)
+        name="norm",
+    )(at, rows_in, gain, shift)
 
 
 def project_rows(kind, ln_ref, weight, bias_ref, tables, out_ref):
@@ -137,7 +134,7 @@
         ).wait()
 
 
-def project_first_kernel(qk_plan, vo_plan, ln_ref, bias_ref, c_ref, a_ref, b_ref, *rest):
+def project_kernel(qk_plan, vo_plan, ln_ref, bias_ref, c_ref, a_ref, b_ref, *rest):
     n = len({p[0] for p in qk_plan})
     qk_refs, vo_refs = rest[:n], rest[n : 2 * n]
     out_ref, w_ref, buffer, sems, out_sems = rest[2 * n :]
@@ -178,14 +175,14 @@
         project_rows(kind, ln_ref, buffer[kind % 2], bias_ref, (c_ref, a_ref, b_ref), out_ref)
 
 
-def project_first(ln, qk, vo, bias, tables):
+def project(ln, qk, vo, bias, tables):
     many, _, size, width = ln.shape
     heads = bias.shape[1]
     table = pl.BlockSpec((many, 1, size, PAIR), lambda i: (0, 0, 0, 0), pipeline_mode=once)
     hbm = pl.BlockSpec(memory_space=pl.ANY)
     last = lambda i: jnp.minimum(i, 2)
     return pl.pallas_call(
-        functools.partial(project_first_kernel, qk[1], vo[1]),
+        functools.partial(project_kernel, qk[1], vo[1]),
         grid=(4,),
         in_specs=[
             pl.BlockSpec((many, 1, size, width), lambda i: (0, 0, 0, 0), pipeline_mode=once),
@@ -199,7 +196,7 @@
             pl.BlockSpec((1, many, 1, size, heads), lambda i: (last(i), 0, 0, 0, 0)),
             hbm,
         ],
-        out_shape=[shape((3, many, 2, size, heads), bf16), shape((4, width, heads), bf16)],
+        out_shape=[shape((3, many, 1, size, heads), bf16), shape((4, width, heads), bf16)],
         scratch_shapes=[
             pltpu.VMEM((2, width, heads), bf16),
             pltpu.SemaphoreType.DMA((2, len(qk[1]))),
@@ -207,37 +204,8 @@
         ],
         compiler_params=params(48),
         cost_estimate=cost(6 * many * size * width * heads, 22 << 20),
-        name="project_first",
+        name="project",
     )(ln, bias[:, None, :], *tables, *qk[0], *vo[0])
-
-
-def project_second_kernel(ln_ref, w_ref, bias_ref, c_ref, a_ref, b_ref, held_ref, out_ref):
-    project_rows(pl.program_id(0), ln_ref, w_ref[0], bias_ref, (c_ref, a_ref, b_ref), out_ref)
-
-
-def project_second(ln, weights, bias, tables, held):
-    many, _, size, width = ln.shape
-    heads = bias.shape[1]
-    table = pl.BlockSpec((many, 1, size, PAIR), lambda i: (0, 1, 0, 0), pipeline_mode=once)
-    return pl.pallas_call(
-        project_second_kernel,
-        grid=(3,),
-        in_specs=[
-            pl.BlockSpec((many, 1, size, width), lambda i: (0, 1, 0, 0), pipeline_mode=once),
-            pl.BlockSpec((1, width, heads), lambda i: (i, 0, 0)),
-            pl.BlockSpec((1, 1, heads), lambda i: (i, 0, 0)),
-            table,
-            table,
-            table,
-            pl.BlockSpec(memory_space=pl.ANY),
-        ],
-        out_specs=pl.BlockSpec((1, many, 1, size, heads), lambda i: (i, 0, 1, 0, 0)),
-        out_shape=shape(held.shape, bf16),
-        input_output_aliases={6: 0},
-        compiler_params=params(48),
-        cost_estimate=cost(6 * many * size * width * heads, 12 << 20),
-        name="project_second",
-    )(ln, weights, bias[:, None, :], *tables, held)
 
 
 def side_lanes(side):
@@ -349,84 +317,97 @@
         name="attend_back")(length, qkv, qkv, qkv, grad_mixed, totals, *tables)
 
 
-def feed_kernel(tile, tile_f, steps, plan1, plan2, ln_ref, mixed_ref, wo_ref, bias_ref, *rest):
+def feed_kernel(steps, late_steps, plan1, plan2, ln_ref, mixed_ref, wo_ref, bias_ref, *rest):
     n1 = len({p[0] for p in plan1})
     w1_refs, w2_refs = rest[:n1], rest[n1 : 2 * n1]
-    (branch_ref, hidden_ref, slope_ref, full1_ref, full2_ref, acc, buf1, buf2, sems1, sems2,
+    (branch_ref, hidden_ref, slope_ref, full1_ref, full2_ref, held, buf1, buf2, sems1, sems2,
      out_sems) = rest[2 * n1 :]
     step = pl.program_id(0)
     slot = lax.rem(step, 2)
-    rows = ln_ref.shape[0]
+    tile_f = buf1.shape[2]
+    tile_d = buf2.shape[1]
     c0 = math.sqrt(2.0 / math.pi)
     c1 = 0.044715
-
-    def start(s, at):
+    plan2 = sorted(plan2, key=lambda p: p[2])
+    per_tile = len(plan2) // late_steps
+
+    def columns(s):
+        return pl.ds(pl.multiple_of(s * tile_f, tile_f), tile_f)
+
+    def start1(s):
+        at = lax.rem(s, 2)
         column = pl.multiple_of(s * tile_f, tile_f)
         assemble_start(w1_refs, plan1, column, tile_f, buf1.at[at], sems1.at[at])
-        assemble_start(w2_refs, plan2, column, tile_f, buf2.at[at], sems2.at[at])
-
-    def outward(s, at):
-        column = pl.multiple_of(s * tile_f, tile_f)
-        return (
-            pltpu.make_async_copy(
-                buf1.at[at], full1_ref.at[:, pl.ds(column, tile_f)], out_sems.at[at, 0]
-            ),
-            pltpu.make_async_copy(
-                buf2.at[at], full2_ref.at[:, pl.ds(column, tile_f)], out_sems.at[at, 1]
-            ),
+
+    def pieces2(tile):
+        at = tile % 2
+        for j, (which, row, place, count) in enumerate(plan2[tile * per_tile : (tile + 1) * per_tile]):
+            yield pltpu.make_async_copy(
+                w2_refs[which].at[pl.ds(row, count), :],
+                buf2.at[at, pl.ds(place - tile * tile_d, count), :],
+                sems2.at[at, j],
+            )
+
+    def out1(s, at):
+        return pltpu.make_async_copy(buf1.at[at], full1_ref.at[:, columns(s)], out_sems.at[at])
+
+    def out2(tile):
+        return pltpu.make_async_copy(
+            buf2.at[tile % 2], full2_ref.at[pl.ds(tile * tile_d, tile_d), :], out_sems.at[2 + tile % 2]
         )
 
     @pl.when(step == 0)
     def _():
-        start(0, 0)
-
-    column = pl.multiple_of(step * tile_f, tile_f)
-    assemble_wait(w1_refs, plan1, column, tile_f, buf1.at[slot], sems1.at[slot])
-    assemble_wait(w2_refs, plan2, column, tile_f, buf2.at[slot], sems2.at[slot])
-    for copy in outward(step, slot):
-        copy.start()
-
-    @pl.when(step > 0)
+        start1(0)
+        for copy in pieces2(0):
+            copy.start()
+
+    @pl.when(step < steps)
     def _():
-        for copy in outward(step - 1, 1 - slot):
-            copy.wait()
-
-    @pl.when(step < steps - 1)
-    def _():
-        start(step + 1, 1 - slot)
-
-    for first in range(0, rows, tile):
-        r = slice(first, first + tile)
-        pre = dot(ln_ref[r, :], buf1[slot], NN) + bias_ref[...]
+        column = pl.multiple_of(step * tile_f, tile_f)
+        assemble_wait(w1_refs, plan1, column, tile_f, buf1.at[slot], sems1.at[slot])
+        out1(step, slot).start()
+
+        @pl.when(step > 0)
+        def _():
+            out1(step - 1, 1 - slot).wait()
+
+        @pl.when(step < steps - 1)
+        def _():
+            start1(step + 1)
+
+        pre = dot(ln_ref[...], buf1[slot], NN) + bias_ref[...]
         square = pre * pre
         bent = jnp.tanh(c0 * (pre + c1 * (square * pre)))
         half_pre = 0.5 * pre
         hidden = (half_pre * (1.0 + bent)).astype(bf16)
-        hidden_ref[r, :] = hidden
-        slope_ref[r, :] = 0.5 * (1.0 + bent) + half_pre * (1.0 - bent * bent) * (
+        hidden_ref[...] = hidden
+        held[step] = hidden
+        slope_ref[...] = 0.5 * (1.0 + bent) + half_pre * (1.0 - bent * bent) * (
             c0 * (1.0 + (3.0 * c1) * square)
         )
 
-    for first in range(0, rows, tile):
-        r = slice(first, first + tile)
-        part = dot(hidden_ref[r, :], buf2[slot], NT)
-
-        @pl.when(step == 0)
-        def _():
-            acc[r, :] = part + dot(mixed_ref[r, :], wo_ref[0], NT)
-
-        @pl.when((step > 0) & (step < steps - 1))
-        def _():
-            acc[r, :] += part
-
         @pl.when(step == steps - 1)
         def _():
-            branch_ref[r, :] = (acc[r, :] + part).astype(bf16)
-
-    @pl.when(step == steps - 1)
-    def _():
-        for copy in outward(step, slot):
-            copy.wait()
+            out1(step, slot).wait()
+
+    for tile in range(late_steps):
+        @pl.when(step == steps + tile)
+        def _():
+            for copy in pieces2(tile):
+                copy.wait()
+            out2(tile).start()
+            if tile > 0:
+                out2(tile - 1).wait()
+            if tile < late_steps - 1:
+                for copy in pieces2(tile + 1):
+                    copy.start()
+            total = dot(mixed_ref[...], wo_ref[0], NT)
+            for k in range(steps):
+                total += dot(held[k], buf2[tile % 2, :, k * tile_f : (k + 1) * tile_f], NT)
+            branch_ref[...] = total.astype(bf16)
+            if tile == late_steps - 1:
+                out2(tile).wait()
 
 
 def feed(ln, mixed, weights, w1, w2, bias, tile_f):
@@ -434,20 +415,26 @@
     hidden = bias.shape[1]
     heads = mixed.shape[1]
     steps = hidden // tile_f
+    tile_d = 512
+    late_steps = width // tile_d
     whole = lambda dims: pl.BlockSpec(dims, lambda i: (0, 0), pipeline_mode=once)
-    by_row = pl.BlockSpec((rows, tile_f), lambda i: (0, i))
+    early = lambda i: jnp.minimum(i, steps - 1)
+    late = lambda i: jnp.maximum(i - steps, 0)
+    by_row = pl.BlockSpec((rows, tile_f), lambda i: (0, early(i)))
     hbm = pl.BlockSpec(memory_space=pl.ANY)
     return pl.pallas_call(
-        functools.partial(feed_kernel, rows, tile_f, steps, w1[1], w2[1]),
-        grid=(steps,),
+        functools.partial(feed_kernel, steps, late_steps, w1[1], w2[1]),
+        grid=(steps + late_steps,),
         in_specs=[
             whole((rows, width)),
             whole((rows, heads)),
-            pl.BlockSpec((1, width, heads), lambda i: (3, 0, 0), pipeline_mode=once),
-            pl.BlockSpec((1, tile_f), lambda i: (0, i)),
+            pl.BlockSpec((1, tile_d, heads), lambda i: (3, late(i), 0)),
+            pl.BlockSpec((1, tile_f), lambda i: (0, early(i))),
         ]
         + [hbm] * (len(w1[0]) + len(w2[0])),
-        out_specs=[whole((rows, width)), by_row, by_row, hbm, hbm],
+        out_specs=[
+            pl.BlockSpec((rows, tile_d), lambda i: (0, late(i))), by_row, by_row, hbm, hbm
+        ],
         out_shape=[
             shape((rows, width), bf16),
             shape((rows, hidden), bf16),
@@ -456,12 +443,12 @@
             shape((width, hidden), bf16),
         ],
         scratch_shapes=[
-            pltpu.VMEM((rows, width), f32),
+            pltpu.VMEM((steps, rows, tile_f), bf16),
             pltpu.VMEM((2, width, tile_f), bf16),
-            pltpu.VMEM((2, width, tile_f), bf16),
+            pltpu.VMEM((2, tile_d, hidden), bf16),
             pltpu.SemaphoreType.DMA((2, len(w1[1]))),
-            pltpu.SemaphoreType.DMA((2, len(w2[1]))),
-            pltpu.SemaphoreType.DMA((2, 2)),
+            pltpu.SemaphoreType.DMA((2, len(w2[1]) // late_steps)),
+            pltpu.SemaphoreType.DMA((4,)),
         ],
         compiler_params=params(58),
         cost_estimate=cost(4 * rows * width * hidden, 56 << 20, rows * hidden),
@@ -469,54 +456,54 @@
     )(ln, mixed, weights, bias, *w1[0], *w2[0])
 
 
-def back_kernel(tile, g_ref, w1_ref, w2_ref, slope_ref, wo_ref, sum_ref, pre_ref, mixed_ref, bias_ref):
+def back_kernel(steps, g_ref, w1_ref, w2_ref, slope_ref, wo_ref, sum_ref, pre_ref, mixed_ref, bias_ref, held):
     step = pl.program_id(0)
-    rows = g_ref.shape[0]
+    tile = pre_ref.shape[1]
 
     @pl.when(step == 0)
     def _():
         mixed_ref[...] = dot(g_ref[...], wo_ref[0], NN).astype(bf16)
 
-    for first in range(0, rows, tile):
-        r = slice(first, first + tile)
-        pre_ref[r, :] = (dot(g_ref[r, :], w2_ref[...], NN) * slope_ref[r, :]).astype(bf16)
-
-    bias_ref[...] = jnp.sum(pre_ref[...].astype(f32), axis=0, keepdims=True)
-    for first in range(0, rows, tile):
-        r = slice(first, first + tile)
-        part = dot(pre_ref[r, :], w1_ref[...], NT)
-
-        @pl.when(step == 0)
-        def _():
-            sum_ref[r, :] = part
-
-        @pl.when(step > 0)
-        def _():
-            sum_ref[r, :] += part
+    @pl.when(step < steps)
+    def _():
+        grad = (dot(g_ref[...], w2_ref[...], NN) * slope_ref[...]).astype(bf16)
+        pre_ref[...] = grad
+        held[step] = grad
+        bias_ref[...] = jnp.sum(grad.astype(f32), axis=0, keepdims=True)
+
+    @pl.when(step >= steps)
+    def _():
+        total = dot(held[0], w1_ref[:, :tile], NT)
+        for k in range(1, steps):
+            total += dot(held[k], w1_ref[:, k * tile : (k + 1) * tile], NT)
+        sum_ref[...] = total
 
 
 def back(grads, w1, w2, slope, weights, tile_f):
     rows, width = grads.shape
     units = slope.shape[1]
     heads = weights.shape[2]
-    weight = pl.BlockSpec((width, tile_f), lambda i: (0, i))
+    steps = units // tile_f
+    tile_d = 512
     whole = lambda dims: pl.BlockSpec(dims, lambda i: (0, 0), pipeline_mode=once)
-    by_row = pl.BlockSpec((rows, tile_f), lambda i: (0, i))
+    early = lambda i: jnp.minimum(i, steps - 1)
+    late = lambda i: jnp.maximum(i - steps, 0)
+    by_row = pl.BlockSpec((rows, tile_f), lambda i: (0, early(i)))
     return pl.pallas_call(
-        functools.partial(back_kernel, rows),
-        grid=(units // tile_f,),
+        functools.partial(back_kernel, steps),
+        grid=(steps + width // tile_d,),
         in_specs=[
             whole((rows, width)),
-            weight,
-            weight,
+            pl.BlockSpec((tile_d, units), lambda i: (late(i), 0)),
+            pl.BlockSpec((width, tile_f), lambda i: (0, early(i))),
             by_row,
             pl.BlockSpec((1, width, heads), lambda i: (3, 0, 0), pipeline_mode=once),
         ],
         out_specs=[
-            whole((rows, width)),
+            pl.BlockSpec((rows, tile_d), lambda i: (0, late(i))),
             by_row,
             whole((rows, heads)),
-            pl.BlockSpec((1, tile_f), lambda i: (0, i)),
+            pl.BlockSpec((1, tile_f), lambda i: (0, early(i))),
         ],
         out_shape=[
             shape((rows, width), f32),
@@ -524,6 +511,7 @@
             shape((rows, heads), bf16),
             shape((1, units), f32),
         ],
+        scratch_shapes=[pltpu.VMEM((steps, rows, tile_f), bf16)],
         compiler_params=params(58),
         cost_estimate=cost(4 * rows * width * units, 40 << 20),
         name="back",
@@ -881,6 +869,11 @@
     return stacks + [(flip(rows, "dp", bit), [m | (1 << bit) for m in masks]) for rows, masks in stacks]
 
 
+def joined_step(stacks, bit):
+    rows = jnp.concatenate([s[0] for s in stacks], 0)
+    return stacks + [(flip(rows, "dp", bit), [m | (1 << bit) for s in stacks for m in s[1]])]
+
+
 def gather_plan(stacks, block, bits):
     plan = []
     for which, (_, masks) in enumerate(stacks):
@@ -1008,9 +1001,7 @@
     routed = receive(firsts, seq_of_slot)
     routed, stack = after((routed, stack))
     extra_rows = 16
-    rows_a, rows_b = routed[:wave_rows], routed[wave_rows:]
-    full_a = lax.all_gather(rows_a, "tensor", axis=0, tiled=True)
-    full_b = lax.all_gather(rows_b, "tensor", axis=0, tiled=True)
+    full = lax.all_gather(routed, "tensor", axis=0, tiled=True)
 
     stack = swap_blocks(stack, tensor_index, 0, tensor_count).reshape(-1)
     extra = jnp.pad(stack, (0, extra_rows * 2 * heads_local - stack.shape[0]))
@@ -1031,8 +1022,10 @@
         fresh = [[(out.pop(0), masks) for _, masks in stacks] for stacks in groups]
         return fresh, out
 
-    (qk_stacks, vo_stacks), (fc1_shard, fc2_shard, row_ids) = held_back(
-        (qk_stacks, vo_stacks), fc1_weight, fc2_weight, jnp.arange(seq_len, dtype=jnp.int32)
+    row_ids, = after((jnp.arange(seq_len, dtype=jnp.int32),), qk_shard)
+    tables = rotary_tables(row_ids, PAIR)
+    (qk_stacks, vo_stacks), (fc1_shard, fc2_shard, *tables) = held_back(
+        (qk_stacks, vo_stacks), fc1_weight, fc2_weight, *tables
     )
     qk_stacks = qk_stacks + core_copies(qk_stacks)
     qk = gather_plan(qk_stacks, block, bits)
@@ -1066,19 +1059,16 @@
         1,
     ).astype(f32)
 
-    tables = after(rotary_tables(row_ids, PAIR))
-    wave_tables = [v.reshape(tensor_count, 2, wave_rows, PAIR) for v in tables]
+    row_tables = [v.reshape(tensor_count, 1, rows_here, PAIR) for v in tables]
     size = length.reshape(1)
-    ln_a = norm_wave(full_a, tensor_count, at, gain, shift, data_count, 0, None)
-    qkv_a, weights = project_first(ln_a, qk, vo, bias_qkv, wave_tables)
-    (fc1_stacks, fc2_stacks), (weights,) = held_back((fc1_stacks, fc2_stacks), weights)
+    (fc1_stacks, fc2_stacks), (gain, shift) = held_back((fc1_stacks, fc2_stacks), gain, shift)
     fc1_far, fc2_far = core_copies(fc1_stacks), core_copies(fc2_stacks)
     for step in range(1, len(x_first)):
-        fc1_stacks = gather_step(fc1_stacks, x_first[step])
-        fc2_stacks = gather_step(fc2_stacks, y_first[step])
-    (fc1_far, fc2_far), (full_b,) = held_back((fc1_far, fc2_far), full_b)
-    ln = norm_wave(full_b, tensor_count, at, gain, shift, data_count, 1, ln_a)
-    qkv = project_second(ln, weights, bias_qkv, wave_tables, qkv_a)
+        fc1_stacks = joined_step(fc1_stacks, x_first[step])
+        fc2_stacks = joined_step(fc2_stacks, y_first[step])
+    ln = norm(full, tensor_count, at, gain, shift, data_count)
+    (fc1_far, fc2_far), (ln,) = held_back((fc1_far, fc2_far), ln)
+    qkv, weights = project(ln, qk, vo, bias_qkv, row_tables)
     ln, qkv = ln.reshape(seq_len, width), qkv.reshape(3, seq_len, heads_local)
     mixed, totals = attend(qkv, size)
     (fc1_stacks, fc2_stacks), (mixed,) = held_back((fc1_stacks, fc2_stacks), mixed)

time: 489 us -> 481 us (0.984)
  Pallas kernels: 237 us -> 224 us
  other arithmetic: 14.9 us -> 21.7 us
    pallas_call x6 -> x4, Pallas kernels: 101 us -> 87.5 us  [the longest x1 33.3 us: feed(): pl.pallas_call(functools.partial(feed_kernel, steps, late_steps, w1[1], w...]
    ppermute x63 -> x59, waiting for transfers between devices: 117 us -> 129 us  [flip(): lax.ppermute(array, axis_name, [(i, i ^ 1 << bit) for i in range(size)])]
    all_gather x2 -> x1, waiting for transfers between devices: 11.3 us -> 0.01 us  [shards(): full = lax.all_gather(routed, 'tensor', axis=0, tiled=True)]
    unnamed x85 -> x93, local copies, waits for them, and re-layouts: 10.9 us -> 16 us
    ppermute x63 -> x59, starting transfers between devices: 54.3 us -> 51.7 us  [flip(): lax.ppermute(array, axis_name, [(i, i ^ 1 << bit) for i in range(size)])]
  transfers between devices with their start and end apart: 68 -> 63, of which waited for: 40 -> 33; matrix products, arithmetic and copies ran while one was open for 6% -> 7% of each run, Pallas kernels for 45% -> 43%
where the time goes in v6:
time: 481 us; the launch traced here: 476 us
  Pallas kernels  224 us (47%)
  waiting for transfers between devices  129 us (27%)
  starting transfers between devices  52.1 us (11%)
  local copies, waits for them, and re-layouts  28.5 us (6%)
  other arithmetic  21.7 us (5%)
  between operations  21 us (4%)
    ppermute x59, waiting for transfers between devices, flip(): lax.ppermute(array, axis_name, [(i, i ^ 1 << bit) for i in range(size)])  129 us
    ppermute x59, starting transfers between devices, flip(): lax.ppermute(array, axis_name, [(i, i ^ 1 << bit) for i in range(size)])  51.7 us
    pallas_call x1, Pallas kernels, feed(): pl.pallas_call(functools.partial(feed_kernel, steps, late_steps, w1[1], w...  33.3 us
    pallas_call x1, Pallas kernels, back(): pl.pallas_call(functools.partial(back_kernel, steps), grid=(steps + width...  30.2 us
    pallas_call x1, Pallas kernels, attend_back(): pl.pallas_call(functools.partial(attend_back_kernel, min(block, rows)), g...  26.8 us
    pallas_call x2, Pallas kernels, feed_weight(): pl.pallas_call(feed_weight_kernel, grid=(units // tile_f,), in_specs=[pl....  26.3 us
    pallas_call x6, Pallas kernels, give(): pl.pallas_call(functools.partial(give_kernel, tuple(numbers)), grid=(out_...  19.4 us
    pallas_call x1, Pallas kernels, attend(): pl.pallas_call(functools.partial(attend_kernel, min(block, rows)), grid_s...  16.6 us
  transfers between devices with their start and end apart: 63, of which 33 were waited for; matrix products, arithmetic and copies ran while one was open for 7% of the time, Pallas kernels for 43%

profile of v6, /device:TPU:0, one launch (start us, length us, event | category | flops | bytes accessed | tf_op | source)
XLA Modules:
  0.0 476.4 jit_solution(772978109498214495)
XLA Ops:
  13.1 10.4 %collective-permute-done.3 = bf16[128,2048]{1,0:T(8,128)(2,1)S(1)} collective-permute-done((bf16[128,2048]{1,0:T(8,128)(2,1)S(1)}, bf16[128,2048]{1,0:T(8,128)(2,1)S(1)}, u32[]{:S(2)}, u32[]{:S(2)}) %collective-permute-start.3) | collective-permute-done | bytes 524320 | tf_op jit(solution)/shard_map/ppermute | solution.py:825
  40.9 7.9 %collective-permute-done.5 = bf16[128,2048]{1,0:T(8,128)(2,1)S(1)} collective-permute-done((bf16[128,2048]{1,0:T(8,128)(2,1)S(1)}, bf16[128,2048]{1,0:T(8,128)(2,1)S(1)}, u32[]{:S(2)}, u32[]{:S(2)}) %collective-permute-start.5) | collective-permute-done | bytes 524320 | tf_op jit(solution)/shard_map/ppermute | solution.py:825
  66.1 16.3 %collective-permute-done.11.rest_9_ = bf16[256,1024]{1,0:T(8,128)(2,1)} collective-permute-done((bf16[256,1024]{1,0:T(8,128)(2,1)}, bf16[256,1024]{1,0:T(8,128)(2,1)}, u32[]{:S(2)}, u32[]{:S(2)}) %collective-permute-start.11) | collective-permute-done | bytes 524320 | tf_op jit(solution)/shard_map/ppermute | solution.py:825
  88.3 3.2 fusion
  106.8 17.1 %collective-permute-done.14.rest_1_ = bf16[256,2048]{1,0:T(8,128)(2,1)S(1)} collective-permute-done((bf16[256,2048]{1,0:T(8,128)(2,1)S(1)}, bf16[256,2048]{1,0:T(8,128)(2,1)S(1)}, u32[]{:S(2)}, u32[]{:S(2)}) %collective-permute-start.14) | collective-permute-done | bytes 1048608 | tf_op jit(solution)/shard_map/ppermute | solution.py:825
  137.1 7.4 %norm.1.ln_ref = bf16[4,1,256,2048]{3,2,1,0:T(8,128)(2,1)} custom-call(s32[3]{0:T(128)} %pad_add_fusion.at_ref, bf16[1024,2048]{1,0:T(8,128)(2,1)} %all-gather.3.cloned.1.call-done.x_ref, f32[1,2048]{1,0:T(1,128)} %reshape.253.gain_ref, f32[1,2048]{1,0:T(1,128)} %reshape.254.shift_ref), custom_call_target="tpu_custom_call" | custom-call | flops 8388608 | bytes 3355443 | tf_op jit(solution)/shard_map/norm/pallas_call | solution.py:84
  145.4 16.5 %project.1 = (bf16[3,4,1,256,512]{4,3,2,1,0:T(8,128)(2,1)}, bf16[4,2048,512]{2,1,0:T(8,128)(2,1)}) custom-call(bf16[4,1,256,2048]{3,2,1,0:T(8,128)(2,1)} %norm.1.ln_ref, f32[3,1,512]{2,1,0:T(1,128)} %reshape.255.bias_ref, f32[4,1,256,128]{3,2,1,0:T(8,128)} %bitcast.153, f32[4,1,256,128]{3,2,1,0:T(8,128)} %bitcast.152, f32[4,1,256,128]{3,2,1,0:T(8,128)} %bitcast.151, ...), custom_call_target="tpu_custom_call" | custom-call | flops 2576980480 | bytes 9227468 | tf_op jit(solution)/shard_map/project/pallas_call | solution.py:184
  161.9 16.6 %attend.1 = (bf16[1024,512]{1,0:T(8,128)(2,1)}, f32[4,2,1024]{2,1,0:T(2,128)}) custom-call(s32[1]{0:T(128)} %dynamic_slice.97.len_ref, bf16[3,1024,512]{2,1,0:T(8,128)(2,1)} %bitcast.192, bf16[3,1024,512]{2,1,0:T(8,128)(2,1)} %bitcast.193, bf16[3,1024,512]{2,1,0:T(8,128)(2,1)} %bitcast.194), custom_call_target="tpu_custom_call" | custom-call | flops 3435973888 | bytes 1677721 | tf_op jit(solution)/shard_map/attend/pallas_call | solution.py:251
  181.0 3.3 collective-permute-done.30.rest_5_
  187.3 33.3 %feed.1 = (bf16[1024,2048]{1,0:T(8,128)(2,1)}, bf16[1024,2048]{1,0:T(8,128)(2,1)}, f32[1024,2048]{1,0:T(8,128)}, bf16[2048,2048]{1,0:T(8,128)(2,1)}, bf16[2048,2048]{1,0:T(8,128)(2,1)}) custom-call(bf16[1024,2048]{1,0:T(8,128)(2,1)} %bitcast.147, bf16[1024,512]{1,0:T(8,128)(2,1)} %get-tuple-element.177.mixed_ref, ...), custom_call_target="tpu_custom_call" | custom-call | flops 6871947776 | bytes 23488102 | tf_op jit(solution)/shard_map/feed/pallas_call | solution.py:425
  220.7 30.2 %back.1 = (f32[1024,2048]{1,0:T(8,128)}, bf16[1024,2048]{1,0:T(8,128)(2,1)}, bf16[1024,512]{1,0:T(8,128)(2,1)}, f32[1,2048]{1,0:T(1,128)}) custom-call(bf16[1024,2048]{1,0:T(8,128)(2,1)} %all-gather.5.cloned.1.call-done.g_ref.left_ref, bf16[2048,2048]{1,0:T(8,128)(2,1)} %get-tuple-element.192.w1_ref, bf16[2048,2048]{1,0:T(8,128)(2,1)} %get-tuple-element.193.w2_ref, ...), custom_call_target="tpu_custom_call" | custom-call | flops 6871947776 | bytes 16777216 | tf_op jit(solution)/shard_map/back/pallas_call | solution.py:492
  250.9 13.1 %feed_weight.2 = (bf16[1024,2048]{1,0:T(8,128)(2,1)}, bf16[1024,2048]{1,0:T(8,128)(2,1)}) custom-call(bf16[1024,2048]{1,0:T(8,128)(2,1)} %all-gather.5.cloned.1.call-done.g_ref.left_ref, bf16[1024,2048]{1,0:T(8,128)(2,1)} %get-tuple-element.198.right_ref), custom_call_target="tpu_custom_call" | custom-call | flops 3435973888 | bytes 6710886 | tf_op jit(solution)/shard_map/feed_weight/pallas_call | solution.py:531
  264.2 13.2 %feed_weight.3 = (bf16[1024,2048]{1,0:T(8,128)(2,1)}, bf16[1024,2048]{1,0:T(8,128)(2,1)}) custom-call(bf16[1024,2048]{1,0:T(8,128)(2,1)} %bitcast.148, bf16[1024,2048]{1,0:T(8,128)(2,1)} %get-tuple-element.200.right_ref), custom_call_target="tpu_custom_call" | custom-call | flops 3435973888 | bytes 6710886 | tf_op jit(solution)/shard_map/feed_weight/pallas_call | solution.py:531
  277.7 3.4 give.6
  281.8 3.0 collective-permute-done.32.refs_1_.refs_3_.refs_4_
  284.9 3.3 give.7
  289.0 26.8 %attend_back.1.grad_ref = bf16[3,1024,512]{2,1,0:T(8,128)(2,1)} custom-call(s32[1]{0:T(128)} %dynamic_slice.97.len_ref, bf16[3,1024,512]{2,1,0:T(8,128)(2,1)} %bitcast.195, bf16[3,1024,512]{2,1,0:T(8,128)(2,1)} %bitcast.196, bf16[3,1024,512]{2,1,0:T(8,128)(2,1)} %bitcast.197, bf16[1024,512]{1,0:T(8,128)(2,1)} %get-tuple-element.212.do_ref, ...), custom_call_target="tpu_custom_call" | custom-call | flops 8589934592 | bytes 3355443 | tf_op jit(solution)/shard_map/attend_back/pallas_call | solution.py:309
  315.8 15.0 %weight_grad.1 = (bf16[1024,1024]{1,0:T(8,128)(2,1)}, bf16[1024,1024]{1,0:T(8,128)(2,1)}, bf16[1024,1024]{1,0:T(8,128)(2,1)}, bf16[1024,1024]{1,0:T(8,128)(2,1)}, f32[3,1,512]{2,1,0:T(1,128)}) custom-call(bf16[1024,2048]{1,0:T(8,128)(2,1)} %bitcast.149, bf16[1024,2048]{1,0:T(8,128)(2,1)} %all-gather.5.cloned.1.call-done.g_ref.left_ref, ...), custom_call_target="tpu_custom_call" | custom-call | flops 3435973888 | bytes 8388608 | tf_op jit(solution)/shard_map/weight_grad/pallas_call | solution.py:600
  330.9 12.2 %ln_grad.1 = bf16[1024,2048]{1,0:T(8,128)(2,1)} custom-call(bf16[3,1024,512]{2,1,0:T(8,128)(2,1)} %attend_back.1.grad_ref, bf16[4,2048,512]{2,1,0:T(8,128)(2,1)} %get-tuple-element.178.wo_ref.w_ref, f32[1024,2048]{1,0:T(8,128)} %get-tuple-element.221.sum_ref), custom_call_target="tpu_custom_call" | custom-call | flops 2576980480 | bytes 9227468 | tf_op jit(solution)/shard_map/ln_grad/pallas_call | solution.py:557
  350.4 3.5 give.8
  357.3 3.1 give.9
  362.5 3.1 give.10
  367.5 12.9 %collective-permute-done.40.refs_2_ = bf16[512,1024]{1,0:T(8,128)(2,1)} collective-permute-done((bf16[512,1024]{1,0:T(8,128)(2,1)}, bf16[512,1024]{1,0:T(8,128)(2,1)}, u32[]{:S(2)}, u32[]{:S(2)}) %collective-permute-start.40) | collective-permute-done | bytes 1048608 | tf_op jit(solution)/shard_map/ppermute | solution.py:825
  381.8 3.7 finish.1
  394.3 10.1 %collective-permute-done.46.refs_3_ = bf16[256,1024]{1,0:T(8,128)(2,1)} collective-permute-done((bf16[256,1024]{1,0:T(8,128)(2,1)}, bf16[256,1024]{1,0:T(8,128)(2,1)}, u32[]{:S(2)}, u32[]{:S(2)}) %collective-permute-start.46) | collective-permute-done | bytes 524320 | tf_op jit(solution)/shard_map/ppermute | solution.py:825
  404.3 3.6 final.2
  407.9 3.6 final.3
  415.2 3.8 final_attention.1
  419.5 5.2 %norm_back.1 = (bf16[128,2048]{1,0:T(8,128)(2,1)}, bf16[128,2048]{1,0:T(8,128)(2,1)}, f32[2,2048]{1,0:T(2,128)}) custom-call(s32[3]{0:T(128)} %pad_add_fusion.at_ref, bf16[256,2048]{1,0:T(8,128)(2,1)} %reduce-scatter.5.cloned.1.call-done.sum_ref, bf16[256,2048]{1,0:T(8,128)(2,1)} %pad_maximum_fusion.6.rows_ref, bf16[256,2048]{1,0:T(8,128)(2,1)} %bitcast.150, ...), custom_call_target="tpu_custom_call" | custom-call | flops 4194304 | bytes 1677721 | tf_op jit(solution)/shard_map/norm_back/pallas_call | solution.py:695
  436.1 5.6 %collective-permute-done.48 = bf16[128,2048]{1,0:T(8,128)(2,1)S(1)} collective-permute-done((bf16[128,2048]{1,0:T(8,128)(2,1)S(1)}, bf16[128,2048]{1,0:T(8,128)(2,1)S(1)}, u32[]{:S(2)}, u32[]{:S(2)}) %collective-permute-start.48) | collective-permute-done | bytes 524320 | tf_op jit(solution)/shard_map/ppermute | solution.py:825
  459.2 5.2 %collective-permute-done.55 = bf16[128,2048]{1,0:T(8,128)(2,1)S(1)} collective-permute-done((bf16[128,2048]{1,0:T(8,128)(2,1)S(1)}, bf16[128,2048]{1,0:T(8,128)(2,1)S(1)}, u32[]{:S(2)}, u32[]{:S(2)}) %collective-permute-start.55) | collective-permute-done | bytes 524320 | tf_op jit(solution)/shard_map/ppermute | solution.py:825
  464.5 3.4 collective-permute-done.54
  (330 shorter events, 136.1 us)
Async XLA Ops:
  7.2 129.9 %all-gather.3.cloned.1.call-start = ((), (), s32[]{:S(2)}) async-start(), calls=%async_computation.2 | async-start | bytes 5242880 | tf_op jit(solution)/shard_map/all_gather | solution.py:1004
  8.6 15.0 %collective-permute-start.3 = (bf16[128,2048]{1,0:T(8,128)(2,1)S(1)}, bf16[128,2048]{1,0:T(8,128)(2,1)S(1)}, u32[]{:S(2)}, u32[]{:S(2)}) collective-permute-start(bf16[128,2048]{1,0:T(8,128)(2,1)S(1)} %get-tuple-element.288), channel_id=1, source_target_pairs={{0,16},{4,20},{8,24},{12,28},{16,0},{20,4},{24,8},{28,12},{1,17},{... | collective-permute-start | bytes 1572872 | tf_op jit(solution)/shard_map/ppermute | solution.py:825
  11.6 13.4 %collective-permute-start = (bf16[128,2048]{1,0:T(8,128)(2,1)S(1)}, bf16[128,2048]{1,0:T(8,128)(2,1)S(1)}, u32[]{:S(2)}, u32[]{:S(2)}) collective-permute-start(bf16[128,2048]{1,0:T(8,128)(2,1)S(1)} %get-tuple-element.287), channel_id=1, source_target_pairs={{0,8},{4,12},{8,0},{12,4},{16,24},{20,28},{24,16},{28,20},{1,9},{5... | collective-permute-start | bytes 1572872 | tf_op jit(solution)/shard_map/ppermute | solution.py:825
  25.1 12.8 %collective-permute-start.1 = (bf16[2,128,2048]{2,1,0:T(8,128)(2,1)S(1)}, bf16[2,128,2048]{2,1,0:T(8,128)(2,1)}, u32[]{:S(2)}, u32[]{:S(2)}) collective-permute-start(bf16[2,128,2048]{2,1,0:T(8,128)(2,1)S(1)} %pad_maximum_fusion.4), channel_id=1, source_target_pairs={{0,4},{4,0},{8,12},{12,8},{16,20},{20,16},{24,28},{28,24},{1,5},{5... | collective-permute-start | bytes 3145736 | tf_op jit(solution)/shard_map/ppermute | solution.py:825
  52.8 167.8 %all-gather.5.cloned.1.call-start = ((), (), s32[]{:S(2)}) async-start(), calls=%async_computation.3 | async-start | bytes 5242880 | tf_op jit(solution)/shard_map/all_gather | solution.py:1046
  58.6 25.8 %collective-permute-start.8 = (bf16[272,1024]{1,0:T(8,128)(2,1)}, bf16[272,1024]{1,0:T(8,128)(2,1)}, u32[]{:S(2)}, u32[]{:S(2)}) collective-permute-start(bf16[272,1024]{1,0:T(8,128)(2,1)} %pad_maximum_fusion.9.rest_0_), channel_id=1, source_target_pairs={{0,8},{4,12},{8,0},{12,4},{16,24},{20,28},{24,16},{28,20},{1,9},{5... | collective-permute-start | bytes 1671176 | tf_op jit(solution)/shard_map/ppermute | solution.py:825
  59.1 32.4 %collective-permute-start.9 = (bf16[272,1024]{1,0:T(8,128)(2,1)}, bf16[272,1024]{1,0:T(8,128)(2,1)}, u32[]{:S(2)}, u32[]{:S(2)}) collective-permute-start(bf16[272,1024]{1,0:T(8,128)(2,1)} %pad_maximum_fusion.9.rest_0_), channel_id=1, source_target_pairs={{0,16},{4,20},{8,24},{12,28},{16,0},{20,4},{24,8},{28,12},{1,17},{... | collective-permute-start | bytes 1671176 | tf_op jit(solution)/shard_map/ppermute | solution.py:825
  60.5 21.8 %collective-permute-start.11 = (bf16[256,1024]{1,0:T(8,128)(2,1)}, bf16[256,1024]{1,0:T(8,128)(2,1)}, u32[]{:S(2)}, u32[]{:S(2)}) collective-permute-start(bf16[256,1024]{1,0:T(8,128)(2,1)} %pad_maximum_fusion.10.rest_8_), channel_id=1, source_target_pairs={{0,16},{4,20},{8,24},{12,28},{16,0},{20,4},{24,8},{28,12},{1,17},{... | collective-permute-start | bytes 1572872 | tf_op jit(solution)/shard_map/ppermute | solution.py:825
  61.1 30.4 %collective-permute-start.12 = (bf16[256,1024]{1,0:T(8,128)(2,1)}, bf16[256,1024]{1,0:T(8,128)(2,1)}, u32[]{:S(2)}, u32[]{:S(2)}) collective-permute-start(bf16[256,1024]{1,0:T(8,128)(2,1)} %pad_maximum_fusion.10.rest_8_), channel_id=1, source_target_pairs={{0,8},{4,12},{8,0},{12,4},{16,24},{20,28},{24,16},{28,20},{1,9},{5... | collective-permute-start | bytes 1572872 | tf_op jit(solution)/shard_map/ppermute | solution.py:825
  87.9 243.0 %reduce-scatter.3.cloned.1.call-start = ((), (), s32[]{:S(2)}) async-start(), calls=%async_computation.4 | async-start | bytes 5242880 | tf_op jit(solution)/shard_map/reduce_scatter | solution.py:1081
  98.8 25.1 %collective-permute-start.14 = (bf16[256,2048]{1,0:T(8,128)(2,1)S(1)}, bf16[256,2048]{1,0:T(8,128)(2,1)S(1)}, u32[]{:S(2)}, u32[]{:S(2)}) collective-permute-start(bf16[256,2048]{1,0:T(8,128)(2,1)S(1)} %copy-done.1), channel_id=1, source_target_pairs={{0,8},{4,12},{8,0},{12,4},{16,24},{20,28},{24,16},{28,20},{1,9},{5... | collective-permute-start | bytes 3145736 | tf_op jit(solution)/shard_map/ppermute | solution.py:825
  100.1 25.0 %collective-permute-start.15 = (bf16[256,2048]{1,0:T(8,128)(2,1)S(1)}, bf16[256,2048]{1,0:T(8,128)(2,1)}, u32[]{:S(2)}, u32[]{:S(2)}) collective-permute-start(bf16[256,2048]{1,0:T(8,128)(2,1)S(1)} %copy-done.2), channel_id=1, source_target_pairs={{0,16},{4,20},{8,24},{12,28},{16,0},{20,4},{24,8},{28,12},{1,17},{... | collective-permute-start | bytes 3145736 | tf_op jit(solution)/shard_map/ppermute | solution.py:825
  130.3 48.4 %collective-permute-start.28 = (bf16[512,2048]{1,0:T(8,128)(2,1)}, bf16[512,2048]{1,0:T(8,128)(2,1)}, u32[]{:S(2)}, u32[]{:S(2)}) collective-permute-start(bf16[512,2048]{1,0:T(8,128)(2,1)} %pad_maximum_fusion.2), channel_id=1, source_target_pairs={{0,16},{4,20},{8,24},{12,28},{16,0},{20,4},{24,8},{28,12},{1,17},{... | collective-permute-start | bytes 6291464 | tf_op jit(solution)/shard_map/ppermute | solution.py:825
  131.7 48.1 %collective-permute-start.29 = (bf16[512,2048]{1,0:T(8,128)(2,1)}, bf16[512,2048]{1,0:T(8,128)(2,1)}, u32[]{:S(2)}, u32[]{:S(2)}) collective-permute-start(bf16[512,2048]{1,0:T(8,128)(2,1)} %pad_maximum_fusion.3), channel_id=1, source_target_pairs={{0,8},{4,12},{8,0},{12,4},{16,24},{20,28},{24,16},{28,20},{1,9},{5... | collective-permute-start | bytes 6291464 | tf_op jit(solution)/shard_map/ppermute | solution.py:825
  220.7 198.8 %reduce-scatter.5.cloned.1.call-start = ((), (), s32[]{:S(2)}) async-start(), calls=%async_computation.5 | async-start | bytes 5242880 | tf_op jit(solution)/shard_map/reduce_scatter | solution.py:1114
  264.0 13.7 %collective-permute-start.33 = (bf16[1024,2048]{1,0:T(8,128)(2,1)}, bf16[1024,2048]{1,0:T(8,128)(2,1)}, u32[]{:S(2)}, u32[]{:S(2)}) collective-permute-start(bf16[1024,2048]{1,0:T(8,128)(2,1)} %get-tuple-element.199), channel_id=1, source_target_pairs={{0,4},{4,0},{8,12},{12,8},{16,20},{20,16},{24,28},{28,24},{1,5},{5... | collective-permute-start | bytes 12582920 | tf_op jit(solution)/shard_map/ppermute | solution.py:825
  281.1 49.7 %collective-permute-start.34 = (bf16[512,1024]{1,0:T(8,128)(2,1)}, bf16[512,1024]{1,0:T(8,128)(2,1)}, u32[]{:S(2)}, u32[]{:S(2)}) collective-permute-start(bf16[512,1024]{1,0:T(8,128)(2,1)} %get-tuple-element.206), channel_id=1, source_target_pairs={{0,8},{4,12},{8,0},{12,4},{16,24},{20,28},{24,16},{28,20},{1,9},{5... | collective-permute-start | bytes 3145736 | tf_op jit(solution)/shard_map/ppermute | solution.py:825
  281.8 49.0 %collective-permute-start.35 = (bf16[512,1024]{1,0:T(8,128)(2,1)}, bf16[512,1024]{1,0:T(8,128)(2,1)}, u32[]{:S(2)}, u32[]{:S(2)}) collective-permute-start(bf16[512,1024]{1,0:T(8,128)(2,1)} %get-tuple-element.207), channel_id=1, source_target_pairs={{0,16},{4,20},{8,24},{12,28},{16,0},{20,4},{24,8},{28,12},{1,17},{... | collective-permute-start | bytes 3145736 | tf_op jit(solution)/shard_map/ppermute | solution.py:825
  288.2 42.7 %collective-permute-start.36 = (bf16[512,1024]{1,0:T(8,128)(2,1)}, bf16[512,1024]{1,0:T(8,128)(2,1)}, u32[]{:S(2)}, u32[]{:S(2)}) collective-permute-start(bf16[512,1024]{1,0:T(8,128)(2,1)} %get-tuple-element.210), channel_id=1, source_target_pairs={{0,8},{4,12},{8,0},{12,4},{16,24},{20,28},{24,16},{28,20},{1,9},{5... | collective-permute-start | bytes 3145736 | tf_op jit(solution)/shard_map/ppermute | solution.py:825
  288.9 42.0 %collective-permute-start.37 = (bf16[512,1024]{1,0:T(8,128)(2,1)}, bf16[512,1024]{1,0:T(8,128)(2,1)}, u32[]{:S(2)}, u32[]{:S(2)}) collective-permute-start(bf16[512,1024]{1,0:T(8,128)(2,1)} %get-tuple-element.211), channel_id=1, source_target_pairs={{0,16},{4,20},{8,24},{12,28},{16,0},{20,4},{24,8},{28,12},{1,17},{... | collective-permute-start | bytes 3145736 | tf_op jit(solution)/shard_map/ppermute | solution.py:825
  354.0 26.4 %collective-permute-start.40 = (bf16[512,1024]{1,0:T(8,128)(2,1)}, bf16[512,1024]{1,0:T(8,128)(2,1)}, u32[]{:S(2)}, u32[]{:S(2)}) collective-permute-start(bf16[512,1024]{1,0:T(8,128)(2,1)} %get-tuple-element.226), channel_id=1, source_target_pairs={{0,8},{4,12},{8,0},{12,4},{16,24},{20,28},{24,16},{28,20},{1,9},{5... | collective-permute-start | bytes 3145736 | tf_op jit(solution)/shard_map/ppermute | solution.py:825
  355.5 30.1 %collective-permute-start.41 = (bf16[512,1024]{1,0:T(8,128)(2,1)}, bf16[512,1024]{1,0:T(8,128)(2,1)}, u32[]{:S(2)}, u32[]{:S(2)}) collective-permute-start(bf16[512,1024]{1,0:T(8,128)(2,1)} %get-tuple-element.227), channel_id=1, source_target_pairs={{0,16},{4,20},{8,24},{12,28},{16,0},{20,4},{24,8},{28,12},{1,17},{... | collective-permute-start | bytes 3145736 | tf_op jit(solution)/shard_map/ppermute | solution.py:825
  360.4 32.7 %collective-permute-start.44 = (bf16[256,1024]{1,0:T(8,128)(2,1)}, bf16[256,1024]{1,0:T(8,128)(2,1)}, u32[]{:S(2)}, u32[]{:S(2)}) collective-permute-start(bf16[256,1024]{1,0:T(8,128)(2,1)} %get-tuple-element.231), channel_id=1, source_target_pairs={{0,16},{4,20},{8,24},{12,28},{16,0},{20,4},{24,8},{28,12},{1,17},{... | collective-permute-start | bytes 1572872 | tf_op jit(solution)/shard_map/ppermute | solution.py:825
  361.9 32.4 %collective-permute-start.45 = (bf16[256,1024]{1,0:T(8,128)(2,1)}, bf16[256,1024]{1,0:T(8,128)(2,1)}, u32[]{:S(2)}, u32[]{:S(2)}) collective-permute-start(bf16[256,1024]{1,0:T(8,128)(2,1)} %get-tuple-element.232), channel_id=1, source_target_pairs={{0,8},{4,12},{8,0},{12,4},{16,24},{20,28},{24,16},{28,20},{1,9},{5... | collective-permute-start | bytes 1572872 | tf_op jit(solution)/shard_map/ppermute | solution.py:825
  365.5 38.8 %collective-permute-start.46 = (bf16[256,1024]{1,0:T(8,128)(2,1)}, bf16[256,1024]{1,0:T(8,128)(2,1)}, u32[]{:S(2)}, u32[]{:S(2)}) collective-permute-start(bf16[256,1024]{1,0:T(8,128)(2,1)} %get-tuple-element.236), channel_id=1, source_target_pairs={{0,16},{4,20},{8,24},{12,28},{16,0},{20,4},{24,8},{28,12},{1,17},{... | collective-permute-start | bytes 1572872 | tf_op jit(solution)/shard_map/ppermute | solution.py:825
  380.4 24.0 %collective-permute-start.47 = (bf16[256,1024]{1,0:T(8,128)(2,1)}, bf16[256,1024]{1,0:T(8,128)(2,1)}, u32[]{:S(2)}, u32[]{:S(2)}) collective-permute-start(bf16[256,1024]{1,0:T(8,128)(2,1)} %get-tuple-element.237), channel_id=1, source_target_pairs={{0,8},{4,12},{8,0},{12,4},{16,24},{20,28},{24,16},{28,20},{1,9},{5... | collective-permute-start | bytes 1572872 | tf_op jit(solution)/shard_map/ppermute | solution.py:825
  388.6 25.8 %collective-permute-start.42 = (bf16[256,1024]{1,0:T(8,128)(2,1)}, bf16[256,1024]{1,0:T(8,128)(2,1)S(1)}, u32[]{:S(2)}, u32[]{:S(2)}) collective-permute-start(bf16[256,1024]{1,0:T(8,128)(2,1)} %get-tuple-element.245), channel_id=1, source_target_pairs={{0,16},{4,20},{8,24},{12,28},{16,0},{20,4},{24,8},{28,12},{1,17},{... | collective-permute-start | bytes 1572872 | tf_op jit(solution)/shard_map/ppermute | solution.py:825
  393.1 21.3 %collective-permute-start.43 = (bf16[256,1024]{1,0:T(8,128)(2,1)}, bf16[256,1024]{1,0:T(8,128)(2,1)}, u32[]{:S(2)}, u32[]{:S(2)}) collective-permute-start(bf16[256,1024]{1,0:T(8,128)(2,1)} %get-tuple-element.246), channel_id=1, source_target_pairs={{0,8},{4,12},{8,0},{12,4},{16,24},{20,28},{24,16},{28,20},{1,9},{5... | collective-permute-start | bytes 1572872 | tf_op jit(solution)/shard_map/ppermute | solution.py:825
  428.3 13.5 %collective-permute-start.48 = (bf16[128,2048]{1,0:T(8,128)(2,1)S(1)}, bf16[128,2048]{1,0:T(8,128)(2,1)S(1)}, u32[]{:S(2)}, u32[]{:S(2)}) collective-permute-start(bf16[128,2048]{1,0:T(8,128)(2,1)S(1)} %copy-done.17), channel_id=1, source_target_pairs={{0,8},{4,12},{8,0},{12,4},{16,24},{20,28},{24,16},{28,20},{1,9},{5... | collective-permute-start | bytes 1572872 | tf_op jit(solution)/shard_map/ppermute | solution.py:825
  429.8 13.1 %collective-permute-start.49 = (bf16[128,2048]{1,0:T(8,128)(2,1)S(1)}, bf16[128,2048]{1,0:T(8,128)(2,1)S(1)}, u32[]{:S(2)}, u32[]{:S(2)}) collective-permute-start(bf16[128,2048]{1,0:T(8,128)(2,1)S(1)} %copy-done.16), channel_id=1, source_target_pairs={{0,16},{4,20},{8,24},{12,28},{16,0},{20,4},{24,8},{28,12},{1,17},{... | collective-permute-start | bytes 1572872 | tf_op jit(solution)/shard_map/ppermute | solution.py:825
  450.7 13.8 %collective-permute-start.55 = (bf16[128,2048]{1,0:T(8,128)(2,1)S(1)}, bf16[128,2048]{1,0:T(8,128)(2,1)S(1)}, u32[]{:S(2)}, u32[]{:S(2)}) collective-permute-start(bf16[128,2048]{1,0:T(8,128)(2,1)S(1)} %get-tuple-element.272), channel_id=1, source_target_pairs={{0,8},{4,12},{8,0},{12,4},{16,24},{20,28},{24,16},{28,20},{1,9},{5... | collective-permute-start | bytes 1572872 | tf_op jit(solution)/shard_map/ppermute | solution.py:825
  455.3 12.6 %collective-permute-start.54 = (bf16[128,2048]{1,0:T(8,128)(2,1)S(1)}, bf16[128,2048]{1,0:T(8,128)(2,1)S(1)}, u32[]{:S(2)}, u32[]{:S(2)}) collective-permute-start(bf16[128,2048]{1,0:T(8,128)(2,1)S(1)} %get-tuple-element.270), channel_id=1, source_target_pairs={{0,16},{4,20},{8,24},{12,28},{16,0},{20,4},{24,8},{28,12},{1,17},{... | collective-permute-start | bytes 1572872 | tf_op jit(solution)/shard_map/ppermute | solution.py:825
  (63 other events, 379.7 us)
Sparse Core Ops, SparseCore 0:
  52.9 78.9 all-gather.2
  133.5 79.2 all-gather.4
  220.8 74.5 reduce-scatter.2
  343.2 76.2 reduce-scatter.4

commit v7 on v6

--- a/solution.py
+++ b/solution.py
@@ -382,7 +382,7 @@
         half_pre = 0.5 * pre
         hidden = (half_pre * (1.0 + bent)).astype(bf16)
         hidden_ref[...] = hidden
-        held[step] = hidden
+        held[:, columns(step)] = hidden
         slope_ref[...] = 0.5 * (1.0 + bent) + half_pre * (1.0 - bent * bent) * (
             c0 * (1.0 + (3.0 * c1) * square)
         )
@@ -402,9 +402,7 @@
             if tile < late_steps - 1:
                 for copy in pieces2(tile + 1):
                     copy.start()
-            total = dot(mixed_ref[...], wo_ref[0], NT)
-            for k in range(steps):
-                total += dot(held[k], buf2[tile % 2, :, k * tile_f : (k + 1) * tile_f], NT)
+            total = dot(held[...], buf2[tile % 2], NT) + dot(mixed_ref[...], wo_ref[0], NT)
             branch_ref[...] = total.astype(bf16)
             if tile == late_steps - 1:
                 out2(tile).wait()
@@ -443,7 +441,7 @@
             shape((width, hidden), bf16),
         ],
         scratch_shapes=[
-            pltpu.VMEM((steps, rows, tile_f), bf16),
+            pltpu.VMEM((rows, hidden), bf16),
             pltpu.VMEM((2, width, tile_f), bf16),
             pltpu.VMEM((2, tile_d, hidden), bf16),
             pltpu.SemaphoreType.DMA((2, len(w1[1]))),
@@ -468,15 +466,12 @@
     def _():
         grad = (dot(g_ref[...], w2_ref[...], NN) * slope_ref[...]).astype(bf16)
         pre_ref[...] = grad
-        held[step] = grad
+        held[:, pl.ds(pl.multiple_of(step * tile, tile), tile)] = grad
         bias_ref[...] = jnp.sum(grad.astype(f32), axis=0, keepdims=True)
 
     @pl.when(step >= steps)
     def _():
-        total = dot(held[0], w1_ref[:, :tile], NT)
-        for k in range(1, steps):
-            total += dot(held[k], w1_ref[:, k * tile : (k + 1) * tile], NT)
-        sum_ref[...] = total
+        sum_ref[...] = dot(held[...], w1_ref[...], NT)
 
 
 def back(grads, w1, w2, slope, weights, tile_f):
@@ -511,7 +506,7 @@
             shape((rows, heads), bf16),
             shape((1, units), f32),
         ],
-        scratch_shapes=[pltpu.VMEM((steps, rows, tile_f), bf16)],
+        scratch_shapes=[pltpu.VMEM((rows, units), bf16)],
         compiler_params=params(58),
         cost_estimate=cost(4 * rows * width * units, 40 << 20),
         name="back",
@@ -1012,6 +1007,10 @@
     qk_shard, vo_shard = after((qk_shard, vo_shard), routed)
     qk_stacks = gather_step([(qk_shard, [0])], x_first[0])
     vo_stacks = gather_step([(vo_shard, [0])], y_first[0])
+    first_qk, first_vo, fc1_shard, fc2_shard = after(
+        (qk_stacks[1][0], vo_stacks[1][0], fc1_weight, fc2_weight)
+    )
+    qk_stacks[1], vo_stacks[1] = (first_qk, qk_stacks[1][1]), (first_vo, vo_stacks[1][1])
     for step in range(1, len(x_first)):
         qk_stacks = gather_step(qk_stacks, x_first[step])
         vo_stacks = gather_step(vo_stacks, y_first[step])
@@ -1024,9 +1023,7 @@
 
     row_ids, = after((jnp.arange(seq_len, dtype=jnp.int32),), qk_shard)
     tables = rotary_tables(row_ids, PAIR)
-    (qk_stacks, vo_stacks), (fc1_shard, fc2_shard, *tables) = held_back(
-        (qk_stacks, vo_stacks), fc1_weight, fc2_weight, *tables
-    )
+    (qk_stacks, vo_stacks), tables = held_back((qk_stacks, vo_stacks), *tables)
     qk_stacks = qk_stacks + core_copies(qk_stacks)
     qk = gather_plan(qk_stacks, block, bits)
     by_mask = sorted(qk_stacks, key=lambda st: st[1][0])

time: 481 us -> 473 us (0.983)
  waiting for transfers between devices: 129 us -> 124 us
    ppermute x59, waiting for transfers between devices: 129 us -> 121 us  [flip(): lax.ppermute(array, axis_name, [(i, i ^ 1 << bit) for i in range(size)])]
  transfers between devices with their start and end apart: 63 -> 63, of which waited for: 33 -> 31; matrix products, arithmetic and copies ran while one was open for 7% -> 8% of each run, Pallas kernels for 43% -> 44%
where the time goes in v7:
time: 473 us; the launch traced here: 469 us
  Pallas kernels  223 us (47%)
  waiting for transfers between devices  124 us (26%)
  starting transfers between devices  50.6 us (11%)
  local copies, waits for them, and re-layouts  28.7 us (6%)
  other arithmetic  21.7 us (5%)
  between operations  21.1 us (4%)
    ppermute x59, waiting for transfers between devices, flip(): lax.ppermute(array, axis_name, [(i, i ^ 1 << bit) for i in range(size)])  121 us
    ppermute x59, starting transfers between devices, flip(): lax.ppermute(array, axis_name, [(i, i ^ 1 << bit) for i in range(size)])  50.2 us
    pallas_call x1, Pallas kernels, feed(): pl.pallas_call(functools.partial(feed_kernel, steps, late_steps, w1[1], w...  33.3 us
    pallas_call x1, Pallas kernels, back(): pl.pallas_call(functools.partial(back_kernel, steps), grid=(steps + width...  29.8 us
    pallas_call x1, Pallas kernels, attend_back(): pl.pallas_call(functools.partial(attend_back_kernel, min(block, rows)), g...  26.8 us
    pallas_call x2, Pallas kernels, feed_weight(): pl.pallas_call(feed_weight_kernel, grid=(units // tile_f,), in_specs=[pl....  26.2 us
    pallas_call x6, Pallas kernels, give(): pl.pallas_call(functools.partial(give_kernel, tuple(numbers)), grid=(out_...  19.3 us
    pallas_call x1, Pallas kernels, project(): pl.pallas_call(functools.partial(project_kernel, qk[1], vo[1]), grid=(4,)...  16.9 us
  transfers between devices with their start and end apart: 63, of which 31 were waited for; matrix products, arithmetic and copies ran while one was open for 8% of the time, Pallas kernels for 44%

profile of v7, /device:TPU:0, one launch (start us, length us, event | category | flops | bytes accessed | tf_op | source)
XLA Modules:
  0.0 469.1 jit_solution(9726052079409771079)
XLA Ops:
  13.1 10.4 %collective-permute-done.3 = bf16[128,2048]{1,0:T(8,128)(2,1)S(1)} collective-permute-done((bf16[128,2048]{1,0:T(8,128)(2,1)S(1)}, bf16[128,2048]{1,0:T(8,128)(2,1)S(1)}, u32[]{:S(2)}, u32[]{:S(2)}) %collective-permute-start.3) | collective-permute-done | bytes 524320 | tf_op jit(solution)/shard_map/ppermute | solution.py:820
  40.9 7.9 %collective-permute-done.5 = bf16[128,2048]{1,0:T(8,128)(2,1)S(1)} collective-permute-done((bf16[128,2048]{1,0:T(8,128)(2,1)S(1)}, bf16[128,2048]{1,0:T(8,128)(2,1)S(1)}, u32[]{:S(2)}, u32[]{:S(2)}) %collective-permute-start.5) | collective-permute-done | bytes 524320 | tf_op jit(solution)/shard_map/ppermute | solution.py:820
  66.1 17.0 %collective-permute-done.9.rest_9_ = bf16[256,1024]{1,0:T(8,128)(2,1)} collective-permute-done((bf16[256,1024]{1,0:T(8,128)(2,1)}, bf16[256,1024]{1,0:T(8,128)(2,1)}, u32[]{:S(2)}, u32[]{:S(2)}) %collective-permute-start.9) | collective-permute-done | bytes 524320 | tf_op jit(solution)/shard_map/ppermute | solution.py:820
  88.5 3.2 fusion
  92.9 6.0 %collective-permute-done.15.rest_11_ = bf16[256,1024]{1,0:T(8,128)(2,1)} collective-permute-done((bf16[256,1024]{1,0:T(8,128)(2,1)}, bf16[256,1024]{1,0:T(8,128)(2,1)}, u32[]{:S(2)}, u32[]{:S(2)}) %collective-permute-start.15) | collective-permute-done | bytes 524320 | tf_op jit(solution)/shard_map/ppermute | solution.py:820
  108.8 7.6 %collective-permute-done.10.rest_1_ = bf16[256,2048]{1,0:T(8,128)(2,1)S(1)} collective-permute-done((bf16[256,2048]{1,0:T(8,128)(2,1)S(1)}, bf16[256,2048]{1,0:T(8,128)(2,1)S(1)}, u32[]{:S(2)}, u32[]{:S(2)}) %collective-permute-start.10) | collective-permute-done | bytes 1048608 | tf_op jit(solution)/shard_map/ppermute | solution.py:820
  131.9 7.3 %norm.1.ln_ref = bf16[4,1,256,2048]{3,2,1,0:T(8,128)(2,1)} custom-call(s32[3]{0:T(128)} %pad_add_fusion.at_ref, bf16[1024,2048]{1,0:T(8,128)(2,1)} %all-gather.3.cloned.1.call-done.x_ref, f32[1,2048]{1,0:T(1,128)} %reshape.253.gain_ref, f32[1,2048]{1,0:T(1,128)} %reshape.254.shift_ref), custom_call_target="tpu_custom_call" | custom-call | flops 8388608 | bytes 3355443 | tf_op jit(solution)/shard_map/norm/pallas_call | solution.py:84
  140.0 16.9 %project.1 = (bf16[3,4,1,256,512]{4,3,2,1,0:T(8,128)(2,1)}, bf16[4,2048,512]{2,1,0:T(8,128)(2,1)}) custom-call(bf16[4,1,256,2048]{3,2,1,0:T(8,128)(2,1)} %norm.1.ln_ref, f32[3,1,512]{2,1,0:T(1,128)} %reshape.255.bias_ref, f32[4,1,256,128]{3,2,1,0:T(8,128)} %bitcast.153, f32[4,1,256,128]{3,2,1,0:T(8,128)} %bitcast.152, f32[4,1,256,128]{3,2,1,0:T(8,128)} %bitcast.151, ...), custom_call_target="tpu_custom_call" | custom-call | flops 2576980480 | bytes 9227468 | tf_op jit(solution)/shard_map/project/pallas_call | solution.py:184
  157.0 16.5 %attend.1 = (bf16[1024,512]{1,0:T(8,128)(2,1)}, f32[4,2,1024]{2,1,0:T(2,128)}) custom-call(s32[1]{0:T(128)} %dynamic_slice.97.len_ref, bf16[3,1024,512]{2,1,0:T(8,128)(2,1)} %bitcast.192, bf16[3,1024,512]{2,1,0:T(8,128)(2,1)} %bitcast.193, bf16[3,1024,512]{2,1,0:T(8,128)(2,1)} %bitcast.194), custom_call_target="tpu_custom_call" | custom-call | flops 3435973888 | bytes 1677721 | tf_op jit(solution)/shard_map/attend/pallas_call | solution.py:251
  174.8 3.3 collective-permute-done.30.rest_5_
  181.1 33.3 %feed.1 = (bf16[1024,2048]{1,0:T(8,128)(2,1)}, bf16[1024,2048]{1,0:T(8,128)(2,1)}, f32[1024,2048]{1,0:T(8,128)}, bf16[2048,2048]{1,0:T(8,128)(2,1)}, bf16[2048,2048]{1,0:T(8,128)(2,1)}) custom-call(bf16[1024,2048]{1,0:T(8,128)(2,1)} %bitcast.147, bf16[1024,512]{1,0:T(8,128)(2,1)} %get-tuple-element.181.mixed_ref, ...), custom_call_target="tpu_custom_call" | custom-call | flops 6871947776 | bytes 23488102 | tf_op jit(solution)/shard_map/feed/pallas_call | solution.py:423
  214.4 29.8 %back.1 = (f32[1024,2048]{1,0:T(8,128)}, bf16[1024,2048]{1,0:T(8,128)(2,1)}, bf16[1024,512]{1,0:T(8,128)(2,1)}, f32[1,2048]{1,0:T(1,128)}) custom-call(bf16[1024,2048]{1,0:T(8,128)(2,1)} %all-gather.5.cloned.1.call-done.g_ref.left_ref, bf16[2048,2048]{1,0:T(8,128)(2,1)} %get-tuple-element.196.w1_ref, bf16[2048,2048]{1,0:T(8,128)(2,1)} %get-tuple-element.197.w2_ref, ...), custom_call_target="tpu_custom_call" | custom-call | flops 6871947776 | bytes 16777216 | tf_op jit(solution)/shard_map/back/pallas_call | solution.py:487
  244.2 13.1 %feed_weight.2 = (bf16[1024,2048]{1,0:T(8,128)(2,1)}, bf16[1024,2048]{1,0:T(8,128)(2,1)}) custom-call(bf16[1024,2048]{1,0:T(8,128)(2,1)} %all-gather.5.cloned.1.call-done.g_ref.left_ref, bf16[1024,2048]{1,0:T(8,128)(2,1)} %get-tuple-element.202.right_ref), custom_call_target="tpu_custom_call" | custom-call | flops 3435973888 | bytes 6710886 | tf_op jit(solution)/shard_map/feed_weight/pallas_call | solution.py:526
  257.3 13.1 %feed_weight.3 = (bf16[1024,2048]{1,0:T(8,128)(2,1)}, bf16[1024,2048]{1,0:T(8,128)(2,1)}) custom-call(bf16[1024,2048]{1,0:T(8,128)(2,1)} %bitcast.148, bf16[1024,2048]{1,0:T(8,128)(2,1)} %get-tuple-element.204.right_ref), custom_call_target="tpu_custom_call" | custom-call | flops 3435973888 | bytes 6710886 | tf_op jit(solution)/shard_map/feed_weight/pallas_call | solution.py:526
  271.0 3.3 give.6
  278.1 3.4 give.7
  284.2 26.8 %attend_back.1.grad_ref = bf16[3,1024,512]{2,1,0:T(8,128)(2,1)} custom-call(s32[1]{0:T(128)} %dynamic_slice.97.len_ref, bf16[3,1024,512]{2,1,0:T(8,128)(2,1)} %bitcast.195, bf16[3,1024,512]{2,1,0:T(8,128)(2,1)} %bitcast.196, bf16[3,1024,512]{2,1,0:T(8,128)(2,1)} %bitcast.197, bf16[1024,512]{1,0:T(8,128)(2,1)} %get-tuple-element.216.do_ref, ...), custom_call_target="tpu_custom_call" | custom-call | flops 8589934592 | bytes 3355443 | tf_op jit(solution)/shard_map/attend_back/pallas_call | solution.py:309
  311.1 15.0 %weight_grad.1 = (bf16[1024,1024]{1,0:T(8,128)(2,1)}, bf16[1024,1024]{1,0:T(8,128)(2,1)}, bf16[1024,1024]{1,0:T(8,128)(2,1)}, bf16[1024,1024]{1,0:T(8,128)(2,1)}, f32[3,1,512]{2,1,0:T(1,128)}) custom-call(bf16[1024,2048]{1,0:T(8,128)(2,1)} %bitcast.149, bf16[1024,2048]{1,0:T(8,128)(2,1)} %all-gather.5.cloned.1.call-done.g_ref.left_ref, ...), custom_call_target="tpu_custom_call" | custom-call | flops 3435973888 | bytes 8388608 | tf_op jit(solution)/shard_map/weight_grad/pallas_call | solution.py:595
  326.1 12.2 %ln_grad.1 = bf16[1024,2048]{1,0:T(8,128)(2,1)} custom-call(bf16[3,1024,512]{2,1,0:T(8,128)(2,1)} %attend_back.1.grad_ref, bf16[4,2048,512]{2,1,0:T(8,128)(2,1)} %get-tuple-element.182.wo_ref.w_ref, f32[1024,2048]{1,0:T(8,128)} %get-tuple-element.225.sum_ref), custom_call_target="tpu_custom_call" | custom-call | flops 2576980480 | bytes 9227468 | tf_op jit(solution)/shard_map/ln_grad/pallas_call | solution.py:552
  345.7 3.5 give.8
  361.4 14.2 %collective-permute-done.40.refs_2_ = bf16[512,1024]{1,0:T(8,128)(2,1)} collective-permute-done((bf16[512,1024]{1,0:T(8,128)(2,1)}, bf16[512,1024]{1,0:T(8,128)(2,1)}, u32[]{:S(2)}, u32[]{:S(2)}) %collective-permute-start.40) | collective-permute-done | bytes 1048608 | tf_op jit(solution)/shard_map/ppermute | solution.py:820
  376.4 3.7 finish.1
  383.7 4.0 collective-permute-done.44.refs_3_
  389.5 9.4 %collective-permute-done.46.refs_3_ = bf16[256,1024]{1,0:T(8,128)(2,1)} collective-permute-done((bf16[256,1024]{1,0:T(8,128)(2,1)}, bf16[256,1024]{1,0:T(8,128)(2,1)}, u32[]{:S(2)}, u32[]{:S(2)}) %collective-permute-start.46) | collective-permute-done | bytes 524320 | tf_op jit(solution)/shard_map/ppermute | solution.py:820
  398.9 3.6 final.2
  402.5 3.6 final.3
  409.7 3.8 final_attention.1
  413.6 5.2 %norm_back.1 = (bf16[128,2048]{1,0:T(8,128)(2,1)}, bf16[128,2048]{1,0:T(8,128)(2,1)}, f32[2,2048]{1,0:T(2,128)}) custom-call(s32[3]{0:T(128)} %pad_add_fusion.at_ref, bf16[256,2048]{1,0:T(8,128)(2,1)} %reduce-scatter.5.cloned.1.call-done.sum_ref, bf16[256,2048]{1,0:T(8,128)(2,1)} %pad_maximum_fusion.6.rows_ref, bf16[256,2048]{1,0:T(8,128)(2,1)} %bitcast.150, ...), custom_call_target="tpu_custom_call" | custom-call | flops 4194304 | bytes 1677721 | tf_op jit(solution)/shard_map/norm_back/pallas_call | solution.py:690
  426.6 3.1 collective-permute-done.51
  429.7 4.7 %collective-permute-done.48 = bf16[128,2048]{1,0:T(8,128)(2,1)S(1)} collective-permute-done((bf16[128,2048]{1,0:T(8,128)(2,1)S(1)}, bf16[128,2048]{1,0:T(8,128)(2,1)S(1)}, u32[]{:S(2)}, u32[]{:S(2)}) %collective-permute-start.48) | collective-permute-done | bytes 524320 | tf_op jit(solution)/shard_map/ppermute | solution.py:820
  452.0 5.2 %collective-permute-done.55 = bf16[128,2048]{1,0:T(8,128)(2,1)S(1)} collective-permute-done((bf16[128,2048]{1,0:T(8,128)(2,1)S(1)}, bf16[128,2048]{1,0:T(8,128)(2,1)S(1)}, u32[]{:S(2)}, u32[]{:S(2)}) %collective-permute-start.55) | collective-permute-done | bytes 524320 | tf_op jit(solution)/shard_map/ppermute | solution.py:820
  457.2 3.4 collective-permute-done.54
  (330 shorter events, 134.4 us)
Async XLA Ops:
  7.2 124.8 %all-gather.3.cloned.1.call-start = ((), (), s32[]{:S(2)}) async-start(), calls=%async_computation.2 | async-start | bytes 5242880 | tf_op jit(solution)/shard_map/all_gather | solution.py:999
  8.6 15.0 %collective-permute-start.3 = (bf16[128,2048]{1,0:T(8,128)(2,1)S(1)}, bf16[128,2048]{1,0:T(8,128)(2,1)S(1)}, u32[]{:S(2)}, u32[]{:S(2)}) collective-permute-start(bf16[128,2048]{1,0:T(8,128)(2,1)S(1)} %get-tuple-element.292), channel_id=1, source_target_pairs={{0,16},{4,20},{8,24},{12,28},{16,0},{20,4},{24,8},{28,12},{1,17},{... | collective-permute-start | bytes 1572872 | tf_op jit(solution)/shard_map/ppermute | solution.py:820
  52.8 161.6 %all-gather.5.cloned.1.call-start = ((), (), s32[]{:S(2)}) async-start(), calls=%async_computation.3 | async-start | bytes 5242880 | tf_op jit(solution)/shard_map/all_gather | solution.py:1043
  58.6 24.6 %collective-permute-start.8 = (bf16[272,1024]{1,0:T(8,128)(2,1)}, bf16[272,1024]{1,0:T(8,128)(2,1)}, u32[]{:S(2)}, u32[]{:S(2)}) collective-permute-start(bf16[272,1024]{1,0:T(8,128)(2,1)} %pad_maximum_fusion.9.rest_0_), channel_id=1, source_target_pairs={{0,8},{4,12},{8,0},{12,4},{16,24},{20,28},{24,16},{28,20},{1,9},{5... | collective-permute-start | bytes 1671176 | tf_op jit(solution)/shard_map/ppermute | solution.py:820
  59.1 33.8 %collective-permute-start.12 = (bf16[272,1024]{1,0:T(8,128)(2,1)}, bf16[272,1024]{1,0:T(8,128)(2,1)}, u32[]{:S(2)}, u32[]{:S(2)}) collective-permute-start(bf16[272,1024]{1,0:T(8,128)(2,1)} %pad_maximum_fusion.9.rest_0_), channel_id=1, source_target_pairs={{0,16},{4,20},{8,24},{12,28},{16,0},{20,4},{24,8},{28,12},{1,17},{... | collective-permute-start | bytes 1671176 | tf_op jit(solution)/shard_map/ppermute | solution.py:820
  60.5 22.6 %collective-permute-start.9 = (bf16[256,1024]{1,0:T(8,128)(2,1)}, bf16[256,1024]{1,0:T(8,128)(2,1)}, u32[]{:S(2)}, u32[]{:S(2)}) collective-permute-start(bf16[256,1024]{1,0:T(8,128)(2,1)} %pad_maximum_fusion.10.rest_8_), channel_id=1, source_target_pairs={{0,16},{4,20},{8,24},{12,28},{16,0},{20,4},{24,8},{28,12},{1,17},{... | collective-permute-start | bytes 1572872 | tf_op jit(solution)/shard_map/ppermute | solution.py:820
  61.1 31.2 %collective-permute-start.14 = (bf16[256,1024]{1,0:T(8,128)(2,1)}, bf16[256,1024]{1,0:T(8,128)(2,1)}, u32[]{:S(2)}, u32[]{:S(2)}) collective-permute-start(bf16[256,1024]{1,0:T(8,128)(2,1)} %pad_maximum_fusion.10.rest_8_), channel_id=1, source_target_pairs={{0,8},{4,12},{8,0},{12,4},{16,24},{20,28},{24,16},{28,20},{1,9},{5... | collective-permute-start | bytes 1572872 | tf_op jit(solution)/shard_map/ppermute | solution.py:820
  83.1 15.9 %collective-permute-start.13 = (bf16[272,1024]{1,0:T(8,128)(2,1)}, bf16[272,1024]{1,0:T(8,128)(2,1)}, u32[]{:S(2)}, u32[]{:S(2)}) collective-permute-start(bf16[272,1024]{1,0:T(8,128)(2,1)} %collective-permute-done.8.rest_1_), channel_id=1, source_target_pairs={{0,16},{4,20},{8,24},{12,28},{16,0},{20,4},{24,8},{28,12},{1,17},{... | collective-permute-start | bytes 1671176 | tf_op jit(solution)/shard_map/ppermute | solution.py:820
  84.6 14.3 %collective-permute-start.15 = (bf16[256,1024]{1,0:T(8,128)(2,1)}, bf16[256,1024]{1,0:T(8,128)(2,1)}, u32[]{:S(2)}, u32[]{:S(2)}) collective-permute-start(bf16[256,1024]{1,0:T(8,128)(2,1)} %collective-permute-done.9.rest_9_), channel_id=1, source_target_pairs={{0,8},{4,12},{8,0},{12,4},{16,24},{20,28},{24,16},{28,20},{1,9},{5... | collective-permute-start | bytes 1572872 | tf_op jit(solution)/shard_map/ppermute | solution.py:820
  88.2 237.9 %reduce-scatter.3.cloned.1.call-start = ((), (), s32[]{:S(2)}) async-start(), calls=%async_computation.4 | async-start | bytes 5242880 | tf_op jit(solution)/shard_map/reduce_scatter | solution.py:1078
  91.7 24.7 %collective-permute-start.10 = (bf16[256,2048]{1,0:T(8,128)(2,1)S(1)}, bf16[256,2048]{1,0:T(8,128)(2,1)S(1)}, u32[]{:S(2)}, u32[]{:S(2)}) collective-permute-start(bf16[256,2048]{1,0:T(8,128)(2,1)S(1)} %copy-done.1), channel_id=1, source_target_pairs={{0,8},{4,12},{8,0},{12,4},{16,24},{20,28},{24,16},{28,20},{1,9},{5... | collective-permute-start | bytes 3145736 | tf_op jit(solution)/shard_map/ppermute | solution.py:820
  92.3 24.5 %collective-permute-start.11 = (bf16[256,2048]{1,0:T(8,128)(2,1)S(1)}, bf16[256,2048]{1,0:T(8,128)(2,1)}, u32[]{:S(2)}, u32[]{:S(2)}) collective-permute-start(bf16[256,2048]{1,0:T(8,128)(2,1)S(1)} %copy-done.2), channel_id=1, source_target_pairs={{0,16},{4,20},{8,24},{12,28},{16,0},{20,4},{24,8},{28,12},{1,17},{... | collective-permute-start | bytes 3145736 | tf_op jit(solution)/shard_map/ppermute | solution.py:820
  122.0 51.5 %collective-permute-start.28 = (bf16[512,2048]{1,0:T(8,128)(2,1)}, bf16[512,2048]{1,0:T(8,128)(2,1)}, u32[]{:S(2)}, u32[]{:S(2)}) collective-permute-start(bf16[512,2048]{1,0:T(8,128)(2,1)} %pad_maximum_fusion.2), channel_id=1, source_target_pairs={{0,16},{4,20},{8,24},{12,28},{16,0},{20,4},{24,8},{28,12},{1,17},{... | collective-permute-start | bytes 6291464 | tf_op jit(solution)/shard_map/ppermute | solution.py:820
  123.4 50.1 %collective-permute-start.29 = (bf16[512,2048]{1,0:T(8,128)(2,1)}, bf16[512,2048]{1,0:T(8,128)(2,1)}, u32[]{:S(2)}, u32[]{:S(2)}) collective-permute-start(bf16[512,2048]{1,0:T(8,128)(2,1)} %pad_maximum_fusion.3), channel_id=1, source_target_pairs={{0,8},{4,12},{8,0},{12,4},{16,24},{20,28},{24,16},{28,20},{1,9},{5... | collective-permute-start | bytes 6291464 | tf_op jit(solution)/shard_map/ppermute | solution.py:820
  124.9 14.3 %collective-permute-start.25 = (bf16[256,1024]{1,0:T(8,128)(2,1)}, bf16[256,1024]{1,0:T(8,128)(2,1)}, u32[]{:S(2)}, u32[]{:S(2)}) collective-permute-start(bf16[256,1024]{1,0:T(8,128)(2,1)} %collective-permute-done.9.rest_9_), channel_id=1, source_target_pairs={{0,4},{4,0},{8,12},{12,8},{16,20},{20,16},{24,28},{28,24},{1,5},{5... | collective-permute-start | bytes 1572872 | tf_op jit(solution)/shard_map/ppermute | solution.py:820
  125.0 14.3 %collective-permute-start.26 = (bf16[256,1024]{1,0:T(8,128)(2,1)}, bf16[256,1024]{1,0:T(8,128)(2,1)S(1)}, u32[]{:S(2)}, u32[]{:S(2)}) collective-permute-start(bf16[256,1024]{1,0:T(8,128)(2,1)} %collective-permute-done.14.rest_10_), channel_id=1, source_target_pairs={{0,4},{4,0},{8,12},{12,8},{16,20},{20,16},{24,28},{28,24},{1,5},{5... | collective-permute-start | bytes 1572872 | tf_op jit(solution)/shard_map/ppermute | solution.py:820
  214.4 199.1 %reduce-scatter.5.cloned.1.call-start = ((), (), s32[]{:S(2)}) async-start(), calls=%async_computation.5 | async-start | bytes 5242880 | tf_op jit(solution)/shard_map/reduce_scatter | solution.py:1111
  257.3 13.6 %collective-permute-start.33 = (bf16[1024,2048]{1,0:T(8,128)(2,1)}, bf16[1024,2048]{1,0:T(8,128)(2,1)}, u32[]{:S(2)}, u32[]{:S(2)}) collective-permute-start(bf16[1024,2048]{1,0:T(8,128)(2,1)} %get-tuple-element.203), channel_id=1, source_target_pairs={{0,4},{4,0},{8,12},{12,8},{16,20},{20,16},{24,28},{28,24},{1,5},{5... | collective-permute-start | bytes 12582920 | tf_op jit(solution)/shard_map/ppermute | solution.py:820
  274.3 51.7 %collective-permute-start.34 = (bf16[512,1024]{1,0:T(8,128)(2,1)}, bf16[512,1024]{1,0:T(8,128)(2,1)}, u32[]{:S(2)}, u32[]{:S(2)}) collective-permute-start(bf16[512,1024]{1,0:T(8,128)(2,1)} %get-tuple-element.210), channel_id=1, source_target_pairs={{0,8},{4,12},{8,0},{12,4},{16,24},{20,28},{24,16},{28,20},{1,9},{5... | collective-permute-start | bytes 3145736 | tf_op jit(solution)/shard_map/ppermute | solution.py:820
  275.6 50.4 %collective-permute-start.35 = (bf16[512,1024]{1,0:T(8,128)(2,1)}, bf16[512,1024]{1,0:T(8,128)(2,1)}, u32[]{:S(2)}, u32[]{:S(2)}) collective-permute-start(bf16[512,1024]{1,0:T(8,128)(2,1)} %get-tuple-element.211), channel_id=1, source_target_pairs={{0,16},{4,20},{8,24},{12,28},{16,0},{20,4},{24,8},{28,12},{1,17},{... | collective-permute-start | bytes 3145736 | tf_op jit(solution)/shard_map/ppermute | solution.py:820
  281.5 44.6 %collective-permute-start.36 = (bf16[512,1024]{1,0:T(8,128)(2,1)}, bf16[512,1024]{1,0:T(8,128)(2,1)}, u32[]{:S(2)}, u32[]{:S(2)}) collective-permute-start(bf16[512,1024]{1,0:T(8,128)(2,1)} %get-tuple-element.214), channel_id=1, source_target_pairs={{0,8},{4,12},{8,0},{12,4},{16,24},{20,28},{24,16},{28,20},{1,9},{5... | collective-permute-start | bytes 3145736 | tf_op jit(solution)/shard_map/ppermute | solution.py:820
  282.8 43.3 %collective-permute-start.37 = (bf16[512,1024]{1,0:T(8,128)(2,1)}, bf16[512,1024]{1,0:T(8,128)(2,1)}, u32[]{:S(2)}, u32[]{:S(2)}) collective-permute-start(bf16[512,1024]{1,0:T(8,128)(2,1)} %get-tuple-element.215), channel_id=1, source_target_pairs={{0,16},{4,20},{8,24},{12,28},{16,0},{20,4},{24,8},{28,12},{1,17},{... | collective-permute-start | bytes 3145736 | tf_op jit(solution)/shard_map/ppermute | solution.py:820
  349.2 26.4 %collective-permute-start.40 = (bf16[512,1024]{1,0:T(8,128)(2,1)}, bf16[512,1024]{1,0:T(8,128)(2,1)}, u32[]{:S(2)}, u32[]{:S(2)}) collective-permute-start(bf16[512,1024]{1,0:T(8,128)(2,1)} %get-tuple-element.230), channel_id=1, source_target_pairs={{0,8},{4,12},{8,0},{12,4},{16,24},{20,28},{24,16},{28,20},{1,9},{5... | collective-permute-start | bytes 3145736 | tf_op jit(solution)/shard_map/ppermute | solution.py:820
  350.1 30.0 %collective-permute-start.41 = (bf16[512,1024]{1,0:T(8,128)(2,1)}, bf16[512,1024]{1,0:T(8,128)(2,1)}, u32[]{:S(2)}, u32[]{:S(2)}) collective-permute-start(bf16[512,1024]{1,0:T(8,128)(2,1)} %get-tuple-element.231), channel_id=1, source_target_pairs={{0,16},{4,20},{8,24},{12,28},{16,0},{20,4},{24,8},{28,12},{1,17},{... | collective-permute-start | bytes 3145736 | tf_op jit(solution)/shard_map/ppermute | solution.py:820
  353.7 34.0 %collective-permute-start.44 = (bf16[256,1024]{1,0:T(8,128)(2,1)}, bf16[256,1024]{1,0:T(8,128)(2,1)}, u32[]{:S(2)}, u32[]{:S(2)}) collective-permute-start(bf16[256,1024]{1,0:T(8,128)(2,1)} %get-tuple-element.235), channel_id=1, source_target_pairs={{0,16},{4,20},{8,24},{12,28},{16,0},{20,4},{24,8},{28,12},{1,17},{... | collective-permute-start | bytes 1572872 | tf_op jit(solution)/shard_map/ppermute | solution.py:820
  356.5 33.0 %collective-permute-start.45 = (bf16[256,1024]{1,0:T(8,128)(2,1)}, bf16[256,1024]{1,0:T(8,128)(2,1)}, u32[]{:S(2)}, u32[]{:S(2)}) collective-permute-start(bf16[256,1024]{1,0:T(8,128)(2,1)} %get-tuple-element.236), channel_id=1, source_target_pairs={{0,8},{4,12},{8,0},{12,4},{16,24},{20,28},{24,16},{28,20},{1,9},{5... | collective-permute-start | bytes 1572872 | tf_op jit(solution)/shard_map/ppermute | solution.py:820
  360.7 38.2 %collective-permute-start.46 = (bf16[256,1024]{1,0:T(8,128)(2,1)}, bf16[256,1024]{1,0:T(8,128)(2,1)}, u32[]{:S(2)}, u32[]{:S(2)}) collective-permute-start(bf16[256,1024]{1,0:T(8,128)(2,1)} %get-tuple-element.240), channel_id=1, source_target_pairs={{0,16},{4,20},{8,24},{12,28},{16,0},{20,4},{24,8},{28,12},{1,17},{... | collective-permute-start | bytes 1572872 | tf_op jit(solution)/shard_map/ppermute | solution.py:820
  375.6 23.4 %collective-permute-start.47 = (bf16[256,1024]{1,0:T(8,128)(2,1)}, bf16[256,1024]{1,0:T(8,128)(2,1)}, u32[]{:S(2)}, u32[]{:S(2)}) collective-permute-start(bf16[256,1024]{1,0:T(8,128)(2,1)} %get-tuple-element.241), channel_id=1, source_target_pairs={{0,8},{4,12},{8,0},{12,4},{16,24},{20,28},{24,16},{28,20},{1,9},{5... | collective-permute-start | bytes 1572872 | tf_op jit(solution)/shard_map/ppermute | solution.py:820
  383.1 25.8 %collective-permute-start.42 = (bf16[256,1024]{1,0:T(8,128)(2,1)}, bf16[256,1024]{1,0:T(8,128)(2,1)S(1)}, u32[]{:S(2)}, u32[]{:S(2)}) collective-permute-start(bf16[256,1024]{1,0:T(8,128)(2,1)} %get-tuple-element.249), channel_id=1, source_target_pairs={{0,16},{4,20},{8,24},{12,28},{16,0},{20,4},{24,8},{28,12},{1,17},{... | collective-permute-start | bytes 1572872 | tf_op jit(solution)/shard_map/ppermute | solution.py:820
  387.7 21.2 %collective-permute-start.43 = (bf16[256,1024]{1,0:T(8,128)(2,1)}, bf16[256,1024]{1,0:T(8,128)(2,1)}, u32[]{:S(2)}, u32[]{:S(2)}) collective-permute-start(bf16[256,1024]{1,0:T(8,128)(2,1)} %get-tuple-element.250), channel_id=1, source_target_pairs={{0,8},{4,12},{8,0},{12,4},{16,24},{20,28},{24,16},{28,20},{1,9},{5... | collective-permute-start | bytes 1572872 | tf_op jit(solution)/shard_map/ppermute | solution.py:820
  421.0 13.4 %collective-permute-start.48 = (bf16[128,2048]{1,0:T(8,128)(2,1)S(1)}, bf16[128,2048]{1,0:T(8,128)(2,1)S(1)}, u32[]{:S(2)}, u32[]{:S(2)}) collective-permute-start(bf16[128,2048]{1,0:T(8,128)(2,1)S(1)} %copy-done.17), channel_id=1, source_target_pairs={{0,8},{4,12},{8,0},{12,4},{16,24},{20,28},{24,16},{28,20},{1,9},{5... | collective-permute-start | bytes 1572872 | tf_op jit(solution)/shard_map/ppermute | solution.py:820
  443.4 13.8 %collective-permute-start.55 = (bf16[128,2048]{1,0:T(8,128)(2,1)S(1)}, bf16[128,2048]{1,0:T(8,128)(2,1)S(1)}, u32[]{:S(2)}, u32[]{:S(2)}) collective-permute-start(bf16[128,2048]{1,0:T(8,128)(2,1)S(1)} %get-tuple-element.276), channel_id=1, source_target_pairs={{0,8},{4,12},{8,0},{12,4},{16,24},{20,28},{24,16},{28,20},{1,9},{5... | collective-permute-start | bytes 1572872 | tf_op jit(solution)/shard_map/ppermute | solution.py:820
  (63 other events, 368.2 us)
Sparse Core Ops, SparseCore 0:
  52.9 78.9 all-gather.2
  133.5 79.2 all-gather.4
  215.1 75.2 reduce-scatter.2
  338.4 73.7 reduce-scatter.4

commit v8 on v7

--- a/solution.py
+++ b/solution.py
@@ -85,10 +85,10 @@
         functools.partial(norm_kernel, blocks),
         grid_spec=pltpu.PrefetchScalarGridSpec(
             num_scalar_prefetch=1,
-            grid=(count,),
-            in_specs=[pl.BlockSpec((rows, width), lambda j, n: (j, 0)), vector, vector],
-            out_specs=pl.BlockSpec((1, 1, rows, width), lambda j, n: (j, 0, 0, 0)),
-            scratch_shapes=[pltpu.VMEM((rows, width), bf16)],
+            grid=(2 * count,),
+            in_specs=[pl.BlockSpec((rows // 2, width), lambda j, n: (j, 0)), vector, vector],
+            out_specs=pl.BlockSpec((1, 1, rows // 2, width), lambda j, n: (j // 2, 0, j % 2, 0)),
+            scratch_shapes=[pltpu.VMEM((rows // 2, width), bf16)],
         ),
         out_shape=shape((count, 1, rows, width), bf16),
         compiler_params=params(32),
@@ -676,26 +676,35 @@
         - normed * jnp.mean(grad_norm * normed, -1, keepdims=True)
     )
     slot = (cot_ref[...].astype(f32) + back).astype(bf16)
-    half = first_ref.shape[0]
-    first_ref[...] = slot[:half]
-    second_ref[...] = slot[half:]
-    vector_ref[0:1] = jnp.sum(grad_ln * normed, 0, keepdims=True)
-    vector_ref[1:2] = jnp.sum(grad_ln, 0, keepdims=True)
+    gain_sum = jnp.sum(grad_ln * normed, 0, keepdims=True)
+    shift_sum = jnp.sum(grad_ln, 0, keepdims=True)
+
+    @pl.when(pl.program_id(0) == 0)
+    def _():
+        first_ref[...] = slot
+        vector_ref[0:1] = gain_sum
+        vector_ref[1:2] = shift_sum
+
+    @pl.when(pl.program_id(0) == 1)
+    def _():
+        second_ref[...] = slot
+        vector_ref[0:1] += gain_sum
+        vector_ref[1:2] += shift_sum
 
 
 def norm_back(total, rows_in, cot, gain, at, blocks):
     rows, width = rows_in.shape
-    whole = pl.BlockSpec((rows, width), lambda i, n: (0, 0))
+    whole = pl.BlockSpec((rows // 2, width), lambda i, n: (i, 0))
     vector = pl.BlockSpec((1, width), lambda i, n: (0, 0))
     return pl.pallas_call(
         functools.partial(norm_back_kernel, blocks),
         grid_spec=pltpu.PrefetchScalarGridSpec(
             num_scalar_prefetch=1,
-            grid=(1,),
+            grid=(2,),
             in_specs=[whole, whole, whole, vector],
             out_specs=[pl.BlockSpec((rows // 2, width), lambda i, n: (0, 0))] * 2
             + [pl.BlockSpec((2, width), lambda i, n: (0, 0))],
-            scratch_shapes=[pltpu.VMEM((rows, width), bf16)],
+            scratch_shapes=[pltpu.VMEM((rows // 2, width), bf16)],
         ),
         out_shape=[shape((rows // 2, width), bf16)] * 2 + [shape((2, width), f32)],
         compiler_params=params(32),

time: 473 us -> 475 us (level)
  no operation moved by 1% of the time
where the time goes in v8:
time: 475 us; the launch traced here: 470 us
  Pallas kernels  225 us (47%)
  waiting for transfers between devices  124 us (26%)
  starting transfers between devices  50.1 us (11%)
  local copies, waits for them, and re-layouts  28.7 us (6%)
  other arithmetic  21.7 us (5%)
  between operations  21.1 us (4%)
    ppermute x59, waiting for transfers between devices, flip(): lax.ppermute(array, axis_name, [(i, i ^ 1 << bit) for i in range(size)])  121 us
    ppermute x59, starting transfers between devices, flip(): lax.ppermute(array, axis_name, [(i, i ^ 1 << bit) for i in range(size)])  49.7 us
    pallas_call x1, Pallas kernels, feed(): pl.pallas_call(functools.partial(feed_kernel, steps, late_steps, w1[1], w...  33.3 us
    pallas_call x1, Pallas kernels, back(): pl.pallas_call(functools.partial(back_kernel, steps), grid=(steps + width...  30.1 us
    pallas_call x1, Pallas kernels, attend_back(): pl.pallas_call(functools.partial(attend_back_kernel, min(block, rows)), g...  26.8 us
    pallas_call x2, Pallas kernels, feed_weight(): pl.pallas_call(feed_weight_kernel, grid=(units // tile_f,), in_specs=[pl....  26.3 us
    pallas_call x6, Pallas kernels, give(): pl.pallas_call(functools.partial(give_kernel, tuple(numbers)), grid=(out_...  19.3 us
    pallas_call x1, Pallas kernels, project(): pl.pallas_call(functools.partial(project_kernel, qk[1], vo[1]), grid=(4,)...  16.6 us
  transfers between devices with their start and end apart: 63, of which 31 were waited for; matrix products, arithmetic and copies ran while one was open for 8% of the time, Pallas kernels for 44%

profile of v8, /device:TPU:0, one launch (start us, length us, event | category | flops | bytes accessed | tf_op | source)
XLA Modules:
  0.0 470.4 jit_solution(1091252343214359836)
XLA Ops:
  13.1 10.4 %collective-permute-done.3 = bf16[128,2048]{1,0:T(8,128)(2,1)S(1)} collective-permute-done((bf16[128,2048]{1,0:T(8,128)(2,1)S(1)}, bf16[128,2048]{1,0:T(8,128)(2,1)S(1)}, u32[]{:S(2)}, u32[]{:S(2)}) %collective-permute-start.3) | collective-permute-done | bytes 524320 | tf_op jit(solution)/shard_map/ppermute | solution.py:829
  40.9 7.9 %collective-permute-done.5 = bf16[128,2048]{1,0:T(8,128)(2,1)S(1)} collective-permute-done((bf16[128,2048]{1,0:T(8,128)(2,1)S(1)}, bf16[128,2048]{1,0:T(8,128)(2,1)S(1)}, u32[]{:S(2)}, u32[]{:S(2)}) %collective-permute-start.5) | collective-permute-done | bytes 524320 | tf_op jit(solution)/shard_map/ppermute | solution.py:829
  66.1 17.0 %collective-permute-done.9.rest_9_ = bf16[256,1024]{1,0:T(8,128)(2,1)} collective-permute-done((bf16[256,1024]{1,0:T(8,128)(2,1)}, bf16[256,1024]{1,0:T(8,128)(2,1)}, u32[]{:S(2)}, u32[]{:S(2)}) %collective-permute-start.9) | collective-permute-done | bytes 524320 | tf_op jit(solution)/shard_map/ppermute | solution.py:829
  88.5 3.2 fusion
  92.9 6.0 %collective-permute-done.15.rest_11_ = bf16[256,1024]{1,0:T(8,128)(2,1)} collective-permute-done((bf16[256,1024]{1,0:T(8,128)(2,1)}, bf16[256,1024]{1,0:T(8,128)(2,1)}, u32[]{:S(2)}, u32[]{:S(2)}) %collective-permute-start.15) | collective-permute-done | bytes 524320 | tf_op jit(solution)/shard_map/ppermute | solution.py:829
  108.8 7.6 %collective-permute-done.10.rest_1_ = bf16[256,2048]{1,0:T(8,128)(2,1)S(1)} collective-permute-done((bf16[256,2048]{1,0:T(8,128)(2,1)S(1)}, bf16[256,2048]{1,0:T(8,128)(2,1)S(1)}, u32[]{:S(2)}, u32[]{:S(2)}) %collective-permute-start.10) | collective-permute-done | bytes 1048608 | tf_op jit(solution)/shard_map/ppermute | solution.py:829
  131.9 9.0 %norm.1.ln_ref = bf16[4,1,256,2048]{3,2,1,0:T(8,128)(2,1)} custom-call(s32[3]{0:T(128)} %pad_add_fusion.at_ref, bf16[1024,2048]{1,0:T(8,128)(2,1)} %all-gather.3.cloned.1.call-done.x_ref, f32[1,2048]{1,0:T(1,128)} %reshape.253.gain_ref, f32[1,2048]{1,0:T(1,128)} %reshape.254.shift_ref), custom_call_target="tpu_custom_call" | custom-call | flops 8388608 | bytes 3355443 | tf_op jit(solution)/shard_map/norm/pallas_call | solution.py:84
  141.7 16.6 %project.1 = (bf16[3,4,1,256,512]{4,3,2,1,0:T(8,128)(2,1)}, bf16[4,2048,512]{2,1,0:T(8,128)(2,1)}) custom-call(bf16[4,1,256,2048]{3,2,1,0:T(8,128)(2,1)} %norm.1.ln_ref, f32[3,1,512]{2,1,0:T(1,128)} %reshape.255.bias_ref, f32[4,1,256,128]{3,2,1,0:T(8,128)} %bitcast.153, f32[4,1,256,128]{3,2,1,0:T(8,128)} %bitcast.152, f32[4,1,256,128]{3,2,1,0:T(8,128)} %bitcast.151, ...), custom_call_target="tpu_custom_call" | custom-call | flops 2576980480 | bytes 9227468 | tf_op jit(solution)/shard_map/project/pallas_call | solution.py:184
  158.4 16.6 %attend.1 = (bf16[1024,512]{1,0:T(8,128)(2,1)}, f32[4,2,1024]{2,1,0:T(2,128)}) custom-call(s32[1]{0:T(128)} %dynamic_slice.97.len_ref, bf16[3,1024,512]{2,1,0:T(8,128)(2,1)} %bitcast.192, bf16[3,1024,512]{2,1,0:T(8,128)(2,1)} %bitcast.193, bf16[3,1024,512]{2,1,0:T(8,128)(2,1)} %bitcast.194), custom_call_target="tpu_custom_call" | custom-call | flops 3435973888 | bytes 1677721 | tf_op jit(solution)/shard_map/attend/pallas_call | solution.py:251
  176.2 3.3 collective-permute-done.30.rest_5_
  182.5 33.3 %feed.1 = (bf16[1024,2048]{1,0:T(8,128)(2,1)}, bf16[1024,2048]{1,0:T(8,128)(2,1)}, f32[1024,2048]{1,0:T(8,128)}, bf16[2048,2048]{1,0:T(8,128)(2,1)}, bf16[2048,2048]{1,0:T(8,128)(2,1)}) custom-call(bf16[1024,2048]{1,0:T(8,128)(2,1)} %bitcast.147, bf16[1024,512]{1,0:T(8,128)(2,1)} %get-tuple-element.181.mixed_ref, ...), custom_call_target="tpu_custom_call" | custom-call | flops 6871947776 | bytes 23488102 | tf_op jit(solution)/shard_map/feed/pallas_call | solution.py:423
  215.9 30.1 %back.1 = (f32[1024,2048]{1,0:T(8,128)}, bf16[1024,2048]{1,0:T(8,128)(2,1)}, bf16[1024,512]{1,0:T(8,128)(2,1)}, f32[1,2048]{1,0:T(1,128)}) custom-call(bf16[1024,2048]{1,0:T(8,128)(2,1)} %all-gather.5.cloned.1.call-done.g_ref.left_ref, bf16[2048,2048]{1,0:T(8,128)(2,1)} %get-tuple-element.196.w1_ref, bf16[2048,2048]{1,0:T(8,128)(2,1)} %get-tuple-element.197.w2_ref, ...), custom_call_target="tpu_custom_call" | custom-call | flops 6871947776 | bytes 16777216 | tf_op jit(solution)/shard_map/back/pallas_call | solution.py:487
  246.1 13.1 %feed_weight.2 = (bf16[1024,2048]{1,0:T(8,128)(2,1)}, bf16[1024,2048]{1,0:T(8,128)(2,1)}) custom-call(bf16[1024,2048]{1,0:T(8,128)(2,1)} %all-gather.5.cloned.1.call-done.g_ref.left_ref, bf16[1024,2048]{1,0:T(8,128)(2,1)} %get-tuple-element.202.right_ref), custom_call_target="tpu_custom_call" | custom-call | flops 3435973888 | bytes 6710886 | tf_op jit(solution)/shard_map/feed_weight/pallas_call | solution.py:526
  259.2 13.2 %feed_weight.3 = (bf16[1024,2048]{1,0:T(8,128)(2,1)}, bf16[1024,2048]{1,0:T(8,128)(2,1)}) custom-call(bf16[1024,2048]{1,0:T(8,128)(2,1)} %bitcast.148, bf16[1024,2048]{1,0:T(8,128)(2,1)} %get-tuple-element.204.right_ref), custom_call_target="tpu_custom_call" | custom-call | flops 3435973888 | bytes 6710886 | tf_op jit(solution)/shard_map/feed_weight/pallas_call | solution.py:526
  272.9 3.4 give.6
  280.0 3.3 give.7
  286.2 26.8 %attend_back.1.grad_ref = bf16[3,1024,512]{2,1,0:T(8,128)(2,1)} custom-call(s32[1]{0:T(128)} %dynamic_slice.97.len_ref, bf16[3,1024,512]{2,1,0:T(8,128)(2,1)} %bitcast.195, bf16[3,1024,512]{2,1,0:T(8,128)(2,1)} %bitcast.196, bf16[3,1024,512]{2,1,0:T(8,128)(2,1)} %bitcast.197, bf16[1024,512]{1,0:T(8,128)(2,1)} %get-tuple-element.216.do_ref, ...), custom_call_target="tpu_custom_call" | custom-call | flops 8589934592 | bytes 3355443 | tf_op jit(solution)/shard_map/attend_back/pallas_call | solution.py:309
  313.0 15.0 %weight_grad.1 = (bf16[1024,1024]{1,0:T(8,128)(2,1)}, bf16[1024,1024]{1,0:T(8,128)(2,1)}, bf16[1024,1024]{1,0:T(8,128)(2,1)}, bf16[1024,1024]{1,0:T(8,128)(2,1)}, f32[3,1,512]{2,1,0:T(1,128)}) custom-call(bf16[1024,2048]{1,0:T(8,128)(2,1)} %bitcast.149, bf16[1024,2048]{1,0:T(8,128)(2,1)} %all-gather.5.cloned.1.call-done.g_ref.left_ref, ...), custom_call_target="tpu_custom_call" | custom-call | flops 3435973888 | bytes 8388608 | tf_op jit(solution)/shard_map/weight_grad/pallas_call | solution.py:595
  328.1 12.2 %ln_grad.1 = bf16[1024,2048]{1,0:T(8,128)(2,1)} custom-call(bf16[3,1024,512]{2,1,0:T(8,128)(2,1)} %attend_back.1.grad_ref, bf16[4,2048,512]{2,1,0:T(8,128)(2,1)} %get-tuple-element.182.wo_ref.w_ref, f32[1024,2048]{1,0:T(8,128)} %get-tuple-element.225.sum_ref), custom_call_target="tpu_custom_call" | custom-call | flops 2576980480 | bytes 9227468 | tf_op jit(solution)/shard_map/ln_grad/pallas_call | solution.py:552
  347.6 3.5 give.8
  363.1 14.4 %collective-permute-done.40.refs_2_ = bf16[512,1024]{1,0:T(8,128)(2,1)} collective-permute-done((bf16[512,1024]{1,0:T(8,128)(2,1)}, bf16[512,1024]{1,0:T(8,128)(2,1)}, u32[]{:S(2)}, u32[]{:S(2)}) %collective-permute-start.40) | collective-permute-done | bytes 1048608 | tf_op jit(solution)/shard_map/ppermute | solution.py:829
  378.1 3.7 finish.1
  385.5 3.9 collective-permute-done.44.refs_3_
  391.4 9.2 %collective-permute-done.46.refs_3_ = bf16[256,1024]{1,0:T(8,128)(2,1)} collective-permute-done((bf16[256,1024]{1,0:T(8,128)(2,1)}, bf16[256,1024]{1,0:T(8,128)(2,1)}, u32[]{:S(2)}, u32[]{:S(2)}) %collective-permute-start.46) | collective-permute-done | bytes 524320 | tf_op jit(solution)/shard_map/ppermute | solution.py:829
  400.6 3.6 final.2
  404.2 3.6 final.3
  411.4 3.8 final_attention.1
  415.3 5.1 %norm_back.1 = (bf16[128,2048]{1,0:T(8,128)(2,1)}, bf16[128,2048]{1,0:T(8,128)(2,1)}, f32[2,2048]{1,0:T(2,128)}) custom-call(s32[3]{0:T(128)} %pad_add_fusion.at_ref, bf16[256,2048]{1,0:T(8,128)(2,1)} %reduce-scatter.5.cloned.1.call-done.sum_ref, bf16[256,2048]{1,0:T(8,128)(2,1)} %pad_maximum_fusion.6.rows_ref, bf16[256,2048]{1,0:T(8,128)(2,1)} %bitcast.150, ...), custom_call_target="tpu_custom_call" | custom-call | flops 4194304 | bytes 1677721 | tf_op jit(solution)/shard_map/norm_back/pallas_call | solution.py:699
  428.0 3.4 collective-permute-done.51
  431.3 4.4 collective-permute-done.48
  453.3 5.2 %collective-permute-done.55 = bf16[128,2048]{1,0:T(8,128)(2,1)S(1)} collective-permute-done((bf16[128,2048]{1,0:T(8,128)(2,1)S(1)}, bf16[128,2048]{1,0:T(8,128)(2,1)S(1)}, u32[]{:S(2)}, u32[]{:S(2)}) %collective-permute-start.55) | collective-permute-done | bytes 524320 | tf_op jit(solution)/shard_map/ppermute | solution.py:829
  458.6 3.4 collective-permute-done.54
  (330 shorter events, 134.0 us)
Async XLA Ops:
  7.2 124.8 %all-gather.3.cloned.1.call-start = ((), (), s32[]{:S(2)}) async-start(), calls=%async_computation.2 | async-start | bytes 5242880 | tf_op jit(solution)/shard_map/all_gather | solution.py:1008
  8.6 15.0 %collective-permute-start.3 = (bf16[128,2048]{1,0:T(8,128)(2,1)S(1)}, bf16[128,2048]{1,0:T(8,128)(2,1)S(1)}, u32[]{:S(2)}, u32[]{:S(2)}) collective-permute-start(bf16[128,2048]{1,0:T(8,128)(2,1)S(1)} %get-tuple-element.292), channel_id=1, source_target_pairs={{0,16},{4,20},{8,24},{12,28},{16,0},{20,4},{24,8},{28,12},{1,17},{... | collective-permute-start | bytes 1572872 | tf_op jit(solution)/shard_map/ppermute | solution.py:829
  52.8 163.0 %all-gather.5.cloned.1.call-start = ((), (), s32[]{:S(2)}) async-start(), calls=%async_computation.3 | async-start | bytes 5242880 | tf_op jit(solution)/shard_map/all_gather | solution.py:1052
  58.6 24.6 %collective-permute-start.8 = (bf16[272,1024]{1,0:T(8,128)(2,1)}, bf16[272,1024]{1,0:T(8,128)(2,1)}, u32[]{:S(2)}, u32[]{:S(2)}) collective-permute-start(bf16[272,1024]{1,0:T(8,128)(2,1)} %pad_maximum_fusion.9.rest_0_), channel_id=1, source_target_pairs={{0,8},{4,12},{8,0},{12,4},{16,24},{20,28},{24,16},{28,20},{1,9},{5... | collective-permute-start | bytes 1671176 | tf_op jit(solution)/shard_map/ppermute | solution.py:829
  59.1 33.8 %collective-permute-start.12 = (bf16[272,1024]{1,0:T(8,128)(2,1)}, bf16[272,1024]{1,0:T(8,128)(2,1)}, u32[]{:S(2)}, u32[]{:S(2)}) collective-permute-start(bf16[272,1024]{1,0:T(8,128)(2,1)} %pad_maximum_fusion.9.rest_0_), channel_id=1, source_target_pairs={{0,16},{4,20},{8,24},{12,28},{16,0},{20,4},{24,8},{28,12},{1,17},{... | collective-permute-start | bytes 1671176 | tf_op jit(solution)/shard_map/ppermute | solution.py:829
  60.5 22.6 %collective-permute-start.9 = (bf16[256,1024]{1,0:T(8,128)(2,1)}, bf16[256,1024]{1,0:T(8,128)(2,1)}, u32[]{:S(2)}, u32[]{:S(2)}) collective-permute-start(bf16[256,1024]{1,0:T(8,128)(2,1)} %pad_maximum_fusion.10.rest_8_), channel_id=1, source_target_pairs={{0,16},{4,20},{8,24},{12,28},{16,0},{20,4},{24,8},{28,12},{1,17},{... | collective-permute-start | bytes 1572872 | tf_op jit(solution)/shard_map/ppermute | solution.py:829
  61.1 31.2 %collective-permute-start.14 = (bf16[256,1024]{1,0:T(8,128)(2,1)}, bf16[256,1024]{1,0:T(8,128)(2,1)}, u32[]{:S(2)}, u32[]{:S(2)}) collective-permute-start(bf16[256,1024]{1,0:T(8,128)(2,1)} %pad_maximum_fusion.10.rest_8_), channel_id=1, source_target_pairs={{0,8},{4,12},{8,0},{12,4},{16,24},{20,28},{24,16},{28,20},{1,9},{5... | collective-permute-start | bytes 1572872 | tf_op jit(solution)/shard_map/ppermute | solution.py:829
  83.1 15.9 %collective-permute-start.13 = (bf16[272,1024]{1,0:T(8,128)(2,1)}, bf16[272,1024]{1,0:T(8,128)(2,1)}, u32[]{:S(2)}, u32[]{:S(2)}) collective-permute-start(bf16[272,1024]{1,0:T(8,128)(2,1)} %collective-permute-done.8.rest_1_), channel_id=1, source_target_pairs={{0,16},{4,20},{8,24},{12,28},{16,0},{20,4},{24,8},{28,12},{1,17},{... | collective-permute-start | bytes 1671176 | tf_op jit(solution)/shard_map/ppermute | solution.py:829
  84.6 14.3 %collective-permute-start.15 = (bf16[256,1024]{1,0:T(8,128)(2,1)}, bf16[256,1024]{1,0:T(8,128)(2,1)}, u32[]{:S(2)}, u32[]{:S(2)}) collective-permute-start(bf16[256,1024]{1,0:T(8,128)(2,1)} %collective-permute-done.9.rest_9_), channel_id=1, source_target_pairs={{0,8},{4,12},{8,0},{12,4},{16,24},{20,28},{24,16},{28,20},{1,9},{5... | collective-permute-start | bytes 1572872 | tf_op jit(solution)/shard_map/ppermute | solution.py:829
  88.2 239.8 %reduce-scatter.3.cloned.1.call-start = ((), (), s32[]{:S(2)}) async-start(), calls=%async_computation.4 | async-start | bytes 5242880 | tf_op jit(solution)/shard_map/reduce_scatter | solution.py:1087
  91.7 24.7 %collective-permute-start.10 = (bf16[256,2048]{1,0:T(8,128)(2,1)S(1)}, bf16[256,2048]{1,0:T(8,128)(2,1)S(1)}, u32[]{:S(2)}, u32[]{:S(2)}) collective-permute-start(bf16[256,2048]{1,0:T(8,128)(2,1)S(1)} %copy-done.1), channel_id=1, source_target_pairs={{0,8},{4,12},{8,0},{12,4},{16,24},{20,28},{24,16},{28,20},{1,9},{5... | collective-permute-start | bytes 3145736 | tf_op jit(solution)/shard_map/ppermute | solution.py:829
  92.3 24.5 %collective-permute-start.11 = (bf16[256,2048]{1,0:T(8,128)(2,1)S(1)}, bf16[256,2048]{1,0:T(8,128)(2,1)}, u32[]{:S(2)}, u32[]{:S(2)}) collective-permute-start(bf16[256,2048]{1,0:T(8,128)(2,1)S(1)} %copy-done.2), channel_id=1, source_target_pairs={{0,16},{4,20},{8,24},{12,28},{16,0},{20,4},{24,8},{28,12},{1,17},{... | collective-permute-start | bytes 3145736 | tf_op jit(solution)/shard_map/ppermute | solution.py:829
  122.0 52.9 %collective-permute-start.28 = (bf16[512,2048]{1,0:T(8,128)(2,1)}, bf16[512,2048]{1,0:T(8,128)(2,1)}, u32[]{:S(2)}, u32[]{:S(2)}) collective-permute-start(bf16[512,2048]{1,0:T(8,128)(2,1)} %pad_maximum_fusion.2), channel_id=1, source_target_pairs={{0,16},{4,20},{8,24},{12,28},{16,0},{20,4},{24,8},{28,12},{1,17},{... | collective-permute-start | bytes 6291464 | tf_op jit(solution)/shard_map/ppermute | solution.py:829
  123.4 51.5 %collective-permute-start.29 = (bf16[512,2048]{1,0:T(8,128)(2,1)}, bf16[512,2048]{1,0:T(8,128)(2,1)}, u32[]{:S(2)}, u32[]{:S(2)}) collective-permute-start(bf16[512,2048]{1,0:T(8,128)(2,1)} %pad_maximum_fusion.3), channel_id=1, source_target_pairs={{0,8},{4,12},{8,0},{12,4},{16,24},{20,28},{24,16},{28,20},{1,9},{5... | collective-permute-start | bytes 6291464 | tf_op jit(solution)/shard_map/ppermute | solution.py:829
  124.9 16.0 %collective-permute-start.25 = (bf16[256,1024]{1,0:T(8,128)(2,1)}, bf16[256,1024]{1,0:T(8,128)(2,1)}, u32[]{:S(2)}, u32[]{:S(2)}) collective-permute-start(bf16[256,1024]{1,0:T(8,128)(2,1)} %collective-permute-done.9.rest_9_), channel_id=1, source_target_pairs={{0,4},{4,0},{8,12},{12,8},{16,20},{20,16},{24,28},{28,24},{1,5},{5... | collective-permute-start | bytes 1572872 | tf_op jit(solution)/shard_map/ppermute | solution.py:829
  125.0 16.0 %collective-permute-start.26 = (bf16[256,1024]{1,0:T(8,128)(2,1)}, bf16[256,1024]{1,0:T(8,128)(2,1)S(1)}, u32[]{:S(2)}, u32[]{:S(2)}) collective-permute-start(bf16[256,1024]{1,0:T(8,128)(2,1)} %collective-permute-done.14.rest_10_), channel_id=1, source_target_pairs={{0,4},{4,0},{8,12},{12,8},{16,20},{20,16},{24,28},{28,24},{1,5},{5... | collective-permute-start | bytes 1572872 | tf_op jit(solution)/shard_map/ppermute | solution.py:829
  127.3 13.7 %collective-permute-start.27 = (bf16[256,1024]{1,0:T(8,128)(2,1)}, bf16[256,1024]{1,0:T(8,128)(2,1)}, u32[]{:S(2)}, u32[]{:S(2)}) collective-permute-start(bf16[256,1024]{1,0:T(8,128)(2,1)} %collective-permute-done.15.rest_11_), channel_id=1, source_target_pairs={{0,4},{4,0},{8,12},{12,8},{16,20},{20,16},{24,28},{28,24},{1,5},{5... | collective-permute-start | bytes 1572872 | tf_op jit(solution)/shard_map/ppermute | solution.py:829
  215.9 199.4 %reduce-scatter.5.cloned.1.call-start = ((), (), s32[]{:S(2)}) async-start(), calls=%async_computation.5 | async-start | bytes 5242880 | tf_op jit(solution)/shard_map/reduce_scatter | solution.py:1120
  259.2 13.7 %collective-permute-start.33 = (bf16[1024,2048]{1,0:T(8,128)(2,1)}, bf16[1024,2048]{1,0:T(8,128)(2,1)}, u32[]{:S(2)}, u32[]{:S(2)}) collective-permute-start(bf16[1024,2048]{1,0:T(8,128)(2,1)} %get-tuple-element.203), channel_id=1, source_target_pairs={{0,4},{4,0},{8,12},{12,8},{16,20},{20,16},{24,28},{28,24},{1,5},{5... | collective-permute-start | bytes 12582920 | tf_op jit(solution)/shard_map/ppermute | solution.py:829
  276.2 51.8 %collective-permute-start.34 = (bf16[512,1024]{1,0:T(8,128)(2,1)}, bf16[512,1024]{1,0:T(8,128)(2,1)}, u32[]{:S(2)}, u32[]{:S(2)}) collective-permute-start(bf16[512,1024]{1,0:T(8,128)(2,1)} %get-tuple-element.210), channel_id=1, source_target_pairs={{0,8},{4,12},{8,0},{12,4},{16,24},{20,28},{24,16},{28,20},{1,9},{5... | collective-permute-start | bytes 3145736 | tf_op jit(solution)/shard_map/ppermute | solution.py:829
  277.5 50.5 %collective-permute-start.35 = (bf16[512,1024]{1,0:T(8,128)(2,1)}, bf16[512,1024]{1,0:T(8,128)(2,1)}, u32[]{:S(2)}, u32[]{:S(2)}) collective-permute-start(bf16[512,1024]{1,0:T(8,128)(2,1)} %get-tuple-element.211), channel_id=1, source_target_pairs={{0,16},{4,20},{8,24},{12,28},{16,0},{20,4},{24,8},{28,12},{1,17},{... | collective-permute-start | bytes 3145736 | tf_op jit(solution)/shard_map/ppermute | solution.py:829
  283.3 44.7 %collective-permute-start.36 = (bf16[512,1024]{1,0:T(8,128)(2,1)}, bf16[512,1024]{1,0:T(8,128)(2,1)}, u32[]{:S(2)}, u32[]{:S(2)}) collective-permute-start(bf16[512,1024]{1,0:T(8,128)(2,1)} %get-tuple-element.214), channel_id=1, source_target_pairs={{0,8},{4,12},{8,0},{12,4},{16,24},{20,28},{24,16},{28,20},{1,9},{5... | collective-permute-start | bytes 3145736 | tf_op jit(solution)/shard_map/ppermute | solution.py:829
  284.6 43.4 %collective-permute-start.37 = (bf16[512,1024]{1,0:T(8,128)(2,1)}, bf16[512,1024]{1,0:T(8,128)(2,1)}, u32[]{:S(2)}, u32[]{:S(2)}) collective-permute-start(bf16[512,1024]{1,0:T(8,128)(2,1)} %get-tuple-element.215), channel_id=1, source_target_pairs={{0,16},{4,20},{8,24},{12,28},{16,0},{20,4},{24,8},{28,12},{1,17},{... | collective-permute-start | bytes 3145736 | tf_op jit(solution)/shard_map/ppermute | solution.py:829
  351.1 26.4 %collective-permute-start.40 = (bf16[512,1024]{1,0:T(8,128)(2,1)}, bf16[512,1024]{1,0:T(8,128)(2,1)}, u32[]{:S(2)}, u32[]{:S(2)}) collective-permute-start(bf16[512,1024]{1,0:T(8,128)(2,1)} %get-tuple-element.230), channel_id=1, source_target_pairs={{0,8},{4,12},{8,0},{12,4},{16,24},{20,28},{24,16},{28,20},{1,9},{5... | collective-permute-start | bytes 3145736 | tf_op jit(solution)/shard_map/ppermute | solution.py:829
  351.8 30.0 %collective-permute-start.41 = (bf16[512,1024]{1,0:T(8,128)(2,1)}, bf16[512,1024]{1,0:T(8,128)(2,1)}, u32[]{:S(2)}, u32[]{:S(2)}) collective-permute-start(bf16[512,1024]{1,0:T(8,128)(2,1)} %get-tuple-element.231), channel_id=1, source_target_pairs={{0,16},{4,20},{8,24},{12,28},{16,0},{20,4},{24,8},{28,12},{1,17},{... | collective-permute-start | bytes 3145736 | tf_op jit(solution)/shard_map/ppermute | solution.py:829
  355.5 33.9 %collective-permute-start.44 = (bf16[256,1024]{1,0:T(8,128)(2,1)}, bf16[256,1024]{1,0:T(8,128)(2,1)}, u32[]{:S(2)}, u32[]{:S(2)}) collective-permute-start(bf16[256,1024]{1,0:T(8,128)(2,1)} %get-tuple-element.235), channel_id=1, source_target_pairs={{0,16},{4,20},{8,24},{12,28},{16,0},{20,4},{24,8},{28,12},{1,17},{... | collective-permute-start | bytes 1572872 | tf_op jit(solution)/shard_map/ppermute | solution.py:829
  358.2 33.2 %collective-permute-start.45 = (bf16[256,1024]{1,0:T(8,128)(2,1)}, bf16[256,1024]{1,0:T(8,128)(2,1)}, u32[]{:S(2)}, u32[]{:S(2)}) collective-permute-start(bf16[256,1024]{1,0:T(8,128)(2,1)} %get-tuple-element.236), channel_id=1, source_target_pairs={{0,8},{4,12},{8,0},{12,4},{16,24},{20,28},{24,16},{28,20},{1,9},{5... | collective-permute-start | bytes 1572872 | tf_op jit(solution)/shard_map/ppermute | solution.py:829
  362.6 38.0 %collective-permute-start.46 = (bf16[256,1024]{1,0:T(8,128)(2,1)}, bf16[256,1024]{1,0:T(8,128)(2,1)}, u32[]{:S(2)}, u32[]{:S(2)}) collective-permute-start(bf16[256,1024]{1,0:T(8,128)(2,1)} %get-tuple-element.240), channel_id=1, source_target_pairs={{0,16},{4,20},{8,24},{12,28},{16,0},{20,4},{24,8},{28,12},{1,17},{... | collective-permute-start | bytes 1572872 | tf_op jit(solution)/shard_map/ppermute | solution.py:829
  377.5 23.1 %collective-permute-start.47 = (bf16[256,1024]{1,0:T(8,128)(2,1)}, bf16[256,1024]{1,0:T(8,128)(2,1)}, u32[]{:S(2)}, u32[]{:S(2)}) collective-permute-start(bf16[256,1024]{1,0:T(8,128)(2,1)} %get-tuple-element.241), channel_id=1, source_target_pairs={{0,8},{4,12},{8,0},{12,4},{16,24},{20,28},{24,16},{28,20},{1,9},{5... | collective-permute-start | bytes 1572872 | tf_op jit(solution)/shard_map/ppermute | solution.py:829
  384.9 25.8 %collective-permute-start.42 = (bf16[256,1024]{1,0:T(8,128)(2,1)}, bf16[256,1024]{1,0:T(8,128)(2,1)S(1)}, u32[]{:S(2)}, u32[]{:S(2)}) collective-permute-start(bf16[256,1024]{1,0:T(8,128)(2,1)} %get-tuple-element.249), channel_id=1, source_target_pairs={{0,16},{4,20},{8,24},{12,28},{16,0},{20,4},{24,8},{28,12},{1,17},{... | collective-permute-start | bytes 1572872 | tf_op jit(solution)/shard_map/ppermute | solution.py:829
  389.4 21.2 %collective-permute-start.43 = (bf16[256,1024]{1,0:T(8,128)(2,1)}, bf16[256,1024]{1,0:T(8,128)(2,1)}, u32[]{:S(2)}, u32[]{:S(2)}) collective-permute-start(bf16[256,1024]{1,0:T(8,128)(2,1)} %get-tuple-element.250), channel_id=1, source_target_pairs={{0,8},{4,12},{8,0},{12,4},{16,24},{20,28},{24,16},{28,20},{1,9},{5... | collective-permute-start | bytes 1572872 | tf_op jit(solution)/shard_map/ppermute | solution.py:829
  444.7 13.8 %collective-permute-start.55 = (bf16[128,2048]{1,0:T(8,128)(2,1)S(1)}, bf16[128,2048]{1,0:T(8,128)(2,1)S(1)}, u32[]{:S(2)}, u32[]{:S(2)}) collective-permute-start(bf16[128,2048]{1,0:T(8,128)(2,1)S(1)} %get-tuple-element.276), channel_id=1, source_target_pairs={{0,8},{4,12},{8,0},{12,4},{16,24},{20,28},{24,16},{28,20},{1,9},{5... | collective-permute-start | bytes 1572872 | tf_op jit(solution)/shard_map/ppermute | solution.py:829
  (63 other events, 369.6 us)
Sparse Core Ops, SparseCore 0:
  52.9 78.9 all-gather.2
  133.5 79.2 all-gather.4
  216.0 75.4 reduce-scatter.2
  340.4 73.2 reduce-scatter.4
